TPU v7x, 256 devices: a whole 4x4x8 slice. The times are simulated.
256 devices in a mesh: gx: 16 (over z, y_hi), gy: 4 (over y_lo, core), gz: 4 (over x).
Axes of the slice: x: 4, y: 4 (y_hi: 2, y_lo: 2; y = y_hi * 2 + y_lo), z: 8, core: 2. Of those that a mesh axis runs over, the one named last changes fastest.
Arguments:
- electric: float32 [3, 256, 128, 512], P(None, 'gz', 'gx', 'gy'), may hold values from -6 to 6
- magnetic: float32 [3, 256, 128, 512], P(None, 'gz', 'gx', 'gy'), may hold values from -6 to 6
- material: int32 [256, 128, 512], P('gz', 'gx', 'gy'), may hold values from 0 to 7
- layer_map: int32 [256], P('gz'), may hold values from 0 to 3
- permittivity: float32 [4, 8], replicated, may hold values from 1.5 to 5
- conductivity: float32 [4, 8], replicated, may hold values from 0.05 to 2
Outputs:
- electric_next: float32 [3, 256, 128, 512], P(None, 'gz', 'gx', 'gy')
- magnetic_next: float32 [3, 256, 128, 512], P(None, 'gz', 'gx', 'gy')
All inputs are finite; a program needn't handle non-finite values.
Results may differ from a plain program's by a relative error of at most 0.0015.
Values sent between devices are 32-bit elements; how exact they have to be, the bound alone decides.
A program may use at most 64 MiB of HBM per device.

v0:
```python
import jax
import jax.numpy as jnp
from jax import lax
from jax.sharding import PartitionSpec as P
from jax.experimental import pallas as pl
from jax.experimental.pallas import tpu as pltpu

time_step = 0.5
z_courant = 128.0


def from_prev(block, axis):
    count = lax.axis_size(axis)
    return lax.ppermute(block, axis, [(i, i + 1) for i in range(count - 1)])


def from_next(block, axis):
    count = lax.axis_size(axis)
    return lax.ppermute(block, axis, [(i + 1, i) for i in range(count - 1)])


def from_diagonal(block, axes, step_a, step_b):
    size_a = lax.axis_size(axes[0])
    size_b = lax.axis_size(axes[1])
    pairs = []
    for a in range(size_a):
        for b in range(size_b):
            src_a, src_b = a - step_a, b - step_b
            if 0 <= src_a < size_a and 0 <= src_b < size_b:
                pairs.append((src_a * size_b + src_b, a * size_b + b))
    return lax.ppermute(block, axes, pairs)


def lookup(table_values, layer_map, material):
    kind_count, entry_count = table_values.shape
    layer_hot = layer_map[:, None] == lax.broadcasted_iota(jnp.int32, (1, kind_count), 1)
    table_rows = jnp.sum(jnp.where(layer_hot[:, :, None], table_values[None], 0.0), axis=1)
    result = jnp.zeros(material.shape, jnp.float32)
    for entry_index in range(entry_count):
        result = result + jnp.where(
            material == entry_index, table_rows[:, entry_index][:, None, None], 0.0
        )
    return result


def rates(epsilon_cell, sigma_cell):
    half_loss = 0.25 * sigma_cell / epsilon_cell
    drive_rate = 1.0 / (1.0 + half_loss)
    keep_rate = (1.0 - half_loss) * drive_rate
    curl_rate = 0.5 * drive_rate / epsilon_cell
    z_rate = z_courant * drive_rate / epsilon_cell
    stiffness = 4096.0 * drive_rate / epsilon_cell
    return (keep_rate, curl_rate, z_rate, stiffness)


def thomas_kernel(stiff_ref, diag_ref, sx_ref, sy_ref, px_ref, py_ref, lw_ref, hw_ref, ur_ref):
    depth = stiff_ref.shape[0]
    stiff = stiff_ref[0]
    inv = 1.0 / diag_ref[0]
    ur_ref[0] = -stiff * inv
    px_ref[0] = sx_ref[0] * inv
    py_ref[0] = sy_ref[0] * inv
    lw_ref[0] = inv

    def forward(z, carry):
        upper, value_x, value_y, value_low, unused = carry
        stiff = stiff_ref[z]
        inv = 1.0 / (diag_ref[z] + stiff * upper)
        upper = -stiff * inv
        value_x = (sx_ref[z] + stiff * value_x) * inv
        value_y = (sy_ref[z] + stiff * value_y) * inv
        value_low = (stiff * value_low) * inv
        ur_ref[z] = upper
        px_ref[z] = value_x
        py_ref[z] = value_y
        lw_ref[z] = value_low
        return upper, value_x, value_y, value_low, inv

    first = (ur_ref[0], px_ref[0], py_ref[0], lw_ref[0], inv)
    last_x, last_y, last_low, last_high = lax.fori_loop(1, depth, forward, first, unroll=8)[1:]
    low_scale = stiff_ref[0]
    high_scale = stiff_ref[depth - 1]
    lw_ref[depth - 1] = low_scale * last_low
    hw_ref[depth - 1] = high_scale * last_high

    def backward(step, carry):
        z = depth - 2 - step
        next_x, next_y, next_low, next_high = carry
        upper = ur_ref[z]
        next_x = px_ref[z] - upper * next_x
        next_y = py_ref[z] - upper * next_y
        next_low = lw_ref[z] - upper * next_low
        next_high = -upper * next_high
        px_ref[z] = next_x
        py_ref[z] = next_y
        lw_ref[z] = low_scale * next_low
        hw_ref[z] = high_scale * next_high
        return next_x, next_y, next_low, next_high

    lax.fori_loop(0, depth - 1, backward, (last_x, last_y, last_low, last_high), unroll=8)


def solve_slab(stiffness, diagonal, source_x, source_y):
    shape = jax.ShapeDtypeStruct(stiffness.shape, jnp.float32)
    return pl.pallas_call(
        thomas_kernel,
        out_shape=(shape, shape, shape, shape),
        scratch_shapes=[pltpu.VMEM(stiffness.shape, jnp.float32)],
    )(stiffness, diagonal, source_x, source_y)


def advance(pieces, incoming, factor):
    rows_first, rows_last, low_first, low_last, high_first, high_last = pieces
    denominator = 1.0 - low_first * factor
    offset = (rows_first + low_first[None] * incoming) / denominator[None]
    coupling = high_first / denominator
    outgoing = rows_last + low_last[None] * (incoming + factor[None] * offset)
    factor_out = low_last * factor * coupling + high_last
    return (offset, coupling, outgoing, factor_out)


def body(electric, magnetic, material, layer_map, permittivity, conductivity):
    epsilon_cell = lookup(permittivity, layer_map, material)
    sigma_cell = lookup(conductivity, layer_map, material)
    keep_rate, curl_rate, z_rate, stiffness = rates(epsilon_cell, sigma_cell)
    depth_rows, span_x, span_y = material.shape
    slab = lax.axis_index("gz")
    bottom = slab == 0
    first_x = lax.axis_index("gx") == 0
    first_y = lax.axis_index("gy") == 0
    electric_x, electric_y, electric_z = (electric[0], electric[1], electric[2])
    magnetic_x, magnetic_y, magnetic_z = (magnetic[0], magnetic[1], magnetic[2])

    x_high = from_next(jnp.stack([electric_y[:, :1], electric_z[:, :1]]), "gx")
    x_low = from_prev(
        jnp.stack([electric_x[:, -1:], electric_y[:, -1:], magnetic_z[:, -1:]]), "gx"
    )
    y_high = from_next(jnp.stack([electric_x[:, :, :1], electric_z[:, :, :1]]), "gy")
    y_low = from_prev(
        jnp.stack([electric_x[:, :, -1:], electric_y[:, :, -1:], magnetic_z[:, :, -1:]]), "gy"
    )
    z_low = from_prev(
        jnp.stack(
            [electric_x[-1:], electric_y[-1:], electric_z[-1:], magnetic_x[-1:], magnetic_y[-1:]]
        ),
        "gz",
    )
    z_high = from_next(jnp.stack([electric_x[:1], electric_y[:1]]), "gz")
    corner_ex = from_diagonal(electric_x[:, -1:, :1], ("gx", "gy"), 1, -1)
    corner_ey = from_diagonal(electric_y[:, :1, -1:], ("gx", "gy"), -1, 1)
    corner_zx = from_diagonal(electric_z[-1:, :1, :], ("gx", "gz"), -1, 1)
    corner_zy = from_diagonal(electric_z[-1:, :, :1], ("gy", "gz"), -1, 1)

    ey_xh, ez_xh = x_high[0], x_high[1]
    ex_xl, ey_xl, hz_xl = x_low[0], x_low[1], x_low[2]
    ex_yh, ez_yh = y_high[0], y_high[1]
    ex_yl, ey_yl, hz_yl = y_low[0], y_low[1], y_low[2]
    ex_zl, ey_zl, ez_zl, hx_zl, hy_zl = z_low[0], z_low[1], z_low[2], z_low[3], z_low[4]
    ex_zh, ey_zh = z_high[0], z_high[1]

    ey_next_x = jnp.concatenate([electric_y[:, 1:], ey_xh], axis=1)
    ex_next_y = jnp.concatenate([electric_x[:, :, 1:], ex_yh], axis=2)
    face_term = (ey_next_x - electric_y) - (ex_next_y - electric_x)
    magnetic_z_new = magnetic_z - time_step * face_term
    ey_yl_next_x = jnp.concatenate([ey_yl[:, 1:], corner_ey], axis=1)
    face_yl = (ey_yl_next_x - ey_yl) - (electric_x[:, :, :1] - ex_yl)
    hz_new_yl = jnp.where(first_y, 0.0, hz_yl - time_step * face_yl)
    ex_xl_next_y = jnp.concatenate([ex_xl[:, :, 1:], corner_ex], axis=2)
    face_xl = (electric_y[:, :1] - ey_xl) - (ex_xl_next_y - ex_xl)
    hz_new_xl = jnp.where(first_x, 0.0, hz_xl - time_step * face_xl)
    hz_before_y = jnp.concatenate([hz_new_yl, magnetic_z_new[:, :, :-1]], axis=2)
    hz_before_x = jnp.concatenate([hz_new_xl, magnetic_z_new[:, :-1]], axis=1)

    ez_next_x = jnp.concatenate([electric_z[:, 1:], ez_xh], axis=1)
    ez_next_y = jnp.concatenate([electric_z[:, :, 1:], ez_yh], axis=2)
    slope_zx = ez_next_x - electric_z
    slope_zy = ez_next_y - electric_z
    slope_zx_below = jnp.concatenate([ez_zl[:, 1:], corner_zx], axis=1) - ez_zl
    slope_zy_below = jnp.concatenate([ez_zl[:, :, 1:], corner_zy], axis=2) - ez_zl

    def second_z(field, below, above):
        column = jnp.concatenate([below, field, above], axis=0)
        rise_steps = column[1:] - column[:-1]
        level_index = lax.broadcasted_iota(jnp.int32, rise_steps.shape, 0)
        rise_steps = jnp.where(jnp.logical_and(bottom, level_index == 0), 0.0, rise_steps)
        return rise_steps[1:] - rise_steps[:-1]

    def down_z(field, below):
        return field - jnp.concatenate([below, field[:-1]], axis=0)

    quarter_z = 0.25 * z_rate
    source_x = (
        keep_rate * electric_x
        + stiffness * second_z(electric_x, ex_zl, ex_zh)
        + curl_rate * (magnetic_z_new - hz_before_y)
        - z_rate * down_z(magnetic_y, hy_zl)
        - quarter_z * down_z(slope_zx, slope_zx_below)
    )
    source_y = (
        keep_rate * electric_y
        + stiffness * second_z(electric_y, ey_zl, ey_zh)
        + z_rate * down_z(magnetic_x, hx_zl)
        - quarter_z * down_z(slope_zy, slope_zy_below)
        - curl_rate * (magnetic_z_new - hz_before_x)
    )
    level_index = lax.broadcasted_iota(jnp.int32, stiffness.shape, 0)
    diagonal = 1.0 + 2.0 * stiffness
    diagonal = jnp.where(jnp.logical_and(bottom, level_index == 0), 1.0 + stiffness, diagonal)
    partial_x, partial_y, low_weight, high_weight = solve_slab(
        stiffness, diagonal, source_x, source_y
    )

    own = jnp.concatenate(
        [
            jnp.stack([partial_x[0], partial_y[0], partial_x[-1], partial_y[-1]]),
            jnp.stack([low_weight[0], low_weight[-1], high_weight[0], high_weight[-1]]),
        ],
        axis=0,
    )
    slab_count = lax.axis_size("gz")
    gathered = [own]
    for shift in range(1, slab_count):
        gathered.append(
            lax.ppermute(own, "gz", [(i, (i + shift) % slab_count) for i in range(slab_count)])
        )
    gathered = jnp.stack(gathered)
    slabs = []
    for index in range(slab_count):
        chosen = lax.dynamic_index_in_dim(
            gathered, (slab - index) % slab_count, axis=0, keepdims=False
        )
        slabs.append(
            (chosen[0:2], chosen[2:4], chosen[4], chosen[5], chosen[6], chosen[7])
        )

    incoming_all = []
    factor_all = []
    offset_all = []
    coupling_all = []
    incoming = jnp.zeros((2,) + partial_x.shape[1:], jnp.float32)
    factor = jnp.zeros_like(low_weight[0])
    for index in range(slab_count):
        if index > 0:
            incoming, factor = outgoing, factor_out
        offset, coupling, outgoing, factor_out = advance(slabs[index], incoming, factor)
        incoming_all.append(incoming)
        factor_all.append(factor)
        offset_all.append(offset)
        coupling_all.append(coupling)
    following_all = [None] * slab_count
    leading_all = [None] * slab_count
    following = jnp.zeros((2,) + partial_x.shape[1:], jnp.float32)
    for index in reversed(range(slab_count)):
        if index < slab_count - 1:
            following = leading_all[index + 1]
        following_all[index] = following
        leading_all[index] = offset_all[index] + coupling_all[index][None] * following

    def pick(values):
        return lax.dynamic_index_in_dim(jnp.stack(values), slab, axis=0, keepdims=False)

    incoming = pick(incoming_all)
    factor = pick(factor_all)
    following = pick(following_all)
    leading = pick(leading_all)

    previous_last = incoming + factor[None] * leading
    electric_x_new = (
        partial_x + previous_last[0][None] * low_weight + following[0][None] * high_weight
    )
    electric_y_new = (
        partial_y + previous_last[1][None] * low_weight + following[1][None] * high_weight
    )
    sum_x = electric_x + electric_x_new
    sum_y = electric_y + electric_y_new
    top_x = ex_zh[0] + following[0]
    top_y = ey_zh[0] + following[1]
    rise_x = jnp.concatenate([sum_x[1:], top_x[None]], axis=0) - sum_x
    rise_y = jnp.concatenate([sum_y[1:], top_y[None]], axis=0) - sum_y
    magnetic_y_new = magnetic_y - 0.5 * z_courant * rise_x + time_step * slope_zx
    magnetic_x_new = magnetic_x - time_step * slope_zy + 0.5 * z_courant * rise_y
    before_hy = from_prev(magnetic_y_new[:, -1:, :], "gx")
    before_hx = from_prev(magnetic_x_new[:, :, -1:], "gy")
    change_hy = magnetic_y_new - jnp.concatenate([before_hy, magnetic_y_new[:, :-1]], axis=1)
    change_hx = magnetic_x_new - jnp.concatenate([before_hx, magnetic_x_new[:, :, :-1]], axis=2)
    electric_z_new = keep_rate * electric_z + curl_rate * (change_hy - change_hx)
    return (
        jnp.stack([electric_x_new, electric_y_new, electric_z_new]),
        jnp.stack([magnetic_x_new, magnetic_y_new, magnetic_z_new]),
    )


def solution(mesh):
    return jax.shard_map(
        body,
        mesh=mesh,
        in_specs=(
            P(None, "gz", "gx", "gy"),
            P(None, "gz", "gx", "gy"),
            P("gz", "gx", "gy"),
            P("gz"),
            P(),
            P(),
        ),
        out_specs=(P(None, "gz", "gx", "gy"), P(None, "gz", "gx", "gy")),
        check_vma=False,
    )
```

profile of v0, /device:TPU:131, one launch (start us, length us, event | category | flops | bytes accessed | tf_op | source)
XLA Modules:
  0.0 117.1 jit_solution(4241869473105768169)
XLA Ops:
  2.0 3.1 %collective-permute-start.1 = (f32[5,1,8,128]{3,2,1,0:T(8,128)}, f32[5,1,8,128]{3,2,1,0:T(8,128)}, u32[]{:S(2)}, u32[]{:S(2)}) collective-permute-start(f32[5,1,8,128]{3,2,1,0:T(8,128)} %pad_maximum_fusion.8), channel_id=1, source_target_pairs={{0,1},{1,2},{2,3},{4,5},{5,6},{6,7},{8,9},{9,10},{10,11},{12,13},{... | collective-permute-start | bytes 61448 | tf_op jit(solution)/shard_map/ppermute | solution.py:14
  5.8 2.7 %collective-permute-start = (f32[2,1,8,128]{3,2,1,0:T(8,128)S(1)}, f32[2,1,8,128]{3,2,1,0:T(8,128)S(1)}, u32[]{:S(2)}, u32[]{:S(2)}) collective-permute-start(f32[2,1,8,128]{3,2,1,0:T(8,128)S(1)} %stack.118), channel_id=1, source_target_pairs={{1,0},{2,1},{3,2},{5,4},{6,5},{7,6},{9,8},{10,9},{11,10},{13,12},{... | collective-permute-start | bytes 24584 | tf_op jit(solution)/shard_map/ppermute | solution.py:19
  8.5 1.2 slice_bitcast_fusion.3
  10.4 4.4 %collective-permute-start.2 = (f32[2,64,1,128]{3,1,2,0:T(8,128)}, f32[2,64,1,128]{3,1,2,0:T(8,128)}, u32[]{:S(2)}, u32[]{:S(2)}) collective-permute-start(f32[2,64,1,128]{3,1,2,0:T(8,128)} %pad_maximum_fusion.7), channel_id=1, source_target_pairs={{16,0},{32,16},{48,32},{64,48},{80,64},{96,80},{112,96},{128,112},... | collective-permute-start | bytes 196616 | tf_op jit(solution)/shard_map/ppermute | solution.py:19
  15.2 1.1 copy.756
  16.3 3.4 %collective-permute-start.3 = (f32[2,64,8,1]{3,1,2,0:T(8,128)}, f32[2,64,8,1]{3,1,2,0:T(8,128)}, u32[]{:S(2)}, u32[]{:S(2)}) collective-permute-start(f32[2,64,8,1]{3,1,2,0:T(8,128)} %copy.756), channel_id=1, source_target_pairs={{4,0},{8,4},{12,8},{5,1},{9,5},{13,9},{6,2},{10,6},{14,10},{7,3},{... | collective-permute-start | bytes 12296 | tf_op jit(solution)/shard_map/ppermute | solution.py:19
  20.4 2.0 %collective-permute-start.9 = (f32[64,1,1]{2,0,1:T(8,128)}, f32[64,1,1]{2,0,1:T(8,128)}, u32[]{:S(2)}, u32[]{:S(2)}) collective-permute-start(f32[64,1,1]{2,0,1:T(8,128)} %slice.557), channel_id=1, source_target_pairs={{4,16},{8,20},{12,24},{20,32},{24,36},{28,40},{36,48},{40,52},{44,... | collective-permute-start | bytes 776 | tf_op jit(solution)/shard_map/ppermute | solution.py:31
  25.8 1.0 copy_compare_fusion.7
  27.6 2.4 %fusion.86 = (f32[64,8,128]{2,0,1:T(8,128)}, f32[64,8,128]{2,0,1:T(8,128)S(1)}, f32[64,8,128]{2,0,1:T(8,128)S(1)}) fusion(f32[1,64,8,128]{3,2,1,0:T(8,128)S(1)} %get-tuple-element.61, pred[64,8,128]{2,0,1:T(8,128)(4,1)} %get-tuple-element.83, f32[64]{0:T(128)S(1)} %get-tuple-element.131, pred[64,8,128]{2,0,1:T(8,128)(4,1)} %get-tuple-element.82, ...), kind=kLoop, calls=%fused_computation.261 | loop fusion | flops 2424832 | bytes 1576960 | tf_op jit(solution)/shard_map/mul | solution.py:286
  32.9 1.1 fusion.99
  39.4 1.1 fusion.30
  44.2 1.0 fusion.3
  46.6 0.9 fusion.5
  50.0 5.5 %collective-permute-start.8 = (f32[3,64,1,128]{3,1,2,0:T(8,128)}, f32[3,64,1,128]{3,1,2,0:T(8,128)S(1)}, u32[]{:S(2)}, u32[]{:S(2)}) collective-permute-start(f32[3,64,1,128]{3,1,2,0:T(8,128)} %pad_maximum_fusion.6), channel_id=1, source_target_pairs={{0,16},{16,32},{32,48},{48,64},{64,80},{80,96},{96,112},{112,128},... | collective-permute-start | bytes 294920 | tf_op jit(solution)/shard_map/ppermute | solution.py:14
  55.5 1.9 %collective-permute-start.7 = (f32[1,8,1]{2,1,0:T(8,128)}, f32[1,8,1]{2,1,0:T(8,128)}, u32[]{:S(2)}, u32[]{:S(2)}) collective-permute-start(f32[1,8,1]{2,1,0:T(8,128)} %slice.548), channel_id=1, source_target_pairs={{4,1},{5,2},{6,3},{8,5},{9,6},{10,7},{12,9},{13,10},{14,11},{20,17... | collective-permute-start | bytes 104 | tf_op jit(solution)/shard_map/ppermute | solution.py:31
  57.4 3.8 %collective-permute-start.6 = (f32[1,1,128]{2,1,0:T(1,128)}, f32[1,1,128]{2,1,0:T(1,128)}, u32[]{:S(2)}, u32[]{:S(2)}) collective-permute-start(f32[1,1,128]{2,1,0:T(1,128)} %slice.539), channel_id=1, source_target_pairs={{16,1},{17,2},{18,3},{32,17},{33,18},{34,19},{48,33},{49,34},{50,3... | collective-permute-start | bytes 1544 | tf_op jit(solution)/shard_map/ppermute | solution.py:31
  61.9 6.2 %collective-permute-start.5 = (f32[64,1,1]{2,1,0:T(1,128)}, f32[64,1,1]{2,1,0:T(1,128)}, u32[]{:S(2)}, u32[]{:S(2)}) collective-permute-start(f32[64,1,1]{2,1,0:T(1,128)} %slice.532), channel_id=1, source_target_pairs={{16,4},{20,8},{24,12},{32,20},{36,24},{40,28},{48,36},{52,40},{56,... | collective-permute-start | bytes 776 | tf_op jit(solution)/shard_map/ppermute | solution.py:31
  68.2 0.9 copy-done.3
  73.3 3.2 %collective-permute-start.4 = (f32[3,64,8,1]{1,2,3,0:T(8,128)}, f32[3,64,8,1]{1,2,3,0:T(8,128)S(1)}, u32[]{:S(2)}, u32[]{:S(2)}) collective-permute-start(f32[3,64,8,1]{1,2,3,0:T(8,128)} %pad_maximum_fusion.9), channel_id=1, source_target_pairs={{0,4},{4,8},{8,12},{1,5},{5,9},{9,13},{2,6},{6,10},{10,14},{3,7},{... | collective-permute-start | bytes 18440 | tf_op jit(solution)/shard_map/ppermute | solution.py:14
  76.5 1.4 %copy.763 = f32[64,1,1]{0,1,2:T(1,128)} copy(f32[64,1,1]{2,1,0:T(1,128)} %collective-permute-done.5) | data formatting | bytes 512 | tf_op jit(solution)/shard_map/ppermute | solution.py:31
  82.0 1.2 %subtract_select_fusion = f32[64,8,1]{2,1,0:T(8,128)S(1)} fusion(f32[64,8,1]{2,1,0:T(8,128)} %copy.766, f32[64,8,1]{2,1,0:T(8,128)} %copy.765, f32[64,8,1]{2,1,0:T(8,128)} %copy.764, pred[]{:T(512)S(6)} %eq.93, f32[64,8,128]{2,1,0:T(8,128)S(1)} %get-tuple-element.59), kind=kLoop, calls=%fused_computation.68 | loop fusion | flops 2560 | bytes 10241 | tf_op jit(solution)/shard_map/jit(_where)/select_n | solution.py:167
  83.4 1.3 %fusion.11.sx_ref = f32[64,8,128]{2,1,0:T(8,128)} fusion(f32[64,8,128]{2,1,0:T(8,128)S(1)} %bitcast_subtract_fusion, f32[64,8,127]{2,1,0:T(8,128)S(1)} %bitcast.278, f32[64,8,1]{2,1,0:T(8,128)S(1)} %subtract_select_fusion, f32[64,8,128]{2,1,0:T(8,128)S(1)} %copy_divide_fusion, f32[63,8,128]{2,1,0:T(8,128)S(1)} %copy-done.13, ...), kind=kLoop, calls=%fused_computation.23 | loop fusion | flops 786432 | bytes 2883584 | tf_op jit(solution)/shard_map/sub | solution.py:193
  85.7 1.3 %fusion.17.sy_ref = f32[64,8,128]{2,1,0:T(8,128)} fusion(f32[64,8,128]{2,1,0:T(8,128)S(1)} %copy_divide_fusion, f32[63,8,128]{2,1,0:T(8,128)S(1)} %copy-done.12, f32[1,8,128]{2,1,0:T(8,128)S(1)} %get-tuple-element.89, f32[64,8,128]{2,1,0:T(8,128)S(1)} %get-tuple-element.55, f32[63,8,128]{2,1,0:T(8,128)S(1)} %copy-done.14, ...), kind=kLoop, calls=%fused_computation.33 | loop fusion | flops 786432 | bytes 2883584 | tf_op jit(solution)/shard_map/sub | solution.py:200
  86.9 3.1 %shard_map.77 = (f32[64,8,128]{2,1,0:T(8,128)}, f32[64,8,128]{2,1,0:T(8,128)}, f32[64,8,128]{2,1,0:T(8,128)}, f32[64,8,128]{2,1,0:T(8,128)}) custom-call(f32[64,8,128]{2,1,0:T(8,128)} %copy.790.stiff_ref, f32[64,8,128]{2,1,0:T(8,128)} %copy.791.diag_ref, f32[64,8,128]{2,1,0:T(8,128)} %fusion.11.sx_ref, f32[64,8,128]{2,1,0:T(8,128)} %fusion.17.sy_ref), custom_call_target="tpu_custom_call" | custom-call | tf_op jit(solution)/shard_map/pallas_call | solution.py:105
  95.5 2.8 %collective-permute-start.11 = (f32[8,8,128]{2,1,0:T(8,128)S(1)}, f32[8,8,128]{2,1,0:T(8,128)S(1)}, u32[]{:S(2)}, u32[]{:S(2)}) collective-permute-start(f32[8,8,128]{2,1,0:T(8,128)S(1)} %constant_dynamic-update-slice_fusion), channel_id=1, source_target_pairs={{0,2},{1,3},{2,0},{3,1},{4,6},{5,7},{6,4},{7,5},{8,10},{9,11},{10,... | collective-permute-start | bytes 98312 | tf_op jit(solution)/shard_map/ppermute | solution.py:224
  99.0 0.9 collective-permute-done.11
  99.8 1.7 %collective-permute-done.12 = f32[8,8,128]{2,1,0:T(8,128)S(1)} collective-permute-done((f32[8,8,128]{2,1,0:T(8,128)S(1)}, f32[8,8,128]{2,1,0:T(8,128)S(1)}, u32[]{:S(2)}, u32[]{:S(2)}) %collective-permute-start.12) | collective-permute-done | bytes 32800 | tf_op jit(solution)/shard_map/ppermute | solution.py:224
  103.1 4.3 %collective-permute-start.14 = (f32[64,8,1]{2,1,0:T(8,128)S(1)}, f32[64,8,1]{2,1,0:T(8,128)S(1)}, u32[]{:S(2)}, u32[]{:S(2)}) collective-permute-start(f32[64,8,1]{2,1,0:T(8,128)S(1)} %slice.567), channel_id=1, source_target_pairs={{0,4},{4,8},{8,12},{1,5},{5,9},{9,13},{2,6},{6,10},{10,14},{3,7},{... | collective-permute-start | bytes 6152 | tf_op jit(solution)/shard_map/ppermute | solution.py:14
  107.5 2.7 %collective-permute-start.13 = (f32[64,1,128]{2,1,0:T(1,128)S(1)}, f32[64,1,128]{2,1,0:T(1,128)S(1)}, u32[]{:S(2)}, u32[]{:S(2)}) collective-permute-start(f32[64,1,128]{2,1,0:T(1,128)S(1)} %slice.564), channel_id=1, source_target_pairs={{0,16},{16,32},{32,48},{48,64},{64,80},{80,96},{96,112},{112,128},... | collective-permute-start | bytes 98312 | tf_op jit(solution)/shard_map/ppermute | solution.py:14
  110.2 1.0 pad_maximum_fusion.1
  111.2 4.6 %collective-permute-done.13 = f32[64,1,128]{2,1,0:T(1,128)S(1)} collective-permute-done((f32[64,1,128]{2,1,0:T(1,128)S(1)}, f32[64,1,128]{2,1,0:T(1,128)S(1)}, u32[]{:S(2)}, u32[]{:S(2)}) %collective-permute-start.13) | collective-permute-done | bytes 32800 | tf_op jit(solution)/shard_map/ppermute | solution.py:14
  116.1 0.9 pad_maximum_fusion
  (182 shorter events, 41.9 us)
Async XLA Ops:
  2.0 33.8 %collective-permute-start.1 = (f32[5,1,8,128]{3,2,1,0:T(8,128)}, f32[5,1,8,128]{3,2,1,0:T(8,128)}, u32[]{:S(2)}, u32[]{:S(2)}) collective-permute-start(f32[5,1,8,128]{3,2,1,0:T(8,128)} %pad_maximum_fusion.8), channel_id=1, source_target_pairs={{0,1},{1,2},{2,3},{4,5},{5,6},{6,7},{8,9},{9,10},{10,11},{12,13},{... | collective-permute-start | bytes 61448 | tf_op jit(solution)/shard_map/ppermute | solution.py:14
  5.8 30.0 %collective-permute-start = (f32[2,1,8,128]{3,2,1,0:T(8,128)S(1)}, f32[2,1,8,128]{3,2,1,0:T(8,128)S(1)}, u32[]{:S(2)}, u32[]{:S(2)}) collective-permute-start(f32[2,1,8,128]{3,2,1,0:T(8,128)S(1)} %stack.118), channel_id=1, source_target_pairs={{1,0},{2,1},{3,2},{5,4},{6,5},{7,6},{9,8},{10,9},{11,10},{13,12},{... | collective-permute-start | bytes 24584 | tf_op jit(solution)/shard_map/ppermute | solution.py:19
  10.4 28.1 %collective-permute-start.2 = (f32[2,64,1,128]{3,1,2,0:T(8,128)}, f32[2,64,1,128]{3,1,2,0:T(8,128)}, u32[]{:S(2)}, u32[]{:S(2)}) collective-permute-start(f32[2,64,1,128]{3,1,2,0:T(8,128)} %pad_maximum_fusion.7), channel_id=1, source_target_pairs={{16,0},{32,16},{48,32},{64,48},{80,64},{96,80},{112,96},{128,112},... | collective-permute-start | bytes 196616 | tf_op jit(solution)/shard_map/ppermute | solution.py:19
  16.3 16.6 %collective-permute-start.3 = (f32[2,64,8,1]{3,1,2,0:T(8,128)}, f32[2,64,8,1]{3,1,2,0:T(8,128)}, u32[]{:S(2)}, u32[]{:S(2)}) collective-permute-start(f32[2,64,8,1]{3,1,2,0:T(8,128)} %copy.756), channel_id=1, source_target_pairs={{4,0},{8,4},{12,8},{5,1},{9,5},{13,9},{6,2},{10,6},{14,10},{7,3},{... | collective-permute-start | bytes 12296 | tf_op jit(solution)/shard_map/ppermute | solution.py:19
  20.4 4.3 %copy-start.1 = (f32[3,64,8,128]{3,2,1,0:T(8,128)S(1)}, f32[3,64,8,128]{3,2,1,0:T(8,128)}, u32[]{:S(2)}) copy-start(f32[3,64,8,128]{3,2,1,0:T(8,128)} %param.7) | copy-start | bytes 2359300
  20.4 64.4 %collective-permute-start.9 = (f32[64,1,1]{2,0,1:T(8,128)}, f32[64,1,1]{2,0,1:T(8,128)}, u32[]{:S(2)}, u32[]{:S(2)}) collective-permute-start(f32[64,1,1]{2,0,1:T(8,128)} %slice.557), channel_id=1, source_target_pairs={{4,16},{8,20},{12,24},{20,32},{24,36},{28,40},{36,48},{40,52},{44,... | collective-permute-start | bytes 776 | tf_op jit(solution)/shard_map/ppermute | solution.py:31
  37.1 2.2 %copy-start.17 = (f32[1,64,7,128]{3,1,2,0:T(8,128)S(1)}, f32[1,64,7,128]{3,1,2,0:T(8,128)}, u32[]{:S(2)}) copy-start(f32[1,64,7,128]{3,1,2,0:T(8,128)} %get-tuple-element.69) | copy-start | bytes 688132
  37.1 2.2 %copy-start = (f32[3,64,8,128]{3,2,1,0:T(8,128)S(1)}, f32[3,64,8,128]{3,2,1,0:T(8,128)}, u32[]{:S(2)}) copy-start(f32[3,64,8,128]{3,2,1,0:T(8,128)} %param.6) | copy-start | bytes 2359300
  42.5 1.7 %copy-start.18 = (f32[64,7,128]{2,0,1:T(8,128)S(1)}, f32[64,7,128]{2,0,1:T(8,128)}, u32[]{:S(2)}) copy-start(f32[64,7,128]{2,0,1:T(8,128)} %get-tuple-element.70) | copy-start | bytes 688132
  42.5 1.6 %copy-start.9 = (f32[64,8,127]{2,0,1:T(8,128)S(1)}, f32[64,8,127]{2,0,1:T(8,128)}, u32[]{:S(2)}) copy-start(f32[64,8,127]{2,0,1:T(8,128)} %get-tuple-element.68) | copy-start | bytes 780292
  48.6 12.6 %copy-start.8 = (f32[64,8,1]{2,1,0:T(8,128)S(1)}, f32[64,8,1]{2,1,0:T(8,128)}, u32[]{:S(2)}) copy-start(f32[64,8,1]{2,1,0:T(8,128)} %slice.528) | copy-start | bytes 6148
  49.4 18.8 %copy-start.16 = (f32[64,7,128]{2,0,1:T(8,128)S(1)}, f32[64,7,128]{2,0,1:T(8,128)}, u32[]{:S(2)}) copy-start(f32[64,7,128]{2,0,1:T(8,128)} %slice.536) | copy-start | bytes 688132
  50.0 34.7 %collective-permute-start.8 = (f32[3,64,1,128]{3,1,2,0:T(8,128)}, f32[3,64,1,128]{3,1,2,0:T(8,128)S(1)}, u32[]{:S(2)}, u32[]{:S(2)}) collective-permute-start(f32[3,64,1,128]{3,1,2,0:T(8,128)} %pad_maximum_fusion.6), channel_id=1, source_target_pairs={{0,16},{16,32},{32,48},{48,64},{64,80},{80,96},{96,112},{112,128},... | collective-permute-start | bytes 294920 | tf_op jit(solution)/shard_map/ppermute | solution.py:14
  55.5 22.4 %collective-permute-start.7 = (f32[1,8,1]{2,1,0:T(8,128)}, f32[1,8,1]{2,1,0:T(8,128)}, u32[]{:S(2)}, u32[]{:S(2)}) collective-permute-start(f32[1,8,1]{2,1,0:T(8,128)} %slice.548), channel_id=1, source_target_pairs={{4,1},{5,2},{6,3},{8,5},{9,6},{10,7},{12,9},{13,10},{14,11},{20,17... | collective-permute-start | bytes 104 | tf_op jit(solution)/shard_map/ppermute | solution.py:31
  57.4 20.5 %collective-permute-start.6 = (f32[1,1,128]{2,1,0:T(1,128)}, f32[1,1,128]{2,1,0:T(1,128)}, u32[]{:S(2)}, u32[]{:S(2)}) collective-permute-start(f32[1,1,128]{2,1,0:T(1,128)} %slice.539), channel_id=1, source_target_pairs={{16,1},{17,2},{18,3},{32,17},{33,18},{34,19},{48,33},{49,34},{50,3... | collective-permute-start | bytes 1544 | tf_op jit(solution)/shard_map/ppermute | solution.py:31
  61.9 11.4 %collective-permute-start.5 = (f32[64,1,1]{2,1,0:T(1,128)}, f32[64,1,1]{2,1,0:T(1,128)}, u32[]{:S(2)}, u32[]{:S(2)}) collective-permute-start(f32[64,1,1]{2,1,0:T(1,128)} %slice.532), channel_id=1, source_target_pairs={{16,4},{20,8},{24,12},{32,20},{36,24},{40,28},{48,36},{52,40},{56,... | collective-permute-start | bytes 776 | tf_op jit(solution)/shard_map/ppermute | solution.py:31
  73.3 4.6 %copy-start.29 = (f32[1,7,128]{2,1,0:T(8,128)S(1)}, f32[1,7,128]{2,1,0:T(8,128)}, u32[]{:S(2)}) copy-start(f32[1,7,128]{2,1,0:T(8,128)} %slice.451) | copy-start | bytes 10756
  73.3 4.6 %copy-start.30 = (f32[1,8,127]{2,1,0:T(8,128)S(1)}, f32[1,8,127]{2,1,0:T(8,128)}, u32[]{:S(2)}) copy-start(f32[1,8,127]{2,1,0:T(8,128)} %slice.464) | copy-start | bytes 12196
  73.3 5.4 %collective-permute-start.4 = (f32[3,64,8,1]{1,2,3,0:T(8,128)}, f32[3,64,8,1]{1,2,3,0:T(8,128)S(1)}, u32[]{:S(2)}, u32[]{:S(2)}) collective-permute-start(f32[3,64,8,1]{1,2,3,0:T(8,128)} %pad_maximum_fusion.9), channel_id=1, source_target_pairs={{0,4},{4,8},{8,12},{1,5},{5,9},{9,13},{2,6},{6,10},{10,14},{3,7},{... | collective-permute-start | bytes 18440 | tf_op jit(solution)/shard_map/ppermute | solution.py:14
  82.0 1.3 %copy-start.4 = (f32[64,8,128]{2,0,1:T(8,128)S(1)}, f32[64,8,128]{2,0,1:T(8,128)}, u32[]{:S(2)}) copy-start(f32[64,8,128]{2,0,1:T(8,128)} %get-tuple-element.71) | copy-start | bytes 786436
  82.0 1.3 %copy-start.13 = (f32[63,8,128]{2,1,0:T(8,128)S(1)}, f32[63,8,128]{2,1,0:T(8,128)}, u32[]{:S(2)}) copy-start(f32[63,8,128]{2,1,0:T(8,128)} %get-tuple-element.58) | copy-start | bytes 774148
  82.0 1.4 %copy-start.15 = (f32[63,8,128]{2,1,0:T(8,128)S(1)}, f32[63,8,128]{2,1,0:T(8,128)}, u32[]{:S(2)}) copy-start(f32[63,8,128]{2,1,0:T(8,128)} %slice.540) | copy-start | bytes 774148
  83.4 2.2 %copy-start.12 = (f32[63,8,128]{2,1,0:T(8,128)S(1)}, f32[63,8,128]{2,1,0:T(8,128)}, u32[]{:S(2)}) copy-start(f32[63,8,128]{2,1,0:T(8,128)} %get-tuple-element.57) | copy-start | bytes 774148
  83.4 2.2 %copy-start.14 = (f32[63,8,128]{2,1,0:T(8,128)S(1)}, f32[63,8,128]{2,1,0:T(8,128)}, u32[]{:S(2)}) copy-start(f32[63,8,128]{2,1,0:T(8,128)} %slice.549) | copy-start | bytes 774148
  94.8 7.8 %copy-start.22 = (f32[64,8,128]{2,1,0:T(8,128)S(1)}, f32[64,8,128]{2,1,0:T(8,128)}, u32[]{:S(2)}) copy-start(f32[64,8,128]{2,1,0:T(8,128)} %get-tuple-element.9) | copy-start | bytes 786436
  95.5 3.4 %collective-permute-start.10 = (f32[8,8,128]{2,1,0:T(8,128)S(1)}, f32[8,8,128]{2,1,0:T(8,128)S(1)}, u32[]{:S(2)}, u32[]{:S(2)}) collective-permute-start(f32[8,8,128]{2,1,0:T(8,128)S(1)} %constant_dynamic-update-slice_fusion), channel_id=1, source_target_pairs={{0,1},{1,2},{2,3},{3,0},{4,5},{5,6},{6,7},{7,4},{8,9},{9,10},{10,1... | collective-permute-start | bytes 98312 | tf_op jit(solution)/shard_map/ppermute | solution.py:224
  95.5 4.3 %collective-permute-start.11 = (f32[8,8,128]{2,1,0:T(8,128)S(1)}, f32[8,8,128]{2,1,0:T(8,128)S(1)}, u32[]{:S(2)}, u32[]{:S(2)}) collective-permute-start(f32[8,8,128]{2,1,0:T(8,128)S(1)} %constant_dynamic-update-slice_fusion), channel_id=1, source_target_pairs={{0,2},{1,3},{2,0},{3,1},{4,6},{5,7},{6,4},{7,5},{8,10},{9,11},{10,... | collective-permute-start | bytes 98312 | tf_op jit(solution)/shard_map/ppermute | solution.py:224
  98.4 3.1 %collective-permute-start.12 = (f32[8,8,128]{2,1,0:T(8,128)S(1)}, f32[8,8,128]{2,1,0:T(8,128)S(1)}, u32[]{:S(2)}, u32[]{:S(2)}) collective-permute-start(f32[8,8,128]{2,1,0:T(8,128)S(1)} %constant_dynamic-update-slice_fusion), channel_id=1, source_target_pairs={{0,3},{1,0},{2,1},{3,2},{4,7},{5,4},{6,5},{7,6},{8,11},{9,8},{10,9... | collective-permute-start | bytes 98312 | tf_op jit(solution)/shard_map/ppermute | solution.py:224
  102.9 7.3 %copy-start.7 = (f32[1,64,8,128]{3,2,1,0:T(8,128)S(1)}, f32[1,64,8,128]{3,2,1,0:T(8,128)}, u32[]{:S(2)}) copy-start(f32[1,64,8,128]{3,2,1,0:T(8,128)} %get-tuple-element.49) | copy-start | bytes 786436
  103.1 8.1 %collective-permute-start.14 = (f32[64,8,1]{2,1,0:T(8,128)S(1)}, f32[64,8,1]{2,1,0:T(8,128)S(1)}, u32[]{:S(2)}, u32[]{:S(2)}) collective-permute-start(f32[64,8,1]{2,1,0:T(8,128)S(1)} %slice.567), channel_id=1, source_target_pairs={{0,4},{4,8},{8,12},{1,5},{5,9},{9,13},{2,6},{6,10},{10,14},{3,7},{... | collective-permute-start | bytes 6152 | tf_op jit(solution)/shard_map/ppermute | solution.py:14
  107.5 8.3 %collective-permute-start.13 = (f32[64,1,128]{2,1,0:T(1,128)S(1)}, f32[64,1,128]{2,1,0:T(1,128)S(1)}, u32[]{:S(2)}, u32[]{:S(2)}) collective-permute-start(f32[64,1,128]{2,1,0:T(1,128)S(1)} %slice.564), channel_id=1, source_target_pairs={{0,16},{16,32},{32,48},{48,64},{64,80},{80,96},{96,112},{112,128},... | collective-permute-start | bytes 98312 | tf_op jit(solution)/shard_map/ppermute | solution.py:14
  110.2 5.5 %copy-start.11 = (f32[64,8,128]{2,0,1:T(8,128)S(1)}, f32[64,8,128]{2,0,1:T(8,128)}, u32[]{:S(2)}) copy-start(f32[64,8,128]{2,0,1:T(8,128)} %get-tuple-element.12) | copy-start | bytes 786436
  (21 other events, 17.9 us)
where the time goes:
time: 118 us; the launch traced here: 117 us
  starting transfers between devices  46 us (39%)
  local copies, waits for them, and re-layouts  38 us (32%)
  other arithmetic  21.6 us (18%)
  waiting for transfers between devices  7.13 us (6%)
  Pallas kernels  3.08 us (3%)
  between operations  1.21 us (1%)
    ppermute x5, starting transfers between devices, from_prev(): return lax.ppermute(block, axis, [(i, i + 1) for i in range(count - 1)])  18.8 us
    ppermute x4, starting transfers between devices, from_diagonal(): return lax.ppermute(block, axes, pairs)  13.9 us
    unnamed x82, local copies, waits for them, and re-layouts  10.7 us
    ppermute x3, starting transfers between devices, from_next(): return lax.ppermute(block, axis, [(i + 1, i) for i in range(count - 1)])  10.5 us
    ppermute x5, waiting for transfers between devices, from_prev(): return lax.ppermute(block, axis, [(i, i + 1) for i in range(count - 1)])  4.56 us
    pallas_call x1, Pallas kernels, solve_slab(): pl.pallas_call(thomas_kernel, out_shape=(shape, shape, shape, shape), scr...  3.08 us
    ppermute x3, starting transfers between devices, body(): lax.ppermute(own, 'gz', [(i, (i + shift) % slab_count) for i in range(sla...  2.84 us
    ppermute x3, waiting for transfers between devices, body(): lax.ppermute(own, 'gz', [(i, (i + shift) % slab_count) for i in range(sla...  2.55 us
  transfers between devices with their start and end apart: 15, of which 3 were waited for; matrix products, arithmetic and copies ran while one was open for 36% of the time, Pallas kernels for 0%

commit v1 on v0

--- a/solution.py
+++ b/solution.py
@@ -53,7 +53,9 @@
     return (keep_rate, curl_rate, z_rate, stiffness)
 
 
-def thomas_kernel(stiff_ref, diag_ref, sx_ref, sy_ref, px_ref, py_ref, lw_ref, hw_ref, ur_ref):
+def thomas_kernel(
+    stiff_ref, diag_ref, sx_ref, sy_ref, px_ref, py_ref, lw_ref, hw_ref, edge_ref, ur_ref
+):
     depth = stiff_ref.shape[0]
     stiff = stiff_ref[0]
     inv = 1.0 / diag_ref[0]
@@ -98,13 +100,22 @@
         return next_x, next_y, next_low, next_high
 
     lax.fori_loop(0, depth - 1, backward, (last_x, last_y, last_low, last_high), unroll=8)
+    edge_ref[0] = px_ref[0]
+    edge_ref[1] = py_ref[0]
+    edge_ref[2] = px_ref[depth - 1]
+    edge_ref[3] = py_ref[depth - 1]
+    edge_ref[4] = lw_ref[0]
+    edge_ref[5] = lw_ref[depth - 1]
+    edge_ref[6] = hw_ref[0]
+    edge_ref[7] = hw_ref[depth - 1]
 
 
 def solve_slab(stiffness, diagonal, source_x, source_y):
     shape = jax.ShapeDtypeStruct(stiffness.shape, jnp.float32)
+    edges = jax.ShapeDtypeStruct((8,) + stiffness.shape[1:], jnp.float32)
     return pl.pallas_call(
         thomas_kernel,
-        out_shape=(shape, shape, shape, shape),
+        out_shape=(shape, shape, shape, shape, edges),
         scratch_shapes=[pltpu.VMEM(stiffness.shape, jnp.float32)],
     )(stiffness, diagonal, source_x, source_y)
 
@@ -206,17 +217,10 @@
     level_index = lax.broadcasted_iota(jnp.int32, stiffness.shape, 0)
     diagonal = 1.0 + 2.0 * stiffness
     diagonal = jnp.where(jnp.logical_and(bottom, level_index == 0), 1.0 + stiffness, diagonal)
-    partial_x, partial_y, low_weight, high_weight = solve_slab(
+    partial_x, partial_y, low_weight, high_weight, own = solve_slab(
         stiffness, diagonal, source_x, source_y
     )
 
-    own = jnp.concatenate(
-        [
-            jnp.stack([partial_x[0], partial_y[0], partial_x[-1], partial_y[-1]]),
-            jnp.stack([low_weight[0], low_weight[-1], high_weight[0], high_weight[-1]]),
-        ],
-        axis=0,
-    )
     slab_count = lax.axis_size("gz")
     gathered = [own]
     for shift in range(1, slab_count):

time: 118 us -> 114 us (0.966)
  local copies, waits for them, and re-layouts: 38 us -> 32.5 us
    unnamed x82 -> x75, local copies, waits for them, and re-layouts: 10.7 us -> 6.01 us
  transfers between devices with their start and end apart: 15 -> 15, of which waited for: 3 -> 3; matrix products, arithmetic and copies ran while one was open for 36% -> 37% of each run, Pallas kernels for 0% -> 0%
where the time goes in v1:
time: 114 us; the launch traced here: 113 us
  starting transfers between devices  46 us (40%)
  local copies, waits for them, and re-layouts  32.5 us (29%)
  other arithmetic  22.6 us (20%)
  waiting for transfers between devices  7.33 us (6%)
  Pallas kernels  3.08 us (3%)
  between operations  1.2 us (1%)
    ppermute x5, starting transfers between devices, from_prev(): return lax.ppermute(block, axis, [(i, i + 1) for i in range(count - 1)])  18.8 us
    ppermute x4, starting transfers between devices, from_diagonal(): return lax.ppermute(block, axes, pairs)  13.9 us
    ppermute x3, starting transfers between devices, from_next(): return lax.ppermute(block, axis, [(i + 1, i) for i in range(count - 1)])  10.5 us
    unnamed x75, local copies, waits for them, and re-layouts  6.01 us
    ppermute x5, waiting for transfers between devices, from_prev(): return lax.ppermute(block, axis, [(i, i + 1) for i in range(count - 1)])  4.56 us
    pallas_call x1, Pallas kernels, solve_slab(): pl.pallas_call(thomas_kernel, out_shape=(shape, shape, shape, shape, edge...  3.08 us
    ppermute x3, starting transfers between devices, body(): lax.ppermute(own, 'gz', [(i, (i + shift) % slab_count) for i in range(sla...  2.84 us
    ppermute x3, waiting for transfers between devices, body(): lax.ppermute(own, 'gz', [(i, (i + shift) % slab_count) for i in range(sla...  2.75 us
  transfers between devices with their start and end apart: 15, of which 3 were waited for; matrix products, arithmetic and copies ran while one was open for 37% of the time, Pallas kernels for 0%

profile of v1, /device:TPU:131, one launch (start us, length us, event | category | flops | bytes accessed | tf_op | source)
XLA Modules:
  0.0 112.7 jit_solution(7230366719339259831)
XLA Ops:
  2.0 3.1 %collective-permute-start.1 = (f32[5,1,8,128]{3,2,1,0:T(8,128)}, f32[5,1,8,128]{3,2,1,0:T(8,128)}, u32[]{:S(2)}, u32[]{:S(2)}) collective-permute-start(f32[5,1,8,128]{3,2,1,0:T(8,128)} %pad_maximum_fusion.8), channel_id=1, source_target_pairs={{0,1},{1,2},{2,3},{4,5},{5,6},{6,7},{8,9},{9,10},{10,11},{12,13},{... | collective-permute-start | bytes 61448 | tf_op jit(solution)/shard_map/ppermute | solution.py:14
  5.8 2.7 %collective-permute-start = (f32[2,1,8,128]{3,2,1,0:T(8,128)S(1)}, f32[2,1,8,128]{3,2,1,0:T(8,128)S(1)}, u32[]{:S(2)}, u32[]{:S(2)}) collective-permute-start(f32[2,1,8,128]{3,2,1,0:T(8,128)S(1)} %stack.118), channel_id=1, source_target_pairs={{1,0},{2,1},{3,2},{5,4},{6,5},{7,6},{9,8},{10,9},{11,10},{13,12},{... | collective-permute-start | bytes 24584 | tf_op jit(solution)/shard_map/ppermute | solution.py:19
  8.5 1.2 %slice_bitcast_fusion.3 = (f32[64,8,128]{2,1,0:T(8,128)S(1)}, f32[1,64,8,128]{3,2,1,0:T(8,128)S(1)}, f32[1,64,8,128]{3,2,1,0:T(8,128)S(1)}) fusion(f32[3,64,8,128]{3,2,1,0:T(8,128)} %param.6), kind=kLoop, calls=%fused_computation.79 | loop fusion | bytes 1572864 | tf_op jit(solution)/shard_map/squeeze | solution.py:142
  10.4 4.4 %collective-permute-start.2 = (f32[2,64,1,128]{3,1,2,0:T(8,128)}, f32[2,64,1,128]{3,1,2,0:T(8,128)}, u32[]{:S(2)}, u32[]{:S(2)}) collective-permute-start(f32[2,64,1,128]{3,1,2,0:T(8,128)} %pad_maximum_fusion.7), channel_id=1, source_target_pairs={{16,0},{32,16},{48,32},{64,48},{80,64},{96,80},{112,96},{128,112},... | collective-permute-start | bytes 196616 | tf_op jit(solution)/shard_map/ppermute | solution.py:19
  15.2 1.1 copy.756
  16.3 3.4 %collective-permute-start.3 = (f32[2,64,8,1]{3,1,2,0:T(8,128)}, f32[2,64,8,1]{3,1,2,0:T(8,128)}, u32[]{:S(2)}, u32[]{:S(2)}) collective-permute-start(f32[2,64,8,1]{3,1,2,0:T(8,128)} %copy.756), channel_id=1, source_target_pairs={{4,0},{8,4},{12,8},{5,1},{9,5},{13,9},{6,2},{10,6},{14,10},{7,3},{... | collective-permute-start | bytes 12296 | tf_op jit(solution)/shard_map/ppermute | solution.py:19
  20.4 2.0 %collective-permute-start.9 = (f32[64,1,1]{2,0,1:T(8,128)}, f32[64,1,1]{2,0,1:T(8,128)}, u32[]{:S(2)}, u32[]{:S(2)}) collective-permute-start(f32[64,1,1]{2,0,1:T(8,128)} %slice.525), channel_id=1, source_target_pairs={{4,16},{8,20},{12,24},{20,32},{24,36},{28,40},{36,48},{40,52},{44,... | collective-permute-start | bytes 776 | tf_op jit(solution)/shard_map/ppermute | solution.py:31
  25.8 1.0 copy_compare_fusion.7
  27.6 2.4 %fusion.86 = (f32[64,8,128]{2,0,1:T(8,128)}, f32[64,8,128]{2,0,1:T(8,128)S(1)}, f32[64,8,128]{2,0,1:T(8,128)S(1)}) fusion(f32[1,64,8,128]{3,2,1,0:T(8,128)S(1)} %get-tuple-element.63, pred[64,8,128]{2,0,1:T(8,128)(4,1)} %get-tuple-element.85, f32[64]{0:T(128)S(1)} %get-tuple-element.133, pred[64,8,128]{2,0,1:T(8,128)(4,1)} %get-tuple-element.84, ...), kind=kLoop, calls=%fused_computation.253 | loop fusion | flops 2424832 | bytes 1576960 | tf_op jit(solution)/shard_map/mul | solution.py:290
  32.9 1.1 fusion.99
  39.4 1.1 fusion.30
  44.2 1.0 fusion.3
  46.6 0.9 fusion.5
  50.0 5.5 %collective-permute-start.8 = (f32[3,64,1,128]{3,1,2,0:T(8,128)}, f32[3,64,1,128]{3,1,2,0:T(8,128)S(1)}, u32[]{:S(2)}, u32[]{:S(2)}) collective-permute-start(f32[3,64,1,128]{3,1,2,0:T(8,128)} %pad_maximum_fusion.6), channel_id=1, source_target_pairs={{0,16},{16,32},{32,48},{48,64},{64,80},{80,96},{96,112},{112,128},... | collective-permute-start | bytes 294920 | tf_op jit(solution)/shard_map/ppermute | solution.py:14
  55.5 1.9 %collective-permute-start.7 = (f32[1,8,1]{2,1,0:T(8,128)}, f32[1,8,1]{2,1,0:T(8,128)}, u32[]{:S(2)}, u32[]{:S(2)}) collective-permute-start(f32[1,8,1]{2,1,0:T(8,128)} %slice.516), channel_id=1, source_target_pairs={{4,1},{5,2},{6,3},{8,5},{9,6},{10,7},{12,9},{13,10},{14,11},{20,17... | collective-permute-start | bytes 104 | tf_op jit(solution)/shard_map/ppermute | solution.py:31
  57.4 3.8 %collective-permute-start.6 = (f32[1,1,128]{2,1,0:T(1,128)}, f32[1,1,128]{2,1,0:T(1,128)}, u32[]{:S(2)}, u32[]{:S(2)}) collective-permute-start(f32[1,1,128]{2,1,0:T(1,128)} %slice.507), channel_id=1, source_target_pairs={{16,1},{17,2},{18,3},{32,17},{33,18},{34,19},{48,33},{49,34},{50,3... | collective-permute-start | bytes 1544 | tf_op jit(solution)/shard_map/ppermute | solution.py:31
  61.9 6.2 %collective-permute-start.5 = (f32[64,1,1]{2,1,0:T(1,128)}, f32[64,1,1]{2,1,0:T(1,128)}, u32[]{:S(2)}, u32[]{:S(2)}) collective-permute-start(f32[64,1,1]{2,1,0:T(1,128)} %slice.500), channel_id=1, source_target_pairs={{16,4},{20,8},{24,12},{32,20},{36,24},{40,28},{48,36},{52,40},{56,... | collective-permute-start | bytes 776 | tf_op jit(solution)/shard_map/ppermute | solution.py:31
  73.3 3.2 %collective-permute-start.4 = (f32[3,64,8,1]{1,2,3,0:T(8,128)}, f32[3,64,8,1]{1,2,3,0:T(8,128)S(1)}, u32[]{:S(2)}, u32[]{:S(2)}) collective-permute-start(f32[3,64,8,1]{1,2,3,0:T(8,128)} %pad_maximum_fusion.9), channel_id=1, source_target_pairs={{0,4},{4,8},{8,12},{1,5},{5,9},{9,13},{2,6},{6,10},{10,14},{3,7},{... | collective-permute-start | bytes 18440 | tf_op jit(solution)/shard_map/ppermute | solution.py:14
  76.5 1.4 %copy.763 = f32[64,1,1]{0,1,2:T(1,128)} copy(f32[64,1,1]{2,1,0:T(1,128)} %collective-permute-done.5) | data formatting | bytes 512 | tf_op jit(solution)/shard_map/ppermute | solution.py:31
  82.0 1.2 %subtract_select_fusion = f32[64,8,1]{2,1,0:T(8,128)S(1)} fusion(f32[64,8,1]{2,1,0:T(8,128)} %copy.766, f32[64,8,1]{2,1,0:T(8,128)} %copy.765, f32[64,8,1]{2,1,0:T(8,128)} %copy.764, pred[]{:T(512)S(6)} %eq.93, f32[64,8,128]{2,1,0:T(8,128)S(1)} %get-tuple-element.61), kind=kLoop, calls=%fused_computation.68 | loop fusion | flops 2560 | bytes 10241 | tf_op jit(solution)/shard_map/jit(_where)/select_n | solution.py:178
  83.4 1.3 %fusion.11.sx_ref = f32[64,8,128]{2,1,0:T(8,128)} fusion(f32[64,8,128]{2,1,0:T(8,128)S(1)} %bitcast_subtract_fusion, f32[64,8,127]{2,1,0:T(8,128)S(1)} %bitcast.278, f32[64,8,1]{2,1,0:T(8,128)S(1)} %subtract_select_fusion, f32[64,8,128]{2,1,0:T(8,128)S(1)} %copy_divide_fusion, f32[63,8,128]{2,1,0:T(8,128)S(1)} %copy-done.13, ...), kind=kLoop, calls=%fused_computation.23 | loop fusion | flops 786432 | bytes 2883584 | tf_op jit(solution)/shard_map/sub | solution.py:204
  85.7 1.3 %fusion.17.sy_ref = f32[64,8,128]{2,1,0:T(8,128)} fusion(f32[64,8,128]{2,1,0:T(8,128)S(1)} %copy_divide_fusion, f32[63,8,128]{2,1,0:T(8,128)S(1)} %copy-done.12, f32[1,8,128]{2,1,0:T(8,128)S(1)} %get-tuple-element.91, f32[64,8,128]{2,1,0:T(8,128)S(1)} %get-tuple-element.57, f32[63,8,128]{2,1,0:T(8,128)S(1)} %copy-done.14, ...), kind=kLoop, calls=%fused_computation.33 | loop fusion | flops 786432 | bytes 2883584 | tf_op jit(solution)/shard_map/sub | solution.py:211
  86.9 3.1 %shard_map.77 = (f32[64,8,128]{2,1,0:T(8,128)}, f32[64,8,128]{2,1,0:T(8,128)}, f32[64,8,128]{2,1,0:T(8,128)}, f32[64,8,128]{2,1,0:T(8,128)}, f32[8,8,128]{2,1,0:T(8,128)}) custom-call(f32[64,8,128]{2,1,0:T(8,128)} %copy.790.stiff_ref, f32[64,8,128]{2,1,0:T(8,128)} %copy.791.diag_ref, f32[64,8,128]{2,1,0:T(8,128)} %fusion.11.sx_ref, f32[64,8,128]{2,1,0:T(8,128)} %fusion.17.sy_ref), custom_call_target="tpu_custom_call" | custom-call | tf_op jit(solution)/shard_map/pallas_call | solution.py:116
  90.0 2.8 %collective-permute-start.11 = (f32[8,8,128]{2,1,0:T(8,128)}, f32[8,8,128]{2,1,0:T(8,128)S(1)}, u32[]{:S(2)}, u32[]{:S(2)}) collective-permute-start(f32[8,8,128]{2,1,0:T(8,128)} %get-tuple-element.8), channel_id=1, source_target_pairs={{0,2},{1,3},{2,0},{3,1},{4,6},{5,7},{6,4},{7,5},{8,10},{9,11},{10,... | collective-permute-start | bytes 98312 | tf_op jit(solution)/shard_map/ppermute | solution.py:228
  93.4 1.1 collective-permute-done.11
  94.6 1.6 %collective-permute-done.12 = f32[8,8,128]{2,1,0:T(8,128)S(1)} collective-permute-done((f32[8,8,128]{2,1,0:T(8,128)}, f32[8,8,128]{2,1,0:T(8,128)S(1)}, u32[]{:S(2)}, u32[]{:S(2)}) %collective-permute-start.12) | collective-permute-done | bytes 32800 | tf_op jit(solution)/shard_map/ppermute | solution.py:228
  97.3 1.1 bitcast_add_fusion.7
  98.7 4.3 %collective-permute-start.14 = (f32[64,8,1]{2,1,0:T(8,128)S(1)}, f32[64,8,1]{2,1,0:T(8,128)S(1)}, u32[]{:S(2)}, u32[]{:S(2)}) collective-permute-start(f32[64,8,1]{2,1,0:T(8,128)S(1)} %slice.535), channel_id=1, source_target_pairs={{0,4},{4,8},{8,12},{1,5},{5,9},{9,13},{2,6},{6,10},{10,14},{3,7},{... | collective-permute-start | bytes 6152 | tf_op jit(solution)/shard_map/ppermute | solution.py:14
  103.1 2.7 %collective-permute-start.13 = (f32[64,1,128]{2,1,0:T(1,128)S(1)}, f32[64,1,128]{2,1,0:T(1,128)S(1)}, u32[]{:S(2)}, u32[]{:S(2)}) collective-permute-start(f32[64,1,128]{2,1,0:T(1,128)S(1)} %slice.532), channel_id=1, source_target_pairs={{0,16},{16,32},{32,48},{48,64},{64,80},{80,96},{96,112},{112,128},... | collective-permute-start | bytes 98312 | tf_op jit(solution)/shard_map/ppermute | solution.py:14
  105.9 1.0 pad_maximum_fusion.1
  106.8 4.6 %collective-permute-done.13 = f32[64,1,128]{2,1,0:T(1,128)S(1)} collective-permute-done((f32[64,1,128]{2,1,0:T(1,128)S(1)}, f32[64,1,128]{2,1,0:T(1,128)S(1)}, u32[]{:S(2)}, u32[]{:S(2)}) %collective-permute-start.13) | collective-permute-done | bytes 32800 | tf_op jit(solution)/shard_map/ppermute | solution.py:14
  111.8 0.9 pad_maximum_fusion
  (174 shorter events, 37.2 us)
Async XLA Ops:
  2.0 33.8 %collective-permute-start.1 = (f32[5,1,8,128]{3,2,1,0:T(8,128)}, f32[5,1,8,128]{3,2,1,0:T(8,128)}, u32[]{:S(2)}, u32[]{:S(2)}) collective-permute-start(f32[5,1,8,128]{3,2,1,0:T(8,128)} %pad_maximum_fusion.8), channel_id=1, source_target_pairs={{0,1},{1,2},{2,3},{4,5},{5,6},{6,7},{8,9},{9,10},{10,11},{12,13},{... | collective-permute-start | bytes 61448 | tf_op jit(solution)/shard_map/ppermute | solution.py:14
  5.8 30.0 %collective-permute-start = (f32[2,1,8,128]{3,2,1,0:T(8,128)S(1)}, f32[2,1,8,128]{3,2,1,0:T(8,128)S(1)}, u32[]{:S(2)}, u32[]{:S(2)}) collective-permute-start(f32[2,1,8,128]{3,2,1,0:T(8,128)S(1)} %stack.118), channel_id=1, source_target_pairs={{1,0},{2,1},{3,2},{5,4},{6,5},{7,6},{9,8},{10,9},{11,10},{13,12},{... | collective-permute-start | bytes 24584 | tf_op jit(solution)/shard_map/ppermute | solution.py:19
  10.4 28.1 %collective-permute-start.2 = (f32[2,64,1,128]{3,1,2,0:T(8,128)}, f32[2,64,1,128]{3,1,2,0:T(8,128)}, u32[]{:S(2)}, u32[]{:S(2)}) collective-permute-start(f32[2,64,1,128]{3,1,2,0:T(8,128)} %pad_maximum_fusion.7), channel_id=1, source_target_pairs={{16,0},{32,16},{48,32},{64,48},{80,64},{96,80},{112,96},{128,112},... | collective-permute-start | bytes 196616 | tf_op jit(solution)/shard_map/ppermute | solution.py:19
  16.3 16.6 %collective-permute-start.3 = (f32[2,64,8,1]{3,1,2,0:T(8,128)}, f32[2,64,8,1]{3,1,2,0:T(8,128)}, u32[]{:S(2)}, u32[]{:S(2)}) collective-permute-start(f32[2,64,8,1]{3,1,2,0:T(8,128)} %copy.756), channel_id=1, source_target_pairs={{4,0},{8,4},{12,8},{5,1},{9,5},{13,9},{6,2},{10,6},{14,10},{7,3},{... | collective-permute-start | bytes 12296 | tf_op jit(solution)/shard_map/ppermute | solution.py:19
  20.4 4.3 %copy-start.1 = (f32[3,64,8,128]{3,2,1,0:T(8,128)S(1)}, f32[3,64,8,128]{3,2,1,0:T(8,128)}, u32[]{:S(2)}) copy-start(f32[3,64,8,128]{3,2,1,0:T(8,128)} %param.7) | copy-start | bytes 2359300
  20.4 64.4 %collective-permute-start.9 = (f32[64,1,1]{2,0,1:T(8,128)}, f32[64,1,1]{2,0,1:T(8,128)}, u32[]{:S(2)}, u32[]{:S(2)}) collective-permute-start(f32[64,1,1]{2,0,1:T(8,128)} %slice.525), channel_id=1, source_target_pairs={{4,16},{8,20},{12,24},{20,32},{24,36},{28,40},{36,48},{40,52},{44,... | collective-permute-start | bytes 776 | tf_op jit(solution)/shard_map/ppermute | solution.py:31
  37.1 2.2 %copy-start.17 = (f32[1,64,7,128]{3,1,2,0:T(8,128)S(1)}, f32[1,64,7,128]{3,1,2,0:T(8,128)}, u32[]{:S(2)}) copy-start(f32[1,64,7,128]{3,1,2,0:T(8,128)} %get-tuple-element.71) | copy-start | bytes 688132
  37.1 2.2 %copy-start = (f32[3,64,8,128]{3,2,1,0:T(8,128)S(1)}, f32[3,64,8,128]{3,2,1,0:T(8,128)}, u32[]{:S(2)}) copy-start(f32[3,64,8,128]{3,2,1,0:T(8,128)} %param.6) | copy-start | bytes 2359300
  42.5 1.7 %copy-start.18 = (f32[64,7,128]{2,0,1:T(8,128)S(1)}, f32[64,7,128]{2,0,1:T(8,128)}, u32[]{:S(2)}) copy-start(f32[64,7,128]{2,0,1:T(8,128)} %get-tuple-element.72) | copy-start | bytes 688132
  42.5 1.6 %copy-start.9 = (f32[64,8,127]{2,0,1:T(8,128)S(1)}, f32[64,8,127]{2,0,1:T(8,128)}, u32[]{:S(2)}) copy-start(f32[64,8,127]{2,0,1:T(8,128)} %get-tuple-element.70) | copy-start | bytes 780292
  48.6 12.6 %copy-start.8 = (f32[64,8,1]{2,1,0:T(8,128)S(1)}, f32[64,8,1]{2,1,0:T(8,128)}, u32[]{:S(2)}) copy-start(f32[64,8,1]{2,1,0:T(8,128)} %slice.496) | copy-start | bytes 6148
  49.4 18.8 %copy-start.16 = (f32[64,7,128]{2,0,1:T(8,128)S(1)}, f32[64,7,128]{2,0,1:T(8,128)}, u32[]{:S(2)}) copy-start(f32[64,7,128]{2,0,1:T(8,128)} %slice.504) | copy-start | bytes 688132
  50.0 34.7 %collective-permute-start.8 = (f32[3,64,1,128]{3,1,2,0:T(8,128)}, f32[3,64,1,128]{3,1,2,0:T(8,128)S(1)}, u32[]{:S(2)}, u32[]{:S(2)}) collective-permute-start(f32[3,64,1,128]{3,1,2,0:T(8,128)} %pad_maximum_fusion.6), channel_id=1, source_target_pairs={{0,16},{16,32},{32,48},{48,64},{64,80},{80,96},{96,112},{112,128},... | collective-permute-start | bytes 294920 | tf_op jit(solution)/shard_map/ppermute | solution.py:14
  55.5 22.4 %collective-permute-start.7 = (f32[1,8,1]{2,1,0:T(8,128)}, f32[1,8,1]{2,1,0:T(8,128)}, u32[]{:S(2)}, u32[]{:S(2)}) collective-permute-start(f32[1,8,1]{2,1,0:T(8,128)} %slice.516), channel_id=1, source_target_pairs={{4,1},{5,2},{6,3},{8,5},{9,6},{10,7},{12,9},{13,10},{14,11},{20,17... | collective-permute-start | bytes 104 | tf_op jit(solution)/shard_map/ppermute | solution.py:31
  57.4 20.5 %collective-permute-start.6 = (f32[1,1,128]{2,1,0:T(1,128)}, f32[1,1,128]{2,1,0:T(1,128)}, u32[]{:S(2)}, u32[]{:S(2)}) collective-permute-start(f32[1,1,128]{2,1,0:T(1,128)} %slice.507), channel_id=1, source_target_pairs={{16,1},{17,2},{18,3},{32,17},{33,18},{34,19},{48,33},{49,34},{50,3... | collective-permute-start | bytes 1544 | tf_op jit(solution)/shard_map/ppermute | solution.py:31
  61.9 11.4 %collective-permute-start.5 = (f32[64,1,1]{2,1,0:T(1,128)}, f32[64,1,1]{2,1,0:T(1,128)}, u32[]{:S(2)}, u32[]{:S(2)}) collective-permute-start(f32[64,1,1]{2,1,0:T(1,128)} %slice.500), channel_id=1, source_target_pairs={{16,4},{20,8},{24,12},{32,20},{36,24},{40,28},{48,36},{52,40},{56,... | collective-permute-start | bytes 776 | tf_op jit(solution)/shard_map/ppermute | solution.py:31
  73.3 4.6 %copy-start.29 = (f32[1,7,128]{2,1,0:T(8,128)S(1)}, f32[1,7,128]{2,1,0:T(8,128)}, u32[]{:S(2)}) copy-start(f32[1,7,128]{2,1,0:T(8,128)} %slice.427) | copy-start | bytes 10756
  73.3 4.6 %copy-start.30 = (f32[1,8,127]{2,1,0:T(8,128)S(1)}, f32[1,8,127]{2,1,0:T(8,128)}, u32[]{:S(2)}) copy-start(f32[1,8,127]{2,1,0:T(8,128)} %slice.440) | copy-start | bytes 12196
  73.3 5.4 %collective-permute-start.4 = (f32[3,64,8,1]{1,2,3,0:T(8,128)}, f32[3,64,8,1]{1,2,3,0:T(8,128)S(1)}, u32[]{:S(2)}, u32[]{:S(2)}) collective-permute-start(f32[3,64,8,1]{1,2,3,0:T(8,128)} %pad_maximum_fusion.9), channel_id=1, source_target_pairs={{0,4},{4,8},{8,12},{1,5},{5,9},{9,13},{2,6},{6,10},{10,14},{3,7},{... | collective-permute-start | bytes 18440 | tf_op jit(solution)/shard_map/ppermute | solution.py:14
  82.0 1.3 %copy-start.4 = (f32[64,8,128]{2,0,1:T(8,128)S(1)}, f32[64,8,128]{2,0,1:T(8,128)}, u32[]{:S(2)}) copy-start(f32[64,8,128]{2,0,1:T(8,128)} %get-tuple-element.73) | copy-start | bytes 786436
  82.0 1.3 %copy-start.13 = (f32[63,8,128]{2,1,0:T(8,128)S(1)}, f32[63,8,128]{2,1,0:T(8,128)}, u32[]{:S(2)}) copy-start(f32[63,8,128]{2,1,0:T(8,128)} %get-tuple-element.60) | copy-start | bytes 774148
  82.0 1.4 %copy-start.15 = (f32[63,8,128]{2,1,0:T(8,128)S(1)}, f32[63,8,128]{2,1,0:T(8,128)}, u32[]{:S(2)}) copy-start(f32[63,8,128]{2,1,0:T(8,128)} %slice.508) | copy-start | bytes 774148
  83.4 2.2 %copy-start.12 = (f32[63,8,128]{2,1,0:T(8,128)S(1)}, f32[63,8,128]{2,1,0:T(8,128)}, u32[]{:S(2)}) copy-start(f32[63,8,128]{2,1,0:T(8,128)} %get-tuple-element.59) | copy-start | bytes 774148
  83.4 2.2 %copy-start.14 = (f32[63,8,128]{2,1,0:T(8,128)S(1)}, f32[63,8,128]{2,1,0:T(8,128)}, u32[]{:S(2)}) copy-start(f32[63,8,128]{2,1,0:T(8,128)} %slice.517) | copy-start | bytes 774148
  90.0 3.4 %collective-permute-start.10 = (f32[8,8,128]{2,1,0:T(8,128)}, f32[8,8,128]{2,1,0:T(8,128)S(1)}, u32[]{:S(2)}, u32[]{:S(2)}) collective-permute-start(f32[8,8,128]{2,1,0:T(8,128)} %get-tuple-element.8), channel_id=1, source_target_pairs={{0,1},{1,2},{2,3},{3,0},{4,5},{5,6},{6,7},{7,4},{8,9},{9,10},{10,1... | collective-permute-start | bytes 98312 | tf_op jit(solution)/shard_map/ppermute | solution.py:228
  90.0 4.6 %collective-permute-start.11 = (f32[8,8,128]{2,1,0:T(8,128)}, f32[8,8,128]{2,1,0:T(8,128)S(1)}, u32[]{:S(2)}, u32[]{:S(2)}) collective-permute-start(f32[8,8,128]{2,1,0:T(8,128)} %get-tuple-element.8), channel_id=1, source_target_pairs={{0,2},{1,3},{2,0},{3,1},{4,6},{5,7},{6,4},{7,5},{8,10},{9,11},{10,... | collective-permute-start | bytes 98312 | tf_op jit(solution)/shard_map/ppermute | solution.py:228
  92.8 3.4 %collective-permute-start.12 = (f32[8,8,128]{2,1,0:T(8,128)}, f32[8,8,128]{2,1,0:T(8,128)S(1)}, u32[]{:S(2)}, u32[]{:S(2)}) collective-permute-start(f32[8,8,128]{2,1,0:T(8,128)} %get-tuple-element.8), channel_id=1, source_target_pairs={{0,3},{1,0},{2,1},{3,2},{4,7},{5,4},{6,5},{7,6},{8,11},{9,8},{10,9... | collective-permute-start | bytes 98312 | tf_op jit(solution)/shard_map/ppermute | solution.py:228
  92.8 3.4 %copy-start.25 = (f32[8,8,128]{2,1,0:T(8,128)S(1)}, f32[8,8,128]{2,1,0:T(8,128)}, u32[]{:S(2)}) copy-start(f32[8,8,128]{2,1,0:T(8,128)} %get-tuple-element.8) | copy-start | bytes 98308
  98.6 7.3 %copy-start.7 = (f32[1,64,8,128]{3,2,1,0:T(8,128)S(1)}, f32[1,64,8,128]{3,2,1,0:T(8,128)}, u32[]{:S(2)}) copy-start(f32[1,64,8,128]{3,2,1,0:T(8,128)} %get-tuple-element.51) | copy-start | bytes 786436
  98.7 8.1 %collective-permute-start.14 = (f32[64,8,1]{2,1,0:T(8,128)S(1)}, f32[64,8,1]{2,1,0:T(8,128)S(1)}, u32[]{:S(2)}, u32[]{:S(2)}) collective-permute-start(f32[64,8,1]{2,1,0:T(8,128)S(1)} %slice.535), channel_id=1, source_target_pairs={{0,4},{4,8},{8,12},{1,5},{5,9},{9,13},{2,6},{6,10},{10,14},{3,7},{... | collective-permute-start | bytes 6152 | tf_op jit(solution)/shard_map/ppermute | solution.py:14
  103.1 8.3 %collective-permute-start.13 = (f32[64,1,128]{2,1,0:T(1,128)S(1)}, f32[64,1,128]{2,1,0:T(1,128)S(1)}, u32[]{:S(2)}, u32[]{:S(2)}) collective-permute-start(f32[64,1,128]{2,1,0:T(1,128)S(1)} %slice.532), channel_id=1, source_target_pairs={{0,16},{16,32},{32,48},{48,64},{64,80},{80,96},{96,112},{112,128},... | collective-permute-start | bytes 98312 | tf_op jit(solution)/shard_map/ppermute | solution.py:14
  105.9 5.5 %copy-start.11 = (f32[64,8,128]{2,0,1:T(8,128)S(1)}, f32[64,8,128]{2,0,1:T(8,128)}, u32[]{:S(2)}) copy-start(f32[64,8,128]{2,0,1:T(8,128)} %get-tuple-element.14) | copy-start | bytes 786436
  (21 other events, 17.9 us)

commit v2 on v1

--- a/solution.py
+++ b/solution.py
@@ -120,6 +120,111 @@
     )(stiffness, diagonal, source_x, source_y)
 
 
+def source_kernel(
+    flag_ref, e_ref, h_ref, rate_ref, xh_ref, xl_ref, yh_ref, yl_ref, zl_ref, zh_ref,
+    cex_ref, cey_ref, czx_ref, czy_ref, sx_ref, sy_ref, hzn_ref, szx_ref, szy_ref,
+):
+    depth, rows, lanes = sx_ref.shape
+    bottom = flag_ref[0] == 1
+    first_x = flag_ref[1] == 1
+    first_y = flag_ref[2] == 1
+    sub = lax.broadcasted_iota(jnp.int32, (rows, lanes), 0)
+    lane = lax.broadcasted_iota(jnp.int32, (rows, lanes), 1)
+
+    def full(value):
+        return jnp.broadcast_to(value, (rows, lanes))
+
+    def next_x(tile, edge):
+        return jnp.where(sub == rows - 1, full(edge), pltpu.roll(tile, rows - 1, 0))
+
+    def prev_x(tile, edge):
+        return jnp.where(sub == 0, full(edge), pltpu.roll(tile, 1, 0))
+
+    def next_y(tile, edge):
+        return jnp.where(lane == lanes - 1, full(edge), pltpu.roll(tile, lanes - 1, 1))
+
+    def prev_y(tile, edge):
+        return jnp.where(lane == 0, full(edge), pltpu.roll(tile, 1, 1))
+
+    def row(z, below, above, first_row):
+        ex, ey, ez = e_ref[0, z], e_ref[1, z], e_ref[2, z]
+        hx, hy, hz = h_ref[0, z], h_ref[1, z], h_ref[2, z]
+        keep, curl, zrate, stiff = rate_ref[0, z], rate_ref[1, z], rate_ref[2, z], rate_ref[3, z]
+        ey_xh, ez_xh = full(xh_ref[0, z]), full(xh_ref[1, z])
+        ex_xl, ey_xl, hz_xl = full(xl_ref[0, z]), full(xl_ref[1, z]), full(xl_ref[2, z])
+        ex_yh, ez_yh = full(yh_ref[0, z]), full(yh_ref[1, z])
+        ex_yl, ey_yl, hz_yl = full(yl_ref[0, z]), full(yl_ref[1, z]), full(yl_ref[2, z])
+        corner_ex = full(cex_ref[z])
+        corner_ey = full(cey_ref[z])
+        hz_new = hz - time_step * ((next_x(ey, ey_xh) - ey) - (next_y(ex, ex_yh) - ex))
+        ex_py = prev_y(ex, ex_yl)
+        ey_py = prev_y(ey, ey_yl)
+        hz_py = prev_y(hz, hz_yl)
+        face_py = (next_x(ey_py, prev_y(ey_xh, corner_ey)) - ey_py) - (ex - ex_py)
+        hz_new_py = hz_py - time_step * face_py
+        hz_new_py = jnp.where(jnp.logical_and(first_y, lane == 0), 0.0, hz_new_py)
+        ex_px = prev_x(ex, ex_xl)
+        ey_px = prev_x(ey, ey_xl)
+        hz_px = prev_x(hz, hz_xl)
+        face_px = (ey - ey_px) - (next_y(ex_px, prev_x(ex_yh, corner_ex)) - ex_px)
+        hz_new_px = hz_px - time_step * face_px
+        hz_new_px = jnp.where(jnp.logical_and(first_x, sub == 0), 0.0, hz_new_px)
+        slope_zx = next_x(ez, ez_xh) - ez
+        slope_zy = next_y(ez, ez_yh) - ez
+        ex_b, ey_b, hx_b, hy_b, slope_zx_b, slope_zy_b = below
+        ex_a, ey_a = above
+        rise_x = ex - ex_b
+        rise_y = ey - ey_b
+        if first_row:
+            rise_x = jnp.where(bottom, 0.0, rise_x)
+            rise_y = jnp.where(bottom, 0.0, rise_y)
+        quarter_z = 0.25 * zrate
+        sx_ref[z] = (
+            keep * ex
+            + stiff * ((ex_a - ex) - rise_x)
+            + curl * (hz_new - hz_new_py)
+            - zrate * (hy - hy_b)
+            - quarter_z * (slope_zx - slope_zx_b)
+        )
+        sy_ref[z] = (
+            keep * ey
+            + stiff * ((ey_a - ey) - rise_y)
+            + zrate * (hx - hx_b)
+            - quarter_z * (slope_zy - slope_zy_b)
+            - curl * (hz_new - hz_new_px)
+        )
+        hzn_ref[z] = hz_new
+        szx_ref[z] = slope_zx
+        szy_ref[z] = slope_zy
+        return (ex, ey, hx, hy, slope_zx, slope_zy)
+
+    ez_b = zl_ref[2]
+    slope_zx_b = next_x(ez_b, full(czx_ref[...])) - ez_b
+    slope_zy_b = next_y(ez_b, full(czy_ref[...])) - ez_b
+    below = (zl_ref[0], zl_ref[1], zl_ref[3], zl_ref[4], slope_zx_b, slope_zy_b)
+    below = row(0, below, (e_ref[0, 1], e_ref[1, 1]), True)
+
+    def middle(z, below):
+        return row(z, below, (e_ref[0, z + 1], e_ref[1, z + 1]), False)
+
+    below = lax.fori_loop(1, depth - 1, middle, below, unroll=2)
+    row(depth - 1, below, (zh_ref[0], zh_ref[1]), False)
+
+
+def make_sources(flags, electric, magnetic, rate_stack, x_high, x_low, y_high, y_low,
+                 z_low, z_high, corner_ex, corner_ey, corner_zx, corner_zy):
+    shape = jax.ShapeDtypeStruct(electric.shape[1:], jnp.float32)
+    vmem = pl.BlockSpec(memory_space=pltpu.VMEM)
+    smem = pl.BlockSpec(memory_space=pltpu.SMEM)
+    return pl.pallas_call(
+        source_kernel,
+        out_shape=(shape,) * 5,
+        in_specs=[smem] + [vmem] * 13,
+        out_specs=(vmem,) * 5,
+    )(flags, electric, magnetic, rate_stack, x_high, x_low, y_high, y_low,
+      z_low, z_high, corner_ex, corner_ey, corner_zx, corner_zy)
+
+
 def advance(pieces, incoming, factor):
     rows_first, rows_last, low_first, low_last, high_first, high_last = pieces
     denominator = 1.0 - low_first * factor
@@ -162,57 +267,12 @@
     corner_zx = from_diagonal(electric_z[-1:, :1, :], ("gx", "gz"), -1, 1)
     corner_zy = from_diagonal(electric_z[-1:, :, :1], ("gy", "gz"), -1, 1)
 
-    ey_xh, ez_xh = x_high[0], x_high[1]
-    ex_xl, ey_xl, hz_xl = x_low[0], x_low[1], x_low[2]
-    ex_yh, ez_yh = y_high[0], y_high[1]
-    ex_yl, ey_yl, hz_yl = y_low[0], y_low[1], y_low[2]
-    ex_zl, ey_zl, ez_zl, hx_zl, hy_zl = z_low[0], z_low[1], z_low[2], z_low[3], z_low[4]
     ex_zh, ey_zh = z_high[0], z_high[1]
-
-    ey_next_x = jnp.concatenate([electric_y[:, 1:], ey_xh], axis=1)
-    ex_next_y = jnp.concatenate([electric_x[:, :, 1:], ex_yh], axis=2)
-    face_term = (ey_next_x - electric_y) - (ex_next_y - electric_x)
-    magnetic_z_new = magnetic_z - time_step * face_term
-    ey_yl_next_x = jnp.concatenate([ey_yl[:, 1:], corner_ey], axis=1)
-    face_yl = (ey_yl_next_x - ey_yl) - (electric_x[:, :, :1] - ex_yl)
-    hz_new_yl = jnp.where(first_y, 0.0, hz_yl - time_step * face_yl)
-    ex_xl_next_y = jnp.concatenate([ex_xl[:, :, 1:], corner_ex], axis=2)
-    face_xl = (electric_y[:, :1] - ey_xl) - (ex_xl_next_y - ex_xl)
-    hz_new_xl = jnp.where(first_x, 0.0, hz_xl - time_step * face_xl)
-    hz_before_y = jnp.concatenate([hz_new_yl, magnetic_z_new[:, :, :-1]], axis=2)
-    hz_before_x = jnp.concatenate([hz_new_xl, magnetic_z_new[:, :-1]], axis=1)
-
-    ez_next_x = jnp.concatenate([electric_z[:, 1:], ez_xh], axis=1)
-    ez_next_y = jnp.concatenate([electric_z[:, :, 1:], ez_yh], axis=2)
-    slope_zx = ez_next_x - electric_z
-    slope_zy = ez_next_y - electric_z
-    slope_zx_below = jnp.concatenate([ez_zl[:, 1:], corner_zx], axis=1) - ez_zl
-    slope_zy_below = jnp.concatenate([ez_zl[:, :, 1:], corner_zy], axis=2) - ez_zl
-
-    def second_z(field, below, above):
-        column = jnp.concatenate([below, field, above], axis=0)
-        rise_steps = column[1:] - column[:-1]
-        level_index = lax.broadcasted_iota(jnp.int32, rise_steps.shape, 0)
-        rise_steps = jnp.where(jnp.logical_and(bottom, level_index == 0), 0.0, rise_steps)
-        return rise_steps[1:] - rise_steps[:-1]
-
-    def down_z(field, below):
-        return field - jnp.concatenate([below, field[:-1]], axis=0)
-
-    quarter_z = 0.25 * z_rate
-    source_x = (
-        keep_rate * electric_x
-        + stiffness * second_z(electric_x, ex_zl, ex_zh)
-        + curl_rate * (magnetic_z_new - hz_before_y)
-        - z_rate * down_z(magnetic_y, hy_zl)
-        - quarter_z * down_z(slope_zx, slope_zx_below)
-    )
-    source_y = (
-        keep_rate * electric_y
-        + stiffness * second_z(electric_y, ey_zl, ey_zh)
-        + z_rate * down_z(magnetic_x, hx_zl)
-        - quarter_z * down_z(slope_zy, slope_zy_below)
-        - curl_rate * (magnetic_z_new - hz_before_x)
+    flags = jnp.stack([bottom, first_x, first_y]).astype(jnp.int32)
+    rate_stack = jnp.stack([keep_rate, curl_rate, z_rate, stiffness])
+    source_x, source_y, magnetic_z_new, slope_zx, slope_zy = make_sources(
+        flags, electric, magnetic, rate_stack, x_high, x_low, y_high, y_low,
+        z_low[:, 0], z_high[:, 0], corner_ex, corner_ey, corner_zx[0], corner_zy[0],
     )
     level_index = lax.broadcasted_iota(jnp.int32, stiffness.shape, 0)
     diagonal = 1.0 + 2.0 * stiffness

time: 114 us -> 84.6 us (0.74)
  the two profiles are of different devices: /device:TPU:131 before, /device:TPU:97 now
where the time goes in v2:
time: 84.6 us; the launch traced here: 83.2 us
  starting transfers between devices  44.6 us (53%)
  local copies, waits for them, and re-layouts  10 us (12%)
  Pallas kernels  9.63 us (11%)
  other arithmetic  9.33 us (11%)
  waiting for transfers between devices  8.42 us (10%)
  between operations  1.24 us (1%)
    ppermute x5, starting transfers between devices, from_prev(): return lax.ppermute(block, axis, [(i, i + 1) for i in range(count - 1)])  21.5 us
    ppermute x4, starting transfers between devices, from_diagonal(): return lax.ppermute(block, axes, pairs)  14.3 us
    pallas_call x1, Pallas kernels, make_sources(): pl.pallas_call(source_kernel, out_shape=(shape,) * 5, in_specs=[smem] + [...  6.58 us
    ppermute x3, starting transfers between devices, from_next(): return lax.ppermute(block, axis, [(i + 1, i) for i in range(count - 1)])  6.08 us
    unnamed x48, local copies, waits for them, and re-layouts  3.63 us
    ppermute x3, waiting for transfers between devices, body(): lax.ppermute(own, 'gz', [(i, (i + shift) % slab_count) for i in range(sla...  3.52 us
    another operation x3, other arithmetic, body(): rate_stack = jnp.stack([keep_rate, curl_rate, z_rate, stiffness])  3.08 us
    pallas_call x1, Pallas kernels, solve_slab(): pl.pallas_call(thomas_kernel, out_shape=(shape, shape, shape, shape, edge...  3.06 us
  transfers between devices with their start and end apart: 15, of which 5 were waited for; matrix products, arithmetic and copies ran while one was open for 11% of the time, Pallas kernels for 0%

profile of v2, /device:TPU:97, one launch (start us, length us, event | category | flops | bytes accessed | tf_op | source)
XLA Modules:
  0.0 83.2 jit_solution(607474093446534065)
XLA Ops:
  0.6 1.2 %slice_bitcast_fusion = (f32[64,8,128]{2,1,0:T(8,128)S(1)}, f32[64,8,128]{2,1,0:T(8,128)S(1)}, f32[1,64,8,128]{3,2,1,0:T(8,128)S(1)}) fusion(f32[3,64,8,128]{3,2,1,0:T(8,128)} %e_ref.1), kind=kLoop, calls=%fused_computation.24 | loop fusion | bytes 1572864 | tf_op jit(solution)/shard_map/squeeze | solution.py:247
  1.9 0.9 %slice-done = f32[1,64,8,128]{3,2,1,0:T(8,128)S(1)} async-done(((f32[3,64,8,128]{3,2,1,0:T(8,128)}), f32[1,64,8,128]{3,2,1,0:T(8,128)S(1)}, s32[]{:S(2)}) %slice-start) | async-done | bytes 262168 | tf_op jit(solution)/shard_map/slice | solution.py:248
  3.7 3.9 %collective-permute-start.3 = (f32[3,64,8,1]{1,2,3,0:T(8,128)S(1)}, f32[3,64,8,1]{1,2,3,0:T(8,128)S(1)}, u32[]{:S(2)}, u32[]{:S(2)}) collective-permute-start(f32[3,64,8,1]{1,2,3,0:T(8,128)S(1)} %pad_maximum_fusion.7), channel_id=1, source_target_pairs={{0,4},{4,8},{8,12},{1,5},{5,9},{9,13},{2,6},{6,10},{10,14},{3,7},{... | collective-permute-start | bytes 18440 | tf_op jit(solution)/shard_map/ppermute | solution.py:14
  7.7 3.4 %collective-permute-start.6 = (f32[64,1,1]{2,1,0:T(1,128)S(1)}, f32[64,1,1]{2,1,0:T(1,128)S(1)}, u32[]{:S(2)}, u32[]{:S(2)}) collective-permute-start(f32[64,1,1]{2,1,0:T(1,128)S(1)} %slice.341), channel_id=1, source_target_pairs={{4,16},{8,20},{12,24},{20,32},{24,36},{28,40},{36,48},{40,52},{44,... | collective-permute-start | bytes 776 | tf_op jit(solution)/shard_map/ppermute | solution.py:31
  11.1 4.3 %collective-permute-start.7 = (f32[64,1,1]{2,0,1:T(8,128)S(1)}, f32[64,1,1]{2,0,1:T(8,128)S(1)}, u32[]{:S(2)}, u32[]{:S(2)}) collective-permute-start(f32[64,1,1]{2,0,1:T(8,128)S(1)} %slice.342), channel_id=1, source_target_pairs={{16,4},{20,8},{24,12},{32,20},{36,24},{40,28},{48,36},{52,40},{56,... | collective-permute-start | bytes 776 | tf_op jit(solution)/shard_map/ppermute | solution.py:31
  15.4 2.9 %collective-permute-start.8 = (f32[1,1,128]{2,1,0:T(1,128)S(1)}, f32[1,1,128]{2,1,0:T(1,128)S(1)}, u32[]{:S(2)}, u32[]{:S(2)}) collective-permute-start(f32[1,1,128]{2,1,0:T(1,128)S(1)} %slice.343), channel_id=1, source_target_pairs={{16,1},{17,2},{18,3},{32,17},{33,18},{34,19},{48,33},{49,34},{50,3... | collective-permute-start | bytes 1544 | tf_op jit(solution)/shard_map/ppermute | solution.py:31
  18.3 3.7 %collective-permute-start.9 = (f32[1,8,1]{2,1,0:T(8,128)S(1)}, f32[1,8,1]{2,1,0:T(8,128)S(1)}, u32[]{:S(2)}, u32[]{:S(2)}) collective-permute-start(f32[1,8,1]{2,1,0:T(8,128)S(1)} %slice.344), channel_id=1, source_target_pairs={{4,1},{5,2},{6,3},{8,5},{9,6},{10,7},{12,9},{13,10},{14,11},{20,17... | collective-permute-start | bytes 104 | tf_op jit(solution)/shard_map/ppermute | solution.py:31
  22.2 0.7 slice_bitcast_fusion.5
  24.5 1.2 %fusion.9 = (f32[1,64,8,128]{3,2,1,0:T(8,128)S(1)}, f32[64,8,128]{2,1,0:T(8,128)S(1)}, f32[64,8,128]{2,1,0:T(8,128)S(1)}) fusion(pred[64,8,128]{2,1,0:T(8,128)(4,1)S(1)} %get-tuple-element.80, f32[64]{0:T(128)S(1)} %get-tuple-element.110, pred[64,8,128]{2,1,0:T(8,128)(4,1)S(1)} %get-tuple-element.81, f32[64]{0:T(128)S(1)} %get-tuple-element.109, ...), kind=kLoop, calls=%fused_computation.43 | loop fusion | flops 2359296 | bytes 1314816 | tf_op jit(solution)/shard_map/stack | solution.py:272
  25.7 0.9 %fusion.61 = (f32[1,64,8,128]{3,2,1,0:T(8,128)S(1)}, f32[1,64,8,128]{3,2,1,0:T(8,128)S(1)}, f32[64,8,128]{2,1,0:T(8,128)}, f32[64,8,128]{2,1,0:T(8,128)S(1)}) fusion(f32[64,8,128]{2,1,0:T(8,128)S(1)} %get-tuple-element.56, f32[64,8,128]{2,1,0:T(8,128)S(1)} %get-tuple-element.55, pred[64]{0:T(512)(128)(4,1)S(1)} %compare_and_fusion), kind=kLoop, calls=%fused_computation.187 | loop fusion | flops 786432 | bytes 1572928 | tf_op jit(solution)/shard_map/stack | solution.py:272
  26.6 1.1 %pad_maximum_fusion.rate_ref = f32[4,64,8,128]{3,2,1,0:T(8,128)} fusion(f32[1,64,8,128]{3,2,1,0:T(8,128)S(1)} %bitcast.223, f32[1,64,8,128]{3,2,1,0:T(8,128)S(1)} %get-tuple-element.67, f32[1,64,8,128]{3,2,1,0:T(8,128)S(1)} %get-tuple-element.66, f32[1,64,8,128]{3,2,1,0:T(8,128)S(1)} %get-tuple-element.54), kind=kLoop, calls=%fused_computation | loop fusion | flops 786432 | bytes 2097152 | tf_op jit(solution)/shard_map/stack | solution.py:272
  28.6 2.9 %collective-permute-start = (f32[2,64,1,128]{3,1,2,0:T(8,128)S(1)}, f32[2,64,1,128]{3,1,2,0:T(8,128)S(1)}, u32[]{:S(2)}, u32[]{:S(2)}) collective-permute-start(f32[2,64,1,128]{3,1,2,0:T(8,128)S(1)} %pad_maximum_fusion.5), channel_id=1, source_target_pairs={{16,0},{32,16},{48,32},{64,48},{80,64},{96,80},{112,96},{128,112},... | collective-permute-start | bytes 196616 | tf_op jit(solution)/shard_map/ppermute | solution.py:19
  31.5 3.9 %collective-permute-start.1 = (f32[3,64,1,128]{3,1,2,0:T(8,128)S(1)}, f32[3,64,1,128]{3,1,2,0:T(8,128)S(1)}, u32[]{:S(2)}, u32[]{:S(2)}) collective-permute-start(f32[3,64,1,128]{3,1,2,0:T(8,128)S(1)} %pad_maximum_fusion.4), channel_id=1, source_target_pairs={{0,16},{16,32},{32,48},{48,64},{64,80},{80,96},{96,112},{112,128},... | collective-permute-start | bytes 294920 | tf_op jit(solution)/shard_map/ppermute | solution.py:14
  35.5 1.9 %collective-permute-start.2 = (f32[2,64,8,1]{3,2,1,0:T(8,128)S(1)}, f32[2,64,8,1]{3,2,1,0:T(8,128)S(1)}, u32[]{:S(2)}, u32[]{:S(2)}) collective-permute-start(f32[2,64,8,1]{3,2,1,0:T(8,128)S(1)} %copy.108), channel_id=1, source_target_pairs={{4,0},{8,4},{12,8},{5,1},{9,5},{13,9},{6,2},{10,6},{14,10},{7,3},{... | collective-permute-start | bytes 12296 | tf_op jit(solution)/shard_map/ppermute | solution.py:19
  37.4 2.8 %collective-permute-start.4 = (f32[5,1,8,128]{3,2,0,1:T(8,128)S(1)}, f32[5,1,8,128]{3,2,0,1:T(8,128)S(1)}, u32[]{:S(2)}, u32[]{:S(2)}) collective-permute-start(f32[5,1,8,128]{3,2,0,1:T(8,128)S(1)} %pad_maximum_fusion.6), channel_id=1, source_target_pairs={{0,1},{1,2},{2,3},{4,5},{5,6},{6,7},{8,9},{9,10},{10,11},{12,13},{... | collective-permute-start | bytes 61448 | tf_op jit(solution)/shard_map/ppermute | solution.py:14
  40.3 1.3 %collective-permute-start.5 = (f32[2,1,8,128]{3,2,1,0:T(8,128)S(1)}, f32[2,1,8,128]{3,2,1,0:T(8,128)S(1)}, u32[]{:S(2)}, u32[]{:S(2)}) collective-permute-start(f32[2,1,8,128]{3,2,1,0:T(8,128)S(1)} %stack.171), channel_id=1, source_target_pairs={{1,0},{2,1},{3,2},{5,4},{6,5},{7,6},{9,8},{10,9},{11,10},{13,12},{... | collective-permute-start | bytes 24584 | tf_op jit(solution)/shard_map/ppermute | solution.py:19
  42.2 1.2 %copy.114.yl_ref = f32[3,64,8,1]{3,2,1,0:T(8,128)} copy(f32[3,64,8,1]{1,2,3,0:T(8,128)S(1)} %collective-permute-done.3) | data formatting | bytes 12288 | tf_op jit(solution)/shard_map/ppermute | solution.py:14
  43.5 2.5 %collective-permute-done.2.yh_ref = f32[2,64,8,1]{3,2,1,0:T(8,128)S(1)} collective-permute-done((f32[2,64,8,1]{3,2,1,0:T(8,128)S(1)}, f32[2,64,8,1]{3,2,1,0:T(8,128)S(1)}, u32[]{:S(2)}, u32[]{:S(2)}) %collective-permute-start.2) | collective-permute-done | bytes 4128 | tf_op jit(solution)/shard_map/ppermute | solution.py:19
  46.0 0.7 copy-done.4
  46.8 6.6 %shard_map.77 = (f32[64,8,128]{2,1,0:T(8,128)}, f32[64,8,128]{2,1,0:T(8,128)}, f32[64,8,128]{2,1,0:T(8,128)}, f32[64,8,128]{2,1,0:T(8,128)}, f32[64,8,128]{2,1,0:T(8,128)}) custom-call(s32[3]{0:T(128)} %add_convert_fusion.flag_ref, f32[3,64,8,128]{3,2,1,0:T(8,128)} %e_ref.1, f32[3,64,8,128]{3,2,1,0:T(8,128)} %h_ref.1, ...), custom_call_target="tpu_custom_call" | custom-call | tf_op jit(solution)/shard_map/pallas_call | solution.py:219
  53.4 3.1 %shard_map.78 = (f32[64,8,128]{2,1,0:T(8,128)}, f32[64,8,128]{2,1,0:T(8,128)}, f32[64,8,128]{2,1,0:T(8,128)}, f32[64,8,128]{2,1,0:T(8,128)}, f32[8,8,128]{2,1,0:T(8,128)}) custom-call(f32[64,8,128]{2,1,0:T(8,128)} %copy-done.3, f32[64,8,128]{2,1,0:T(8,128)} %get-tuple-element.68.diag_ref, f32[64,8,128]{2,1,0:T(8,128)} %get-tuple-element.12.sx_ref, ...), custom_call_target="tpu_custom_call" | custom-call | tf_op jit(solution)/shard_map/pallas_call | solution.py:116
  56.5 2.7 %collective-permute-start.11 = (f32[8,8,128]{2,1,0:T(8,128)}, f32[8,8,128]{2,1,0:T(8,128)S(1)}, u32[]{:S(2)}, u32[]{:S(2)}) collective-permute-start(f32[8,8,128]{2,1,0:T(8,128)} %get-tuple-element.15), channel_id=1, source_target_pairs={{0,2},{1,3},{2,0},{3,1},{4,6},{5,7},{6,4},{7,5},{8,10},{9,11},{10,... | collective-permute-start | bytes 98312 | tf_op jit(solution)/shard_map/ppermute | solution.py:288
  60.0 1.0 %collective-permute-done.11 = f32[8,8,128]{2,1,0:T(8,128)S(1)} collective-permute-done((f32[8,8,128]{2,1,0:T(8,128)}, f32[8,8,128]{2,1,0:T(8,128)S(1)}, u32[]{:S(2)}, u32[]{:S(2)}) %collective-permute-start.11) | collective-permute-done | bytes 32800 | tf_op jit(solution)/shard_map/ppermute | solution.py:288
  61.0 2.3 %collective-permute-done.10 = f32[8,8,128]{2,1,0:T(8,128)S(1)} collective-permute-done((f32[8,8,128]{2,1,0:T(8,128)}, f32[8,8,128]{2,1,0:T(8,128)S(1)}, u32[]{:S(2)}, u32[]{:S(2)}) %collective-permute-start.10) | collective-permute-done | bytes 32800 | tf_op jit(solution)/shard_map/ppermute | solution.py:288
  63.4 0.8 pad_maximum_fusion.3
  65.2 1.3 %bitcast_add_fusion = (f32[64,8,128]{2,1,0:T(8,128)S(1)}, f32[64,8,128]{2,1,0:T(8,128)S(1)}, f32[64,8,128]{2,1,0:T(8,128)S(1)}, f32[64,8,128]{2,1,0:T(8,128)S(1)}) fusion(f32[3,64,8,128]{3,2,1,0:T(8,128)S(1)} %copy-done, f32[64,8,128]{2,1,0:T(8,128)} %get-tuple-element.17, f32[8,128]{1,0:T(8,128)S(1)} %get-tuple-element.85, ...), kind=kLoop, calls=%fused_computation.18 | loop fusion | flops 655360 | bytes 2637824 | tf_op jit(solution)/shard_map/add | solution.py:339
  66.5 1.1 %copy-done.2 = f32[3,64,8,128]{3,2,1,0:T(8,128)S(1)} copy-done((f32[3,64,8,128]{3,2,1,0:T(8,128)S(1)}, f32[3,64,8,128]{3,2,1,0:T(8,128)}, u32[]{:S(2)}) %copy-start.2) | copy-done | bytes 786456
  67.8 6.6 %collective-permute-start.13 = (f32[64,1,128]{2,1,0:T(1,128)S(1)}, f32[64,1,128]{2,1,0:T(1,128)S(1)}, u32[]{:S(2)}, u32[]{:S(2)}) collective-permute-start(f32[64,1,128]{2,1,0:T(1,128)S(1)} %slice.351), channel_id=1, source_target_pairs={{0,16},{16,32},{32,48},{48,64},{64,80},{80,96},{96,112},{112,128},... | collective-permute-start | bytes 98312 | tf_op jit(solution)/shard_map/ppermute | solution.py:14
  74.5 4.2 %collective-permute-start.14 = (f32[64,8,1]{2,1,0:T(8,128)S(1)}, f32[64,8,1]{2,1,0:T(8,128)S(1)}, u32[]{:S(2)}, u32[]{:S(2)}) collective-permute-start(f32[64,8,1]{2,1,0:T(8,128)S(1)} %slice.355), channel_id=1, source_target_pairs={{0,4},{4,8},{8,12},{1,5},{5,9},{9,13},{2,6},{6,10},{10,14},{3,7},{... | collective-permute-start | bytes 6152 | tf_op jit(solution)/shard_map/ppermute | solution.py:14
  78.8 0.9 %pad_maximum_fusion.2 = f32[3,64,8,128]{3,2,1,0:T(8,128)} fusion(f32[1,64,8,128]{3,2,1,0:T(8,128)S(1)} %bitcast.232, f32[1,64,8,128]{3,2,1,0:T(8,128)S(1)} %bitcast.221, f32[1,64,8,128]{3,2,1,0:T(8,128)S(1)} %bitcast.219), kind=kLoop, calls=%fused_computation.2 | loop fusion | flops 393216 | bytes 1572864 | tf_op jit(solution)/shard_map/stack | solution.py:353
  79.7 2.4 %collective-permute-done.14 = f32[64,8,1]{2,1,0:T(8,128)S(1)} collective-permute-done((f32[64,8,1]{2,1,0:T(8,128)S(1)}, f32[64,8,1]{2,1,0:T(8,128)S(1)}, u32[]{:S(2)}, u32[]{:S(2)}) %collective-permute-start.14) | collective-permute-done | bytes 2080 | tf_op jit(solution)/shard_map/ppermute | solution.py:14
  82.3 0.9 %pad_maximum_fusion.1 = f32[3,64,8,128]{3,2,1,0:T(8,128)} fusion(f32[1,64,8,128]{3,2,1,0:T(8,128)S(1)} %fusion.6, f32[1,64,8,128]{3,2,1,0:T(8,128)S(1)} %bitcast.230, f32[1,64,8,128]{3,2,1,0:T(8,128)S(1)} %bitcast.231), kind=kLoop, calls=%fused_computation.1 | loop fusion | flops 393216 | bytes 1572864 | tf_op jit(solution)/shard_map/stack | solution.py:352
  (104 shorter events, 6.8 us)
Async XLA Ops:
  1.9 1.0 %slice-start = ((f32[3,64,8,128]{3,2,1,0:T(8,128)}), f32[1,64,8,128]{3,2,1,0:T(8,128)S(1)}, s32[]{:S(2)}) async-start(f32[3,64,8,128]{3,2,1,0:T(8,128)} %h_ref.1), calls=%async_computation | async-start | bytes 524288 | tf_op jit(solution)/shard_map/slice | solution.py:248
  3.0 19.2 %copy-start.1 = (f32[3,64,8,128]{3,2,1,0:T(8,128)S(1)}, f32[3,64,8,128]{3,2,1,0:T(8,128)}, u32[]{:S(2)}) copy-start(f32[3,64,8,128]{3,2,1,0:T(8,128)} %h_ref.1) | copy-start | bytes 2359300
  3.7 19.2 %copy-start.5 = (s32[64,8,128]{2,1,0:T(8,128)S(1)}, s32[64,8,128]{2,1,0:T(8,128)}, u32[]{:S(2)}) copy-start(s32[64,8,128]{2,1,0:T(8,128)} %param.8) | copy-start | bytes 786436
  3.7 36.6 %collective-permute-start.3 = (f32[3,64,8,1]{1,2,3,0:T(8,128)S(1)}, f32[3,64,8,1]{1,2,3,0:T(8,128)S(1)}, u32[]{:S(2)}, u32[]{:S(2)}) collective-permute-start(f32[3,64,8,1]{1,2,3,0:T(8,128)S(1)} %pad_maximum_fusion.7), channel_id=1, source_target_pairs={{0,4},{4,8},{8,12},{1,5},{5,9},{9,13},{2,6},{6,10},{10,14},{3,7},{... | collective-permute-start | bytes 18440 | tf_op jit(solution)/shard_map/ppermute | solution.py:14
  7.7 23.9 %collective-permute-start.6 = (f32[64,1,1]{2,1,0:T(1,128)S(1)}, f32[64,1,1]{2,1,0:T(1,128)S(1)}, u32[]{:S(2)}, u32[]{:S(2)}) collective-permute-start(f32[64,1,1]{2,1,0:T(1,128)S(1)} %slice.341), channel_id=1, source_target_pairs={{4,16},{8,20},{12,24},{20,32},{24,36},{28,40},{36,48},{40,52},{44,... | collective-permute-start | bytes 776 | tf_op jit(solution)/shard_map/ppermute | solution.py:31
  11.1 24.4 %collective-permute-start.7 = (f32[64,1,1]{2,0,1:T(8,128)S(1)}, f32[64,1,1]{2,0,1:T(8,128)S(1)}, u32[]{:S(2)}, u32[]{:S(2)}) collective-permute-start(f32[64,1,1]{2,0,1:T(8,128)S(1)} %slice.342), channel_id=1, source_target_pairs={{16,4},{20,8},{24,12},{32,20},{36,24},{40,28},{48,36},{52,40},{56,... | collective-permute-start | bytes 776 | tf_op jit(solution)/shard_map/ppermute | solution.py:31
  15.4 22.0 %collective-permute-start.8 = (f32[1,1,128]{2,1,0:T(1,128)S(1)}, f32[1,1,128]{2,1,0:T(1,128)S(1)}, u32[]{:S(2)}, u32[]{:S(2)}) collective-permute-start(f32[1,1,128]{2,1,0:T(1,128)S(1)} %slice.343), channel_id=1, source_target_pairs={{16,1},{17,2},{18,3},{32,17},{33,18},{34,19},{48,33},{49,34},{50,3... | collective-permute-start | bytes 1544 | tf_op jit(solution)/shard_map/ppermute | solution.py:31
  18.3 10.3 %collective-permute-start.9 = (f32[1,8,1]{2,1,0:T(8,128)S(1)}, f32[1,8,1]{2,1,0:T(8,128)S(1)}, u32[]{:S(2)}, u32[]{:S(2)}) collective-permute-start(f32[1,8,1]{2,1,0:T(8,128)S(1)} %slice.344), channel_id=1, source_target_pairs={{4,1},{5,2},{6,3},{8,5},{9,6},{10,7},{12,9},{13,10},{14,11},{20,17... | collective-permute-start | bytes 104 | tf_op jit(solution)/shard_map/ppermute | solution.py:31
  26.6 1.1 %copy-start.3 = (f32[64,8,128]{2,1,0:T(8,128)}, f32[64,8,128]{2,1,0:T(8,128)S(1)}, u32[]{:S(2)}) copy-start(f32[64,8,128]{2,1,0:T(8,128)S(1)} %get-tuple-element.69.stiff_ref) | copy-start | bytes 786436
  28.6 14.8 %copy-start.17 = (f32[1,8,1]{2,1,0:T(8,128)}, f32[1,8,1]{2,1,0:T(8,128)S(1)}, u32[]{:S(2)}) copy-start(f32[1,8,1]{2,1,0:T(8,128)S(1)} %collective-permute-done.9) | copy-start | bytes 100
  28.6 17.4 %collective-permute-start = (f32[2,64,1,128]{3,1,2,0:T(8,128)S(1)}, f32[2,64,1,128]{3,1,2,0:T(8,128)S(1)}, u32[]{:S(2)}, u32[]{:S(2)}) collective-permute-start(f32[2,64,1,128]{3,1,2,0:T(8,128)S(1)} %pad_maximum_fusion.5), channel_id=1, source_target_pairs={{16,0},{32,16},{48,32},{64,48},{80,64},{96,80},{112,96},{128,112},... | collective-permute-start | bytes 196616 | tf_op jit(solution)/shard_map/ppermute | solution.py:19
  31.5 11.9 %copy-start.12 = (f32[64,1,1]{2,1,0:T(1,128)}, f32[64,1,1]{2,1,0:T(1,128)S(1)}, u32[]{:S(2)}) copy-start(f32[64,1,1]{2,1,0:T(1,128)S(1)} %collective-permute-done.6.cex_ref) | copy-start | bytes 772
  31.5 14.5 %collective-permute-start.1 = (f32[3,64,1,128]{3,1,2,0:T(8,128)S(1)}, f32[3,64,1,128]{3,1,2,0:T(8,128)S(1)}, u32[]{:S(2)}, u32[]{:S(2)}) collective-permute-start(f32[3,64,1,128]{3,1,2,0:T(8,128)S(1)} %pad_maximum_fusion.4), channel_id=1, source_target_pairs={{0,16},{16,32},{32,48},{48,64},{64,80},{80,96},{96,112},{112,128},... | collective-permute-start | bytes 294920 | tf_op jit(solution)/shard_map/ppermute | solution.py:14
  35.5 8.0 %copy-start.13 = (f32[64,1,1]{2,0,1:T(8,128)}, f32[64,1,1]{2,0,1:T(8,128)S(1)}, u32[]{:S(2)}) copy-start(f32[64,1,1]{2,0,1:T(8,128)S(1)} %collective-permute-done.7) | copy-start | bytes 772
  35.5 10.5 %collective-permute-start.2 = (f32[2,64,8,1]{3,2,1,0:T(8,128)S(1)}, f32[2,64,8,1]{3,2,1,0:T(8,128)S(1)}, u32[]{:S(2)}, u32[]{:S(2)}) collective-permute-start(f32[2,64,8,1]{3,2,1,0:T(8,128)S(1)} %copy.108), channel_id=1, source_target_pairs={{4,0},{8,4},{12,8},{5,1},{9,5},{13,9},{6,2},{10,6},{14,10},{7,3},{... | collective-permute-start | bytes 12296 | tf_op jit(solution)/shard_map/ppermute | solution.py:19
  37.4 4.2 %copy-start.20 = (f32[1,1,128]{2,1,0:T(1,128)}, f32[1,1,128]{2,1,0:T(1,128)S(1)}, u32[]{:S(2)}) copy-start(f32[1,1,128]{2,1,0:T(1,128)S(1)} %collective-permute-done.8) | copy-start | bytes 1540
  37.4 8.6 %collective-permute-start.4 = (f32[5,1,8,128]{3,2,0,1:T(8,128)S(1)}, f32[5,1,8,128]{3,2,0,1:T(8,128)S(1)}, u32[]{:S(2)}, u32[]{:S(2)}) collective-permute-start(f32[5,1,8,128]{3,2,0,1:T(8,128)S(1)} %pad_maximum_fusion.6), channel_id=1, source_target_pairs={{0,1},{1,2},{2,3},{4,5},{5,6},{6,7},{8,9},{9,10},{10,11},{12,13},{... | collective-permute-start | bytes 61448 | tf_op jit(solution)/shard_map/ppermute | solution.py:14
  40.3 5.7 %collective-permute-start.5 = (f32[2,1,8,128]{3,2,1,0:T(8,128)S(1)}, f32[2,1,8,128]{3,2,1,0:T(8,128)S(1)}, u32[]{:S(2)}, u32[]{:S(2)}) collective-permute-start(f32[2,1,8,128]{3,2,1,0:T(8,128)S(1)} %stack.171), channel_id=1, source_target_pairs={{1,0},{2,1},{3,2},{5,4},{6,5},{7,6},{9,8},{10,9},{11,10},{13,12},{... | collective-permute-start | bytes 24584 | tf_op jit(solution)/shard_map/ppermute | solution.py:19
  46.0 0.8 copy-start.4
  46.0 0.8 copy-start.14
  56.5 8.7 %copy-start = (f32[3,64,8,128]{3,2,1,0:T(8,128)S(1)}, f32[3,64,8,128]{3,2,1,0:T(8,128)}, u32[]{:S(2)}) copy-start(f32[3,64,8,128]{3,2,1,0:T(8,128)} %e_ref.1) | copy-start | bytes 2359300
  56.5 3.6 %collective-permute-start.12 = (f32[8,8,128]{2,1,0:T(8,128)}, f32[8,8,128]{2,1,0:T(8,128)S(1)}, u32[]{:S(2)}, u32[]{:S(2)}) collective-permute-start(f32[8,8,128]{2,1,0:T(8,128)} %get-tuple-element.15), channel_id=1, source_target_pairs={{0,3},{1,0},{2,1},{3,2},{4,7},{5,4},{6,5},{7,6},{8,11},{9,8},{10,9... | collective-permute-start | bytes 98312 | tf_op jit(solution)/shard_map/ppermute | solution.py:288
  56.5 4.6 %collective-permute-start.11 = (f32[8,8,128]{2,1,0:T(8,128)}, f32[8,8,128]{2,1,0:T(8,128)S(1)}, u32[]{:S(2)}, u32[]{:S(2)}) collective-permute-start(f32[8,8,128]{2,1,0:T(8,128)} %get-tuple-element.15), channel_id=1, source_target_pairs={{0,2},{1,3},{2,0},{3,1},{4,6},{5,7},{6,4},{7,5},{8,10},{9,11},{10,... | collective-permute-start | bytes 98312 | tf_op jit(solution)/shard_map/ppermute | solution.py:288
  59.2 4.2 %collective-permute-start.10 = (f32[8,8,128]{2,1,0:T(8,128)}, f32[8,8,128]{2,1,0:T(8,128)S(1)}, u32[]{:S(2)}, u32[]{:S(2)}) collective-permute-start(f32[8,8,128]{2,1,0:T(8,128)} %get-tuple-element.15), channel_id=1, source_target_pairs={{0,1},{1,2},{2,3},{3,0},{4,5},{5,6},{6,7},{7,4},{8,9},{9,10},{10,1... | collective-permute-start | bytes 98312 | tf_op jit(solution)/shard_map/ppermute | solution.py:288
  64.1 1.0 %copy-start.15 = (f32[2,1,8,128]{3,2,1,0:T(8,128)S(1)}, f32[2,1,8,128]{3,2,1,0:T(8,128)}, u32[]{:S(2)}) copy-start(f32[2,1,8,128]{3,2,1,0:T(8,128)} %copy-done.14) | copy-start | bytes 24580
  64.2 1.0 %copy-start.8 = (f32[64,8,128]{2,1,0:T(8,128)S(1)}, f32[64,8,128]{2,1,0:T(8,128)}, u32[]{:S(2)}) copy-start(f32[64,8,128]{2,1,0:T(8,128)} %get-tuple-element.14) | copy-start | bytes 786436
  65.1 1.4 %copy-start.6 = (f32[64,8,128]{2,1,0:T(8,128)S(1)}, f32[64,8,128]{2,1,0:T(8,128)}, u32[]{:S(2)}) copy-start(f32[64,8,128]{2,1,0:T(8,128)} %get-tuple-element.19) | copy-start | bytes 786436
  65.2 1.4 %copy-start.7 = (f32[64,8,128]{2,1,0:T(8,128)S(1)}, f32[64,8,128]{2,1,0:T(8,128)}, u32[]{:S(2)}) copy-start(f32[64,8,128]{2,1,0:T(8,128)} %get-tuple-element.20) | copy-start | bytes 786436
  66.4 1.1 %copy-start.2 = (f32[3,64,8,128]{3,2,1,0:T(8,128)S(1)}, f32[3,64,8,128]{3,2,1,0:T(8,128)}, u32[]{:S(2)}) copy-start(f32[3,64,8,128]{3,2,1,0:T(8,128)} %h_ref.1) | copy-start | bytes 2359300
  67.8 14.3 %collective-permute-start.13 = (f32[64,1,128]{2,1,0:T(1,128)S(1)}, f32[64,1,128]{2,1,0:T(1,128)S(1)}, u32[]{:S(2)}, u32[]{:S(2)}) collective-permute-start(f32[64,1,128]{2,1,0:T(1,128)S(1)} %slice.351), channel_id=1, source_target_pairs={{0,16},{16,32},{32,48},{48,64},{64,80},{80,96},{96,112},{112,128},... | collective-permute-start | bytes 98312 | tf_op jit(solution)/shard_map/ppermute | solution.py:14
  74.4 4.4 %copy-start.9 = (f32[64,8,128]{2,1,0:T(8,128)S(1)}, f32[64,8,128]{2,1,0:T(8,128)}, u32[]{:S(2)}) copy-start(f32[64,8,128]{2,1,0:T(8,128)} %get-tuple-element.21) | copy-start | bytes 786436
  74.5 7.5 %collective-permute-start.14 = (f32[64,8,1]{2,1,0:T(8,128)S(1)}, f32[64,8,1]{2,1,0:T(8,128)S(1)}, u32[]{:S(2)}, u32[]{:S(2)}) collective-permute-start(f32[64,8,1]{2,1,0:T(8,128)S(1)} %slice.355), channel_id=1, source_target_pairs={{0,4},{4,8},{8,12},{1,5},{5,9},{9,13},{2,6},{6,10},{10,14},{3,7},{... | collective-permute-start | bytes 6152 | tf_op jit(solution)/shard_map/ppermute | solution.py:14
  (6 other events, 4.4 us)

commit v3 on v2

--- a/solution.py
+++ b/solution.py
@@ -121,8 +121,8 @@
 
 
 def source_kernel(
-    flag_ref, e_ref, h_ref, rate_ref, xh_ref, xl_ref, yh_ref, yl_ref, zl_ref, zh_ref,
-    cex_ref, cey_ref, czx_ref, czy_ref, sx_ref, sy_ref, hzn_ref, szx_ref, szy_ref,
+    flag_ref, e_ref, h_ref, rate_ref, xh_ref, xl_ref, yh_ref, yl_ref,
+    cex_ref, cey_ref, sx_ref, sy_ref, hzn_ref, szx_ref, szy_ref,
 ):
     depth, rows, lanes = sx_ref.shape
     bottom = flag_ref[0] == 1
@@ -198,31 +198,28 @@
         szy_ref[z] = slope_zy
         return (ex, ey, hx, hy, slope_zx, slope_zy)
 
-    ez_b = zl_ref[2]
-    slope_zx_b = next_x(ez_b, full(czx_ref[...])) - ez_b
-    slope_zy_b = next_y(ez_b, full(czy_ref[...])) - ez_b
-    below = (zl_ref[0], zl_ref[1], zl_ref[3], zl_ref[4], slope_zx_b, slope_zy_b)
-    below = row(0, below, (e_ref[0, 1], e_ref[1, 1]), True)
+    zero = jnp.zeros((rows, lanes), jnp.float32)
+    below = row(0, (zero,) * 6, (e_ref[0, 1], e_ref[1, 1]), True)
 
     def middle(z, below):
         return row(z, below, (e_ref[0, z + 1], e_ref[1, z + 1]), False)
 
     below = lax.fori_loop(1, depth - 1, middle, below, unroll=2)
-    row(depth - 1, below, (zh_ref[0], zh_ref[1]), False)
+    row(depth - 1, below, (zero, zero), False)
 
 
 def make_sources(flags, electric, magnetic, rate_stack, x_high, x_low, y_high, y_low,
-                 z_low, z_high, corner_ex, corner_ey, corner_zx, corner_zy):
+                 corner_ex, corner_ey):
     shape = jax.ShapeDtypeStruct(electric.shape[1:], jnp.float32)
     vmem = pl.BlockSpec(memory_space=pltpu.VMEM)
     smem = pl.BlockSpec(memory_space=pltpu.SMEM)
     return pl.pallas_call(
         source_kernel,
         out_shape=(shape,) * 5,
-        in_specs=[smem] + [vmem] * 13,
+        in_specs=[smem] + [vmem] * 9,
         out_specs=(vmem,) * 5,
     )(flags, electric, magnetic, rate_stack, x_high, x_low, y_high, y_low,
-      z_low, z_high, corner_ex, corner_ey, corner_zx, corner_zy)
+      corner_ex, corner_ey)
 
 
 def advance(pieces, incoming, factor):
@@ -255,30 +252,25 @@
     y_low = from_prev(
         jnp.stack([electric_x[:, :, -1:], electric_y[:, :, -1:], magnetic_z[:, :, -1:]]), "gy"
     )
-    z_low = from_prev(
-        jnp.stack(
-            [electric_x[-1:], electric_y[-1:], electric_z[-1:], magnetic_x[-1:], magnetic_y[-1:]]
-        ),
-        "gz",
-    )
-    z_high = from_next(jnp.stack([electric_x[:1], electric_y[:1]]), "gz")
     corner_ex = from_diagonal(electric_x[:, -1:, :1], ("gx", "gy"), 1, -1)
     corner_ey = from_diagonal(electric_y[:, :1, -1:], ("gx", "gy"), -1, 1)
-    corner_zx = from_diagonal(electric_z[-1:, :1, :], ("gx", "gz"), -1, 1)
-    corner_zy = from_diagonal(electric_z[-1:, :, :1], ("gy", "gz"), -1, 1)
-
-    ex_zh, ey_zh = z_high[0], z_high[1]
+
     flags = jnp.stack([bottom, first_x, first_y]).astype(jnp.int32)
     rate_stack = jnp.stack([keep_rate, curl_rate, z_rate, stiffness])
     source_x, source_y, magnetic_z_new, slope_zx, slope_zy = make_sources(
         flags, electric, magnetic, rate_stack, x_high, x_low, y_high, y_low,
-        z_low[:, 0], z_high[:, 0], corner_ex, corner_ey, corner_zx[0], corner_zy[0],
+        corner_ex, corner_ey,
     )
     level_index = lax.broadcasted_iota(jnp.int32, stiffness.shape, 0)
     diagonal = 1.0 + 2.0 * stiffness
     diagonal = jnp.where(jnp.logical_and(bottom, level_index == 0), 1.0 + stiffness, diagonal)
-    partial_x, partial_y, low_weight, high_weight, own = solve_slab(
+    partial_x, partial_y, low_weight, high_weight, edges = solve_slab(
         stiffness, diagonal, source_x, source_y
+    )
+    below_x = electric_x[-1] + (magnetic_y[-1] + 0.25 * slope_zx[-1]) / 32.0
+    below_y = electric_y[-1] + (0.25 * slope_zy[-1] - magnetic_x[-1]) / 32.0
+    own = jnp.concatenate(
+        [edges, jnp.stack([below_x, below_y, electric_x[0], electric_y[0]])], axis=0
     )
 
     slab_count = lax.axis_size("gz")
@@ -293,9 +285,20 @@
         chosen = lax.dynamic_index_in_dim(
             gathered, (slab - index) % slab_count, axis=0, keepdims=False
         )
-        slabs.append(
-            (chosen[0:2], chosen[2:4], chosen[4], chosen[5], chosen[6], chosen[7])
-        )
+        slabs.append(chosen)
+    zero_pair = jnp.zeros((2,) + partial_x.shape[1:], jnp.float32)
+    below_all = [zero_pair] + [slabs[index][8:10] for index in range(slab_count - 1)]
+    above_all = [slabs[index][10:12] for index in range(1, slab_count)] + [zero_pair]
+    for index in range(slab_count):
+        chosen = slabs[index]
+        low_first, low_last, high_first, high_last = chosen[4], chosen[5], chosen[6], chosen[7]
+        rows_first = (
+            chosen[0:2] + below_all[index] * low_first[None] + above_all[index] * high_first[None]
+        )
+        rows_last = (
+            chosen[2:4] + below_all[index] * low_last[None] + above_all[index] * high_last[None]
+        )
+        slabs[index] = (rows_first, rows_last, low_first, low_last, high_first, high_last)
 
     incoming_all = []
     factor_all = []
@@ -327,8 +330,11 @@
     factor = pick(factor_all)
     following = pick(following_all)
     leading = pick(leading_all)
-
-    previous_last = incoming + factor[None] * leading
+    below = pick(below_all)
+    above = pick(above_all)
+
+    previous_last = incoming + factor[None] * leading + below
+    following = following + above
     electric_x_new = (
         partial_x + previous_last[0][None] * low_weight + following[0][None] * high_weight
     )
@@ -337,8 +343,8 @@
     )
     sum_x = electric_x + electric_x_new
     sum_y = electric_y + electric_y_new
-    top_x = ex_zh[0] + following[0]
-    top_y = ey_zh[0] + following[1]
+    top_x = following[0]
+    top_y = following[1]
     rise_x = jnp.concatenate([sum_x[1:], top_x[None]], axis=0) - sum_x
     rise_y = jnp.concatenate([sum_y[1:], top_y[None]], axis=0) - sum_y
     magnetic_y_new = magnetic_y - 0.5 * z_courant * rise_x + time_step * slope_zx

time: 84.6 us -> 72.3 us (0.85)
  starting transfers between devices: 44.6 us -> 34.5 us
  local copies, waits for them, and re-layouts: 10 us -> 8.56 us
    ppermute x5 -> x4, starting transfers between devices: 21.5 us -> 15.2 us  [from_prev(): return lax.ppermute(block, axis, [(i, i + 1) for i in range(count - 1)])]
    ppermute x4 -> x2, starting transfers between devices: 14.3 us -> 8.04 us  [from_diagonal(): return lax.ppermute(block, axes, pairs)]
    ppermute x4 -> x2, waiting for transfers between devices: 0.01 us -> 2.94 us  [from_diagonal(): return lax.ppermute(block, axes, pairs)]
    ppermute x3 -> x2, waiting for transfers between devices: 2.52 us -> 0.01 us  [from_next(): return lax.ppermute(block, axis, [(i + 1, i) for i in range(count - 1)])]
    ppermute x3 -> x2, starting transfers between devices: 6.08 us -> 7.63 us  [from_next(): return lax.ppermute(block, axis, [(i + 1, i) for i in range(count - 1)])]
    add x1, other arithmetic: 1.27 us -> 0.1 us  [body(): sum_y = electric_y + electric_y_new]
    slice x2, local copies, waits for them, and re-layouts: 0.95 us -> 0.01 us  [body(): magnetic_x, magnetic_y, magnetic_z = (magnetic[0], magnetic[1], magnetic[2])]
    ppermute x3, starting transfers between devices: 2.71 us -> 3.6 us  [body(): lax.ppermute(own, 'gz', [(i, (i + shift) % slab_count) for i in range(sla...]
  transfers between devices with their start and end apart: 15 -> 11, of which waited for: 5 -> 4; matrix products, arithmetic and copies ran while one was open for 11% -> 12% of each run, Pallas kernels for 0% -> 0%
where the time goes in v3:
time: 72.3 us; the launch traced here: 71.1 us
  starting transfers between devices  34.5 us (48%)
  Pallas kernels  9.74 us (13%)
  other arithmetic  8.66 us (12%)
  waiting for transfers between devices  8.59 us (12%)
  local copies, waits for them, and re-layouts  8.56 us (12%)
  between operations  1.07 us (1%)
    ppermute x4, starting transfers between devices, from_prev(): return lax.ppermute(block, axis, [(i, i + 1) for i in range(count - 1)])  15.2 us
    ppermute x2, starting transfers between devices, from_diagonal(): return lax.ppermute(block, axes, pairs)  8.04 us
    ppermute x2, starting transfers between devices, from_next(): return lax.ppermute(block, axis, [(i + 1, i) for i in range(count - 1)])  7.63 us
    pallas_call x1, Pallas kernels, make_sources(): pl.pallas_call(source_kernel, out_shape=(shape,) * 5, in_specs=[smem] + [...  6.6 us
    unnamed x38, local copies, waits for them, and re-layouts  3.86 us
    ppermute x3, starting transfers between devices, body(): lax.ppermute(own, 'gz', [(i, (i + shift) % slab_count) for i in range(sla...  3.6 us
    ppermute x3, waiting for transfers between devices, body(): lax.ppermute(own, 'gz', [(i, (i + shift) % slab_count) for i in range(sla...  3.28 us
    pallas_call x1, Pallas kernels, solve_slab(): pl.pallas_call(thomas_kernel, out_shape=(shape, shape, shape, shape, edge...  3.14 us
  transfers between devices with their start and end apart: 11, of which 4 were waited for; matrix products, arithmetic and copies ran while one was open for 12% of the time, Pallas kernels for 0%

profile of v3, /device:TPU:97, one launch (start us, length us, event | category | flops | bytes accessed | tf_op | source)
XLA Modules:
  0.0 71.1 jit_solution(16278808778689468665)
XLA Ops:
  0.6 1.2 %slice_bitcast_fusion = (f32[64,8,128]{2,1,0:T(8,128)S(1)}, f32[64,8,128]{2,1,0:T(8,128)S(1)}, f32[1,64,8,128]{3,2,1,0:T(8,128)S(1)}) fusion(f32[3,64,8,128]{3,2,1,0:T(8,128)} %e_ref.1), kind=kLoop, calls=%fused_computation.24 | loop fusion | bytes 1572864 | tf_op jit(solution)/shard_map/squeeze | solution.py:244
  1.9 0.6 pad_maximum_fusion.5
  2.5 4.5 %collective-permute-start = (f32[2,64,1,128]{3,1,2,0:T(8,128)}, f32[2,64,1,128]{3,1,2,0:T(8,128)}, u32[]{:S(2)}, u32[]{:S(2)}) collective-permute-start(f32[2,64,1,128]{3,1,2,0:T(8,128)} %pad_maximum_fusion.5), channel_id=1, source_target_pairs={{16,0},{32,16},{48,32},{64,48},{80,64},{96,80},{112,96},{128,112},... | collective-permute-start | bytes 196616 | tf_op jit(solution)/shard_map/ppermute | solution.py:19
  7.2 2.4 %collective-permute-start.1 = (f32[3,64,1,128]{3,1,2,0:T(8,128)S(1)}, f32[3,64,1,128]{3,1,2,0:T(8,128)}, u32[]{:S(2)}, u32[]{:S(2)}) collective-permute-start(f32[3,64,1,128]{3,1,2,0:T(8,128)S(1)} %pad_maximum_fusion.4), channel_id=1, source_target_pairs={{0,16},{16,32},{32,48},{48,64},{64,80},{80,96},{96,112},{112,128},... | collective-permute-start | bytes 294920 | tf_op jit(solution)/shard_map/ppermute | solution.py:14
  10.3 3.1 %collective-permute-start.2 = (f32[2,64,8,1]{3,2,1,0:T(8,128)S(1)}, f32[2,64,8,1]{3,2,1,0:T(8,128)S(1)}, u32[]{:S(2)}, u32[]{:S(2)}) collective-permute-start(f32[2,64,8,1]{3,2,1,0:T(8,128)S(1)} %copy.90), channel_id=1, source_target_pairs={{4,0},{8,4},{12,8},{5,1},{9,5},{13,9},{6,2},{10,6},{14,10},{7,3},{... | collective-permute-start | bytes 12296 | tf_op jit(solution)/shard_map/ppermute | solution.py:19
  14.2 3.1 %collective-permute-start.3 = (f32[3,64,8,1]{1,2,3,0:T(8,128)S(1)}, f32[3,64,8,1]{1,2,3,0:T(8,128)S(1)}, u32[]{:S(2)}, u32[]{:S(2)}) collective-permute-start(f32[3,64,8,1]{1,2,3,0:T(8,128)S(1)} %pad_maximum_fusion.6), channel_id=1, source_target_pairs={{0,4},{4,8},{8,12},{1,5},{5,9},{9,13},{2,6},{6,10},{10,14},{3,7},{... | collective-permute-start | bytes 18440 | tf_op jit(solution)/shard_map/ppermute | solution.py:14
  17.3 6.1 %collective-permute-start.4 = (f32[64,1,1]{2,1,0:T(1,128)S(1)}, f32[64,1,1]{2,1,0:T(1,128)S(1)}, u32[]{:S(2)}, u32[]{:S(2)}) collective-permute-start(f32[64,1,1]{2,1,0:T(1,128)S(1)} %slice.381), channel_id=1, source_target_pairs={{4,16},{8,20},{12,24},{20,32},{24,36},{28,40},{36,48},{40,52},{44,... | collective-permute-start | bytes 776 | tf_op jit(solution)/shard_map/ppermute | solution.py:31
  24.2 0.7 copy-done.15
  24.9 1.2 %fusion.9 = (f32[1,64,8,128]{3,2,1,0:T(8,128)S(1)}, f32[64,8,128]{2,1,0:T(8,128)S(1)}, f32[64,8,128]{2,1,0:T(8,128)S(1)}) fusion(pred[64,8,128]{2,1,0:T(8,128)(4,1)S(1)} %get-tuple-element.92, f32[64]{0:T(128)S(1)} %get-tuple-element.123, pred[64,8,128]{2,1,0:T(8,128)(4,1)S(1)} %get-tuple-element.93, f32[64]{0:T(128)S(1)} %get-tuple-element.122, ...), kind=kLoop, calls=%fused_computation.43 | loop fusion | flops 2359296 | bytes 1314816 | tf_op jit(solution)/shard_map/stack | solution.py:259
  26.1 0.9 %fusion.89 = (f32[1,64,8,128]{3,2,1,0:T(8,128)S(1)}, f32[1,64,8,128]{3,2,1,0:T(8,128)S(1)}, f32[64,8,128]{2,1,0:T(8,128)}, f32[64,8,128]{2,1,0:T(8,128)S(1)}) fusion(f32[64,8,128]{2,1,0:T(8,128)S(1)} %get-tuple-element.68, f32[64,8,128]{2,1,0:T(8,128)S(1)} %get-tuple-element.67, pred[64]{0:T(512)(128)(4,1)S(1)} %compare_and_fusion), kind=kLoop, calls=%fused_computation.229 | loop fusion | flops 786432 | bytes 1572928 | tf_op jit(solution)/shard_map/stack | solution.py:259
  27.0 1.1 %pad_maximum_fusion.rate_ref = f32[4,64,8,128]{3,2,1,0:T(8,128)} fusion(f32[1,64,8,128]{3,2,1,0:T(8,128)S(1)} %bitcast.241, f32[1,64,8,128]{3,2,1,0:T(8,128)S(1)} %get-tuple-element.79, f32[1,64,8,128]{3,2,1,0:T(8,128)S(1)} %get-tuple-element.78, f32[1,64,8,128]{3,2,1,0:T(8,128)S(1)} %get-tuple-element.66), kind=kLoop, calls=%fused_computation | loop fusion | flops 786432 | bytes 2097152 | tf_op jit(solution)/shard_map/stack | solution.py:259
  28.1 1.9 %collective-permute-start.5 = (f32[64,1,1]{2,0,1:T(8,128)S(1)}, f32[64,1,1]{2,0,1:T(8,128)S(1)}, u32[]{:S(2)}, u32[]{:S(2)}) collective-permute-start(f32[64,1,1]{2,0,1:T(8,128)S(1)} %slice.382), channel_id=1, source_target_pairs={{16,4},{20,8},{24,12},{32,20},{36,24},{40,28},{48,36},{52,40},{56,... | collective-permute-start | bytes 776 | tf_op jit(solution)/shard_map/ppermute | solution.py:31
  30.0 0.7 add_convert_fusion.flag_ref
  30.7 1.2 %copy.94.yl_ref = f32[3,64,8,1]{3,2,1,0:T(8,128)} copy(f32[3,64,8,1]{1,2,3,0:T(8,128)S(1)} %collective-permute-done.3) | data formatting | bytes 12288 | tf_op jit(solution)/shard_map/ppermute | solution.py:14
  31.9 2.9 %collective-permute-done.5 = f32[64,1,1]{2,0,1:T(8,128)S(1)} collective-permute-done((f32[64,1,1]{2,0,1:T(8,128)S(1)}, f32[64,1,1]{2,0,1:T(8,128)S(1)}, u32[]{:S(2)}, u32[]{:S(2)}) %collective-permute-start.5) | collective-permute-done | bytes 288 | tf_op jit(solution)/shard_map/ppermute | solution.py:31
  34.9 0.6 copy-done.13
  35.6 6.6 %shard_map.77 = (f32[64,8,128]{2,1,0:T(8,128)}, f32[64,8,128]{2,1,0:T(8,128)}, f32[64,8,128]{2,1,0:T(8,128)}, f32[64,8,128]{2,1,0:T(8,128)}, f32[64,8,128]{2,1,0:T(8,128)}) custom-call(s32[3]{0:T(128)} %add_convert_fusion.flag_ref, f32[3,64,8,128]{3,2,1,0:T(8,128)} %e_ref.1, f32[3,64,8,128]{3,2,1,0:T(8,128)} %h_ref.1, ...), custom_call_target="tpu_custom_call" | custom-call | tf_op jit(solution)/shard_map/pallas_call | solution.py:216
  42.2 3.1 %shard_map.78 = (f32[64,8,128]{2,1,0:T(8,128)}, f32[64,8,128]{2,1,0:T(8,128)}, f32[64,8,128]{2,1,0:T(8,128)}, f32[64,8,128]{2,1,0:T(8,128)}, f32[8,8,128]{2,1,0:T(8,128)}) custom-call(f32[64,8,128]{2,1,0:T(8,128)} %copy-done.2, f32[64,8,128]{2,1,0:T(8,128)} %get-tuple-element.80.diag_ref, f32[64,8,128]{2,1,0:T(8,128)} %get-tuple-element.12.sx_ref, ...), custom_call_target="tpu_custom_call" | custom-call | tf_op jit(solution)/shard_map/pallas_call | solution.py:116
  45.4 0.8 %constant_dynamic-update-slice_fusion.4 = f32[12,8,128]{2,1,0:T(8,128)S(1)} fusion(f32[8,8,128]{2,1,0:T(8,128)} %get-tuple-element.15), kind=kLoop, calls=%fused_computation.104 | loop fusion | bytes 65536
  46.2 0.7 constant_dynamic-update-slice_fusion.2
  46.9 2.5 %collective-permute-start.8 = (f32[12,8,128]{2,1,0:T(8,128)S(1)}, f32[12,8,128]{2,1,0:T(8,128)S(1)}, u32[]{:S(2)}, u32[]{:S(2)}) collective-permute-start(f32[12,8,128]{2,1,0:T(8,128)S(1)} %constant_dynamic-update-slice_fusion), channel_id=1, source_target_pairs={{0,3},{1,0},{2,1},{3,2},{4,7},{5,4},{6,5},{7,6},{8,11},{9,8},{10,9... | collective-permute-start | bytes 147464 | tf_op jit(solution)/shard_map/ppermute | solution.py:280
  49.3 0.5 collective-permute-start.7
  49.9 0.6 collective-permute-start.6
  50.5 0.6 dynamic-slice.23
  51.0 2.8 %collective-permute-done.7 = f32[12,8,128]{2,1,0:T(8,128)S(1)} collective-permute-done((f32[12,8,128]{2,1,0:T(8,128)S(1)}, f32[12,8,128]{2,1,0:T(8,128)S(1)}, u32[]{:S(2)}, u32[]{:S(2)}) %collective-permute-start.7) | collective-permute-done | bytes 49184 | tf_op jit(solution)/shard_map/ppermute | solution.py:280
  54.7 0.6 fusion.65
  55.7 0.9 %copy-done.5 = f32[64,8,128]{2,1,0:T(8,128)S(1)} copy-done((f32[64,8,128]{2,1,0:T(8,128)S(1)}, f32[64,8,128]{2,1,0:T(8,128)}, u32[]{:S(2)}) %copy-start.5) | copy-done | bytes 262168
  56.8 4.7 %collective-permute-start.9 = (f32[64,1,128]{2,1,0:T(1,128)S(1)}, f32[64,1,128]{2,1,0:T(1,128)S(1)}, u32[]{:S(2)}, u32[]{:S(2)}) collective-permute-start(f32[64,1,128]{2,1,0:T(1,128)S(1)} %slice.388), channel_id=1, source_target_pairs={{0,16},{16,32},{32,48},{48,64},{64,80},{80,96},{96,112},{112,128},... | collective-permute-start | bytes 98312 | tf_op jit(solution)/shard_map/ppermute | solution.py:14
  61.7 5.0 %collective-permute-start.10 = (f32[64,8,1]{2,1,0:T(8,128)S(1)}, f32[64,8,1]{2,1,0:T(8,128)S(1)}, u32[]{:S(2)}, u32[]{:S(2)}) collective-permute-start(f32[64,8,1]{2,1,0:T(8,128)S(1)} %slice.391), channel_id=1, source_target_pairs={{0,4},{4,8},{8,12},{1,5},{5,9},{9,13},{2,6},{6,10},{10,14},{3,7},{... | collective-permute-start | bytes 6152 | tf_op jit(solution)/shard_map/ppermute | solution.py:14
  66.7 0.9 %pad_maximum_fusion.2 = f32[3,64,8,128]{3,2,1,0:T(8,128)} fusion(f32[1,64,8,128]{3,2,1,0:T(8,128)S(1)} %bitcast.250, f32[1,64,8,128]{3,2,1,0:T(8,128)S(1)} %bitcast.239, f32[1,64,8,128]{3,2,1,0:T(8,128)S(1)} %bitcast.237), kind=kLoop, calls=%fused_computation.2 | loop fusion | flops 393216 | bytes 1572864 | tf_op jit(solution)/shard_map/stack | solution.py:359
  67.6 2.4 %collective-permute-done.10 = f32[64,8,1]{2,1,0:T(8,128)S(1)} collective-permute-done((f32[64,8,1]{2,1,0:T(8,128)S(1)}, f32[64,8,1]{2,1,0:T(8,128)S(1)}, u32[]{:S(2)}, u32[]{:S(2)}) %collective-permute-start.10) | collective-permute-done | bytes 2080 | tf_op jit(solution)/shard_map/ppermute | solution.py:14
  70.2 0.9 %pad_maximum_fusion.1 = f32[3,64,8,128]{3,2,1,0:T(8,128)} fusion(f32[1,64,8,128]{3,2,1,0:T(8,128)S(1)} %fusion.6, f32[1,64,8,128]{3,2,1,0:T(8,128)S(1)} %bitcast.248, f32[1,64,8,128]{3,2,1,0:T(8,128)S(1)} %bitcast.249), kind=kLoop, calls=%fused_computation.1 | loop fusion | flops 393216 | bytes 1572864 | tf_op jit(solution)/shard_map/stack | solution.py:358
  (85 shorter events, 4.4 us)
Async XLA Ops:
  2.5 4.5 %slice-start = ((f32[3,64,8,128]{3,2,1,0:T(8,128)}), f32[1,64,8,128]{3,2,1,0:T(8,128)S(1)}, s32[]{:S(2)}) async-start(f32[3,64,8,128]{3,2,1,0:T(8,128)} %h_ref.1), calls=%async_computation | async-start | bytes 524288 | tf_op jit(solution)/shard_map/slice | solution.py:245
  2.5 32.3 %collective-permute-start = (f32[2,64,1,128]{3,1,2,0:T(8,128)}, f32[2,64,1,128]{3,1,2,0:T(8,128)}, u32[]{:S(2)}, u32[]{:S(2)}) collective-permute-start(f32[2,64,1,128]{3,1,2,0:T(8,128)} %pad_maximum_fusion.5), channel_id=1, source_target_pairs={{16,0},{32,16},{48,32},{64,48},{80,64},{96,80},{112,96},{128,112},... | collective-permute-start | bytes 196616 | tf_op jit(solution)/shard_map/ppermute | solution.py:19
  7.2 27.7 %collective-permute-start.1 = (f32[3,64,1,128]{3,1,2,0:T(8,128)S(1)}, f32[3,64,1,128]{3,1,2,0:T(8,128)}, u32[]{:S(2)}, u32[]{:S(2)}) collective-permute-start(f32[3,64,1,128]{3,1,2,0:T(8,128)S(1)} %pad_maximum_fusion.4), channel_id=1, source_target_pairs={{0,16},{16,32},{32,48},{48,64},{64,80},{80,96},{96,112},{112,128},... | collective-permute-start | bytes 294920 | tf_op jit(solution)/shard_map/ppermute | solution.py:14
  10.3 24.5 %collective-permute-start.2 = (f32[2,64,8,1]{3,2,1,0:T(8,128)S(1)}, f32[2,64,8,1]{3,2,1,0:T(8,128)S(1)}, u32[]{:S(2)}, u32[]{:S(2)}) collective-permute-start(f32[2,64,8,1]{3,2,1,0:T(8,128)S(1)} %copy.90), channel_id=1, source_target_pairs={{4,0},{8,4},{12,8},{5,1},{9,5},{13,9},{6,2},{10,6},{14,10},{7,3},{... | collective-permute-start | bytes 12296 | tf_op jit(solution)/shard_map/ppermute | solution.py:19
  13.7 9.7 %copy-start.6 = (s32[64,8,128]{2,1,0:T(8,128)S(1)}, s32[64,8,128]{2,1,0:T(8,128)}, u32[]{:S(2)}) copy-start(s32[64,8,128]{2,1,0:T(8,128)} %param.8) | copy-start | bytes 786436
  14.2 13.9 %collective-permute-start.3 = (f32[3,64,8,1]{1,2,3,0:T(8,128)S(1)}, f32[3,64,8,1]{1,2,3,0:T(8,128)S(1)}, u32[]{:S(2)}, u32[]{:S(2)}) collective-permute-start(f32[3,64,8,1]{1,2,3,0:T(8,128)S(1)} %pad_maximum_fusion.6), channel_id=1, source_target_pairs={{0,4},{4,8},{8,12},{1,5},{5,9},{9,13},{2,6},{6,10},{10,14},{3,7},{... | collective-permute-start | bytes 18440 | tf_op jit(solution)/shard_map/ppermute | solution.py:14
  17.3 14.6 %collective-permute-start.4 = (f32[64,1,1]{2,1,0:T(1,128)S(1)}, f32[64,1,1]{2,1,0:T(1,128)S(1)}, u32[]{:S(2)}, u32[]{:S(2)}) collective-permute-start(f32[64,1,1]{2,1,0:T(1,128)S(1)} %slice.381), channel_id=1, source_target_pairs={{4,16},{8,20},{12,24},{20,32},{24,36},{28,40},{36,48},{40,52},{44,... | collective-permute-start | bytes 776 | tf_op jit(solution)/shard_map/ppermute | solution.py:31
  23.5 0.7 copy-start.16
  24.1 0.7 copy-start.15
  24.1 0.7 copy-start.14
  27.0 1.1 %copy-start.2 = (f32[64,8,128]{2,1,0:T(8,128)}, f32[64,8,128]{2,1,0:T(8,128)S(1)}, u32[]{:S(2)}) copy-start(f32[64,8,128]{2,1,0:T(8,128)S(1)} %get-tuple-element.81.stiff_ref) | copy-start | bytes 786436
  28.1 6.7 %collective-permute-start.5 = (f32[64,1,1]{2,0,1:T(8,128)S(1)}, f32[64,1,1]{2,0,1:T(8,128)S(1)}, u32[]{:S(2)}, u32[]{:S(2)}) collective-permute-start(f32[64,1,1]{2,0,1:T(8,128)S(1)} %slice.382), channel_id=1, source_target_pairs={{16,4},{20,8},{24,12},{32,20},{36,24},{40,28},{48,36},{52,40},{56,... | collective-permute-start | bytes 776 | tf_op jit(solution)/shard_map/ppermute | solution.py:31
  31.9 3.0 %copy-start.12 = (f32[64,1,1]{2,1,0:T(1,128)}, f32[64,1,1]{2,1,0:T(1,128)S(1)}, u32[]{:S(2)}) copy-start(f32[64,1,1]{2,1,0:T(1,128)S(1)} %collective-permute-done.4.cex_ref) | copy-start | bytes 772
  34.8 0.6 copy-start.13
  34.8 0.8 %copy-start.3 = (f32[2,64,8,1]{3,2,1,0:T(8,128)}, f32[2,64,8,1]{3,2,1,0:T(8,128)S(1)}, u32[]{:S(2)}) copy-start(f32[2,64,8,1]{3,2,1,0:T(8,128)S(1)} %collective-permute-done.2.yh_ref) | copy-start | bytes 12292
  35.6 10.5 %copy-start.1 = (f32[3,64,8,128]{3,2,1,0:T(8,128)S(1)}, f32[3,64,8,128]{3,2,1,0:T(8,128)}, u32[]{:S(2)}) copy-start(f32[3,64,8,128]{3,2,1,0:T(8,128)} %h_ref.1) | copy-start | bytes 2359300
  42.2 3.9 %copy-start = (f32[3,64,8,128]{3,2,1,0:T(8,128)S(1)}, f32[3,64,8,128]{3,2,1,0:T(8,128)}, u32[]{:S(2)}) copy-start(f32[3,64,8,128]{3,2,1,0:T(8,128)} %e_ref.1) | copy-start | bytes 2359300
  42.2 3.9 %copy-start.4 = (f32[64,8,128]{2,1,0:T(8,128)S(1)}, f32[64,8,128]{2,1,0:T(8,128)}, u32[]{:S(2)}) copy-start(f32[64,8,128]{2,1,0:T(8,128)} %get-tuple-element.16) | copy-start | bytes 786436
  46.9 4.2 %collective-permute-start.8 = (f32[12,8,128]{2,1,0:T(8,128)S(1)}, f32[12,8,128]{2,1,0:T(8,128)S(1)}, u32[]{:S(2)}, u32[]{:S(2)}) collective-permute-start(f32[12,8,128]{2,1,0:T(8,128)S(1)} %constant_dynamic-update-slice_fusion), channel_id=1, source_target_pairs={{0,3},{1,0},{2,1},{3,2},{4,7},{5,4},{6,5},{7,6},{8,11},{9,8},{10,9... | collective-permute-start | bytes 147464 | tf_op jit(solution)/shard_map/ppermute | solution.py:280
  49.3 4.5 %collective-permute-start.7 = (f32[12,8,128]{2,1,0:T(8,128)S(1)}, f32[12,8,128]{2,1,0:T(8,128)S(1)}, u32[]{:S(2)}, u32[]{:S(2)}) collective-permute-start(f32[12,8,128]{2,1,0:T(8,128)S(1)} %constant_dynamic-update-slice_fusion), channel_id=1, source_target_pairs={{0,2},{1,3},{2,0},{3,1},{4,6},{5,7},{6,4},{7,5},{8,10},{9,11},{10,... | collective-permute-start | bytes 147464 | tf_op jit(solution)/shard_map/ppermute | solution.py:280
  49.9 4.5 %collective-permute-start.6 = (f32[12,8,128]{2,1,0:T(8,128)S(1)}, f32[12,8,128]{2,1,0:T(8,128)S(1)}, u32[]{:S(2)}, u32[]{:S(2)}) collective-permute-start(f32[12,8,128]{2,1,0:T(8,128)S(1)} %constant_dynamic-update-slice_fusion), channel_id=1, source_target_pairs={{0,1},{1,2},{2,3},{3,0},{4,5},{5,6},{6,7},{7,4},{8,9},{9,10},{10,1... | collective-permute-start | bytes 147464 | tf_op jit(solution)/shard_map/ppermute | solution.py:280
  54.3 1.0 %copy-start.10 = (f32[64,8,128]{2,1,0:T(8,128)S(1)}, f32[64,8,128]{2,1,0:T(8,128)}, u32[]{:S(2)}) copy-start(f32[64,8,128]{2,1,0:T(8,128)} %get-tuple-element.19) | copy-start | bytes 786436
  54.4 1.0 %copy-start.9 = (f32[64,8,128]{2,1,0:T(8,128)S(1)}, f32[64,8,128]{2,1,0:T(8,128)}, u32[]{:S(2)}) copy-start(f32[64,8,128]{2,1,0:T(8,128)} %get-tuple-element.18) | copy-start | bytes 786436
  54.5 1.0 %copy-start.7 = (f32[64,8,128]{2,1,0:T(8,128)S(1)}, f32[64,8,128]{2,1,0:T(8,128)}, u32[]{:S(2)}) copy-start(f32[64,8,128]{2,1,0:T(8,128)} %get-tuple-element.14) | copy-start | bytes 786436
  54.5 1.1 %copy-start.8 = (f32[64,8,128]{2,1,0:T(8,128)S(1)}, f32[64,8,128]{2,1,0:T(8,128)}, u32[]{:S(2)}) copy-start(f32[64,8,128]{2,1,0:T(8,128)} %get-tuple-element.20) | copy-start | bytes 786436
  55.7 1.0 %copy-start.5 = (f32[64,8,128]{2,1,0:T(8,128)S(1)}, f32[64,8,128]{2,1,0:T(8,128)}, u32[]{:S(2)}) copy-start(f32[64,8,128]{2,1,0:T(8,128)} %get-tuple-element.17) | copy-start | bytes 786436
  56.8 13.1 %collective-permute-start.9 = (f32[64,1,128]{2,1,0:T(1,128)S(1)}, f32[64,1,128]{2,1,0:T(1,128)S(1)}, u32[]{:S(2)}, u32[]{:S(2)}) collective-permute-start(f32[64,1,128]{2,1,0:T(1,128)S(1)} %slice.388), channel_id=1, source_target_pairs={{0,16},{16,32},{32,48},{48,64},{64,80},{80,96},{96,112},{112,128},... | collective-permute-start | bytes 98312 | tf_op jit(solution)/shard_map/ppermute | solution.py:14
  61.5 5.1 %copy-start.11 = (f32[64,8,128]{2,1,0:T(8,128)S(1)}, f32[64,8,128]{2,1,0:T(8,128)}, u32[]{:S(2)}) copy-start(f32[64,8,128]{2,1,0:T(8,128)} %get-tuple-element.21) | copy-start | bytes 786436
  61.7 8.3 %collective-permute-start.10 = (f32[64,8,1]{2,1,0:T(8,128)S(1)}, f32[64,8,1]{2,1,0:T(8,128)S(1)}, u32[]{:S(2)}, u32[]{:S(2)}) collective-permute-start(f32[64,8,1]{2,1,0:T(8,128)S(1)} %slice.391), channel_id=1, source_target_pairs={{0,4},{4,8},{8,12},{1,5},{5,9},{9,13},{2,6},{6,10},{10,14},{3,7},{... | collective-permute-start | bytes 6152 | tf_op jit(solution)/shard_map/ppermute | solution.py:14

commit v4 on v3

--- a/solution.py
+++ b/solution.py
@@ -122,7 +122,8 @@
 
 def source_kernel(
     flag_ref, e_ref, h_ref, rate_ref, xh_ref, xl_ref, yh_ref, yl_ref,
-    cex_ref, cey_ref, sx_ref, sy_ref, hzn_ref, szx_ref, szy_ref,
+    cex_ref, cey_ref, hzn_ref, szx_ref, szy_ref, px_ref, py_ref, lw_ref, hw_ref, edge_ref,
+    sx_ref, sy_ref, diag_ref, ur_ref,
 ):
     depth, rows, lanes = sx_ref.shape
     bottom = flag_ref[0] == 1
@@ -175,9 +176,11 @@
         ex_a, ey_a = above
         rise_x = ex - ex_b
         rise_y = ey - ey_b
+        diag_ref[z] = 1.0 + 2.0 * stiff
         if first_row:
             rise_x = jnp.where(bottom, 0.0, rise_x)
             rise_y = jnp.where(bottom, 0.0, rise_y)
+            diag_ref[z] = jnp.where(bottom, 1.0 + stiff, 1.0 + 2.0 * stiff)
         quarter_z = 0.25 * zrate
         sx_ref[z] = (
             keep * ex
@@ -206,18 +209,27 @@
 
     below = lax.fori_loop(1, depth - 1, middle, below, unroll=2)
     row(depth - 1, below, (zero, zero), False)
+    thomas_kernel(
+        rate_ref.at[3], diag_ref, sx_ref, sy_ref, px_ref, py_ref, lw_ref, hw_ref, edge_ref, ur_ref
+    )
+    edge_ref[8] = e_ref[0, depth - 1] + (h_ref[1, depth - 1] + 0.25 * szx_ref[depth - 1]) / 32.0
+    edge_ref[9] = e_ref[1, depth - 1] + (0.25 * szy_ref[depth - 1] - h_ref[0, depth - 1]) / 32.0
+    edge_ref[10] = e_ref[0, 0]
+    edge_ref[11] = e_ref[1, 0]
 
 
 def make_sources(flags, electric, magnetic, rate_stack, x_high, x_low, y_high, y_low,
                  corner_ex, corner_ey):
     shape = jax.ShapeDtypeStruct(electric.shape[1:], jnp.float32)
+    edges = jax.ShapeDtypeStruct((12,) + electric.shape[2:], jnp.float32)
     vmem = pl.BlockSpec(memory_space=pltpu.VMEM)
     smem = pl.BlockSpec(memory_space=pltpu.SMEM)
     return pl.pallas_call(
         source_kernel,
-        out_shape=(shape,) * 5,
+        out_shape=(shape,) * 7 + (edges,),
         in_specs=[smem] + [vmem] * 9,
-        out_specs=(vmem,) * 5,
+        out_specs=(vmem,) * 8,
+        scratch_shapes=[pltpu.VMEM(electric.shape[1:], jnp.float32)] * 4,
     )(flags, electric, magnetic, rate_stack, x_high, x_low, y_high, y_low,
       corner_ex, corner_ey)
 
@@ -257,22 +269,11 @@
 
     flags = jnp.stack([bottom, first_x, first_y]).astype(jnp.int32)
     rate_stack = jnp.stack([keep_rate, curl_rate, z_rate, stiffness])
-    source_x, source_y, magnetic_z_new, slope_zx, slope_zy = make_sources(
+    (magnetic_z_new, slope_zx, slope_zy, partial_x, partial_y, low_weight, high_weight,
+     own) = make_sources(
         flags, electric, magnetic, rate_stack, x_high, x_low, y_high, y_low,
         corner_ex, corner_ey,
     )
-    level_index = lax.broadcasted_iota(jnp.int32, stiffness.shape, 0)
-    diagonal = 1.0 + 2.0 * stiffness
-    diagonal = jnp.where(jnp.logical_and(bottom, level_index == 0), 1.0 + stiffness, diagonal)
-    partial_x, partial_y, low_weight, high_weight, edges = solve_slab(
-        stiffness, diagonal, source_x, source_y
-    )
-    below_x = electric_x[-1] + (magnetic_y[-1] + 0.25 * slope_zx[-1]) / 32.0
-    below_y = electric_y[-1] + (0.25 * slope_zy[-1] - magnetic_x[-1]) / 32.0
-    own = jnp.concatenate(
-        [edges, jnp.stack([below_x, below_y, electric_x[0], electric_y[0]])], axis=0
-    )
-
     slab_count = lax.axis_size("gz")
     gathered = [own]
     for shift in range(1, slab_count):

time: 72.3 us -> 69.6 us (0.963)
  waiting for transfers between devices: 8.59 us -> 2.09 us
  starting transfers between devices: 34.5 us -> 40.4 us
  Pallas kernels: 9.74 us -> 7.71 us
    ppermute x4, starting transfers between devices: 15.2 us -> 22.6 us  [from_prev(): return lax.ppermute(block, axis, [(i, i + 1) for i in range(count - 1)])]
    ppermute x2, waiting for transfers between devices: 2.94 us -> 0.01 us  [from_diagonal(): return lax.ppermute(block, axes, pairs)]
    ppermute x2, starting transfers between devices: 7.63 us -> 5.21 us  [from_next(): return lax.ppermute(block, axis, [(i + 1, i) for i in range(count - 1)])]
    ppermute x4, waiting for transfers between devices: 2.36 us -> 0.06 us  [from_prev(): return lax.ppermute(block, axis, [(i, i + 1) for i in range(count - 1)])]
    pallas_call x2 -> x1, Pallas kernels: 9.74 us -> 7.71 us  [make_sources(): pl.pallas_call(source_kernel, out_shape=(shape,) * 7 + (edges,), in_specs...]
    ppermute x3, starting transfers between devices: 3.6 us -> 4.88 us  [body(): lax.ppermute(own, 'gz', [(i, (i + shift) % slab_count) for i in range(sla...]
    ppermute x3, waiting for transfers between devices: 3.28 us -> 2.01 us  [body(): lax.ppermute(own, 'gz', [(i, (i + shift) % slab_count) for i in range(sla...]
    add x1, other arithmetic: 0.1 us -> 1.19 us  [body(): sum_y = electric_y + electric_y_new]
  transfers between devices with their start and end apart: 11 -> 11, of which waited for: 4 -> 3; matrix products, arithmetic and copies ran while one was open for 12% -> 10% of each run, Pallas kernels for 0% -> 0%
where the time goes in v4:
time: 69.6 us; the launch traced here: 68.7 us
  starting transfers between devices  40.4 us (58%)
  local copies, waits for them, and re-layouts  8.9 us (13%)
  other arithmetic  8.45 us (12%)
  Pallas kernels  7.71 us (11%)
  waiting for transfers between devices  2.09 us (3%)
  between operations  1.13 us (2%)
    ppermute x4, starting transfers between devices, from_prev(): return lax.ppermute(block, axis, [(i, i + 1) for i in range(count - 1)])  22.6 us
    pallas_call x1, Pallas kernels, make_sources(): pl.pallas_call(source_kernel, out_shape=(shape,) * 7 + (edges,), in_specs...  7.71 us
    ppermute x2, starting transfers between devices, from_diagonal(): return lax.ppermute(block, axes, pairs)  7.67 us
    ppermute x2, starting transfers between devices, from_next(): return lax.ppermute(block, axis, [(i + 1, i) for i in range(count - 1)])  5.21 us
    ppermute x3, starting transfers between devices, body(): lax.ppermute(own, 'gz', [(i, (i + shift) % slab_count) for i in range(sla...  4.88 us
    unnamed x33, local copies, waits for them, and re-layouts  3.1 us
    another operation x3, other arithmetic, body(): rate_stack = jnp.stack([keep_rate, curl_rate, z_rate, stiffness])  2.31 us
    ppermute x3, waiting for transfers between devices, body(): lax.ppermute(own, 'gz', [(i, (i + shift) % slab_count) for i in range(sla...  2.01 us
  transfers between devices with their start and end apart: 11, of which 3 were waited for; matrix products, arithmetic and copies ran while one was open for 10% of the time, Pallas kernels for 0%

profile of v4, /device:TPU:97, one launch (start us, length us, event | category | flops | bytes accessed | tf_op | source)
XLA Modules:
  0.0 68.7 jit_solution(12574630328652879298)
XLA Ops:
  0.6 1.2 %slice_bitcast_fusion = (f32[64,8,128]{2,1,0:T(8,128)S(1)}, f32[64,8,128]{2,1,0:T(8,128)S(1)}, f32[64,8,128]{2,1,0:T(8,128)S(1)}) fusion(f32[3,64,8,128]{3,2,1,0:T(8,128)} %e_ref.1), kind=kLoop, calls=%fused_computation.21 | loop fusion | bytes 1572864 | tf_op jit(solution)/shard_map/squeeze | solution.py:256
  2.4 1.0 %slice-done = f32[1,64,8,128]{3,2,1,0:T(8,128)S(1)} async-done(((f32[3,64,8,128]{3,2,1,0:T(8,128)}), f32[1,64,8,128]{3,2,1,0:T(8,128)S(1)}, s32[]{:S(2)}) %slice-start) | async-done | bytes 262168 | tf_op jit(solution)/shard_map/slice | solution.py:257
  3.7 3.8 %collective-permute-start.3 = (f32[3,64,8,1]{1,2,3,0:T(8,128)S(1)}, f32[3,64,8,1]{1,2,3,0:T(8,128)S(1)}, u32[]{:S(2)}, u32[]{:S(2)}) collective-permute-start(f32[3,64,8,1]{1,2,3,0:T(8,128)S(1)} %pad_maximum_fusion.6), channel_id=1, source_target_pairs={{0,4},{4,8},{8,12},{1,5},{5,9},{9,13},{2,6},{6,10},{10,14},{3,7},{... | collective-permute-start | bytes 18440 | tf_op jit(solution)/shard_map/ppermute | solution.py:14
  7.6 4.5 %collective-permute-start.1 = (f32[3,64,1,128]{3,1,2,0:T(8,128)S(1)}, f32[3,64,1,128]{3,1,2,0:T(8,128)S(1)}, u32[]{:S(2)}, u32[]{:S(2)}) collective-permute-start(f32[3,64,1,128]{3,1,2,0:T(8,128)S(1)} %pad_maximum_fusion.4), channel_id=1, source_target_pairs={{0,16},{16,32},{32,48},{48,64},{64,80},{80,96},{96,112},{112,128},... | collective-permute-start | bytes 294920 | tf_op jit(solution)/shard_map/ppermute | solution.py:14
  12.4 0.3 copy.121
  12.7 2.1 %collective-permute-start.2 = (f32[2,64,8,1]{3,2,1,0:T(8,128)S(1)}, f32[2,64,8,1]{3,2,1,0:T(8,128)S(1)}, u32[]{:S(2)}, u32[]{:S(2)}) collective-permute-start(f32[2,64,8,1]{3,2,1,0:T(8,128)S(1)} %copy.121), channel_id=1, source_target_pairs={{4,0},{8,4},{12,8},{5,1},{9,5},{13,9},{6,2},{10,6},{14,10},{7,3},{... | collective-permute-start | bytes 12296 | tf_op jit(solution)/shard_map/ppermute | solution.py:19
  14.8 3.2 %collective-permute-start = (f32[2,64,1,128]{3,1,2,0:T(8,128)S(1)}, f32[2,64,1,128]{3,1,2,0:T(8,128)S(1)}, u32[]{:S(2)}, u32[]{:S(2)}) collective-permute-start(f32[2,64,1,128]{3,1,2,0:T(8,128)S(1)} %pad_maximum_fusion.5), channel_id=1, source_target_pairs={{16,0},{32,16},{48,32},{64,48},{80,64},{96,80},{112,96},{128,112},... | collective-permute-start | bytes 196616 | tf_op jit(solution)/shard_map/ppermute | solution.py:19
  18.0 2.4 %collective-permute-start.4 = (f32[64,1,1]{2,1,0:T(1,128)S(1)}, f32[64,1,1]{2,1,0:T(1,128)S(1)}, u32[]{:S(2)}, u32[]{:S(2)}) collective-permute-start(f32[64,1,1]{2,1,0:T(1,128)S(1)} %slice.331), channel_id=1, source_target_pairs={{4,16},{8,20},{12,24},{20,32},{24,36},{28,40},{36,48},{40,52},{44,... | collective-permute-start | bytes 776 | tf_op jit(solution)/shard_map/ppermute | solution.py:31
  20.5 0.3 broadcast_compare_fusion.7
  20.8 0.3 copy-done.13
  21.3 1.2 %fusion.9 = (f32[1,64,8,128]{3,2,1,0:T(8,128)S(1)}, f32[64,8,128]{2,1,0:T(8,128)S(1)}, f32[64,8,128]{2,1,0:T(8,128)S(1)}) fusion(pred[64,8,128]{2,1,0:T(8,128)(4,1)S(1)} %get-tuple-element.85, f32[64]{0:T(128)S(1)} %get-tuple-element.116, pred[64,8,128]{2,1,0:T(8,128)(4,1)S(1)} %get-tuple-element.86, f32[64]{0:T(128)S(1)} %get-tuple-element.115, ...), kind=kLoop, calls=%fused_computation.40 | loop fusion | flops 2359296 | bytes 1314816 | tf_op jit(solution)/shard_map/stack | solution.py:271
  22.5 1.0 %pad_maximum_fusion.rate_ref = f32[4,64,8,128]{3,2,1,0:T(8,128)} fusion(f32[1,64,8,128]{3,2,1,0:T(8,128)S(1)} %get-tuple-element.73, f32[1,64,8,128]{3,2,1,0:T(8,128)S(1)} %get-tuple-element.74, f32[1,64,8,128]{3,2,1,0:T(8,128)S(1)} %get-tuple-element.72, f32[1,64,8,128]{3,2,1,0:T(8,128)S(1)} %get-tuple-element.62), kind=kLoop, calls=%fused_computation | loop fusion | flops 786432 | bytes 2097152 | tf_op jit(solution)/shard_map/stack | solution.py:271
  23.7 5.3 %collective-permute-start.5 = (f32[64,1,1]{2,1,0:T(1,128)S(1)}, f32[64,1,1]{2,1,0:T(1,128)S(1)}, u32[]{:S(2)}, u32[]{:S(2)}) collective-permute-start(f32[64,1,1]{2,1,0:T(1,128)S(1)} %slice.332), channel_id=1, source_target_pairs={{16,4},{20,8},{24,12},{32,20},{36,24},{40,28},{48,36},{52,40},{56,... | collective-permute-start | bytes 776 | tf_op jit(solution)/shard_map/ppermute | solution.py:31
  29.0 0.6 add_convert_fusion.flag_ref
  29.6 1.2 %copy.126.yl_ref = f32[3,64,8,1]{3,2,1,0:T(8,128)} copy(f32[3,64,8,1]{1,2,3,0:T(8,128)S(1)} %collective-permute-done.3) | data formatting | bytes 12288 | tf_op jit(solution)/shard_map/ppermute | solution.py:14
  30.9 0.5 copy-done.11
  31.6 7.7 %shard_map.77 = (f32[64,8,128]{2,1,0:T(8,128)}, f32[64,8,128]{2,1,0:T(8,128)}, f32[64,8,128]{2,1,0:T(8,128)}, f32[64,8,128]{2,1,0:T(8,128)}, f32[64,8,128]{2,1,0...) custom-call(s32[3]{0:T(128)} %add_convert_fusion.flag_ref, ...), custom_call_target="tpu_custom_call" | custom-call | tf_op jit(solution)/shard_map/pallas_call | solution.py:227
  39.4 1.3 %collective-permute-start.6 = (f32[12,8,128]{2,1,0:T(8,128)}, f32[12,8,128]{2,1,0:T(8,128)S(1)}, u32[]{:S(2)}, u32[]{:S(2)}) collective-permute-start(f32[12,8,128]{2,1,0:T(8,128)} %get-tuple-element.11), channel_id=1, source_target_pairs={{0,1},{1,2},{2,3},{3,0},{4,5},{5,6},{6,7},{7,4},{8,9},{9,10},{10,1... | collective-permute-start | bytes 147464 | tf_op jit(solution)/shard_map/ppermute | solution.py:281
  40.6 2.5 %collective-permute-start.7 = (f32[12,8,128]{2,1,0:T(8,128)}, f32[12,8,128]{2,1,0:T(8,128)S(1)}, u32[]{:S(2)}, u32[]{:S(2)}) collective-permute-start(f32[12,8,128]{2,1,0:T(8,128)} %get-tuple-element.11), channel_id=1, source_target_pairs={{0,2},{1,3},{2,0},{3,1},{4,6},{5,7},{6,4},{7,5},{8,10},{9,11},{10,... | collective-permute-start | bytes 147464 | tf_op jit(solution)/shard_map/ppermute | solution.py:281
  43.1 1.2 %collective-permute-start.8 = (f32[12,8,128]{2,1,0:T(8,128)}, f32[12,8,128]{2,1,0:T(8,128)S(1)}, u32[]{:S(2)}, u32[]{:S(2)}) collective-permute-start(f32[12,8,128]{2,1,0:T(8,128)} %get-tuple-element.11), channel_id=1, source_target_pairs={{0,3},{1,0},{2,1},{3,2},{4,7},{5,4},{6,5},{7,6},{8,11},{9,8},{10,9... | collective-permute-start | bytes 147464 | tf_op jit(solution)/shard_map/ppermute | solution.py:281
  44.2 0.6 dynamic-slice.23
  44.8 1.0 %collective-permute-done.7 = f32[12,8,128]{2,1,0:T(8,128)S(1)} collective-permute-done((f32[12,8,128]{2,1,0:T(8,128)}, f32[12,8,128]{2,1,0:T(8,128)S(1)}, u32[]{:S(2)}, u32[]{:S(2)}) %collective-permute-start.7) | collective-permute-done | bytes 49184 | tf_op jit(solution)/shard_map/ppermute | solution.py:281
  45.8 1.0 %collective-permute-done.8 = f32[12,8,128]{2,1,0:T(8,128)S(1)} collective-permute-done((f32[12,8,128]{2,1,0:T(8,128)}, f32[12,8,128]{2,1,0:T(8,128)S(1)}, u32[]{:S(2)}, u32[]{:S(2)}) %collective-permute-start.8) | collective-permute-done | bytes 49184 | tf_op jit(solution)/shard_map/ppermute | solution.py:281
  46.8 0.8 %pad_maximum_fusion.3 = f32[4,12,8,128]{3,2,1,0:T(8,128)S(1)} fusion(f32[1,12,8,128]{3,2,1,0:T(8,128)S(1)} %bitcast.231, f32[1,12,8,128]{3,2,1,0:T(8,128)S(1)} %bitcast.230, f32[1,12,8,128]{3,2,1,0:T(8,128)S(1)} %bitcast.229, f32[1,12,8,128]{3,2,1,0:T(8,128)} %bitcast.228), kind=kLoop, calls=%fused_computation.31 | loop fusion | flops 147456 | bytes 393216 | tf_op jit(solution)/shard_map/stack | solution.py:283
  47.8 0.7 fusion.65
  48.7 0.7 %copy-done.6 = f32[64,8,128]{2,1,0:T(8,128)S(1)} copy-done((f32[64,8,128]{2,1,0:T(8,128)S(1)}, f32[64,8,128]{2,1,0:T(8,128)}, u32[]{:S(2)}) %copy-start.6) | copy-done | bytes 262168
  49.5 1.2 %fusion.87 = (f32[64,8,128]{2,1,0:T(8,128)S(1)}, f32[64,8,128]{2,1,0:T(8,128)S(1)}, f32[64,8,128]{2,1,0:T(8,128)S(1)}, f32[64,8,128]{2,1,0:T(8,128)S(1)}) fusion(f32[3,64,8,128]{3,2,1,0:T(8,128)S(1)} %copy-done, f32[64,8,128]{2,1,0:T(8,128)} %get-tuple-element.13, f32[8,128]{1,0:T(8,128)S(1)} %get-tuple-element.90, f32[64,8,128]{2,1,0:T(8,128)S(1)} %copy-done.7, ...), kind=kLoop, calls=%fused_computation.214 | loop fusion | flops 655360 | bytes 2637824 | tf_op jit(solution)/shard_map/add | solution.py:346
  50.8 1.1 %copy-done.1 = f32[3,64,8,128]{3,2,1,0:T(8,128)S(1)} copy-done((f32[3,64,8,128]{3,2,1,0:T(8,128)S(1)}, f32[3,64,8,128]{3,2,1,0:T(8,128)}, u32[]{:S(2)}) %copy-start.1) | copy-done | bytes 786456
  52.1 4.8 %collective-permute-start.10 = (f32[64,8,1]{2,1,0:T(8,128)S(1)}, f32[64,8,1]{2,1,0:T(8,128)S(1)}, u32[]{:S(2)}, u32[]{:S(2)}) collective-permute-start(f32[64,8,1]{2,1,0:T(8,128)S(1)} %slice.341), channel_id=1, source_target_pairs={{0,4},{4,8},{8,12},{1,5},{5,9},{9,13},{2,6},{6,10},{10,14},{3,7},{... | collective-permute-start | bytes 6152 | tf_op jit(solution)/shard_map/ppermute | solution.py:14
  57.0 9.5 %collective-permute-start.9 = (f32[64,1,128]{2,1,0:T(1,128)S(1)}, f32[64,1,128]{2,1,0:T(1,128)S(1)}, u32[]{:S(2)}, u32[]{:S(2)}) collective-permute-start(f32[64,1,128]{2,1,0:T(1,128)S(1)} %slice.338), channel_id=1, source_target_pairs={{0,16},{16,32},{32,48},{48,64},{64,80},{80,96},{96,112},{112,128},... | collective-permute-start | bytes 98312 | tf_op jit(solution)/shard_map/ppermute | solution.py:14
  66.6 0.9 %pad_maximum_fusion.2 = f32[3,64,8,128]{3,2,1,0:T(8,128)} fusion(f32[1,64,8,128]{3,2,1,0:T(8,128)S(1)} %bitcast.221, f32[1,64,8,128]{3,2,1,0:T(8,128)S(1)} %bitcast.214, f32[1,64,8,128]{3,2,1,0:T(8,128)S(1)} %bitcast.212), kind=kLoop, calls=%fused_computation.2 | loop fusion | flops 393216 | bytes 1572864 | tf_op jit(solution)/shard_map/stack | solution.py:360
  67.8 0.9 %pad_maximum_fusion.1 = f32[3,64,8,128]{3,2,1,0:T(8,128)} fusion(f32[1,64,8,128]{3,2,1,0:T(8,128)S(1)} %fusion.6, f32[1,64,8,128]{3,2,1,0:T(8,128)S(1)} %bitcast.219, f32[1,64,8,128]{3,2,1,0:T(8,128)S(1)} %bitcast.220), kind=kLoop, calls=%fused_computation.1 | loop fusion | flops 393216 | bytes 1572864 | tf_op jit(solution)/shard_map/stack | solution.py:359
  (76 shorter events, 3.0 us)
Async XLA Ops:
  2.4 1.0 %slice-start = ((f32[3,64,8,128]{3,2,1,0:T(8,128)}), f32[1,64,8,128]{3,2,1,0:T(8,128)S(1)}, s32[]{:S(2)}) async-start(f32[3,64,8,128]{3,2,1,0:T(8,128)} %h_ref.1), calls=%async_computation | async-start | bytes 524288 | tf_op jit(solution)/shard_map/slice | solution.py:257
  3.7 20.0 %collective-permute-start.3 = (f32[3,64,8,1]{1,2,3,0:T(8,128)S(1)}, f32[3,64,8,1]{1,2,3,0:T(8,128)S(1)}, u32[]{:S(2)}, u32[]{:S(2)}) collective-permute-start(f32[3,64,8,1]{1,2,3,0:T(8,128)S(1)} %pad_maximum_fusion.6), channel_id=1, source_target_pairs={{0,4},{4,8},{8,12},{1,5},{5,9},{9,13},{2,6},{6,10},{10,14},{3,7},{... | collective-permute-start | bytes 18440 | tf_op jit(solution)/shard_map/ppermute | solution.py:14
  7.6 23.3 %collective-permute-start.1 = (f32[3,64,1,128]{3,1,2,0:T(8,128)S(1)}, f32[3,64,1,128]{3,1,2,0:T(8,128)S(1)}, u32[]{:S(2)}, u32[]{:S(2)}) collective-permute-start(f32[3,64,1,128]{3,1,2,0:T(8,128)S(1)} %pad_maximum_fusion.4), channel_id=1, source_target_pairs={{0,16},{16,32},{32,48},{48,64},{64,80},{80,96},{96,112},{112,128},... | collective-permute-start | bytes 294920 | tf_op jit(solution)/shard_map/ppermute | solution.py:14
  12.7 7.8 %copy-start.3 = (s32[64,8,128]{2,1,0:T(8,128)S(1)}, s32[64,8,128]{2,1,0:T(8,128)}, u32[]{:S(2)}) copy-start(s32[64,8,128]{2,1,0:T(8,128)} %param.8) | copy-start | bytes 786436
  12.7 18.1 %collective-permute-start.2 = (f32[2,64,8,1]{3,2,1,0:T(8,128)S(1)}, f32[2,64,8,1]{3,2,1,0:T(8,128)S(1)}, u32[]{:S(2)}, u32[]{:S(2)}) collective-permute-start(f32[2,64,8,1]{3,2,1,0:T(8,128)S(1)} %copy.121), channel_id=1, source_target_pairs={{4,0},{8,4},{12,8},{5,1},{9,5},{13,9},{6,2},{10,6},{14,10},{7,3},{... | collective-permute-start | bytes 12296 | tf_op jit(solution)/shard_map/ppermute | solution.py:19
  14.8 5.6 %copy-start.15 = (s32[64]{0:T(128)S(1)}, s32[64]{0:T(128)}, u32[]{:S(2)}) copy-start(s32[64]{0:T(128)} %param.9) | copy-start | bytes 772
  14.8 16.0 %collective-permute-start = (f32[2,64,1,128]{3,1,2,0:T(8,128)S(1)}, f32[2,64,1,128]{3,1,2,0:T(8,128)S(1)}, u32[]{:S(2)}, u32[]{:S(2)}) collective-permute-start(f32[2,64,1,128]{3,1,2,0:T(8,128)S(1)} %pad_maximum_fusion.5), channel_id=1, source_target_pairs={{16,0},{32,16},{48,32},{64,48},{80,64},{96,80},{112,96},{128,112},... | collective-permute-start | bytes 196616 | tf_op jit(solution)/shard_map/ppermute | solution.py:19
  18.0 12.8 %collective-permute-start.4 = (f32[64,1,1]{2,1,0:T(1,128)S(1)}, f32[64,1,1]{2,1,0:T(1,128)S(1)}, u32[]{:S(2)}, u32[]{:S(2)}) collective-permute-start(f32[64,1,1]{2,1,0:T(1,128)S(1)} %slice.331), channel_id=1, source_target_pairs={{4,16},{8,20},{12,24},{20,32},{24,36},{28,40},{36,48},{40,52},{44,... | collective-permute-start | bytes 776 | tf_op jit(solution)/shard_map/ppermute | solution.py:31
  20.5 0.7 copy-start.13
  20.5 0.7 %copy-start.14 = (f32[4,8]{1,0:T(4,128)S(1)}, f32[4,8]{1,0:T(4,128)}, u32[]{:S(2)}) copy-start(f32[4,8]{1,0:T(4,128)} %param.10) | copy-start | bytes 388
  23.7 7.1 %collective-permute-start.5 = (f32[64,1,1]{2,1,0:T(1,128)S(1)}, f32[64,1,1]{2,1,0:T(1,128)S(1)}, u32[]{:S(2)}, u32[]{:S(2)}) collective-permute-start(f32[64,1,1]{2,1,0:T(1,128)S(1)} %slice.332), channel_id=1, source_target_pairs={{16,4},{20,8},{24,12},{32,20},{36,24},{40,28},{48,36},{52,40},{56,... | collective-permute-start | bytes 776 | tf_op jit(solution)/shard_map/ppermute | solution.py:31
  30.8 0.6 copy-start.11
  30.8 0.6 copy-start.12
  30.8 0.8 %copy-start.2 = (f32[2,64,8,1]{3,2,1,0:T(8,128)}, f32[2,64,8,1]{3,2,1,0:T(8,128)S(1)}, u32[]{:S(2)}) copy-start(f32[2,64,8,1]{3,2,1,0:T(8,128)S(1)} %collective-permute-done.2.yh_ref) | copy-start | bytes 12292
  30.8 0.8 %copy-start.10 = (f32[2,64,1,128]{3,1,2,0:T(8,128)}, f32[2,64,1,128]{3,1,2,0:T(8,128)S(1)}, u32[]{:S(2)}) copy-start(f32[2,64,1,128]{3,1,2,0:T(8,128)S(1)} %collective-permute-done) | copy-start | bytes 196612
  30.9 0.8 %copy-start.9 = (f32[3,64,1,128]{3,1,2,0:T(8,128)}, f32[3,64,1,128]{3,1,2,0:T(8,128)S(1)}, u32[]{:S(2)}) copy-start(f32[3,64,1,128]{3,1,2,0:T(8,128)S(1)} %collective-permute-done.1) | copy-start | bytes 294916
  39.4 9.3 %copy-start = (f32[3,64,8,128]{3,2,1,0:T(8,128)S(1)}, f32[3,64,8,128]{3,2,1,0:T(8,128)}, u32[]{:S(2)}) copy-start(f32[3,64,8,128]{3,2,1,0:T(8,128)} %e_ref.1) | copy-start | bytes 2359300
  39.4 5.5 %collective-permute-start.6 = (f32[12,8,128]{2,1,0:T(8,128)}, f32[12,8,128]{2,1,0:T(8,128)S(1)}, u32[]{:S(2)}, u32[]{:S(2)}) collective-permute-start(f32[12,8,128]{2,1,0:T(8,128)} %get-tuple-element.11), channel_id=1, source_target_pairs={{0,1},{1,2},{2,3},{3,0},{4,5},{5,6},{6,7},{7,4},{8,9},{9,10},{10,1... | collective-permute-start | bytes 147464 | tf_op jit(solution)/shard_map/ppermute | solution.py:281
  40.6 5.2 %collective-permute-start.7 = (f32[12,8,128]{2,1,0:T(8,128)}, f32[12,8,128]{2,1,0:T(8,128)S(1)}, u32[]{:S(2)}, u32[]{:S(2)}) collective-permute-start(f32[12,8,128]{2,1,0:T(8,128)} %get-tuple-element.11), channel_id=1, source_target_pairs={{0,2},{1,3},{2,0},{3,1},{4,6},{5,7},{6,4},{7,5},{8,10},{9,11},{10,... | collective-permute-start | bytes 147464 | tf_op jit(solution)/shard_map/ppermute | solution.py:281
  43.1 3.8 %collective-permute-start.8 = (f32[12,8,128]{2,1,0:T(8,128)}, f32[12,8,128]{2,1,0:T(8,128)S(1)}, u32[]{:S(2)}, u32[]{:S(2)}) collective-permute-start(f32[12,8,128]{2,1,0:T(8,128)} %get-tuple-element.11), channel_id=1, source_target_pairs={{0,3},{1,0},{2,1},{3,2},{4,7},{5,4},{6,5},{7,6},{8,11},{9,8},{10,9... | collective-permute-start | bytes 147464 | tf_op jit(solution)/shard_map/ppermute | solution.py:281
  48.5 1.0 %copy-start.6 = (f32[64,8,128]{2,1,0:T(8,128)S(1)}, f32[64,8,128]{2,1,0:T(8,128)}, u32[]{:S(2)}) copy-start(f32[64,8,128]{2,1,0:T(8,128)} %get-tuple-element.10) | copy-start | bytes 786436
  48.5 1.0 %copy-start.7 = (f32[64,8,128]{2,1,0:T(8,128)S(1)}, f32[64,8,128]{2,1,0:T(8,128)}, u32[]{:S(2)}) copy-start(f32[64,8,128]{2,1,0:T(8,128)} %get-tuple-element.14) | copy-start | bytes 786436
  49.5 1.3 %copy-start.4 = (f32[64,8,128]{2,1,0:T(8,128)S(1)}, f32[64,8,128]{2,1,0:T(8,128)}, u32[]{:S(2)}) copy-start(f32[64,8,128]{2,1,0:T(8,128)} %get-tuple-element.15) | copy-start | bytes 786436
  49.5 1.3 %copy-start.5 = (f32[64,8,128]{2,1,0:T(8,128)S(1)}, f32[64,8,128]{2,1,0:T(8,128)}, u32[]{:S(2)}) copy-start(f32[64,8,128]{2,1,0:T(8,128)} %get-tuple-element.16) | copy-start | bytes 786436
  50.7 1.1 %copy-start.1 = (f32[3,64,8,128]{3,2,1,0:T(8,128)S(1)}, f32[3,64,8,128]{3,2,1,0:T(8,128)}, u32[]{:S(2)}) copy-start(f32[3,64,8,128]{3,2,1,0:T(8,128)} %h_ref.1) | copy-start | bytes 2359300
  52.0 14.5 %copy-start.8 = (f32[64,8,128]{2,1,0:T(8,128)S(1)}, f32[64,8,128]{2,1,0:T(8,128)}, u32[]{:S(2)}) copy-start(f32[64,8,128]{2,1,0:T(8,128)} %get-tuple-element.17) | copy-start | bytes 786436
  52.1 15.4 %collective-permute-start.10 = (f32[64,8,1]{2,1,0:T(8,128)S(1)}, f32[64,8,1]{2,1,0:T(8,128)S(1)}, u32[]{:S(2)}, u32[]{:S(2)}) collective-permute-start(f32[64,8,1]{2,1,0:T(8,128)S(1)} %slice.341), channel_id=1, source_target_pairs={{0,4},{4,8},{8,12},{1,5},{5,9},{9,13},{2,6},{6,10},{10,14},{3,7},{... | collective-permute-start | bytes 6152 | tf_op jit(solution)/shard_map/ppermute | solution.py:14
  57.0 10.5 %collective-permute-start.9 = (f32[64,1,128]{2,1,0:T(1,128)S(1)}, f32[64,1,128]{2,1,0:T(1,128)S(1)}, u32[]{:S(2)}, u32[]{:S(2)}) collective-permute-start(f32[64,1,128]{2,1,0:T(1,128)S(1)} %slice.338), channel_id=1, source_target_pairs={{0,16},{16,32},{32,48},{48,64},{64,80},{80,96},{96,112},{112,128},... | collective-permute-start | bytes 98312 | tf_op jit(solution)/shard_map/ppermute | solution.py:14

commit v5 on v4

--- a/solution.py
+++ b/solution.py
@@ -275,18 +275,10 @@
         corner_ex, corner_ey,
     )
     slab_count = lax.axis_size("gz")
-    gathered = [own]
-    for shift in range(1, slab_count):
-        gathered.append(
-            lax.ppermute(own, "gz", [(i, (i + shift) % slab_count) for i in range(slab_count)])
-        )
-    gathered = jnp.stack(gathered)
-    slabs = []
-    for index in range(slab_count):
-        chosen = lax.dynamic_index_in_dim(
-            gathered, (slab - index) % slab_count, axis=0, keepdims=False
-        )
-        slabs.append(chosen)
+    gathered = lax.all_to_all(
+        jnp.broadcast_to(own[None], (slab_count,) + own.shape), "gz", 0, 0
+    )
+    slabs = [gathered[index] for index in range(slab_count)]
     zero_pair = jnp.zeros((2,) + partial_x.shape[1:], jnp.float32)
     below_all = [zero_pair] + [slabs[index][8:10] for index in range(slab_count - 1)]
     above_all = [slabs[index][10:12] for index in range(1, slab_count)] + [zero_pair]

time: 69.6 us -> 72.5 us (1.042)
  waiting for transfers between devices: 2.09 us -> 5.33 us
  local copies, waits for them, and re-layouts: 8.9 us -> 10.5 us
  starting transfers between devices: 40.4 us -> 39.4 us
  other arithmetic: 8.45 us -> 7.51 us
    all_to_all x0 -> x1, waiting for transfers between devices: none -> 5.25 us  [body(): lax.all_to_all(jnp.broadcast_to(own[None], (slab_count,) + own.shape), 'g...]
    ppermute x3 -> x0, starting transfers between devices: 4.88 us -> none  [body(): lax.ppermute(own, 'gz', [(i, (i + shift) % slab_count) for i in range(sla...]
    all_to_all x0 -> x1, starting transfers between devices: none -> 4.01 us  [body(): lax.all_to_all(jnp.broadcast_to(own[None], (slab_count,) + own.shape), 'g...]
    ppermute x3 -> x0, waiting for transfers between devices: 2.01 us -> none  [body(): lax.ppermute(own, 'gz', [(i, (i + shift) % slab_count) for i in range(sla...]
    broadcast_in_dim x0 -> x1, local copies, waits for them, and re-layouts: none -> 1.56 us  [body(): jnp.broadcast_to(own[None], (slab_count,) + own.shape)]
    another operation x1, other arithmetic: 0.81 us -> 0.03 us  [body(): above_all[index] * high_first[None]]
    unnamed x33 -> x35, local copies, waits for them, and re-layouts: 3.1 us -> 3.16 us
  transfers between devices with their start and end apart: 11 -> 9, of which waited for: 3 -> 2; matrix products, arithmetic and copies ran while one was open for 10% -> 10% of each run, Pallas kernels for 0% -> 0%
where the time goes in v5:
time: 72.5 us; the launch traced here: 71.6 us
  starting transfers between devices  39.4 us (54%)
  local copies, waits for them, and re-layouts  10.5 us (14%)
  Pallas kernels  7.68 us (11%)
  other arithmetic  7.51 us (10%)
  waiting for transfers between devices  5.33 us (7%)
  between operations  1.15 us (2%)
    ppermute x4, starting transfers between devices, from_prev(): return lax.ppermute(block, axis, [(i, i + 1) for i in range(count - 1)])  22.5 us
    pallas_call x1, Pallas kernels, make_sources(): pl.pallas_call(source_kernel, out_shape=(shape,) * 7 + (edges,), in_specs...  7.68 us
    ppermute x2, starting transfers between devices, from_diagonal(): return lax.ppermute(block, axes, pairs)  7.67 us
    all_to_all x1, waiting for transfers between devices, body(): lax.all_to_all(jnp.broadcast_to(own[None], (slab_count,) + own.shape), 'g...  5.25 us
    ppermute x2, starting transfers between devices, from_next(): return lax.ppermute(block, axis, [(i + 1, i) for i in range(count - 1)])  5.21 us
    all_to_all x1, starting transfers between devices, body(): lax.all_to_all(jnp.broadcast_to(own[None], (slab_count,) + own.shape), 'g...  4.01 us
    unnamed x35, local copies, waits for them, and re-layouts  3.16 us
    another operation x3, other arithmetic, body(): rate_stack = jnp.stack([keep_rate, curl_rate, z_rate, stiffness])  2.31 us
  transfers between devices with their start and end apart: 9, of which 2 were waited for; matrix products, arithmetic and copies ran while one was open for 10% of the time, Pallas kernels for 0%

profile of v5, /device:TPU:97, one launch (start us, length us, event | category | flops | bytes accessed | tf_op | source)
XLA Modules:
  0.0 71.6 jit_solution(107192285546931425)
XLA Ops:
  0.6 1.2 %slice_bitcast_fusion = (f32[64,8,128]{2,1,0:T(8,128)S(1)}, f32[64,8,128]{2,1,0:T(8,128)S(1)}, f32[64,8,128]{2,1,0:T(8,128)S(1)}) fusion(f32[3,64,8,128]{3,2,1,0:T(8,128)} %e_ref.1), kind=kLoop, calls=%fused_computation.21 | loop fusion | bytes 1572864 | tf_op jit(solution)/shard_map/squeeze | solution.py:256
  2.4 1.0 %slice-done = f32[1,64,8,128]{3,2,1,0:T(8,128)S(1)} async-done(((f32[3,64,8,128]{3,2,1,0:T(8,128)}), f32[1,64,8,128]{3,2,1,0:T(8,128)S(1)}, s32[]{:S(2)}) %slice-start) | async-done | bytes 262168 | tf_op jit(solution)/shard_map/slice | solution.py:257
  3.4 0.3 slice_reduce_fusion
  3.7 3.8 %collective-permute-start.3 = (f32[3,64,8,1]{1,2,3,0:T(8,128)S(1)}, f32[3,64,8,1]{1,2,3,0:T(8,128)S(1)}, u32[]{:S(2)}, u32[]{:S(2)}) collective-permute-start(f32[3,64,8,1]{1,2,3,0:T(8,128)S(1)} %pad_maximum_fusion.5), channel_id=1, source_target_pairs={{0,4},{4,8},{8,12},{1,5},{5,9},{9,13},{2,6},{6,10},{10,14},{3,7},{... | collective-permute-start | bytes 18440 | tf_op jit(solution)/shard_map/ppermute | solution.py:14
  7.6 4.5 %collective-permute-start.1 = (f32[3,64,1,128]{3,1,2,0:T(8,128)S(1)}, f32[3,64,1,128]{3,1,2,0:T(8,128)S(1)}, u32[]{:S(2)}, u32[]{:S(2)}) collective-permute-start(f32[3,64,1,128]{3,1,2,0:T(8,128)S(1)} %pad_maximum_fusion.3), channel_id=1, source_target_pairs={{0,16},{16,32},{32,48},{48,64},{64,80},{80,96},{96,112},{112,128},... | collective-permute-start | bytes 294920 | tf_op jit(solution)/shard_map/ppermute | solution.py:14
  12.4 0.3 copy.121
  12.7 2.1 %collective-permute-start.2 = (f32[2,64,8,1]{3,2,1,0:T(8,128)S(1)}, f32[2,64,8,1]{3,2,1,0:T(8,128)S(1)}, u32[]{:S(2)}, u32[]{:S(2)}) collective-permute-start(f32[2,64,8,1]{3,2,1,0:T(8,128)S(1)} %copy.121), channel_id=1, source_target_pairs={{4,0},{8,4},{12,8},{5,1},{9,5},{13,9},{6,2},{10,6},{14,10},{7,3},{... | collective-permute-start | bytes 12296 | tf_op jit(solution)/shard_map/ppermute | solution.py:19
  14.8 3.2 %collective-permute-start = (f32[2,64,1,128]{3,1,2,0:T(8,128)S(1)}, f32[2,64,1,128]{3,1,2,0:T(8,128)S(1)}, u32[]{:S(2)}, u32[]{:S(2)}) collective-permute-start(f32[2,64,1,128]{3,1,2,0:T(8,128)S(1)} %pad_maximum_fusion.4), channel_id=1, source_target_pairs={{16,0},{32,16},{48,32},{64,48},{80,64},{96,80},{112,96},{128,112},... | collective-permute-start | bytes 196616 | tf_op jit(solution)/shard_map/ppermute | solution.py:19
  18.0 2.4 %collective-permute-start.4 = (f32[64,1,1]{2,1,0:T(1,128)S(1)}, f32[64,1,1]{2,1,0:T(1,128)S(1)}, u32[]{:S(2)}, u32[]{:S(2)}) collective-permute-start(f32[64,1,1]{2,1,0:T(1,128)S(1)} %slice.370), channel_id=1, source_target_pairs={{4,16},{8,20},{12,24},{20,32},{24,36},{28,40},{36,48},{40,52},{44,... | collective-permute-start | bytes 776 | tf_op jit(solution)/shard_map/ppermute | solution.py:31
  20.5 0.3 broadcast_compare_fusion.7
  20.8 0.3 copy-done.14
  21.3 1.2 %fusion.9 = (f32[1,64,8,128]{3,2,1,0:T(8,128)S(1)}, f32[64,8,128]{2,1,0:T(8,128)S(1)}, f32[64,8,128]{2,1,0:T(8,128)S(1)}) fusion(pred[64,8,128]{2,1,0:T(8,128)(4,1)S(1)} %get-tuple-element.69, f32[64]{0:T(128)S(1)} %get-tuple-element.125, pred[64,8,128]{2,1,0:T(8,128)(4,1)S(1)} %get-tuple-element.70, f32[64]{0:T(128)S(1)} %get-tuple-element.124, ...), kind=kLoop, calls=%fused_computation.39 | loop fusion | flops 2359296 | bytes 1314816 | tf_op jit(solution)/shard_map/stack | solution.py:271
  22.5 1.1 %pad_maximum_fusion.rate_ref = f32[4,64,8,128]{3,2,1,0:T(8,128)} fusion(f32[1,64,8,128]{3,2,1,0:T(8,128)S(1)} %get-tuple-element.57, f32[1,64,8,128]{3,2,1,0:T(8,128)S(1)} %get-tuple-element.58, f32[1,64,8,128]{3,2,1,0:T(8,128)S(1)} %get-tuple-element.56, f32[1,64,8,128]{3,2,1,0:T(8,128)S(1)} %get-tuple-element.46), kind=kLoop, calls=%fused_computation | loop fusion | flops 786432 | bytes 2097152 | tf_op jit(solution)/shard_map/stack | solution.py:271
  23.7 5.3 %collective-permute-start.5 = (f32[64,1,1]{2,1,0:T(1,128)S(1)}, f32[64,1,1]{2,1,0:T(1,128)S(1)}, u32[]{:S(2)}, u32[]{:S(2)}) collective-permute-start(f32[64,1,1]{2,1,0:T(1,128)S(1)} %slice.371), channel_id=1, source_target_pairs={{16,4},{20,8},{24,12},{32,20},{36,24},{40,28},{48,36},{52,40},{56,... | collective-permute-start | bytes 776 | tf_op jit(solution)/shard_map/ppermute | solution.py:31
  29.0 0.6 add_convert_fusion.flag_ref
  29.6 1.2 %copy.126.yl_ref = f32[3,64,8,1]{3,2,1,0:T(8,128)} copy(f32[3,64,8,1]{1,2,3,0:T(8,128)S(1)} %collective-permute-done.3) | data formatting | bytes 12288 | tf_op jit(solution)/shard_map/ppermute | solution.py:14
  30.9 0.5 copy-done.12
  31.4 0.2 copy-done.2
  31.7 7.7 %shard_map.77 = (f32[64,8,128]{2,1,0:T(8,128)}, f32[64,8,128]{2,1,0:T(8,128)}, f32[64,8,128]{2,1,0:T(8,128)}, f32[64,8,128]{2,1,0:T(8,128)}, f32[64,8,128]{2,1,0...) custom-call(s32[3]{0:T(128)} %add_convert_fusion.flag_ref, ...), custom_call_target="tpu_custom_call" | custom-call | tf_op jit(solution)/shard_map/pallas_call | solution.py:227
  39.4 1.6 %broadcast_in_dim.226 = f32[4,12,8,128]{3,2,1,0:T(8,128)} broadcast(f32[12,8,128]{2,1,0:T(8,128)} %get-tuple-element.11), dimensions={1,2,3} | broadcast | bytes 245760 | tf_op jit(solution)/shard_map/broadcast_in_dim | solution.py:279
  40.9 4.0 %all-to-all-start = ((f32[4,12,8,128]{3,2,1,0:T(8,128)}), f32[4,12,8,128]{3,2,1,0:T(8,128)S(1)}, u32[]{:S(2)}, u32[]{:S(2)}) async-start(f32[4,12,8,128]{3,2,1,0:T(8,128)} %broadcast_in_dim.226), calls=%async_computation | async-start | bytes 393216 | tf_op jit(solution)/shard_map/all_to_all | solution.py:278
  44.9 0.6 dynamic-slice
  45.5 5.3 %all-to-all-done = f32[4,12,8,128]{3,2,1,0:T(8,128)S(1)} async-done(((f32[4,12,8,128]{3,2,1,0:T(8,128)}), f32[4,12,8,128]{3,2,1,0:T(8,128)S(1)}, u32[]{:S(2)}, u32[]{:S(2)}) %all-to-all-start) | async-done | bytes 196640 | tf_op jit(solution)/shard_map/all_to_all | solution.py:278
  50.8 0.7 fusion.49
  51.8 0.7 copy-done.8
  52.6 1.1 %fusion.63 = (f32[64,8,128]{2,1,0:T(8,128)S(1)}, f32[64,8,128]{2,1,0:T(8,128)S(1)}, f32[64,8,128]{2,1,0:T(8,128)S(1)}, f32[64,8,128]{2,1,0:T(8,128)S(1)}) fusion(f32[3,64,8,128]{3,2,1,0:T(8,128)S(1)} %copy-done, f32[64,8,128]{2,1,0:T(8,128)} %get-tuple-element.13, f32[8,128]{1,0:T(8,128)S(1)} %get-tuple-element.99, f32[64,8,128]{2,1,0:T(8,128)S(1)} %copy-done.7, ...), kind=kLoop, calls=%fused_computation.179 | loop fusion | flops 655360 | bytes 2637824 | tf_op jit(solution)/shard_map/add | solution.py:338
  53.8 1.1 %copy-done.1 = f32[3,64,8,128]{3,2,1,0:T(8,128)S(1)} copy-done((f32[3,64,8,128]{3,2,1,0:T(8,128)S(1)}, f32[3,64,8,128]{3,2,1,0:T(8,128)}, u32[]{:S(2)}) %copy-start.1) | copy-done | bytes 786456
  55.2 4.8 %collective-permute-start.7 = (f32[64,8,1]{2,1,0:T(8,128)S(1)}, f32[64,8,1]{2,1,0:T(8,128)S(1)}, u32[]{:S(2)}, u32[]{:S(2)}) collective-permute-start(f32[64,8,1]{2,1,0:T(8,128)S(1)} %slice.409), channel_id=1, source_target_pairs={{0,4},{4,8},{8,12},{1,5},{5,9},{9,13},{2,6},{6,10},{10,14},{3,7},{... | collective-permute-start | bytes 6152 | tf_op jit(solution)/shard_map/ppermute | solution.py:14
  60.0 9.5 %collective-permute-start.6 = (f32[64,1,128]{2,1,0:T(1,128)S(1)}, f32[64,1,128]{2,1,0:T(1,128)S(1)}, u32[]{:S(2)}, u32[]{:S(2)}) collective-permute-start(f32[64,1,128]{2,1,0:T(1,128)S(1)} %slice.406), channel_id=1, source_target_pairs={{0,16},{16,32},{32,48},{48,64},{64,80},{80,96},{96,112},{112,128},... | collective-permute-start | bytes 98312 | tf_op jit(solution)/shard_map/ppermute | solution.py:14
  69.5 0.9 %pad_maximum_fusion.2 = f32[3,64,8,128]{3,2,1,0:T(8,128)} fusion(f32[1,64,8,128]{3,2,1,0:T(8,128)S(1)} %bitcast.245, f32[1,64,8,128]{3,2,1,0:T(8,128)S(1)} %bitcast.238, f32[1,64,8,128]{3,2,1,0:T(8,128)S(1)} %bitcast.236), kind=kLoop, calls=%fused_computation.2 | loop fusion | flops 393216 | bytes 1572864 | tf_op jit(solution)/shard_map/stack | solution.py:352
  70.5 0.2 fusion.6
  70.7 0.9 %pad_maximum_fusion.1 = f32[3,64,8,128]{3,2,1,0:T(8,128)} fusion(f32[1,64,8,128]{3,2,1,0:T(8,128)S(1)} %fusion.6, f32[1,64,8,128]{3,2,1,0:T(8,128)S(1)} %bitcast.243, f32[1,64,8,128]{3,2,1,0:T(8,128)S(1)} %bitcast.244), kind=kLoop, calls=%fused_computation.1 | loop fusion | flops 393216 | bytes 1572864 | tf_op jit(solution)/shard_map/stack | solution.py:351
  (76 shorter events, 2.3 us)
Async XLA Ops:
  2.4 1.0 %slice-start = ((f32[3,64,8,128]{3,2,1,0:T(8,128)}), f32[1,64,8,128]{3,2,1,0:T(8,128)S(1)}, s32[]{:S(2)}) async-start(f32[3,64,8,128]{3,2,1,0:T(8,128)} %h_ref.1), calls=%async_computation.1 | async-start | bytes 524288 | tf_op jit(solution)/shard_map/slice | solution.py:257
  3.7 20.0 %collective-permute-start.3 = (f32[3,64,8,1]{1,2,3,0:T(8,128)S(1)}, f32[3,64,8,1]{1,2,3,0:T(8,128)S(1)}, u32[]{:S(2)}, u32[]{:S(2)}) collective-permute-start(f32[3,64,8,1]{1,2,3,0:T(8,128)S(1)} %pad_maximum_fusion.5), channel_id=1, source_target_pairs={{0,4},{4,8},{8,12},{1,5},{5,9},{9,13},{2,6},{6,10},{10,14},{3,7},{... | collective-permute-start | bytes 18440 | tf_op jit(solution)/shard_map/ppermute | solution.py:14
  7.6 23.3 %collective-permute-start.1 = (f32[3,64,1,128]{3,1,2,0:T(8,128)S(1)}, f32[3,64,1,128]{3,1,2,0:T(8,128)S(1)}, u32[]{:S(2)}, u32[]{:S(2)}) collective-permute-start(f32[3,64,1,128]{3,1,2,0:T(8,128)S(1)} %pad_maximum_fusion.3), channel_id=1, source_target_pairs={{0,16},{16,32},{32,48},{48,64},{64,80},{80,96},{96,112},{112,128},... | collective-permute-start | bytes 294920 | tf_op jit(solution)/shard_map/ppermute | solution.py:14
  12.7 7.8 %copy-start.3 = (s32[64,8,128]{2,1,0:T(8,128)S(1)}, s32[64,8,128]{2,1,0:T(8,128)}, u32[]{:S(2)}) copy-start(s32[64,8,128]{2,1,0:T(8,128)} %param.8) | copy-start | bytes 786436
  12.7 18.1 %collective-permute-start.2 = (f32[2,64,8,1]{3,2,1,0:T(8,128)S(1)}, f32[2,64,8,1]{3,2,1,0:T(8,128)S(1)}, u32[]{:S(2)}, u32[]{:S(2)}) collective-permute-start(f32[2,64,8,1]{3,2,1,0:T(8,128)S(1)} %copy.121), channel_id=1, source_target_pairs={{4,0},{8,4},{12,8},{5,1},{9,5},{13,9},{6,2},{10,6},{14,10},{7,3},{... | collective-permute-start | bytes 12296 | tf_op jit(solution)/shard_map/ppermute | solution.py:19
  14.8 5.6 %copy-start.16 = (s32[64]{0:T(128)S(1)}, s32[64]{0:T(128)}, u32[]{:S(2)}) copy-start(s32[64]{0:T(128)} %param.9) | copy-start | bytes 772
  14.8 16.0 %collective-permute-start = (f32[2,64,1,128]{3,1,2,0:T(8,128)S(1)}, f32[2,64,1,128]{3,1,2,0:T(8,128)S(1)}, u32[]{:S(2)}, u32[]{:S(2)}) collective-permute-start(f32[2,64,1,128]{3,1,2,0:T(8,128)S(1)} %pad_maximum_fusion.4), channel_id=1, source_target_pairs={{16,0},{32,16},{48,32},{64,48},{80,64},{96,80},{112,96},{128,112},... | collective-permute-start | bytes 196616 | tf_op jit(solution)/shard_map/ppermute | solution.py:19
  18.0 12.8 %collective-permute-start.4 = (f32[64,1,1]{2,1,0:T(1,128)S(1)}, f32[64,1,1]{2,1,0:T(1,128)S(1)}, u32[]{:S(2)}, u32[]{:S(2)}) collective-permute-start(f32[64,1,1]{2,1,0:T(1,128)S(1)} %slice.370), channel_id=1, source_target_pairs={{4,16},{8,20},{12,24},{20,32},{24,36},{28,40},{36,48},{40,52},{44,... | collective-permute-start | bytes 776 | tf_op jit(solution)/shard_map/ppermute | solution.py:31
  20.5 0.7 copy-start.14
  20.5 0.7 copy-start.15
  23.7 7.1 %collective-permute-start.5 = (f32[64,1,1]{2,1,0:T(1,128)S(1)}, f32[64,1,1]{2,1,0:T(1,128)S(1)}, u32[]{:S(2)}, u32[]{:S(2)}) collective-permute-start(f32[64,1,1]{2,1,0:T(1,128)S(1)} %slice.371), channel_id=1, source_target_pairs={{16,4},{20,8},{24,12},{32,20},{36,24},{40,28},{48,36},{52,40},{56,... | collective-permute-start | bytes 776 | tf_op jit(solution)/shard_map/ppermute | solution.py:31
  30.8 0.6 copy-start.12
  30.8 0.6 copy-start.13
  30.9 0.8 %copy-start.2 = (f32[2,64,8,1]{3,2,1,0:T(8,128)}, f32[2,64,8,1]{3,2,1,0:T(8,128)S(1)}, u32[]{:S(2)}) copy-start(f32[2,64,8,1]{3,2,1,0:T(8,128)S(1)} %collective-permute-done.2.yh_ref) | copy-start | bytes 12292
  30.9 0.8 %copy-start.11 = (f32[2,64,1,128]{3,1,2,0:T(8,128)}, f32[2,64,1,128]{3,1,2,0:T(8,128)S(1)}, u32[]{:S(2)}) copy-start(f32[2,64,1,128]{3,1,2,0:T(8,128)S(1)} %collective-permute-done) | copy-start | bytes 196612
  30.9 0.8 %copy-start.10 = (f32[3,64,1,128]{3,1,2,0:T(8,128)}, f32[3,64,1,128]{3,1,2,0:T(8,128)S(1)}, u32[]{:S(2)}) copy-start(f32[3,64,1,128]{3,1,2,0:T(8,128)S(1)} %collective-permute-done.1) | copy-start | bytes 294916
  39.4 12.4 %copy-start = (f32[3,64,8,128]{3,2,1,0:T(8,128)S(1)}, f32[3,64,8,128]{3,2,1,0:T(8,128)}, u32[]{:S(2)}) copy-start(f32[3,64,8,128]{3,2,1,0:T(8,128)} %e_ref.1) | copy-start | bytes 2359300
  40.9 9.9 %all-to-all-start = ((f32[4,12,8,128]{3,2,1,0:T(8,128)}), f32[4,12,8,128]{3,2,1,0:T(8,128)S(1)}, u32[]{:S(2)}, u32[]{:S(2)}) async-start(f32[4,12,8,128]{3,2,1,0:T(8,128)} %broadcast_in_dim.226), calls=%async_computation | async-start | bytes 393216 | tf_op jit(solution)/shard_map/all_to_all | solution.py:278
  51.5 1.0 %copy-start.8 = (f32[64,8,128]{2,1,0:T(8,128)S(1)}, f32[64,8,128]{2,1,0:T(8,128)}, u32[]{:S(2)}) copy-start(f32[64,8,128]{2,1,0:T(8,128)} %get-tuple-element.12) | copy-start | bytes 786436
  51.6 1.0 %copy-start.6 = (f32[64,8,128]{2,1,0:T(8,128)S(1)}, f32[64,8,128]{2,1,0:T(8,128)}, u32[]{:S(2)}) copy-start(f32[64,8,128]{2,1,0:T(8,128)} %get-tuple-element.10) | copy-start | bytes 786436
  51.6 1.1 %copy-start.7 = (f32[64,8,128]{2,1,0:T(8,128)S(1)}, f32[64,8,128]{2,1,0:T(8,128)}, u32[]{:S(2)}) copy-start(f32[64,8,128]{2,1,0:T(8,128)} %get-tuple-element.14) | copy-start | bytes 786436
  52.6 1.2 %copy-start.4 = (f32[64,8,128]{2,1,0:T(8,128)S(1)}, f32[64,8,128]{2,1,0:T(8,128)}, u32[]{:S(2)}) copy-start(f32[64,8,128]{2,1,0:T(8,128)} %get-tuple-element.15) | copy-start | bytes 786436
  52.6 1.2 %copy-start.5 = (f32[64,8,128]{2,1,0:T(8,128)S(1)}, f32[64,8,128]{2,1,0:T(8,128)}, u32[]{:S(2)}) copy-start(f32[64,8,128]{2,1,0:T(8,128)} %get-tuple-element.16) | copy-start | bytes 786436
  53.7 1.1 %copy-start.1 = (f32[3,64,8,128]{3,2,1,0:T(8,128)S(1)}, f32[3,64,8,128]{3,2,1,0:T(8,128)}, u32[]{:S(2)}) copy-start(f32[3,64,8,128]{3,2,1,0:T(8,128)} %h_ref.1) | copy-start | bytes 2359300
  55.0 14.4 %copy-start.9 = (f32[64,8,128]{2,1,0:T(8,128)S(1)}, f32[64,8,128]{2,1,0:T(8,128)}, u32[]{:S(2)}) copy-start(f32[64,8,128]{2,1,0:T(8,128)} %get-tuple-element.17) | copy-start | bytes 786436
  55.2 15.2 %collective-permute-start.7 = (f32[64,8,1]{2,1,0:T(8,128)S(1)}, f32[64,8,1]{2,1,0:T(8,128)S(1)}, u32[]{:S(2)}, u32[]{:S(2)}) collective-permute-start(f32[64,8,1]{2,1,0:T(8,128)S(1)} %slice.409), channel_id=1, source_target_pairs={{0,4},{4,8},{8,12},{1,5},{5,9},{9,13},{2,6},{6,10},{10,14},{3,7},{... | collective-permute-start | bytes 6152 | tf_op jit(solution)/shard_map/ppermute | solution.py:14
  60.0 10.5 %collective-permute-start.6 = (f32[64,1,128]{2,1,0:T(1,128)S(1)}, f32[64,1,128]{2,1,0:T(1,128)S(1)}, u32[]{:S(2)}, u32[]{:S(2)}) collective-permute-start(f32[64,1,128]{2,1,0:T(1,128)S(1)} %slice.406), channel_id=1, source_target_pairs={{0,16},{16,32},{32,48},{48,64},{64,80},{80,96},{96,112},{112,128},... | collective-permute-start | bytes 98312 | tf_op jit(solution)/shard_map/ppermute | solution.py:14

commit v6 on v4

--- a/solution.py
+++ b/solution.py
@@ -234,6 +234,43 @@
       corner_ex, corner_ey)
 
 
+def finish_kernel(
+    e_ref, h_ref, px_ref, py_ref, lw_ref, hw_ref, szx_ref, szy_ref, coef_ref,
+    exn_ref, eyn_ref, hxn_ref, hyn_ref,
+):
+    depth = px_ref.shape[0]
+    last_x, last_y, next_x, next_y = coef_ref[0], coef_ref[1], coef_ref[2], coef_ref[3]
+
+    def sums(z):
+        new_x = px_ref[z] + last_x * lw_ref[z] + next_x * hw_ref[z]
+        new_y = py_ref[z] + last_y * lw_ref[z] + next_y * hw_ref[z]
+        exn_ref[z] = new_x
+        eyn_ref[z] = new_y
+        return e_ref[0, z] + new_x, e_ref[1, z] + new_y
+
+    def write(z, sum_x, sum_y, up_x, up_y):
+        rise_x = up_x - sum_x
+        rise_y = up_y - sum_y
+        hyn_ref[z] = h_ref[1, z] - 0.5 * z_courant * rise_x + time_step * szx_ref[z]
+        hxn_ref[z] = h_ref[0, z] - time_step * szy_ref[z] + 0.5 * z_courant * rise_y
+
+    def step(z, carry):
+        sum_x, sum_y = carry
+        up_x, up_y = sums(z + 1)
+        write(z, sum_x, sum_y, up_x, up_y)
+        return up_x, up_y
+
+    sum_x, sum_y = lax.fori_loop(0, depth - 1, step, sums(0), unroll=4)
+    write(depth - 1, sum_x, sum_y, next_x, next_y)
+
+
+def finish(electric, magnetic, px, py, lw, hw, slope_zx, slope_zy, coef):
+    shape = jax.ShapeDtypeStruct(px.shape, jnp.float32)
+    return pl.pallas_call(finish_kernel, out_shape=(shape,) * 4)(
+        electric, magnetic, px, py, lw, hw, slope_zx, slope_zy, coef
+    )
+
+
 def advance(pieces, incoming, factor):
     rows_first, rows_last, low_first, low_last, high_first, high_last = pieces
     denominator = 1.0 - low_first * factor
@@ -336,20 +373,10 @@
 
     previous_last = incoming + factor[None] * leading + below
     following = following + above
-    electric_x_new = (
-        partial_x + previous_last[0][None] * low_weight + following[0][None] * high_weight
-    )
-    electric_y_new = (
-        partial_y + previous_last[1][None] * low_weight + following[1][None] * high_weight
-    )
-    sum_x = electric_x + electric_x_new
-    sum_y = electric_y + electric_y_new
-    top_x = following[0]
-    top_y = following[1]
-    rise_x = jnp.concatenate([sum_x[1:], top_x[None]], axis=0) - sum_x
-    rise_y = jnp.concatenate([sum_y[1:], top_y[None]], axis=0) - sum_y
-    magnetic_y_new = magnetic_y - 0.5 * z_courant * rise_x + time_step * slope_zx
-    magnetic_x_new = magnetic_x - time_step * slope_zy + 0.5 * z_courant * rise_y
+    coef = jnp.concatenate([previous_last, following], axis=0)
+    electric_x_new, electric_y_new, magnetic_x_new, magnetic_y_new = finish(
+        electric, magnetic, partial_x, partial_y, low_weight, high_weight, slope_zx, slope_zy, coef
+    )
     before_hy = from_prev(magnetic_y_new[:, -1:, :], "gx")
     before_hx = from_prev(magnetic_x_new[:, :, -1:], "gy")
     change_hy = magnetic_y_new - jnp.concatenate([before_hy, magnetic_y_new[:, :-1]], axis=1)

time: 69.6 us -> 70.8 us (1.017)
  Pallas kernels: 7.71 us -> 10.8 us
  local copies, waits for them, and re-layouts: 8.9 us -> 7.83 us
    pallas_call x0 -> x1, Pallas kernels: none -> 3.11 us  [finish(): pl.pallas_call(finish_kernel, out_shape=(shape,) * 4)]
    unnamed x33, local copies, waits for them, and re-layouts: 3.1 us -> 1.34 us
    add x2 -> x0, other arithmetic: 1.35 us -> none  [the longest x1 1.19 us: body(): sum_y = electric_y + electric_y_new]
    squeeze x1 -> x0, local copies, waits for them, and re-layouts: 1.16 us -> none  [body(): electric_x, electric_y, electric_z = (electric[0], electric[1], electric[2])]
    slice x1, local copies, waits for them, and re-layouts: 0.12 us -> 1.14 us  [body(): before_hx = from_prev(magnetic_x_new[:, :, -1:], 'gy')]
    another operation x2, other arithmetic: 1.14 us -> 2.15 us  [body(): jnp.stack([electric_x_new, electric_y_new, electric_z_new])]
    slice x6 -> x1, local copies, waits for them, and re-layouts: 0.25 us -> 1.16 us  [body(): electric_x, electric_y, electric_z = (electric[0], electric[1], electric[2])]
    another operation x1, other arithmetic: 0.81 us -> 0.01 us  [body(): gathered = jnp.stack(gathered)]
  transfers between devices with their start and end apart: 11 -> 11, of which waited for: 3 -> 2; matrix products, arithmetic and copies ran while one was open for 10% -> 9% of each run, Pallas kernels for 0% -> 0%
where the time goes in v6:
time: 70.8 us; the launch traced here: 70 us
  starting transfers between devices  40.3 us (57%)
  Pallas kernels  10.8 us (15%)
  other arithmetic  7.94 us (11%)
  local copies, waits for them, and re-layouts  7.83 us (11%)
  waiting for transfers between devices  2.07 us (3%)
  between operations  1.06 us (1%)
    ppermute x4, starting transfers between devices, from_prev(): return lax.ppermute(block, axis, [(i, i + 1) for i in range(count - 1)])  22.6 us
    pallas_call x1, Pallas kernels, make_sources(): pl.pallas_call(source_kernel, out_shape=(shape,) * 7 + (edges,), in_specs...  7.7 us
    ppermute x2, starting transfers between devices, from_diagonal(): return lax.ppermute(block, axes, pairs)  7.67 us
    ppermute x2, starting transfers between devices, from_next(): return lax.ppermute(block, axis, [(i + 1, i) for i in range(count - 1)])  5.21 us
    ppermute x3, starting transfers between devices, body(): lax.ppermute(own, 'gz', [(i, (i + shift) % slab_count) for i in range(sla...  4.81 us
    pallas_call x1, Pallas kernels, finish(): pl.pallas_call(finish_kernel, out_shape=(shape,) * 4)  3.11 us
    another operation x3, other arithmetic, body(): rate_stack = jnp.stack([keep_rate, curl_rate, z_rate, stiffness])  2.32 us
    another operation x2, other arithmetic, body(): jnp.stack([electric_x_new, electric_y_new, electric_z_new])  2.15 us
  transfers between devices with their start and end apart: 11, of which 2 were waited for; matrix products, arithmetic and copies ran while one was open for 9% of the time, Pallas kernels for 0%

profile of v6, /device:TPU:97, one launch (start us, length us, event | category | flops | bytes accessed | tf_op | source)
XLA Modules:
  0.0 70.0 jit_solution(17938623063357251884)
XLA Ops:
  0.6 1.2 %fusion.101 = (f32[1,64,8,128]{3,2,1,0:T(8,128)S(1)}, f32[1,64,8,128]{3,2,1,0:T(8,128)S(1)}, f32[64,8,128]{2,1,0:T(8,128)S(1)}) fusion(f32[3,64,8,128]{3,2,1,0:T(8,128)} %e_ref.3), kind=kLoop, calls=%fused_computation.206 | loop fusion | bytes 1572864 | tf_op jit(solution)/shard_map/slice | solution.py:293
  1.9 0.3 slice_reduce_fusion.2
  2.5 0.9 %slice-done = f32[1,64,8,128]{3,2,1,0:T(8,128)S(1)} async-done(((f32[3,64,8,128]{3,2,1,0:T(8,128)}), f32[1,64,8,128]{3,2,1,0:T(8,128)S(1)}, s32[]{:S(2)}) %slice-start) | async-done | bytes 262168 | tf_op jit(solution)/shard_map/slice | solution.py:294
  3.8 3.8 %collective-permute-start.3 = (f32[3,64,8,1]{1,2,3,0:T(8,128)S(1)}, f32[3,64,8,1]{1,2,3,0:T(8,128)S(1)}, u32[]{:S(2)}, u32[]{:S(2)}) collective-permute-start(f32[3,64,8,1]{1,2,3,0:T(8,128)S(1)} %pad_maximum_fusion.7), channel_id=1, source_target_pairs={{0,4},{4,8},{8,12},{1,5},{5,9},{9,13},{2,6},{6,10},{10,14},{3,7},{... | collective-permute-start | bytes 18440 | tf_op jit(solution)/shard_map/ppermute | solution.py:14
  7.6 4.5 %collective-permute-start.1 = (f32[3,64,1,128]{3,1,2,0:T(8,128)S(1)}, f32[3,64,1,128]{3,1,2,0:T(8,128)S(1)}, u32[]{:S(2)}, u32[]{:S(2)}) collective-permute-start(f32[3,64,1,128]{3,1,2,0:T(8,128)S(1)} %pad_maximum_fusion.4), channel_id=1, source_target_pairs={{0,16},{16,32},{32,48},{48,64},{64,80},{80,96},{96,112},{112,128},... | collective-permute-start | bytes 294920 | tf_op jit(solution)/shard_map/ppermute | solution.py:14
  12.6 2.1 %collective-permute-start.2 = (f32[2,64,8,1]{3,2,1,0:T(8,128)S(1)}, f32[2,64,8,1]{3,2,1,0:T(8,128)S(1)}, u32[]{:S(2)}, u32[]{:S(2)}) collective-permute-start(f32[2,64,8,1]{3,2,1,0:T(8,128)S(1)} %copy.84), channel_id=1, source_target_pairs={{4,0},{8,4},{12,8},{5,1},{9,5},{13,9},{6,2},{10,6},{14,10},{7,3},{... | collective-permute-start | bytes 12296 | tf_op jit(solution)/shard_map/ppermute | solution.py:19
  14.7 3.2 %collective-permute-start = (f32[2,64,1,128]{3,1,2,0:T(8,128)S(1)}, f32[2,64,1,128]{3,1,2,0:T(8,128)S(1)}, u32[]{:S(2)}, u32[]{:S(2)}) collective-permute-start(f32[2,64,1,128]{3,1,2,0:T(8,128)S(1)} %pad_maximum_fusion.5), channel_id=1, source_target_pairs={{16,0},{32,16},{48,32},{64,48},{80,64},{96,80},{112,96},{128,112},... | collective-permute-start | bytes 196616 | tf_op jit(solution)/shard_map/ppermute | solution.py:19
  17.9 2.4 %collective-permute-start.4 = (f32[64,1,1]{2,0,1:T(8,128)S(1)}, f32[64,1,1]{2,0,1:T(8,128)S(1)}, u32[]{:S(2)}, u32[]{:S(2)}) collective-permute-start(f32[64,1,1]{2,0,1:T(8,128)S(1)} %slice.289), channel_id=1, source_target_pairs={{4,16},{8,20},{12,24},{20,32},{24,36},{28,40},{36,48},{40,52},{44,... | collective-permute-start | bytes 776 | tf_op jit(solution)/shard_map/ppermute | solution.py:31
  20.4 0.3 broadcast_compare_fusion.7
  20.7 0.3 copy-done.12
  21.1 1.2 %fusion.4 = (f32[1,64,8,128]{3,2,1,0:T(8,128)S(1)}, f32[64,8,128]{2,1,0:T(8,128)S(1)}, f32[64,8,128]{2,1,0:T(8,128)S(1)}) fusion(pred[64,8,128]{2,1,0:T(8,128)(4,1)S(1)} %get-tuple-element.85, f32[64]{0:T(128)S(1)} %get-tuple-element.110, pred[64,8,128]{2,1,0:T(8,128)(4,1)S(1)} %get-tuple-element.86, f32[64]{0:T(128)S(1)} %get-tuple-element.109, ...), kind=kLoop, calls=%fused_computation.33 | loop fusion | flops 2359296 | bytes 1314816 | tf_op jit(solution)/shard_map/stack | solution.py:308
  22.4 1.1 %pad_maximum_fusion.rate_ref = f32[4,64,8,128]{3,2,1,0:T(8,128)} fusion(f32[1,64,8,128]{3,2,1,0:T(8,128)S(1)} %get-tuple-element.75, f32[1,64,8,128]{3,2,1,0:T(8,128)S(1)} %get-tuple-element.76, f32[1,64,8,128]{3,2,1,0:T(8,128)S(1)} %get-tuple-element.74, f32[1,64,8,128]{3,2,1,0:T(8,128)S(1)} %get-tuple-element.68), kind=kLoop, calls=%fused_computation | loop fusion | flops 786432 | bytes 2097152 | tf_op jit(solution)/shard_map/stack | solution.py:308
  23.6 5.3 %collective-permute-start.5 = (f32[64,1,1]{2,0,1:T(8,128)S(1)}, f32[64,1,1]{2,0,1:T(8,128)S(1)}, u32[]{:S(2)}, u32[]{:S(2)}) collective-permute-start(f32[64,1,1]{2,0,1:T(8,128)S(1)} %slice.290), channel_id=1, source_target_pairs={{16,4},{20,8},{24,12},{32,20},{36,24},{40,28},{48,36},{52,40},{56,... | collective-permute-start | bytes 776 | tf_op jit(solution)/shard_map/ppermute | solution.py:31
  28.8 0.6 add_convert_fusion.flag_ref
  29.4 1.2 %copy.87.yl_ref = f32[3,64,8,1]{3,2,1,0:T(8,128)} copy(f32[3,64,8,1]{1,2,3,0:T(8,128)S(1)} %collective-permute-done.3) | data formatting | bytes 12288 | tf_op jit(solution)/shard_map/ppermute | solution.py:14
  30.7 0.5 copy-done.10
  31.5 7.7 %shard_map.77 = (f32[64,8,128]{2,1,0:T(8,128)}, f32[64,8,128]{2,1,0:T(8,128)}, f32[64,8,128]{2,1,0:T(8,128)}, f32[64,8,128]{2,1,0:T(8,128)}, f32[64,8,128]{2,1,0...) custom-call(s32[3]{0:T(128)} %add_convert_fusion.flag_ref, ...), custom_call_target="tpu_custom_call" | custom-call | tf_op jit(solution)/shard_map/pallas_call | solution.py:227
  39.2 1.2 %collective-permute-start.6 = (f32[12,8,128]{2,1,0:T(8,128)}, f32[12,8,128]{2,1,0:T(8,128)S(1)}, u32[]{:S(2)}, u32[]{:S(2)}) collective-permute-start(f32[12,8,128]{2,1,0:T(8,128)} %get-tuple-element.20), channel_id=1, source_target_pairs={{0,1},{1,2},{2,3},{3,0},{4,5},{5,6},{6,7},{7,4},{8,9},{9,10},{10,1... | collective-permute-start | bytes 147464 | tf_op jit(solution)/shard_map/ppermute | solution.py:318
  40.4 2.5 %collective-permute-start.7 = (f32[12,8,128]{2,1,0:T(8,128)}, f32[12,8,128]{2,1,0:T(8,128)S(1)}, u32[]{:S(2)}, u32[]{:S(2)}) collective-permute-start(f32[12,8,128]{2,1,0:T(8,128)} %get-tuple-element.20), channel_id=1, source_target_pairs={{0,2},{1,3},{2,0},{3,1},{4,6},{5,7},{6,4},{7,5},{8,10},{9,11},{10,... | collective-permute-start | bytes 147464 | tf_op jit(solution)/shard_map/ppermute | solution.py:318
  42.8 1.2 %collective-permute-start.8 = (f32[12,8,128]{2,1,0:T(8,128)}, f32[12,8,128]{2,1,0:T(8,128)S(1)}, u32[]{:S(2)}, u32[]{:S(2)}) collective-permute-start(f32[12,8,128]{2,1,0:T(8,128)} %get-tuple-element.20), channel_id=1, source_target_pairs={{0,3},{1,0},{2,1},{3,2},{4,7},{5,4},{6,5},{7,6},{8,11},{9,8},{10,9... | collective-permute-start | bytes 147464 | tf_op jit(solution)/shard_map/ppermute | solution.py:318
  44.0 0.6 dynamic-slice.23
  44.6 1.0 %collective-permute-done.7 = f32[12,8,128]{2,1,0:T(8,128)S(1)} collective-permute-done((f32[12,8,128]{2,1,0:T(8,128)}, f32[12,8,128]{2,1,0:T(8,128)S(1)}, u32[]{:S(2)}, u32[]{:S(2)}) %collective-permute-start.7) | collective-permute-done | bytes 49184 | tf_op jit(solution)/shard_map/ppermute | solution.py:318
  45.6 1.0 %collective-permute-done.8 = f32[12,8,128]{2,1,0:T(8,128)S(1)} collective-permute-done((f32[12,8,128]{2,1,0:T(8,128)}, f32[12,8,128]{2,1,0:T(8,128)S(1)}, u32[]{:S(2)}, u32[]{:S(2)}) %collective-permute-start.8) | collective-permute-done | bytes 49184 | tf_op jit(solution)/shard_map/ppermute | solution.py:318
  46.8 0.7 fusion.61
  47.6 0.6 pad_maximum_fusion.6.coef_ref
  48.2 3.1 %shard_map.78 = (f32[64,8,128]{2,1,0:T(8,128)}, f32[64,8,128]{2,1,0:T(8,128)}, f32[64,8,128]{2,1,0:T(8,128)}, f32[64,8,128]{2,1,0:T(8,128)}) custom-call(f32[3,64,8,128]{3,2,1,0:T(8,128)} %e_ref.3, f32[3,64,8,128]{3,2,1,0:T(8,128)} %h_ref.3, f32[64,8,128]{2,1,0:T(8,128)} %get-tuple-element.14.px_ref, f32[64,8,128]{2,1,0:T(8,128)} %get-tuple-element.15.py_ref, ...), custom_call_target="tpu_custom_call" | custom-call | tf_op jit(solution)/shard_map/pallas_call | solution.py:269
  51.3 1.1 %slice.277 = f32[64,8,1]{2,1,0:T(8,128)S(1)} slice(f32[64,8,128]{2,1,0:T(8,128)} %get-tuple-element.24), slice={[0:64], [0:8], [127:128]} | slice | bytes 4096 | tf_op jit(solution)/shard_map/slice | solution.py:381
  52.5 4.8 %collective-permute-start.10 = (f32[64,8,1]{2,1,0:T(8,128)S(1)}, f32[64,8,1]{2,1,0:T(8,128)S(1)}, u32[]{:S(2)}, u32[]{:S(2)}) collective-permute-start(f32[64,8,1]{2,1,0:T(8,128)S(1)} %slice.277), channel_id=1, source_target_pairs={{0,4},{4,8},{8,12},{1,5},{5,9},{9,13},{2,6},{6,10},{10,14},{3,7},{... | collective-permute-start | bytes 6152 | tf_op jit(solution)/shard_map/ppermute | solution.py:14
  57.3 9.5 %collective-permute-start.9 = (f32[64,1,128]{2,1,0:T(1,128)S(1)}, f32[64,1,128]{2,1,0:T(1,128)S(1)}, u32[]{:S(2)}, u32[]{:S(2)}) collective-permute-start(f32[64,1,128]{2,1,0:T(1,128)S(1)} %slice.275), channel_id=1, source_target_pairs={{0,16},{16,32},{32,48},{48,64},{64,80},{80,96},{96,112},{112,128},... | collective-permute-start | bytes 98312 | tf_op jit(solution)/shard_map/ppermute | solution.py:14
  66.9 0.9 %pad_maximum_fusion.2 = f32[3,64,8,128]{3,2,1,0:T(8,128)} fusion(f32[1,64,8,128]{3,2,1,0:T(8,128)S(1)} %bitcast.210, f32[1,64,8,128]{3,2,1,0:T(8,128)S(1)} %bitcast.202, f32[1,64,8,128]{3,2,1,0:T(8,128)S(1)} %bitcast.197), kind=kLoop, calls=%fused_computation.2 | loop fusion | flops 393216 | bytes 1572864 | tf_op jit(solution)/shard_map/stack | solution.py:387
  67.9 1.2 %fusion.3 = f32[1,64,8,128]{3,2,1,0:T(8,128)S(1)} fusion(f32[64,8,128]{2,1,0:T(8,128)S(1)} %copy-done.1, f32[64,7,128]{2,1,0:T(8,128)S(1)} %bitcast.203, f32[64,1,128]{2,1,0:T(1,128)S(1)} %collective-permute-done.9, f32[64,8,128]{2,1,0:T(8,128)S(1)} %copy-done, f32[64,8,127]{2,1,0:T(8,128)S(1)} %bitcast.198, f32[64,8,1]{2,1,0:T(8,128)S(1)} %collective-permute-done.10, ...), kind=kLoop, calls=%fused_computation.11 | loop fusion | flops 917504 | bytes 2097152 | tf_op jit(solution)/shard_map/stack | solution.py:386
  69.1 0.9 %pad_maximum_fusion.1 = f32[3,64,8,128]{3,2,1,0:T(8,128)} fusion(f32[1,64,8,128]{3,2,1,0:T(8,128)S(1)} %fusion.3, f32[1,64,8,128]{3,2,1,0:T(8,128)S(1)} %bitcast.212, f32[1,64,8,128]{3,2,1,0:T(8,128)S(1)} %bitcast.211), kind=kLoop, calls=%fused_computation.1 | loop fusion | flops 393216 | bytes 1572864 | tf_op jit(solution)/shard_map/stack | solution.py:386
  (69 shorter events, 2.2 us)
Async XLA Ops:
  2.5 1.0 %slice-start = ((f32[3,64,8,128]{3,2,1,0:T(8,128)}), f32[1,64,8,128]{3,2,1,0:T(8,128)S(1)}, s32[]{:S(2)}) async-start(f32[3,64,8,128]{3,2,1,0:T(8,128)} %h_ref.3), calls=%async_computation | async-start | bytes 524288 | tf_op jit(solution)/shard_map/slice | solution.py:294
  3.8 19.7 %collective-permute-start.3 = (f32[3,64,8,1]{1,2,3,0:T(8,128)S(1)}, f32[3,64,8,1]{1,2,3,0:T(8,128)S(1)}, u32[]{:S(2)}, u32[]{:S(2)}) collective-permute-start(f32[3,64,8,1]{1,2,3,0:T(8,128)S(1)} %pad_maximum_fusion.7), channel_id=1, source_target_pairs={{0,4},{4,8},{8,12},{1,5},{5,9},{9,13},{2,6},{6,10},{10,14},{3,7},{... | collective-permute-start | bytes 18440 | tf_op jit(solution)/shard_map/ppermute | solution.py:14
  7.6 23.0 %collective-permute-start.1 = (f32[3,64,1,128]{3,1,2,0:T(8,128)S(1)}, f32[3,64,1,128]{3,1,2,0:T(8,128)S(1)}, u32[]{:S(2)}, u32[]{:S(2)}) collective-permute-start(f32[3,64,1,128]{3,1,2,0:T(8,128)S(1)} %pad_maximum_fusion.4), channel_id=1, source_target_pairs={{0,16},{16,32},{32,48},{48,64},{64,80},{80,96},{96,112},{112,128},... | collective-permute-start | bytes 294920 | tf_op jit(solution)/shard_map/ppermute | solution.py:14
  12.6 7.7 %copy-start.3 = (s32[64,8,128]{2,1,0:T(8,128)S(1)}, s32[64,8,128]{2,1,0:T(8,128)}, u32[]{:S(2)}) copy-start(s32[64,8,128]{2,1,0:T(8,128)} %param.8) | copy-start | bytes 786436
  12.6 18.0 %collective-permute-start.2 = (f32[2,64,8,1]{3,2,1,0:T(8,128)S(1)}, f32[2,64,8,1]{3,2,1,0:T(8,128)S(1)}, u32[]{:S(2)}, u32[]{:S(2)}) collective-permute-start(f32[2,64,8,1]{3,2,1,0:T(8,128)S(1)} %copy.84), channel_id=1, source_target_pairs={{4,0},{8,4},{12,8},{5,1},{9,5},{13,9},{6,2},{10,6},{14,10},{7,3},{... | collective-permute-start | bytes 12296 | tf_op jit(solution)/shard_map/ppermute | solution.py:19
  14.7 5.6 %copy-start.14 = (s32[64]{0:T(128)S(1)}, s32[64]{0:T(128)}, u32[]{:S(2)}) copy-start(s32[64]{0:T(128)} %param.9) | copy-start | bytes 772
  14.7 15.9 %collective-permute-start = (f32[2,64,1,128]{3,1,2,0:T(8,128)S(1)}, f32[2,64,1,128]{3,1,2,0:T(8,128)S(1)}, u32[]{:S(2)}, u32[]{:S(2)}) collective-permute-start(f32[2,64,1,128]{3,1,2,0:T(8,128)S(1)} %pad_maximum_fusion.5), channel_id=1, source_target_pairs={{16,0},{32,16},{48,32},{64,48},{80,64},{96,80},{112,96},{128,112},... | collective-permute-start | bytes 196616 | tf_op jit(solution)/shard_map/ppermute | solution.py:19
  17.9 12.7 %collective-permute-start.4 = (f32[64,1,1]{2,0,1:T(8,128)S(1)}, f32[64,1,1]{2,0,1:T(8,128)S(1)}, u32[]{:S(2)}, u32[]{:S(2)}) collective-permute-start(f32[64,1,1]{2,0,1:T(8,128)S(1)} %slice.289), channel_id=1, source_target_pairs={{4,16},{8,20},{12,24},{20,32},{24,36},{28,40},{36,48},{40,52},{44,... | collective-permute-start | bytes 776 | tf_op jit(solution)/shard_map/ppermute | solution.py:31
  20.4 0.7 copy-start.12
  20.4 0.7 copy-start.13
  23.6 7.1 %collective-permute-start.5 = (f32[64,1,1]{2,0,1:T(8,128)S(1)}, f32[64,1,1]{2,0,1:T(8,128)S(1)}, u32[]{:S(2)}, u32[]{:S(2)}) collective-permute-start(f32[64,1,1]{2,0,1:T(8,128)S(1)} %slice.290), channel_id=1, source_target_pairs={{16,4},{20,8},{24,12},{32,20},{36,24},{40,28},{48,36},{52,40},{56,... | collective-permute-start | bytes 776 | tf_op jit(solution)/shard_map/ppermute | solution.py:31
  30.6 0.6 copy-start.10
  30.6 0.6 copy-start.11
  30.6 0.8 %copy-start.2 = (f32[2,64,8,1]{3,2,1,0:T(8,128)}, f32[2,64,8,1]{3,2,1,0:T(8,128)S(1)}, u32[]{:S(2)}) copy-start(f32[2,64,8,1]{3,2,1,0:T(8,128)S(1)} %collective-permute-done.2.yh_ref) | copy-start | bytes 12292
  30.7 0.8 %copy-start.8 = (f32[2,64,1,128]{3,1,2,0:T(8,128)}, f32[2,64,1,128]{3,1,2,0:T(8,128)S(1)}, u32[]{:S(2)}) copy-start(f32[2,64,1,128]{3,1,2,0:T(8,128)S(1)} %collective-permute-done) | copy-start | bytes 196612
  30.7 0.8 %copy-start.7 = (f32[3,64,1,128]{3,1,2,0:T(8,128)}, f32[3,64,1,128]{3,1,2,0:T(8,128)S(1)}, u32[]{:S(2)}) copy-start(f32[3,64,1,128]{3,1,2,0:T(8,128)S(1)} %collective-permute-done.1) | copy-start | bytes 294916
  39.2 5.4 %collective-permute-start.6 = (f32[12,8,128]{2,1,0:T(8,128)}, f32[12,8,128]{2,1,0:T(8,128)S(1)}, u32[]{:S(2)}, u32[]{:S(2)}) collective-permute-start(f32[12,8,128]{2,1,0:T(8,128)} %get-tuple-element.20), channel_id=1, source_target_pairs={{0,1},{1,2},{2,3},{3,0},{4,5},{5,6},{6,7},{7,4},{8,9},{9,10},{10,1... | collective-permute-start | bytes 147464 | tf_op jit(solution)/shard_map/ppermute | solution.py:318
  40.4 5.2 %collective-permute-start.7 = (f32[12,8,128]{2,1,0:T(8,128)}, f32[12,8,128]{2,1,0:T(8,128)S(1)}, u32[]{:S(2)}, u32[]{:S(2)}) collective-permute-start(f32[12,8,128]{2,1,0:T(8,128)} %get-tuple-element.20), channel_id=1, source_target_pairs={{0,2},{1,3},{2,0},{3,1},{4,6},{5,7},{6,4},{7,5},{8,10},{9,11},{10,... | collective-permute-start | bytes 147464 | tf_op jit(solution)/shard_map/ppermute | solution.py:318
  42.8 3.8 %collective-permute-start.8 = (f32[12,8,128]{2,1,0:T(8,128)}, f32[12,8,128]{2,1,0:T(8,128)S(1)}, u32[]{:S(2)}, u32[]{:S(2)}) collective-permute-start(f32[12,8,128]{2,1,0:T(8,128)} %get-tuple-element.20), channel_id=1, source_target_pairs={{0,3},{1,0},{2,1},{3,2},{4,7},{5,4},{6,5},{7,6},{8,11},{9,8},{10,9... | collective-permute-start | bytes 147464 | tf_op jit(solution)/shard_map/ppermute | solution.py:318
  44.0 2.6 %copy-start.9 = (f32[12,8,128]{2,1,0:T(8,128)S(1)}, f32[12,8,128]{2,1,0:T(8,128)}, u32[]{:S(2)}) copy-start(f32[12,8,128]{2,1,0:T(8,128)} %get-tuple-element.20) | copy-start | bytes 147460
  48.2 18.7 %copy-start.4 = (f32[64,8,128]{2,1,0:T(8,128)S(1)}, f32[64,8,128]{2,1,0:T(8,128)}, u32[]{:S(2)}) copy-start(f32[64,8,128]{2,1,0:T(8,128)} %get-tuple-element.25) | copy-start | bytes 786436
  51.3 6.0 %copy-start.1 = (f32[64,8,128]{2,1,0:T(8,128)S(1)}, f32[64,8,128]{2,1,0:T(8,128)}, u32[]{:S(2)}) copy-start(f32[64,8,128]{2,1,0:T(8,128)} %get-tuple-element.23) | copy-start | bytes 786436
  51.3 15.6 %copy-start = (f32[64,8,128]{2,1,0:T(8,128)S(1)}, f32[64,8,128]{2,1,0:T(8,128)}, u32[]{:S(2)}) copy-start(f32[64,8,128]{2,1,0:T(8,128)} %get-tuple-element.24) | copy-start | bytes 786436
  52.5 15.4 %collective-permute-start.10 = (f32[64,8,1]{2,1,0:T(8,128)S(1)}, f32[64,8,1]{2,1,0:T(8,128)S(1)}, u32[]{:S(2)}, u32[]{:S(2)}) collective-permute-start(f32[64,8,1]{2,1,0:T(8,128)S(1)} %slice.277), channel_id=1, source_target_pairs={{0,4},{4,8},{8,12},{1,5},{5,9},{9,13},{2,6},{6,10},{10,14},{3,7},{... | collective-permute-start | bytes 6152 | tf_op jit(solution)/shard_map/ppermute | solution.py:14
  57.3 10.5 %collective-permute-start.9 = (f32[64,1,128]{2,1,0:T(1,128)S(1)}, f32[64,1,128]{2,1,0:T(1,128)S(1)}, u32[]{:S(2)}, u32[]{:S(2)}) collective-permute-start(f32[64,1,128]{2,1,0:T(1,128)S(1)} %slice.275), channel_id=1, source_target_pairs={{0,16},{16,32},{32,48},{48,64},{64,80},{80,96},{96,112},{112,128},... | collective-permute-start | bytes 98312 | tf_op jit(solution)/shard_map/ppermute | solution.py:14
  67.9 1.2 %copy-start.5 = (f32[64,8,128]{2,1,0:T(8,128)S(1)}, f32[64,8,128]{2,1,0:T(8,128)}, u32[]{:S(2)}) copy-start(f32[64,8,128]{2,1,0:T(8,128)} %get-tuple-element.21) | copy-start | bytes 786436
  67.9 1.2 %copy-start.6 = (f32[64,8,128]{2,1,0:T(8,128)S(1)}, f32[64,8,128]{2,1,0:T(8,128)}, u32[]{:S(2)}) copy-start(f32[64,8,128]{2,1,0:T(8,128)} %get-tuple-element.22) | copy-start | bytes 786436

commit v7 on v4

--- a/solution.py
+++ b/solution.py
@@ -207,7 +207,7 @@
     def middle(z, below):
         return row(z, below, (e_ref[0, z + 1], e_ref[1, z + 1]), False)
 
-    below = lax.fori_loop(1, depth - 1, middle, below, unroll=2)
+    below = lax.fori_loop(1, depth - 1, middle, below, unroll=8)
     row(depth - 1, below, (zero, zero), False)
     thomas_kernel(
         rate_ref.at[3], diag_ref, sx_ref, sy_ref, px_ref, py_ref, lw_ref, hw_ref, edge_ref, ur_ref

time: 69.6 us -> 68.2 us (0.980)
  Pallas kernels: 7.71 us -> 6.37 us
    pallas_call x1, Pallas kernels: 7.71 us -> 6.37 us  [make_sources(): pl.pallas_call(source_kernel, out_shape=(shape,) * 7 + (edges,), in_specs...]
where the time goes in v7:
time: 68.2 us; the launch traced here: 67.3 us
  starting transfers between devices  40.4 us (59%)
  local copies, waits for them, and re-layouts  8.9 us (13%)
  other arithmetic  8.45 us (12%)
  Pallas kernels  6.37 us (9%)
  waiting for transfers between devices  2.09 us (3%)
  between operations  1.13 us (2%)
    ppermute x4, starting transfers between devices, from_prev(): return lax.ppermute(block, axis, [(i, i + 1) for i in range(count - 1)])  22.6 us
    ppermute x2, starting transfers between devices, from_diagonal(): return lax.ppermute(block, axes, pairs)  7.67 us
    pallas_call x1, Pallas kernels, make_sources(): pl.pallas_call(source_kernel, out_shape=(shape,) * 7 + (edges,), in_specs...  6.37 us
    ppermute x2, starting transfers between devices, from_next(): return lax.ppermute(block, axis, [(i + 1, i) for i in range(count - 1)])  5.21 us
    ppermute x3, starting transfers between devices, body(): lax.ppermute(own, 'gz', [(i, (i + shift) % slab_count) for i in range(sla...  4.88 us
    unnamed x33, local copies, waits for them, and re-layouts  3.1 us
    another operation x3, other arithmetic, body(): rate_stack = jnp.stack([keep_rate, curl_rate, z_rate, stiffness])  2.31 us
    ppermute x3, waiting for transfers between devices, body(): lax.ppermute(own, 'gz', [(i, (i + shift) % slab_count) for i in range(sla...  2.01 us
  transfers between devices with their start and end apart: 11, of which 3 were waited for; matrix products, arithmetic and copies ran while one was open for 10% of the time, Pallas kernels for 0%

profile of v7, /device:TPU:97, one launch (start us, length us, event | category | flops | bytes accessed | tf_op | source)
XLA Modules:
  0.0 67.3 jit_solution(5399875949010475407)
XLA Ops:
  0.6 1.2 %slice_bitcast_fusion = (f32[64,8,128]{2,1,0:T(8,128)S(1)}, f32[64,8,128]{2,1,0:T(8,128)S(1)}, f32[64,8,128]{2,1,0:T(8,128)S(1)}) fusion(f32[3,64,8,128]{3,2,1,0:T(8,128)} %e_ref.1), kind=kLoop, calls=%fused_computation.21 | loop fusion | bytes 1572864 | tf_op jit(solution)/shard_map/squeeze | solution.py:256
  2.4 1.0 %slice-done = f32[1,64,8,128]{3,2,1,0:T(8,128)S(1)} async-done(((f32[3,64,8,128]{3,2,1,0:T(8,128)}), f32[1,64,8,128]{3,2,1,0:T(8,128)S(1)}, s32[]{:S(2)}) %slice-start) | async-done | bytes 262168 | tf_op jit(solution)/shard_map/slice | solution.py:257
  3.7 3.8 %collective-permute-start.3 = (f32[3,64,8,1]{1,2,3,0:T(8,128)S(1)}, f32[3,64,8,1]{1,2,3,0:T(8,128)S(1)}, u32[]{:S(2)}, u32[]{:S(2)}) collective-permute-start(f32[3,64,8,1]{1,2,3,0:T(8,128)S(1)} %pad_maximum_fusion.6), channel_id=1, source_target_pairs={{0,4},{4,8},{8,12},{1,5},{5,9},{9,13},{2,6},{6,10},{10,14},{3,7},{... | collective-permute-start | bytes 18440 | tf_op jit(solution)/shard_map/ppermute | solution.py:14
  7.6 4.5 %collective-permute-start.1 = (f32[3,64,1,128]{3,1,2,0:T(8,128)S(1)}, f32[3,64,1,128]{3,1,2,0:T(8,128)S(1)}, u32[]{:S(2)}, u32[]{:S(2)}) collective-permute-start(f32[3,64,1,128]{3,1,2,0:T(8,128)S(1)} %pad_maximum_fusion.4), channel_id=1, source_target_pairs={{0,16},{16,32},{32,48},{48,64},{64,80},{80,96},{96,112},{112,128},... | collective-permute-start | bytes 294920 | tf_op jit(solution)/shard_map/ppermute | solution.py:14
  12.4 0.3 copy.121
  12.7 2.1 %collective-permute-start.2 = (f32[2,64,8,1]{3,2,1,0:T(8,128)S(1)}, f32[2,64,8,1]{3,2,1,0:T(8,128)S(1)}, u32[]{:S(2)}, u32[]{:S(2)}) collective-permute-start(f32[2,64,8,1]{3,2,1,0:T(8,128)S(1)} %copy.121), channel_id=1, source_target_pairs={{4,0},{8,4},{12,8},{5,1},{9,5},{13,9},{6,2},{10,6},{14,10},{7,3},{... | collective-permute-start | bytes 12296 | tf_op jit(solution)/shard_map/ppermute | solution.py:19
  14.8 3.2 %collective-permute-start = (f32[2,64,1,128]{3,1,2,0:T(8,128)S(1)}, f32[2,64,1,128]{3,1,2,0:T(8,128)S(1)}, u32[]{:S(2)}, u32[]{:S(2)}) collective-permute-start(f32[2,64,1,128]{3,1,2,0:T(8,128)S(1)} %pad_maximum_fusion.5), channel_id=1, source_target_pairs={{16,0},{32,16},{48,32},{64,48},{80,64},{96,80},{112,96},{128,112},... | collective-permute-start | bytes 196616 | tf_op jit(solution)/shard_map/ppermute | solution.py:19
  18.0 2.4 %collective-permute-start.4 = (f32[64,1,1]{2,1,0:T(1,128)S(1)}, f32[64,1,1]{2,1,0:T(1,128)S(1)}, u32[]{:S(2)}, u32[]{:S(2)}) collective-permute-start(f32[64,1,1]{2,1,0:T(1,128)S(1)} %slice.331), channel_id=1, source_target_pairs={{4,16},{8,20},{12,24},{20,32},{24,36},{28,40},{36,48},{40,52},{44,... | collective-permute-start | bytes 776 | tf_op jit(solution)/shard_map/ppermute | solution.py:31
  20.5 0.3 broadcast_compare_fusion.7
  20.8 0.3 copy-done.13
  21.3 1.2 %fusion.9 = (f32[1,64,8,128]{3,2,1,0:T(8,128)S(1)}, f32[64,8,128]{2,1,0:T(8,128)S(1)}, f32[64,8,128]{2,1,0:T(8,128)S(1)}) fusion(pred[64,8,128]{2,1,0:T(8,128)(4,1)S(1)} %get-tuple-element.85, f32[64]{0:T(128)S(1)} %get-tuple-element.116, pred[64,8,128]{2,1,0:T(8,128)(4,1)S(1)} %get-tuple-element.86, f32[64]{0:T(128)S(1)} %get-tuple-element.115, ...), kind=kLoop, calls=%fused_computation.40 | loop fusion | flops 2359296 | bytes 1314816 | tf_op jit(solution)/shard_map/stack | solution.py:271
  22.5 1.0 %pad_maximum_fusion.rate_ref = f32[4,64,8,128]{3,2,1,0:T(8,128)} fusion(f32[1,64,8,128]{3,2,1,0:T(8,128)S(1)} %get-tuple-element.73, f32[1,64,8,128]{3,2,1,0:T(8,128)S(1)} %get-tuple-element.74, f32[1,64,8,128]{3,2,1,0:T(8,128)S(1)} %get-tuple-element.72, f32[1,64,8,128]{3,2,1,0:T(8,128)S(1)} %get-tuple-element.62), kind=kLoop, calls=%fused_computation | loop fusion | flops 786432 | bytes 2097152 | tf_op jit(solution)/shard_map/stack | solution.py:271
  23.7 5.3 %collective-permute-start.5 = (f32[64,1,1]{2,1,0:T(1,128)S(1)}, f32[64,1,1]{2,1,0:T(1,128)S(1)}, u32[]{:S(2)}, u32[]{:S(2)}) collective-permute-start(f32[64,1,1]{2,1,0:T(1,128)S(1)} %slice.332), channel_id=1, source_target_pairs={{16,4},{20,8},{24,12},{32,20},{36,24},{40,28},{48,36},{52,40},{56,... | collective-permute-start | bytes 776 | tf_op jit(solution)/shard_map/ppermute | solution.py:31
  29.0 0.6 add_convert_fusion.flag_ref
  29.6 1.2 %copy.126.yl_ref = f32[3,64,8,1]{3,2,1,0:T(8,128)} copy(f32[3,64,8,1]{1,2,3,0:T(8,128)S(1)} %collective-permute-done.3) | data formatting | bytes 12288 | tf_op jit(solution)/shard_map/ppermute | solution.py:14
  30.9 0.5 copy-done.11
  31.6 6.4 %shard_map.77 = (f32[64,8,128]{2,1,0:T(8,128)}, f32[64,8,128]{2,1,0:T(8,128)}, f32[64,8,128]{2,1,0:T(8,128)}, f32[64,8,128]{2,1,0:T(8,128)}, f32[64,8,128]{2,1,0...) custom-call(s32[3]{0:T(128)} %add_convert_fusion.flag_ref, ...), custom_call_target="tpu_custom_call" | custom-call | tf_op jit(solution)/shard_map/pallas_call | solution.py:227
  38.0 1.3 %collective-permute-start.6 = (f32[12,8,128]{2,1,0:T(8,128)}, f32[12,8,128]{2,1,0:T(8,128)S(1)}, u32[]{:S(2)}, u32[]{:S(2)}) collective-permute-start(f32[12,8,128]{2,1,0:T(8,128)} %get-tuple-element.11), channel_id=1, source_target_pairs={{0,1},{1,2},{2,3},{3,0},{4,5},{5,6},{6,7},{7,4},{8,9},{9,10},{10,1... | collective-permute-start | bytes 147464 | tf_op jit(solution)/shard_map/ppermute | solution.py:281
  39.3 2.5 %collective-permute-start.7 = (f32[12,8,128]{2,1,0:T(8,128)}, f32[12,8,128]{2,1,0:T(8,128)S(1)}, u32[]{:S(2)}, u32[]{:S(2)}) collective-permute-start(f32[12,8,128]{2,1,0:T(8,128)} %get-tuple-element.11), channel_id=1, source_target_pairs={{0,2},{1,3},{2,0},{3,1},{4,6},{5,7},{6,4},{7,5},{8,10},{9,11},{10,... | collective-permute-start | bytes 147464 | tf_op jit(solution)/shard_map/ppermute | solution.py:281
  41.7 1.2 %collective-permute-start.8 = (f32[12,8,128]{2,1,0:T(8,128)}, f32[12,8,128]{2,1,0:T(8,128)S(1)}, u32[]{:S(2)}, u32[]{:S(2)}) collective-permute-start(f32[12,8,128]{2,1,0:T(8,128)} %get-tuple-element.11), channel_id=1, source_target_pairs={{0,3},{1,0},{2,1},{3,2},{4,7},{5,4},{6,5},{7,6},{8,11},{9,8},{10,9... | collective-permute-start | bytes 147464 | tf_op jit(solution)/shard_map/ppermute | solution.py:281
  42.9 0.6 dynamic-slice.23
  43.5 1.0 %collective-permute-done.7 = f32[12,8,128]{2,1,0:T(8,128)S(1)} collective-permute-done((f32[12,8,128]{2,1,0:T(8,128)}, f32[12,8,128]{2,1,0:T(8,128)S(1)}, u32[]{:S(2)}, u32[]{:S(2)}) %collective-permute-start.7) | collective-permute-done | bytes 49184 | tf_op jit(solution)/shard_map/ppermute | solution.py:281
  44.5 1.0 %collective-permute-done.8 = f32[12,8,128]{2,1,0:T(8,128)S(1)} collective-permute-done((f32[12,8,128]{2,1,0:T(8,128)}, f32[12,8,128]{2,1,0:T(8,128)S(1)}, u32[]{:S(2)}, u32[]{:S(2)}) %collective-permute-start.8) | collective-permute-done | bytes 49184 | tf_op jit(solution)/shard_map/ppermute | solution.py:281
  45.5 0.8 %pad_maximum_fusion.3 = f32[4,12,8,128]{3,2,1,0:T(8,128)S(1)} fusion(f32[1,12,8,128]{3,2,1,0:T(8,128)S(1)} %bitcast.231, f32[1,12,8,128]{3,2,1,0:T(8,128)S(1)} %bitcast.230, f32[1,12,8,128]{3,2,1,0:T(8,128)S(1)} %bitcast.229, f32[1,12,8,128]{3,2,1,0:T(8,128)} %bitcast.228), kind=kLoop, calls=%fused_computation.31 | loop fusion | flops 147456 | bytes 393216 | tf_op jit(solution)/shard_map/stack | solution.py:283
  46.5 0.7 fusion.65
  47.4 0.7 %copy-done.6 = f32[64,8,128]{2,1,0:T(8,128)S(1)} copy-done((f32[64,8,128]{2,1,0:T(8,128)S(1)}, f32[64,8,128]{2,1,0:T(8,128)}, u32[]{:S(2)}) %copy-start.6) | copy-done | bytes 262168
  48.2 1.2 %fusion.87 = (f32[64,8,128]{2,1,0:T(8,128)S(1)}, f32[64,8,128]{2,1,0:T(8,128)S(1)}, f32[64,8,128]{2,1,0:T(8,128)S(1)}, f32[64,8,128]{2,1,0:T(8,128)S(1)}) fusion(f32[3,64,8,128]{3,2,1,0:T(8,128)S(1)} %copy-done, f32[64,8,128]{2,1,0:T(8,128)} %get-tuple-element.13, f32[8,128]{1,0:T(8,128)S(1)} %get-tuple-element.90, f32[64,8,128]{2,1,0:T(8,128)S(1)} %copy-done.7, ...), kind=kLoop, calls=%fused_computation.214 | loop fusion | flops 655360 | bytes 2637824 | tf_op jit(solution)/shard_map/add | solution.py:346
  49.4 1.1 %copy-done.1 = f32[3,64,8,128]{3,2,1,0:T(8,128)S(1)} copy-done((f32[3,64,8,128]{3,2,1,0:T(8,128)S(1)}, f32[3,64,8,128]{3,2,1,0:T(8,128)}, u32[]{:S(2)}) %copy-start.1) | copy-done | bytes 786456
  50.8 4.8 %collective-permute-start.10 = (f32[64,8,1]{2,1,0:T(8,128)S(1)}, f32[64,8,1]{2,1,0:T(8,128)S(1)}, u32[]{:S(2)}, u32[]{:S(2)}) collective-permute-start(f32[64,8,1]{2,1,0:T(8,128)S(1)} %slice.341), channel_id=1, source_target_pairs={{0,4},{4,8},{8,12},{1,5},{5,9},{9,13},{2,6},{6,10},{10,14},{3,7},{... | collective-permute-start | bytes 6152 | tf_op jit(solution)/shard_map/ppermute | solution.py:14
  55.7 9.5 %collective-permute-start.9 = (f32[64,1,128]{2,1,0:T(1,128)S(1)}, f32[64,1,128]{2,1,0:T(1,128)S(1)}, u32[]{:S(2)}, u32[]{:S(2)}) collective-permute-start(f32[64,1,128]{2,1,0:T(1,128)S(1)} %slice.338), channel_id=1, source_target_pairs={{0,16},{16,32},{32,48},{48,64},{64,80},{80,96},{96,112},{112,128},... | collective-permute-start | bytes 98312 | tf_op jit(solution)/shard_map/ppermute | solution.py:14
  65.2 0.9 %pad_maximum_fusion.2 = f32[3,64,8,128]{3,2,1,0:T(8,128)} fusion(f32[1,64,8,128]{3,2,1,0:T(8,128)S(1)} %bitcast.221, f32[1,64,8,128]{3,2,1,0:T(8,128)S(1)} %bitcast.214, f32[1,64,8,128]{3,2,1,0:T(8,128)S(1)} %bitcast.212), kind=kLoop, calls=%fused_computation.2 | loop fusion | flops 393216 | bytes 1572864 | tf_op jit(solution)/shard_map/stack | solution.py:360
  66.4 0.9 %pad_maximum_fusion.1 = f32[3,64,8,128]{3,2,1,0:T(8,128)} fusion(f32[1,64,8,128]{3,2,1,0:T(8,128)S(1)} %fusion.6, f32[1,64,8,128]{3,2,1,0:T(8,128)S(1)} %bitcast.219, f32[1,64,8,128]{3,2,1,0:T(8,128)S(1)} %bitcast.220), kind=kLoop, calls=%fused_computation.1 | loop fusion | flops 393216 | bytes 1572864 | tf_op jit(solution)/shard_map/stack | solution.py:359
  (76 shorter events, 3.0 us)
Async XLA Ops:
  2.4 1.0 %slice-start = ((f32[3,64,8,128]{3,2,1,0:T(8,128)}), f32[1,64,8,128]{3,2,1,0:T(8,128)S(1)}, s32[]{:S(2)}) async-start(f32[3,64,8,128]{3,2,1,0:T(8,128)} %h_ref.1), calls=%async_computation | async-start | bytes 524288 | tf_op jit(solution)/shard_map/slice | solution.py:257
  3.7 20.0 %collective-permute-start.3 = (f32[3,64,8,1]{1,2,3,0:T(8,128)S(1)}, f32[3,64,8,1]{1,2,3,0:T(8,128)S(1)}, u32[]{:S(2)}, u32[]{:S(2)}) collective-permute-start(f32[3,64,8,1]{1,2,3,0:T(8,128)S(1)} %pad_maximum_fusion.6), channel_id=1, source_target_pairs={{0,4},{4,8},{8,12},{1,5},{5,9},{9,13},{2,6},{6,10},{10,14},{3,7},{... | collective-permute-start | bytes 18440 | tf_op jit(solution)/shard_map/ppermute | solution.py:14
  7.6 23.3 %collective-permute-start.1 = (f32[3,64,1,128]{3,1,2,0:T(8,128)S(1)}, f32[3,64,1,128]{3,1,2,0:T(8,128)S(1)}, u32[]{:S(2)}, u32[]{:S(2)}) collective-permute-start(f32[3,64,1,128]{3,1,2,0:T(8,128)S(1)} %pad_maximum_fusion.4), channel_id=1, source_target_pairs={{0,16},{16,32},{32,48},{48,64},{64,80},{80,96},{96,112},{112,128},... | collective-permute-start | bytes 294920 | tf_op jit(solution)/shard_map/ppermute | solution.py:14
  12.7 7.8 %copy-start.3 = (s32[64,8,128]{2,1,0:T(8,128)S(1)}, s32[64,8,128]{2,1,0:T(8,128)}, u32[]{:S(2)}) copy-start(s32[64,8,128]{2,1,0:T(8,128)} %param.8) | copy-start | bytes 786436
  12.7 18.1 %collective-permute-start.2 = (f32[2,64,8,1]{3,2,1,0:T(8,128)S(1)}, f32[2,64,8,1]{3,2,1,0:T(8,128)S(1)}, u32[]{:S(2)}, u32[]{:S(2)}) collective-permute-start(f32[2,64,8,1]{3,2,1,0:T(8,128)S(1)} %copy.121), channel_id=1, source_target_pairs={{4,0},{8,4},{12,8},{5,1},{9,5},{13,9},{6,2},{10,6},{14,10},{7,3},{... | collective-permute-start | bytes 12296 | tf_op jit(solution)/shard_map/ppermute | solution.py:19
  14.8 5.6 %copy-start.15 = (s32[64]{0:T(128)S(1)}, s32[64]{0:T(128)}, u32[]{:S(2)}) copy-start(s32[64]{0:T(128)} %param.9) | copy-start | bytes 772
  14.8 16.0 %collective-permute-start = (f32[2,64,1,128]{3,1,2,0:T(8,128)S(1)}, f32[2,64,1,128]{3,1,2,0:T(8,128)S(1)}, u32[]{:S(2)}, u32[]{:S(2)}) collective-permute-start(f32[2,64,1,128]{3,1,2,0:T(8,128)S(1)} %pad_maximum_fusion.5), channel_id=1, source_target_pairs={{16,0},{32,16},{48,32},{64,48},{80,64},{96,80},{112,96},{128,112},... | collective-permute-start | bytes 196616 | tf_op jit(solution)/shard_map/ppermute | solution.py:19
  18.0 12.8 %collective-permute-start.4 = (f32[64,1,1]{2,1,0:T(1,128)S(1)}, f32[64,1,1]{2,1,0:T(1,128)S(1)}, u32[]{:S(2)}, u32[]{:S(2)}) collective-permute-start(f32[64,1,1]{2,1,0:T(1,128)S(1)} %slice.331), channel_id=1, source_target_pairs={{4,16},{8,20},{12,24},{20,32},{24,36},{28,40},{36,48},{40,52},{44,... | collective-permute-start | bytes 776 | tf_op jit(solution)/shard_map/ppermute | solution.py:31
  20.5 0.7 %copy-start.13 = (f32[4,8]{1,0:T(4,128)S(1)}, f32[4,8]{1,0:T(4,128)}, u32[]{:S(2)}) copy-start(f32[4,8]{1,0:T(4,128)} %param.11) | copy-start | bytes 388
  20.5 0.7 %copy-start.14 = (f32[4,8]{1,0:T(4,128)S(1)}, f32[4,8]{1,0:T(4,128)}, u32[]{:S(2)}) copy-start(f32[4,8]{1,0:T(4,128)} %param.10) | copy-start | bytes 388
  23.7 7.1 %collective-permute-start.5 = (f32[64,1,1]{2,1,0:T(1,128)S(1)}, f32[64,1,1]{2,1,0:T(1,128)S(1)}, u32[]{:S(2)}, u32[]{:S(2)}) collective-permute-start(f32[64,1,1]{2,1,0:T(1,128)S(1)} %slice.332), channel_id=1, source_target_pairs={{16,4},{20,8},{24,12},{32,20},{36,24},{40,28},{48,36},{52,40},{56,... | collective-permute-start | bytes 776 | tf_op jit(solution)/shard_map/ppermute | solution.py:31
  30.8 0.6 copy-start.11
  30.8 0.6 copy-start.12
  30.8 0.8 %copy-start.2 = (f32[2,64,8,1]{3,2,1,0:T(8,128)}, f32[2,64,8,1]{3,2,1,0:T(8,128)S(1)}, u32[]{:S(2)}) copy-start(f32[2,64,8,1]{3,2,1,0:T(8,128)S(1)} %collective-permute-done.2.yh_ref) | copy-start | bytes 12292
  30.8 0.8 %copy-start.10 = (f32[2,64,1,128]{3,1,2,0:T(8,128)}, f32[2,64,1,128]{3,1,2,0:T(8,128)S(1)}, u32[]{:S(2)}) copy-start(f32[2,64,1,128]{3,1,2,0:T(8,128)S(1)} %collective-permute-done) | copy-start | bytes 196612
  30.9 0.8 %copy-start.9 = (f32[3,64,1,128]{3,1,2,0:T(8,128)}, f32[3,64,1,128]{3,1,2,0:T(8,128)S(1)}, u32[]{:S(2)}) copy-start(f32[3,64,1,128]{3,1,2,0:T(8,128)S(1)} %collective-permute-done.1) | copy-start | bytes 294916
  38.0 9.3 %copy-start = (f32[3,64,8,128]{3,2,1,0:T(8,128)S(1)}, f32[3,64,8,128]{3,2,1,0:T(8,128)}, u32[]{:S(2)}) copy-start(f32[3,64,8,128]{3,2,1,0:T(8,128)} %e_ref.1) | copy-start | bytes 2359300
  38.0 5.5 %collective-permute-start.6 = (f32[12,8,128]{2,1,0:T(8,128)}, f32[12,8,128]{2,1,0:T(8,128)S(1)}, u32[]{:S(2)}, u32[]{:S(2)}) collective-permute-start(f32[12,8,128]{2,1,0:T(8,128)} %get-tuple-element.11), channel_id=1, source_target_pairs={{0,1},{1,2},{2,3},{3,0},{4,5},{5,6},{6,7},{7,4},{8,9},{9,10},{10,1... | collective-permute-start | bytes 147464 | tf_op jit(solution)/shard_map/ppermute | solution.py:281
  39.3 5.2 %collective-permute-start.7 = (f32[12,8,128]{2,1,0:T(8,128)}, f32[12,8,128]{2,1,0:T(8,128)S(1)}, u32[]{:S(2)}, u32[]{:S(2)}) collective-permute-start(f32[12,8,128]{2,1,0:T(8,128)} %get-tuple-element.11), channel_id=1, source_target_pairs={{0,2},{1,3},{2,0},{3,1},{4,6},{5,7},{6,4},{7,5},{8,10},{9,11},{10,... | collective-permute-start | bytes 147464 | tf_op jit(solution)/shard_map/ppermute | solution.py:281
  41.7 3.8 %collective-permute-start.8 = (f32[12,8,128]{2,1,0:T(8,128)}, f32[12,8,128]{2,1,0:T(8,128)S(1)}, u32[]{:S(2)}, u32[]{:S(2)}) collective-permute-start(f32[12,8,128]{2,1,0:T(8,128)} %get-tuple-element.11), channel_id=1, source_target_pairs={{0,3},{1,0},{2,1},{3,2},{4,7},{5,4},{6,5},{7,6},{8,11},{9,8},{10,9... | collective-permute-start | bytes 147464 | tf_op jit(solution)/shard_map/ppermute | solution.py:281
  47.1 1.0 %copy-start.6 = (f32[64,8,128]{2,1,0:T(8,128)S(1)}, f32[64,8,128]{2,1,0:T(8,128)}, u32[]{:S(2)}) copy-start(f32[64,8,128]{2,1,0:T(8,128)} %get-tuple-element.10) | copy-start | bytes 786436
  47.1 1.0 %copy-start.7 = (f32[64,8,128]{2,1,0:T(8,128)S(1)}, f32[64,8,128]{2,1,0:T(8,128)}, u32[]{:S(2)}) copy-start(f32[64,8,128]{2,1,0:T(8,128)} %get-tuple-element.14) | copy-start | bytes 786436
  48.2 1.3 %copy-start.4 = (f32[64,8,128]{2,1,0:T(8,128)S(1)}, f32[64,8,128]{2,1,0:T(8,128)}, u32[]{:S(2)}) copy-start(f32[64,8,128]{2,1,0:T(8,128)} %get-tuple-element.15) | copy-start | bytes 786436
  48.2 1.3 %copy-start.5 = (f32[64,8,128]{2,1,0:T(8,128)S(1)}, f32[64,8,128]{2,1,0:T(8,128)}, u32[]{:S(2)}) copy-start(f32[64,8,128]{2,1,0:T(8,128)} %get-tuple-element.16) | copy-start | bytes 786436
  49.4 1.1 %copy-start.1 = (f32[3,64,8,128]{3,2,1,0:T(8,128)S(1)}, f32[3,64,8,128]{3,2,1,0:T(8,128)}, u32[]{:S(2)}) copy-start(f32[3,64,8,128]{3,2,1,0:T(8,128)} %h_ref.1) | copy-start | bytes 2359300
  50.7 14.5 %copy-start.8 = (f32[64,8,128]{2,1,0:T(8,128)S(1)}, f32[64,8,128]{2,1,0:T(8,128)}, u32[]{:S(2)}) copy-start(f32[64,8,128]{2,1,0:T(8,128)} %get-tuple-element.17) | copy-start | bytes 786436
  50.8 15.4 %collective-permute-start.10 = (f32[64,8,1]{2,1,0:T(8,128)S(1)}, f32[64,8,1]{2,1,0:T(8,128)S(1)}, u32[]{:S(2)}, u32[]{:S(2)}) collective-permute-start(f32[64,8,1]{2,1,0:T(8,128)S(1)} %slice.341), channel_id=1, source_target_pairs={{0,4},{4,8},{8,12},{1,5},{5,9},{9,13},{2,6},{6,10},{10,14},{3,7},{... | collective-permute-start | bytes 6152 | tf_op jit(solution)/shard_map/ppermute | solution.py:14
  55.7 10.5 %collective-permute-start.9 = (f32[64,1,128]{2,1,0:T(1,128)S(1)}, f32[64,1,128]{2,1,0:T(1,128)S(1)}, u32[]{:S(2)}, u32[]{:S(2)}) collective-permute-start(f32[64,1,128]{2,1,0:T(1,128)S(1)} %slice.338), channel_id=1, source_target_pairs={{0,16},{16,32},{32,48},{48,64},{64,80},{80,96},{96,112},{112,128},... | collective-permute-start | bytes 98312 | tf_op jit(solution)/shard_map/ppermute | solution.py:14

commit v8 on v7

--- a/solution.py
+++ b/solution.py
@@ -79,7 +79,7 @@
         return upper, value_x, value_y, value_low, inv
 
     first = (ur_ref[0], px_ref[0], py_ref[0], lw_ref[0], inv)
-    last_x, last_y, last_low, last_high = lax.fori_loop(1, depth, forward, first, unroll=8)[1:]
+    last_x, last_y, last_low, last_high = lax.fori_loop(1, depth, forward, first, unroll=16)[1:]
     low_scale = stiff_ref[0]
     high_scale = stiff_ref[depth - 1]
     lw_ref[depth - 1] = low_scale * last_low
@@ -99,7 +99,7 @@
         hw_ref[z] = high_scale * next_high
         return next_x, next_y, next_low, next_high
 
-    lax.fori_loop(0, depth - 1, backward, (last_x, last_y, last_low, last_high), unroll=8)
+    lax.fori_loop(0, depth - 1, backward, (last_x, last_y, last_low, last_high), unroll=16)
     edge_ref[0] = px_ref[0]
     edge_ref[1] = py_ref[0]
     edge_ref[2] = px_ref[depth - 1]
@@ -207,7 +207,7 @@
     def middle(z, below):
         return row(z, below, (e_ref[0, z + 1], e_ref[1, z + 1]), False)
 
-    below = lax.fori_loop(1, depth - 1, middle, below, unroll=8)
+    below = lax.fori_loop(1, depth - 1, middle, below, unroll=True)
     row(depth - 1, below, (zero, zero), False)
     thomas_kernel(
         rate_ref.at[3], diag_ref, sx_ref, sy_ref, px_ref, py_ref, lw_ref, hw_ref, edge_ref, ur_ref

time: 68.2 us -> 67.2 us (0.985)
  Pallas kernels: 6.37 us -> 5.37 us
    pallas_call x1, Pallas kernels: 6.37 us -> 5.37 us  [make_sources(): pl.pallas_call(source_kernel, out_shape=(shape,) * 7 + (edges,), in_specs...]
where the time goes in v8:
time: 67.2 us; the launch traced here: 66.3 us
  starting transfers between devices  40.4 us (60%)
  local copies, waits for them, and re-layouts  8.9 us (13%)
  other arithmetic  8.45 us (13%)
  Pallas kernels  5.37 us (8%)
  waiting for transfers between devices  2.09 us (3%)
  between operations  1.13 us (2%)
    ppermute x4, starting transfers between devices, from_prev(): return lax.ppermute(block, axis, [(i, i + 1) for i in range(count - 1)])  22.6 us
    ppermute x2, starting transfers between devices, from_diagonal(): return lax.ppermute(block, axes, pairs)  7.67 us
    pallas_call x1, Pallas kernels, make_sources(): pl.pallas_call(source_kernel, out_shape=(shape,) * 7 + (edges,), in_specs...  5.37 us
    ppermute x2, starting transfers between devices, from_next(): return lax.ppermute(block, axis, [(i + 1, i) for i in range(count - 1)])  5.21 us
    ppermute x3, starting transfers between devices, body(): lax.ppermute(own, 'gz', [(i, (i + shift) % slab_count) for i in range(sla...  4.88 us
    unnamed x33, local copies, waits for them, and re-layouts  3.1 us
    another operation x3, other arithmetic, body(): rate_stack = jnp.stack([keep_rate, curl_rate, z_rate, stiffness])  2.31 us
    ppermute x3, waiting for transfers between devices, body(): lax.ppermute(own, 'gz', [(i, (i + shift) % slab_count) for i in range(sla...  2.01 us
  transfers between devices with their start and end apart: 11, of which 3 were waited for; matrix products, arithmetic and copies ran while one was open for 10% of the time, Pallas kernels for 0%

profile of v8, /device:TPU:97, one launch (start us, length us, event | category | flops | bytes accessed | tf_op | source)
XLA Modules:
  0.0 66.3 jit_solution(16970916830136662842)
XLA Ops:
  0.6 1.2 %slice_bitcast_fusion = (f32[64,8,128]{2,1,0:T(8,128)S(1)}, f32[64,8,128]{2,1,0:T(8,128)S(1)}, f32[64,8,128]{2,1,0:T(8,128)S(1)}) fusion(f32[3,64,8,128]{3,2,1,0:T(8,128)} %e_ref.1), kind=kLoop, calls=%fused_computation.21 | loop fusion | bytes 1572864 | tf_op jit(solution)/shard_map/squeeze | solution.py:256
  2.4 1.0 %slice-done = f32[1,64,8,128]{3,2,1,0:T(8,128)S(1)} async-done(((f32[3,64,8,128]{3,2,1,0:T(8,128)}), f32[1,64,8,128]{3,2,1,0:T(8,128)S(1)}, s32[]{:S(2)}) %slice-start) | async-done | bytes 262168 | tf_op jit(solution)/shard_map/slice | solution.py:257
  3.7 3.8 %collective-permute-start.3 = (f32[3,64,8,1]{1,2,3,0:T(8,128)S(1)}, f32[3,64,8,1]{1,2,3,0:T(8,128)S(1)}, u32[]{:S(2)}, u32[]{:S(2)}) collective-permute-start(f32[3,64,8,1]{1,2,3,0:T(8,128)S(1)} %pad_maximum_fusion.6), channel_id=1, source_target_pairs={{0,4},{4,8},{8,12},{1,5},{5,9},{9,13},{2,6},{6,10},{10,14},{3,7},{... | collective-permute-start | bytes 18440 | tf_op jit(solution)/shard_map/ppermute | solution.py:14
  7.6 4.5 %collective-permute-start.1 = (f32[3,64,1,128]{3,1,2,0:T(8,128)S(1)}, f32[3,64,1,128]{3,1,2,0:T(8,128)S(1)}, u32[]{:S(2)}, u32[]{:S(2)}) collective-permute-start(f32[3,64,1,128]{3,1,2,0:T(8,128)S(1)} %pad_maximum_fusion.4), channel_id=1, source_target_pairs={{0,16},{16,32},{32,48},{48,64},{64,80},{80,96},{96,112},{112,128},... | collective-permute-start | bytes 294920 | tf_op jit(solution)/shard_map/ppermute | solution.py:14
  12.4 0.3 copy.121
  12.7 2.1 %collective-permute-start.2 = (f32[2,64,8,1]{3,2,1,0:T(8,128)S(1)}, f32[2,64,8,1]{3,2,1,0:T(8,128)S(1)}, u32[]{:S(2)}, u32[]{:S(2)}) collective-permute-start(f32[2,64,8,1]{3,2,1,0:T(8,128)S(1)} %copy.121), channel_id=1, source_target_pairs={{4,0},{8,4},{12,8},{5,1},{9,5},{13,9},{6,2},{10,6},{14,10},{7,3},{... | collective-permute-start | bytes 12296 | tf_op jit(solution)/shard_map/ppermute | solution.py:19
  14.8 3.2 %collective-permute-start = (f32[2,64,1,128]{3,1,2,0:T(8,128)S(1)}, f32[2,64,1,128]{3,1,2,0:T(8,128)S(1)}, u32[]{:S(2)}, u32[]{:S(2)}) collective-permute-start(f32[2,64,1,128]{3,1,2,0:T(8,128)S(1)} %pad_maximum_fusion.5), channel_id=1, source_target_pairs={{16,0},{32,16},{48,32},{64,48},{80,64},{96,80},{112,96},{128,112},... | collective-permute-start | bytes 196616 | tf_op jit(solution)/shard_map/ppermute | solution.py:19
  18.0 2.4 %collective-permute-start.4 = (f32[64,1,1]{2,1,0:T(1,128)S(1)}, f32[64,1,1]{2,1,0:T(1,128)S(1)}, u32[]{:S(2)}, u32[]{:S(2)}) collective-permute-start(f32[64,1,1]{2,1,0:T(1,128)S(1)} %slice.331), channel_id=1, source_target_pairs={{4,16},{8,20},{12,24},{20,32},{24,36},{28,40},{36,48},{40,52},{44,... | collective-permute-start | bytes 776 | tf_op jit(solution)/shard_map/ppermute | solution.py:31
  20.5 0.3 broadcast_compare_fusion.7
  20.8 0.3 copy-done.13
  21.3 1.2 %fusion.9 = (f32[1,64,8,128]{3,2,1,0:T(8,128)S(1)}, f32[64,8,128]{2,1,0:T(8,128)S(1)}, f32[64,8,128]{2,1,0:T(8,128)S(1)}) fusion(pred[64,8,128]{2,1,0:T(8,128)(4,1)S(1)} %get-tuple-element.85, f32[64]{0:T(128)S(1)} %get-tuple-element.116, pred[64,8,128]{2,1,0:T(8,128)(4,1)S(1)} %get-tuple-element.86, f32[64]{0:T(128)S(1)} %get-tuple-element.115, ...), kind=kLoop, calls=%fused_computation.40 | loop fusion | flops 2359296 | bytes 1314816 | tf_op jit(solution)/shard_map/stack | solution.py:271
  22.5 1.0 %pad_maximum_fusion.rate_ref = f32[4,64,8,128]{3,2,1,0:T(8,128)} fusion(f32[1,64,8,128]{3,2,1,0:T(8,128)S(1)} %get-tuple-element.73, f32[1,64,8,128]{3,2,1,0:T(8,128)S(1)} %get-tuple-element.74, f32[1,64,8,128]{3,2,1,0:T(8,128)S(1)} %get-tuple-element.72, f32[1,64,8,128]{3,2,1,0:T(8,128)S(1)} %get-tuple-element.62), kind=kLoop, calls=%fused_computation | loop fusion | flops 786432 | bytes 2097152 | tf_op jit(solution)/shard_map/stack | solution.py:271
  23.7 5.3 %collective-permute-start.5 = (f32[64,1,1]{2,1,0:T(1,128)S(1)}, f32[64,1,1]{2,1,0:T(1,128)S(1)}, u32[]{:S(2)}, u32[]{:S(2)}) collective-permute-start(f32[64,1,1]{2,1,0:T(1,128)S(1)} %slice.332), channel_id=1, source_target_pairs={{16,4},{20,8},{24,12},{32,20},{36,24},{40,28},{48,36},{52,40},{56,... | collective-permute-start | bytes 776 | tf_op jit(solution)/shard_map/ppermute | solution.py:31
  29.0 0.6 add_convert_fusion.flag_ref
  29.6 1.2 %copy.126.yl_ref = f32[3,64,8,1]{3,2,1,0:T(8,128)} copy(f32[3,64,8,1]{1,2,3,0:T(8,128)S(1)} %collective-permute-done.3) | data formatting | bytes 12288 | tf_op jit(solution)/shard_map/ppermute | solution.py:14
  30.9 0.5 copy-done.11
  31.6 5.4 %shard_map.77 = (f32[64,8,128]{2,1,0:T(8,128)}, f32[64,8,128]{2,1,0:T(8,128)}, f32[64,8,128]{2,1,0:T(8,128)}, f32[64,8,128]{2,1,0:T(8,128)}, f32[64,8,128]{2,1,0...) custom-call(s32[3]{0:T(128)} %add_convert_fusion.flag_ref, ...), custom_call_target="tpu_custom_call" | custom-call | tf_op jit(solution)/shard_map/pallas_call | solution.py:227
  37.0 1.3 %collective-permute-start.6 = (f32[12,8,128]{2,1,0:T(8,128)}, f32[12,8,128]{2,1,0:T(8,128)S(1)}, u32[]{:S(2)}, u32[]{:S(2)}) collective-permute-start(f32[12,8,128]{2,1,0:T(8,128)} %get-tuple-element.11), channel_id=1, source_target_pairs={{0,1},{1,2},{2,3},{3,0},{4,5},{5,6},{6,7},{7,4},{8,9},{9,10},{10,1... | collective-permute-start | bytes 147464 | tf_op jit(solution)/shard_map/ppermute | solution.py:281
  38.3 2.5 %collective-permute-start.7 = (f32[12,8,128]{2,1,0:T(8,128)}, f32[12,8,128]{2,1,0:T(8,128)S(1)}, u32[]{:S(2)}, u32[]{:S(2)}) collective-permute-start(f32[12,8,128]{2,1,0:T(8,128)} %get-tuple-element.11), channel_id=1, source_target_pairs={{0,2},{1,3},{2,0},{3,1},{4,6},{5,7},{6,4},{7,5},{8,10},{9,11},{10,... | collective-permute-start | bytes 147464 | tf_op jit(solution)/shard_map/ppermute | solution.py:281
  40.7 1.2 %collective-permute-start.8 = (f32[12,8,128]{2,1,0:T(8,128)}, f32[12,8,128]{2,1,0:T(8,128)S(1)}, u32[]{:S(2)}, u32[]{:S(2)}) collective-permute-start(f32[12,8,128]{2,1,0:T(8,128)} %get-tuple-element.11), channel_id=1, source_target_pairs={{0,3},{1,0},{2,1},{3,2},{4,7},{5,4},{6,5},{7,6},{8,11},{9,8},{10,9... | collective-permute-start | bytes 147464 | tf_op jit(solution)/shard_map/ppermute | solution.py:281
  41.9 0.6 dynamic-slice.23
  42.5 1.0 %collective-permute-done.7 = f32[12,8,128]{2,1,0:T(8,128)S(1)} collective-permute-done((f32[12,8,128]{2,1,0:T(8,128)}, f32[12,8,128]{2,1,0:T(8,128)S(1)}, u32[]{:S(2)}, u32[]{:S(2)}) %collective-permute-start.7) | collective-permute-done | bytes 49184 | tf_op jit(solution)/shard_map/ppermute | solution.py:281
  43.5 1.0 %collective-permute-done.8 = f32[12,8,128]{2,1,0:T(8,128)S(1)} collective-permute-done((f32[12,8,128]{2,1,0:T(8,128)}, f32[12,8,128]{2,1,0:T(8,128)S(1)}, u32[]{:S(2)}, u32[]{:S(2)}) %collective-permute-start.8) | collective-permute-done | bytes 49184 | tf_op jit(solution)/shard_map/ppermute | solution.py:281
  44.5 0.8 %pad_maximum_fusion.3 = f32[4,12,8,128]{3,2,1,0:T(8,128)S(1)} fusion(f32[1,12,8,128]{3,2,1,0:T(8,128)S(1)} %bitcast.231, f32[1,12,8,128]{3,2,1,0:T(8,128)S(1)} %bitcast.230, f32[1,12,8,128]{3,2,1,0:T(8,128)S(1)} %bitcast.229, f32[1,12,8,128]{3,2,1,0:T(8,128)} %bitcast.228), kind=kLoop, calls=%fused_computation.31 | loop fusion | flops 147456 | bytes 393216 | tf_op jit(solution)/shard_map/stack | solution.py:283
  45.5 0.7 %fusion.65 = f32[8,128]{1,0:T(8,128)S(1)} fusion(s32[]{:T(128)S(6)} %select_n.124, f32[1,8,128]{2,1,0:T(8,128)S(1)} %get-tuple-element.26, f32[1,8,128]{2,1,0:T(8,128)S(1)} %get-tuple-element.25, f32[1,8,128]{2,1,0:T(8,128)S(1)} %get-tuple-element.24, f32[1]{0:T(128)} %dynamic-slice.23), kind=kLoop, calls=%fused_computation.154 | loop fusion | flops 3072 | bytes 16392 | tf_op jit(solution)/shard_map/mul | solution.py:337
  46.3 0.7 %copy-done.6 = f32[64,8,128]{2,1,0:T(8,128)S(1)} copy-done((f32[64,8,128]{2,1,0:T(8,128)S(1)}, f32[64,8,128]{2,1,0:T(8,128)}, u32[]{:S(2)}) %copy-start.6) | copy-done | bytes 262168
  47.2 1.2 %fusion.87 = (f32[64,8,128]{2,1,0:T(8,128)S(1)}, f32[64,8,128]{2,1,0:T(8,128)S(1)}, f32[64,8,128]{2,1,0:T(8,128)S(1)}, f32[64,8,128]{2,1,0:T(8,128)S(1)}) fusion(f32[3,64,8,128]{3,2,1,0:T(8,128)S(1)} %copy-done, f32[64,8,128]{2,1,0:T(8,128)} %get-tuple-element.13, f32[8,128]{1,0:T(8,128)S(1)} %get-tuple-element.90, f32[64,8,128]{2,1,0:T(8,128)S(1)} %copy-done.7, ...), kind=kLoop, calls=%fused_computation.214 | loop fusion | flops 655360 | bytes 2637824 | tf_op jit(solution)/shard_map/add | solution.py:346
  48.4 1.1 %copy-done.1 = f32[3,64,8,128]{3,2,1,0:T(8,128)S(1)} copy-done((f32[3,64,8,128]{3,2,1,0:T(8,128)S(1)}, f32[3,64,8,128]{3,2,1,0:T(8,128)}, u32[]{:S(2)}) %copy-start.1) | copy-done | bytes 786456
  49.8 4.8 %collective-permute-start.10 = (f32[64,8,1]{2,1,0:T(8,128)S(1)}, f32[64,8,1]{2,1,0:T(8,128)S(1)}, u32[]{:S(2)}, u32[]{:S(2)}) collective-permute-start(f32[64,8,1]{2,1,0:T(8,128)S(1)} %slice.341), channel_id=1, source_target_pairs={{0,4},{4,8},{8,12},{1,5},{5,9},{9,13},{2,6},{6,10},{10,14},{3,7},{... | collective-permute-start | bytes 6152 | tf_op jit(solution)/shard_map/ppermute | solution.py:14
  54.7 9.5 %collective-permute-start.9 = (f32[64,1,128]{2,1,0:T(1,128)S(1)}, f32[64,1,128]{2,1,0:T(1,128)S(1)}, u32[]{:S(2)}, u32[]{:S(2)}) collective-permute-start(f32[64,1,128]{2,1,0:T(1,128)S(1)} %slice.338), channel_id=1, source_target_pairs={{0,16},{16,32},{32,48},{48,64},{64,80},{80,96},{96,112},{112,128},... | collective-permute-start | bytes 98312 | tf_op jit(solution)/shard_map/ppermute | solution.py:14
  64.2 0.9 %pad_maximum_fusion.2 = f32[3,64,8,128]{3,2,1,0:T(8,128)} fusion(f32[1,64,8,128]{3,2,1,0:T(8,128)S(1)} %bitcast.221, f32[1,64,8,128]{3,2,1,0:T(8,128)S(1)} %bitcast.214, f32[1,64,8,128]{3,2,1,0:T(8,128)S(1)} %bitcast.212), kind=kLoop, calls=%fused_computation.2 | loop fusion | flops 393216 | bytes 1572864 | tf_op jit(solution)/shard_map/stack | solution.py:360
  65.4 0.9 %pad_maximum_fusion.1 = f32[3,64,8,128]{3,2,1,0:T(8,128)} fusion(f32[1,64,8,128]{3,2,1,0:T(8,128)S(1)} %fusion.6, f32[1,64,8,128]{3,2,1,0:T(8,128)S(1)} %bitcast.219, f32[1,64,8,128]{3,2,1,0:T(8,128)S(1)} %bitcast.220), kind=kLoop, calls=%fused_computation.1 | loop fusion | flops 393216 | bytes 1572864 | tf_op jit(solution)/shard_map/stack | solution.py:359
  (76 shorter events, 3.0 us)
Async XLA Ops:
  2.4 1.0 %slice-start = ((f32[3,64,8,128]{3,2,1,0:T(8,128)}), f32[1,64,8,128]{3,2,1,0:T(8,128)S(1)}, s32[]{:S(2)}) async-start(f32[3,64,8,128]{3,2,1,0:T(8,128)} %h_ref.1), calls=%async_computation | async-start | bytes 524288 | tf_op jit(solution)/shard_map/slice | solution.py:257
  3.7 20.0 %collective-permute-start.3 = (f32[3,64,8,1]{1,2,3,0:T(8,128)S(1)}, f32[3,64,8,1]{1,2,3,0:T(8,128)S(1)}, u32[]{:S(2)}, u32[]{:S(2)}) collective-permute-start(f32[3,64,8,1]{1,2,3,0:T(8,128)S(1)} %pad_maximum_fusion.6), channel_id=1, source_target_pairs={{0,4},{4,8},{8,12},{1,5},{5,9},{9,13},{2,6},{6,10},{10,14},{3,7},{... | collective-permute-start | bytes 18440 | tf_op jit(solution)/shard_map/ppermute | solution.py:14
  7.6 23.3 %collective-permute-start.1 = (f32[3,64,1,128]{3,1,2,0:T(8,128)S(1)}, f32[3,64,1,128]{3,1,2,0:T(8,128)S(1)}, u32[]{:S(2)}, u32[]{:S(2)}) collective-permute-start(f32[3,64,1,128]{3,1,2,0:T(8,128)S(1)} %pad_maximum_fusion.4), channel_id=1, source_target_pairs={{0,16},{16,32},{32,48},{48,64},{64,80},{80,96},{96,112},{112,128},... | collective-permute-start | bytes 294920 | tf_op jit(solution)/shard_map/ppermute | solution.py:14
  12.7 7.8 %copy-start.3 = (s32[64,8,128]{2,1,0:T(8,128)S(1)}, s32[64,8,128]{2,1,0:T(8,128)}, u32[]{:S(2)}) copy-start(s32[64,8,128]{2,1,0:T(8,128)} %param.8) | copy-start | bytes 786436
  12.7 18.1 %collective-permute-start.2 = (f32[2,64,8,1]{3,2,1,0:T(8,128)S(1)}, f32[2,64,8,1]{3,2,1,0:T(8,128)S(1)}, u32[]{:S(2)}, u32[]{:S(2)}) collective-permute-start(f32[2,64,8,1]{3,2,1,0:T(8,128)S(1)} %copy.121), channel_id=1, source_target_pairs={{4,0},{8,4},{12,8},{5,1},{9,5},{13,9},{6,2},{10,6},{14,10},{7,3},{... | collective-permute-start | bytes 12296 | tf_op jit(solution)/shard_map/ppermute | solution.py:19
  14.8 5.6 %copy-start.15 = (s32[64]{0:T(128)S(1)}, s32[64]{0:T(128)}, u32[]{:S(2)}) copy-start(s32[64]{0:T(128)} %param.9) | copy-start | bytes 772
  14.8 16.0 %collective-permute-start = (f32[2,64,1,128]{3,1,2,0:T(8,128)S(1)}, f32[2,64,1,128]{3,1,2,0:T(8,128)S(1)}, u32[]{:S(2)}, u32[]{:S(2)}) collective-permute-start(f32[2,64,1,128]{3,1,2,0:T(8,128)S(1)} %pad_maximum_fusion.5), channel_id=1, source_target_pairs={{16,0},{32,16},{48,32},{64,48},{80,64},{96,80},{112,96},{128,112},... | collective-permute-start | bytes 196616 | tf_op jit(solution)/shard_map/ppermute | solution.py:19
  18.0 12.8 %collective-permute-start.4 = (f32[64,1,1]{2,1,0:T(1,128)S(1)}, f32[64,1,1]{2,1,0:T(1,128)S(1)}, u32[]{:S(2)}, u32[]{:S(2)}) collective-permute-start(f32[64,1,1]{2,1,0:T(1,128)S(1)} %slice.331), channel_id=1, source_target_pairs={{4,16},{8,20},{12,24},{20,32},{24,36},{28,40},{36,48},{40,52},{44,... | collective-permute-start | bytes 776 | tf_op jit(solution)/shard_map/ppermute | solution.py:31
  20.5 0.7 %copy-start.13 = (f32[4,8]{1,0:T(4,128)S(1)}, f32[4,8]{1,0:T(4,128)}, u32[]{:S(2)}) copy-start(f32[4,8]{1,0:T(4,128)} %param.11) | copy-start | bytes 388
  20.5 0.7 %copy-start.14 = (f32[4,8]{1,0:T(4,128)S(1)}, f32[4,8]{1,0:T(4,128)}, u32[]{:S(2)}) copy-start(f32[4,8]{1,0:T(4,128)} %param.10) | copy-start | bytes 388
  23.7 7.1 %collective-permute-start.5 = (f32[64,1,1]{2,1,0:T(1,128)S(1)}, f32[64,1,1]{2,1,0:T(1,128)S(1)}, u32[]{:S(2)}, u32[]{:S(2)}) collective-permute-start(f32[64,1,1]{2,1,0:T(1,128)S(1)} %slice.332), channel_id=1, source_target_pairs={{16,4},{20,8},{24,12},{32,20},{36,24},{40,28},{48,36},{52,40},{56,... | collective-permute-start | bytes 776 | tf_op jit(solution)/shard_map/ppermute | solution.py:31
  30.8 0.6 copy-start.11
  30.8 0.6 copy-start.12
  30.8 0.8 %copy-start.2 = (f32[2,64,8,1]{3,2,1,0:T(8,128)}, f32[2,64,8,1]{3,2,1,0:T(8,128)S(1)}, u32[]{:S(2)}) copy-start(f32[2,64,8,1]{3,2,1,0:T(8,128)S(1)} %collective-permute-done.2.yh_ref) | copy-start | bytes 12292
  30.8 0.8 %copy-start.10 = (f32[2,64,1,128]{3,1,2,0:T(8,128)}, f32[2,64,1,128]{3,1,2,0:T(8,128)S(1)}, u32[]{:S(2)}) copy-start(f32[2,64,1,128]{3,1,2,0:T(8,128)S(1)} %collective-permute-done) | copy-start | bytes 196612
  30.9 0.8 %copy-start.9 = (f32[3,64,1,128]{3,1,2,0:T(8,128)}, f32[3,64,1,128]{3,1,2,0:T(8,128)S(1)}, u32[]{:S(2)}) copy-start(f32[3,64,1,128]{3,1,2,0:T(8,128)S(1)} %collective-permute-done.1) | copy-start | bytes 294916
  37.0 9.3 %copy-start = (f32[3,64,8,128]{3,2,1,0:T(8,128)S(1)}, f32[3,64,8,128]{3,2,1,0:T(8,128)}, u32[]{:S(2)}) copy-start(f32[3,64,8,128]{3,2,1,0:T(8,128)} %e_ref.1) | copy-start | bytes 2359300
  37.0 5.5 %collective-permute-start.6 = (f32[12,8,128]{2,1,0:T(8,128)}, f32[12,8,128]{2,1,0:T(8,128)S(1)}, u32[]{:S(2)}, u32[]{:S(2)}) collective-permute-start(f32[12,8,128]{2,1,0:T(8,128)} %get-tuple-element.11), channel_id=1, source_target_pairs={{0,1},{1,2},{2,3},{3,0},{4,5},{5,6},{6,7},{7,4},{8,9},{9,10},{10,1... | collective-permute-start | bytes 147464 | tf_op jit(solution)/shard_map/ppermute | solution.py:281
  38.3 5.2 %collective-permute-start.7 = (f32[12,8,128]{2,1,0:T(8,128)}, f32[12,8,128]{2,1,0:T(8,128)S(1)}, u32[]{:S(2)}, u32[]{:S(2)}) collective-permute-start(f32[12,8,128]{2,1,0:T(8,128)} %get-tuple-element.11), channel_id=1, source_target_pairs={{0,2},{1,3},{2,0},{3,1},{4,6},{5,7},{6,4},{7,5},{8,10},{9,11},{10,... | collective-permute-start | bytes 147464 | tf_op jit(solution)/shard_map/ppermute | solution.py:281
  40.7 3.8 %collective-permute-start.8 = (f32[12,8,128]{2,1,0:T(8,128)}, f32[12,8,128]{2,1,0:T(8,128)S(1)}, u32[]{:S(2)}, u32[]{:S(2)}) collective-permute-start(f32[12,8,128]{2,1,0:T(8,128)} %get-tuple-element.11), channel_id=1, source_target_pairs={{0,3},{1,0},{2,1},{3,2},{4,7},{5,4},{6,5},{7,6},{8,11},{9,8},{10,9... | collective-permute-start | bytes 147464 | tf_op jit(solution)/shard_map/ppermute | solution.py:281
  46.1 1.0 %copy-start.6 = (f32[64,8,128]{2,1,0:T(8,128)S(1)}, f32[64,8,128]{2,1,0:T(8,128)}, u32[]{:S(2)}) copy-start(f32[64,8,128]{2,1,0:T(8,128)} %get-tuple-element.10) | copy-start | bytes 786436
  46.1 1.0 %copy-start.7 = (f32[64,8,128]{2,1,0:T(8,128)S(1)}, f32[64,8,128]{2,1,0:T(8,128)}, u32[]{:S(2)}) copy-start(f32[64,8,128]{2,1,0:T(8,128)} %get-tuple-element.14) | copy-start | bytes 786436
  47.2 1.3 %copy-start.4 = (f32[64,8,128]{2,1,0:T(8,128)S(1)}, f32[64,8,128]{2,1,0:T(8,128)}, u32[]{:S(2)}) copy-start(f32[64,8,128]{2,1,0:T(8,128)} %get-tuple-element.15) | copy-start | bytes 786436
  47.2 1.3 %copy-start.5 = (f32[64,8,128]{2,1,0:T(8,128)S(1)}, f32[64,8,128]{2,1,0:T(8,128)}, u32[]{:S(2)}) copy-start(f32[64,8,128]{2,1,0:T(8,128)} %get-tuple-element.16) | copy-start | bytes 786436
  48.4 1.1 %copy-start.1 = (f32[3,64,8,128]{3,2,1,0:T(8,128)S(1)}, f32[3,64,8,128]{3,2,1,0:T(8,128)}, u32[]{:S(2)}) copy-start(f32[3,64,8,128]{3,2,1,0:T(8,128)} %h_ref.1) | copy-start | bytes 2359300
  49.6 14.5 %copy-start.8 = (f32[64,8,128]{2,1,0:T(8,128)S(1)}, f32[64,8,128]{2,1,0:T(8,128)}, u32[]{:S(2)}) copy-start(f32[64,8,128]{2,1,0:T(8,128)} %get-tuple-element.17) | copy-start | bytes 786436
  49.8 15.4 %collective-permute-start.10 = (f32[64,8,1]{2,1,0:T(8,128)S(1)}, f32[64,8,1]{2,1,0:T(8,128)S(1)}, u32[]{:S(2)}, u32[]{:S(2)}) collective-permute-start(f32[64,8,1]{2,1,0:T(8,128)S(1)} %slice.341), channel_id=1, source_target_pairs={{0,4},{4,8},{8,12},{1,5},{5,9},{9,13},{2,6},{6,10},{10,14},{3,7},{... | collective-permute-start | bytes 6152 | tf_op jit(solution)/shard_map/ppermute | solution.py:14
  54.7 10.5 %collective-permute-start.9 = (f32[64,1,128]{2,1,0:T(1,128)S(1)}, f32[64,1,128]{2,1,0:T(1,128)S(1)}, u32[]{:S(2)}, u32[]{:S(2)}) collective-permute-start(f32[64,1,128]{2,1,0:T(1,128)S(1)} %slice.338), channel_id=1, source_target_pairs={{0,16},{16,32},{32,48},{48,64},{64,80},{80,96},{96,112},{112,128},... | collective-permute-start | bytes 98312 | tf_op jit(solution)/shard_map/ppermute | solution.py:14

commit v9 on v8

--- a/solution.py
+++ b/solution.py
@@ -79,7 +79,7 @@
         return upper, value_x, value_y, value_low, inv
 
     first = (ur_ref[0], px_ref[0], py_ref[0], lw_ref[0], inv)
-    last_x, last_y, last_low, last_high = lax.fori_loop(1, depth, forward, first, unroll=16)[1:]
+    last_x, last_y, last_low, last_high = lax.fori_loop(1, depth, forward, first, unroll=True)[1:]
     low_scale = stiff_ref[0]
     high_scale = stiff_ref[depth - 1]
     lw_ref[depth - 1] = low_scale * last_low
@@ -99,7 +99,7 @@
         hw_ref[z] = high_scale * next_high
         return next_x, next_y, next_low, next_high
 
-    lax.fori_loop(0, depth - 1, backward, (last_x, last_y, last_low, last_high), unroll=16)
+    lax.fori_loop(0, depth - 1, backward, (last_x, last_y, last_low, last_high), unroll=True)
     edge_ref[0] = px_ref[0]
     edge_ref[1] = py_ref[0]
     edge_ref[2] = px_ref[depth - 1]

time: 67.2 us -> 66.2 us (0.985)
  Pallas kernels: 5.37 us -> 4.33 us
    pallas_call x1, Pallas kernels: 5.37 us -> 4.33 us  [make_sources(): pl.pallas_call(source_kernel, out_shape=(shape,) * 7 + (edges,), in_specs...]
  transfers between devices with their start and end apart: 11 -> 11, of which waited for: 3 -> 3; matrix products, arithmetic and copies ran while one was open for 10% -> 11% of each run, Pallas kernels for 0% -> 0%
where the time goes in v9:
time: 66.2 us; the launch traced here: 65.3 us
  starting transfers between devices  40.4 us (61%)
  local copies, waits for them, and re-layouts  8.9 us (13%)
  other arithmetic  8.45 us (13%)
  Pallas kernels  4.33 us (7%)
  waiting for transfers between devices  2.09 us (3%)
  between operations  1.13 us (2%)
    ppermute x4, starting transfers between devices, from_prev(): return lax.ppermute(block, axis, [(i, i + 1) for i in range(count - 1)])  22.6 us
    ppermute x2, starting transfers between devices, from_diagonal(): return lax.ppermute(block, axes, pairs)  7.67 us
    ppermute x2, starting transfers between devices, from_next(): return lax.ppermute(block, axis, [(i + 1, i) for i in range(count - 1)])  5.21 us
    ppermute x3, starting transfers between devices, body(): lax.ppermute(own, 'gz', [(i, (i + shift) % slab_count) for i in range(sla...  4.89 us
    pallas_call x1, Pallas kernels, make_sources(): pl.pallas_call(source_kernel, out_shape=(shape,) * 7 + (edges,), in_specs...  4.33 us
    unnamed x33, local copies, waits for them, and re-layouts  3.1 us
    another operation x3, other arithmetic, body(): rate_stack = jnp.stack([keep_rate, curl_rate, z_rate, stiffness])  2.31 us
    ppermute x3, waiting for transfers between devices, body(): lax.ppermute(own, 'gz', [(i, (i + shift) % slab_count) for i in range(sla...  2.01 us
  transfers between devices with their start and end apart: 11, of which 3 were waited for; matrix products, arithmetic and copies ran while one was open for 11% of the time, Pallas kernels for 0%

profile of v9, /device:TPU:97, one launch (start us, length us, event | category | flops | bytes accessed | tf_op | source)
XLA Modules:
  0.0 65.3 jit_solution(15551586982848243821)
XLA Ops:
  0.6 1.2 %slice_bitcast_fusion = (f32[64,8,128]{2,1,0:T(8,128)S(1)}, f32[64,8,128]{2,1,0:T(8,128)S(1)}, f32[64,8,128]{2,1,0:T(8,128)S(1)}) fusion(f32[3,64,8,128]{3,2,1,0:T(8,128)} %e_ref.1), kind=kLoop, calls=%fused_computation.21 | loop fusion | bytes 1572864 | tf_op jit(solution)/shard_map/squeeze | solution.py:256
  2.4 1.0 %slice-done = f32[1,64,8,128]{3,2,1,0:T(8,128)S(1)} async-done(((f32[3,64,8,128]{3,2,1,0:T(8,128)}), f32[1,64,8,128]{3,2,1,0:T(8,128)S(1)}, s32[]{:S(2)}) %slice-start) | async-done | bytes 262168 | tf_op jit(solution)/shard_map/slice | solution.py:257
  3.7 3.8 %collective-permute-start.3 = (f32[3,64,8,1]{1,2,3,0:T(8,128)S(1)}, f32[3,64,8,1]{1,2,3,0:T(8,128)S(1)}, u32[]{:S(2)}, u32[]{:S(2)}) collective-permute-start(f32[3,64,8,1]{1,2,3,0:T(8,128)S(1)} %pad_maximum_fusion.6), channel_id=1, source_target_pairs={{0,4},{4,8},{8,12},{1,5},{5,9},{9,13},{2,6},{6,10},{10,14},{3,7},{... | collective-permute-start | bytes 18440 | tf_op jit(solution)/shard_map/ppermute | solution.py:14
  7.6 4.5 %collective-permute-start.1 = (f32[3,64,1,128]{3,1,2,0:T(8,128)S(1)}, f32[3,64,1,128]{3,1,2,0:T(8,128)S(1)}, u32[]{:S(2)}, u32[]{:S(2)}) collective-permute-start(f32[3,64,1,128]{3,1,2,0:T(8,128)S(1)} %pad_maximum_fusion.4), channel_id=1, source_target_pairs={{0,16},{16,32},{32,48},{48,64},{64,80},{80,96},{96,112},{112,128},... | collective-permute-start | bytes 294920 | tf_op jit(solution)/shard_map/ppermute | solution.py:14
  12.4 0.3 copy.121
  12.7 2.1 %collective-permute-start.2 = (f32[2,64,8,1]{3,2,1,0:T(8,128)S(1)}, f32[2,64,8,1]{3,2,1,0:T(8,128)S(1)}, u32[]{:S(2)}, u32[]{:S(2)}) collective-permute-start(f32[2,64,8,1]{3,2,1,0:T(8,128)S(1)} %copy.121), channel_id=1, source_target_pairs={{4,0},{8,4},{12,8},{5,1},{9,5},{13,9},{6,2},{10,6},{14,10},{7,3},{... | collective-permute-start | bytes 12296 | tf_op jit(solution)/shard_map/ppermute | solution.py:19
  14.8 3.2 %collective-permute-start = (f32[2,64,1,128]{3,1,2,0:T(8,128)S(1)}, f32[2,64,1,128]{3,1,2,0:T(8,128)S(1)}, u32[]{:S(2)}, u32[]{:S(2)}) collective-permute-start(f32[2,64,1,128]{3,1,2,0:T(8,128)S(1)} %pad_maximum_fusion.5), channel_id=1, source_target_pairs={{16,0},{32,16},{48,32},{64,48},{80,64},{96,80},{112,96},{128,112},... | collective-permute-start | bytes 196616 | tf_op jit(solution)/shard_map/ppermute | solution.py:19
  18.0 2.4 %collective-permute-start.4 = (f32[64,1,1]{2,1,0:T(1,128)S(1)}, f32[64,1,1]{2,1,0:T(1,128)S(1)}, u32[]{:S(2)}, u32[]{:S(2)}) collective-permute-start(f32[64,1,1]{2,1,0:T(1,128)S(1)} %slice.331), channel_id=1, source_target_pairs={{4,16},{8,20},{12,24},{20,32},{24,36},{28,40},{36,48},{40,52},{44,... | collective-permute-start | bytes 776 | tf_op jit(solution)/shard_map/ppermute | solution.py:31
  20.5 0.3 broadcast_compare_fusion.7
  20.8 0.3 copy-done.13
  21.3 1.2 %fusion.9 = (f32[1,64,8,128]{3,2,1,0:T(8,128)S(1)}, f32[64,8,128]{2,1,0:T(8,128)S(1)}, f32[64,8,128]{2,1,0:T(8,128)S(1)}) fusion(pred[64,8,128]{2,1,0:T(8,128)(4,1)S(1)} %get-tuple-element.85, f32[64]{0:T(128)S(1)} %get-tuple-element.116, pred[64,8,128]{2,1,0:T(8,128)(4,1)S(1)} %get-tuple-element.86, f32[64]{0:T(128)S(1)} %get-tuple-element.115, ...), kind=kLoop, calls=%fused_computation.40 | loop fusion | flops 2359296 | bytes 1314816 | tf_op jit(solution)/shard_map/stack | solution.py:271
  22.5 1.0 %pad_maximum_fusion.rate_ref = f32[4,64,8,128]{3,2,1,0:T(8,128)} fusion(f32[1,64,8,128]{3,2,1,0:T(8,128)S(1)} %get-tuple-element.73, f32[1,64,8,128]{3,2,1,0:T(8,128)S(1)} %get-tuple-element.74, f32[1,64,8,128]{3,2,1,0:T(8,128)S(1)} %get-tuple-element.72, f32[1,64,8,128]{3,2,1,0:T(8,128)S(1)} %get-tuple-element.62), kind=kLoop, calls=%fused_computation | loop fusion | flops 786432 | bytes 2097152 | tf_op jit(solution)/shard_map/stack | solution.py:271
  23.7 5.3 %collective-permute-start.5 = (f32[64,1,1]{2,1,0:T(1,128)S(1)}, f32[64,1,1]{2,1,0:T(1,128)S(1)}, u32[]{:S(2)}, u32[]{:S(2)}) collective-permute-start(f32[64,1,1]{2,1,0:T(1,128)S(1)} %slice.332), channel_id=1, source_target_pairs={{16,4},{20,8},{24,12},{32,20},{36,24},{40,28},{48,36},{52,40},{56,... | collective-permute-start | bytes 776 | tf_op jit(solution)/shard_map/ppermute | solution.py:31
  29.0 0.6 add_convert_fusion.flag_ref
  29.6 1.2 %copy.126.yl_ref = f32[3,64,8,1]{3,2,1,0:T(8,128)} copy(f32[3,64,8,1]{1,2,3,0:T(8,128)S(1)} %collective-permute-done.3) | data formatting | bytes 12288 | tf_op jit(solution)/shard_map/ppermute | solution.py:14
  30.9 0.5 copy-done.11
  31.6 4.3 %shard_map.77 = (f32[64,8,128]{2,1,0:T(8,128)}, f32[64,8,128]{2,1,0:T(8,128)}, f32[64,8,128]{2,1,0:T(8,128)}, f32[64,8,128]{2,1,0:T(8,128)}, f32[64,8,128]{2,1,0...) custom-call(s32[3]{0:T(128)} %add_convert_fusion.flag_ref, ...), custom_call_target="tpu_custom_call" | custom-call | tf_op jit(solution)/shard_map/pallas_call | solution.py:227
  36.0 1.3 %collective-permute-start.6 = (f32[12,8,128]{2,1,0:T(8,128)}, f32[12,8,128]{2,1,0:T(8,128)S(1)}, u32[]{:S(2)}, u32[]{:S(2)}) collective-permute-start(f32[12,8,128]{2,1,0:T(8,128)} %get-tuple-element.11), channel_id=1, source_target_pairs={{0,1},{1,2},{2,3},{3,0},{4,5},{5,6},{6,7},{7,4},{8,9},{9,10},{10,1... | collective-permute-start | bytes 147464 | tf_op jit(solution)/shard_map/ppermute | solution.py:281
  37.3 2.5 %collective-permute-start.7 = (f32[12,8,128]{2,1,0:T(8,128)}, f32[12,8,128]{2,1,0:T(8,128)S(1)}, u32[]{:S(2)}, u32[]{:S(2)}) collective-permute-start(f32[12,8,128]{2,1,0:T(8,128)} %get-tuple-element.11), channel_id=1, source_target_pairs={{0,2},{1,3},{2,0},{3,1},{4,6},{5,7},{6,4},{7,5},{8,10},{9,11},{10,... | collective-permute-start | bytes 147464 | tf_op jit(solution)/shard_map/ppermute | solution.py:281
  39.7 1.2 %collective-permute-start.8 = (f32[12,8,128]{2,1,0:T(8,128)}, f32[12,8,128]{2,1,0:T(8,128)S(1)}, u32[]{:S(2)}, u32[]{:S(2)}) collective-permute-start(f32[12,8,128]{2,1,0:T(8,128)} %get-tuple-element.11), channel_id=1, source_target_pairs={{0,3},{1,0},{2,1},{3,2},{4,7},{5,4},{6,5},{7,6},{8,11},{9,8},{10,9... | collective-permute-start | bytes 147464 | tf_op jit(solution)/shard_map/ppermute | solution.py:281
  40.9 0.6 dynamic-slice.23
  41.5 1.0 %collective-permute-done.7 = f32[12,8,128]{2,1,0:T(8,128)S(1)} collective-permute-done((f32[12,8,128]{2,1,0:T(8,128)}, f32[12,8,128]{2,1,0:T(8,128)S(1)}, u32[]{:S(2)}, u32[]{:S(2)}) %collective-permute-start.7) | collective-permute-done | bytes 49184 | tf_op jit(solution)/shard_map/ppermute | solution.py:281
  42.4 1.0 %collective-permute-done.8 = f32[12,8,128]{2,1,0:T(8,128)S(1)} collective-permute-done((f32[12,8,128]{2,1,0:T(8,128)}, f32[12,8,128]{2,1,0:T(8,128)S(1)}, u32[]{:S(2)}, u32[]{:S(2)}) %collective-permute-start.8) | collective-permute-done | bytes 49184 | tf_op jit(solution)/shard_map/ppermute | solution.py:281
  43.5 0.8 %pad_maximum_fusion.3 = f32[4,12,8,128]{3,2,1,0:T(8,128)S(1)} fusion(f32[1,12,8,128]{3,2,1,0:T(8,128)S(1)} %bitcast.231, f32[1,12,8,128]{3,2,1,0:T(8,128)S(1)} %bitcast.230, f32[1,12,8,128]{3,2,1,0:T(8,128)S(1)} %bitcast.229, f32[1,12,8,128]{3,2,1,0:T(8,128)} %bitcast.228), kind=kLoop, calls=%fused_computation.31 | loop fusion | flops 147456 | bytes 393216 | tf_op jit(solution)/shard_map/stack | solution.py:283
  44.4 0.7 %fusion.65 = f32[8,128]{1,0:T(8,128)S(1)} fusion(s32[]{:T(128)S(6)} %select_n.124, f32[1,8,128]{2,1,0:T(8,128)S(1)} %get-tuple-element.26, f32[1,8,128]{2,1,0:T(8,128)S(1)} %get-tuple-element.25, f32[1,8,128]{2,1,0:T(8,128)S(1)} %get-tuple-element.24, f32[1]{0:T(128)} %dynamic-slice.23), kind=kLoop, calls=%fused_computation.154 | loop fusion | flops 3072 | bytes 16392 | tf_op jit(solution)/shard_map/mul | solution.py:337
  45.3 0.7 %copy-done.6 = f32[64,8,128]{2,1,0:T(8,128)S(1)} copy-done((f32[64,8,128]{2,1,0:T(8,128)S(1)}, f32[64,8,128]{2,1,0:T(8,128)}, u32[]{:S(2)}) %copy-start.6) | copy-done | bytes 262168
  46.1 1.2 %fusion.87 = (f32[64,8,128]{2,1,0:T(8,128)S(1)}, f32[64,8,128]{2,1,0:T(8,128)S(1)}, f32[64,8,128]{2,1,0:T(8,128)S(1)}, f32[64,8,128]{2,1,0:T(8,128)S(1)}) fusion(f32[3,64,8,128]{3,2,1,0:T(8,128)S(1)} %copy-done, f32[64,8,128]{2,1,0:T(8,128)} %get-tuple-element.13, f32[8,128]{1,0:T(8,128)S(1)} %get-tuple-element.90, f32[64,8,128]{2,1,0:T(8,128)S(1)} %copy-done.7, ...), kind=kLoop, calls=%fused_computation.214 | loop fusion | flops 655360 | bytes 2637824 | tf_op jit(solution)/shard_map/add | solution.py:346
  47.4 1.1 %copy-done.1 = f32[3,64,8,128]{3,2,1,0:T(8,128)S(1)} copy-done((f32[3,64,8,128]{3,2,1,0:T(8,128)S(1)}, f32[3,64,8,128]{3,2,1,0:T(8,128)}, u32[]{:S(2)}) %copy-start.1) | copy-done | bytes 786456
  48.8 4.8 %collective-permute-start.10 = (f32[64,8,1]{2,1,0:T(8,128)S(1)}, f32[64,8,1]{2,1,0:T(8,128)S(1)}, u32[]{:S(2)}, u32[]{:S(2)}) collective-permute-start(f32[64,8,1]{2,1,0:T(8,128)S(1)} %slice.341), channel_id=1, source_target_pairs={{0,4},{4,8},{8,12},{1,5},{5,9},{9,13},{2,6},{6,10},{10,14},{3,7},{... | collective-permute-start | bytes 6152 | tf_op jit(solution)/shard_map/ppermute | solution.py:14
  53.6 9.5 %collective-permute-start.9 = (f32[64,1,128]{2,1,0:T(1,128)S(1)}, f32[64,1,128]{2,1,0:T(1,128)S(1)}, u32[]{:S(2)}, u32[]{:S(2)}) collective-permute-start(f32[64,1,128]{2,1,0:T(1,128)S(1)} %slice.338), channel_id=1, source_target_pairs={{0,16},{16,32},{32,48},{48,64},{64,80},{80,96},{96,112},{112,128},... | collective-permute-start | bytes 98312 | tf_op jit(solution)/shard_map/ppermute | solution.py:14
  63.2 0.9 %pad_maximum_fusion.2 = f32[3,64,8,128]{3,2,1,0:T(8,128)} fusion(f32[1,64,8,128]{3,2,1,0:T(8,128)S(1)} %bitcast.221, f32[1,64,8,128]{3,2,1,0:T(8,128)S(1)} %bitcast.214, f32[1,64,8,128]{3,2,1,0:T(8,128)S(1)} %bitcast.212), kind=kLoop, calls=%fused_computation.2 | loop fusion | flops 393216 | bytes 1572864 | tf_op jit(solution)/shard_map/stack | solution.py:360
  64.4 0.9 %pad_maximum_fusion.1 = f32[3,64,8,128]{3,2,1,0:T(8,128)} fusion(f32[1,64,8,128]{3,2,1,0:T(8,128)S(1)} %fusion.6, f32[1,64,8,128]{3,2,1,0:T(8,128)S(1)} %bitcast.219, f32[1,64,8,128]{3,2,1,0:T(8,128)S(1)} %bitcast.220), kind=kLoop, calls=%fused_computation.1 | loop fusion | flops 393216 | bytes 1572864 | tf_op jit(solution)/shard_map/stack | solution.py:359
  (76 shorter events, 3.0 us)
Async XLA Ops:
  2.4 1.0 %slice-start = ((f32[3,64,8,128]{3,2,1,0:T(8,128)}), f32[1,64,8,128]{3,2,1,0:T(8,128)S(1)}, s32[]{:S(2)}) async-start(f32[3,64,8,128]{3,2,1,0:T(8,128)} %h_ref.1), calls=%async_computation | async-start | bytes 524288 | tf_op jit(solution)/shard_map/slice | solution.py:257
  3.7 20.0 %collective-permute-start.3 = (f32[3,64,8,1]{1,2,3,0:T(8,128)S(1)}, f32[3,64,8,1]{1,2,3,0:T(8,128)S(1)}, u32[]{:S(2)}, u32[]{:S(2)}) collective-permute-start(f32[3,64,8,1]{1,2,3,0:T(8,128)S(1)} %pad_maximum_fusion.6), channel_id=1, source_target_pairs={{0,4},{4,8},{8,12},{1,5},{5,9},{9,13},{2,6},{6,10},{10,14},{3,7},{... | collective-permute-start | bytes 18440 | tf_op jit(solution)/shard_map/ppermute | solution.py:14
  7.6 23.3 %collective-permute-start.1 = (f32[3,64,1,128]{3,1,2,0:T(8,128)S(1)}, f32[3,64,1,128]{3,1,2,0:T(8,128)S(1)}, u32[]{:S(2)}, u32[]{:S(2)}) collective-permute-start(f32[3,64,1,128]{3,1,2,0:T(8,128)S(1)} %pad_maximum_fusion.4), channel_id=1, source_target_pairs={{0,16},{16,32},{32,48},{48,64},{64,80},{80,96},{96,112},{112,128},... | collective-permute-start | bytes 294920 | tf_op jit(solution)/shard_map/ppermute | solution.py:14
  12.7 7.8 %copy-start.3 = (s32[64,8,128]{2,1,0:T(8,128)S(1)}, s32[64,8,128]{2,1,0:T(8,128)}, u32[]{:S(2)}) copy-start(s32[64,8,128]{2,1,0:T(8,128)} %param.8) | copy-start | bytes 786436
  12.7 18.1 %collective-permute-start.2 = (f32[2,64,8,1]{3,2,1,0:T(8,128)S(1)}, f32[2,64,8,1]{3,2,1,0:T(8,128)S(1)}, u32[]{:S(2)}, u32[]{:S(2)}) collective-permute-start(f32[2,64,8,1]{3,2,1,0:T(8,128)S(1)} %copy.121), channel_id=1, source_target_pairs={{4,0},{8,4},{12,8},{5,1},{9,5},{13,9},{6,2},{10,6},{14,10},{7,3},{... | collective-permute-start | bytes 12296 | tf_op jit(solution)/shard_map/ppermute | solution.py:19
  14.8 5.6 %copy-start.15 = (s32[64]{0:T(128)S(1)}, s32[64]{0:T(128)}, u32[]{:S(2)}) copy-start(s32[64]{0:T(128)} %param.9) | copy-start | bytes 772
  14.8 16.0 %collective-permute-start = (f32[2,64,1,128]{3,1,2,0:T(8,128)S(1)}, f32[2,64,1,128]{3,1,2,0:T(8,128)S(1)}, u32[]{:S(2)}, u32[]{:S(2)}) collective-permute-start(f32[2,64,1,128]{3,1,2,0:T(8,128)S(1)} %pad_maximum_fusion.5), channel_id=1, source_target_pairs={{16,0},{32,16},{48,32},{64,48},{80,64},{96,80},{112,96},{128,112},... | collective-permute-start | bytes 196616 | tf_op jit(solution)/shard_map/ppermute | solution.py:19
  18.0 12.8 %collective-permute-start.4 = (f32[64,1,1]{2,1,0:T(1,128)S(1)}, f32[64,1,1]{2,1,0:T(1,128)S(1)}, u32[]{:S(2)}, u32[]{:S(2)}) collective-permute-start(f32[64,1,1]{2,1,0:T(1,128)S(1)} %slice.331), channel_id=1, source_target_pairs={{4,16},{8,20},{12,24},{20,32},{24,36},{28,40},{36,48},{40,52},{44,... | collective-permute-start | bytes 776 | tf_op jit(solution)/shard_map/ppermute | solution.py:31
  20.5 0.7 %copy-start.13 = (f32[4,8]{1,0:T(4,128)S(1)}, f32[4,8]{1,0:T(4,128)}, u32[]{:S(2)}) copy-start(f32[4,8]{1,0:T(4,128)} %param.11) | copy-start | bytes 388
  20.5 0.7 %copy-start.14 = (f32[4,8]{1,0:T(4,128)S(1)}, f32[4,8]{1,0:T(4,128)}, u32[]{:S(2)}) copy-start(f32[4,8]{1,0:T(4,128)} %param.10) | copy-start | bytes 388
  23.7 7.1 %collective-permute-start.5 = (f32[64,1,1]{2,1,0:T(1,128)S(1)}, f32[64,1,1]{2,1,0:T(1,128)S(1)}, u32[]{:S(2)}, u32[]{:S(2)}) collective-permute-start(f32[64,1,1]{2,1,0:T(1,128)S(1)} %slice.332), channel_id=1, source_target_pairs={{16,4},{20,8},{24,12},{32,20},{36,24},{40,28},{48,36},{52,40},{56,... | collective-permute-start | bytes 776 | tf_op jit(solution)/shard_map/ppermute | solution.py:31
  30.8 0.6 copy-start.11
  30.8 0.6 copy-start.12
  30.8 0.8 %copy-start.2 = (f32[2,64,8,1]{3,2,1,0:T(8,128)}, f32[2,64,8,1]{3,2,1,0:T(8,128)S(1)}, u32[]{:S(2)}) copy-start(f32[2,64,8,1]{3,2,1,0:T(8,128)S(1)} %collective-permute-done.2.yh_ref) | copy-start | bytes 12292
  30.8 0.8 %copy-start.10 = (f32[2,64,1,128]{3,1,2,0:T(8,128)}, f32[2,64,1,128]{3,1,2,0:T(8,128)S(1)}, u32[]{:S(2)}) copy-start(f32[2,64,1,128]{3,1,2,0:T(8,128)S(1)} %collective-permute-done) | copy-start | bytes 196612
  30.9 0.8 %copy-start.9 = (f32[3,64,1,128]{3,1,2,0:T(8,128)}, f32[3,64,1,128]{3,1,2,0:T(8,128)S(1)}, u32[]{:S(2)}) copy-start(f32[3,64,1,128]{3,1,2,0:T(8,128)S(1)} %collective-permute-done.1) | copy-start | bytes 294916
  36.0 9.3 %copy-start = (f32[3,64,8,128]{3,2,1,0:T(8,128)S(1)}, f32[3,64,8,128]{3,2,1,0:T(8,128)}, u32[]{:S(2)}) copy-start(f32[3,64,8,128]{3,2,1,0:T(8,128)} %e_ref.1) | copy-start | bytes 2359300
  36.0 5.5 %collective-permute-start.6 = (f32[12,8,128]{2,1,0:T(8,128)}, f32[12,8,128]{2,1,0:T(8,128)S(1)}, u32[]{:S(2)}, u32[]{:S(2)}) collective-permute-start(f32[12,8,128]{2,1,0:T(8,128)} %get-tuple-element.11), channel_id=1, source_target_pairs={{0,1},{1,2},{2,3},{3,0},{4,5},{5,6},{6,7},{7,4},{8,9},{9,10},{10,1... | collective-permute-start | bytes 147464 | tf_op jit(solution)/shard_map/ppermute | solution.py:281
  37.3 5.2 %collective-permute-start.7 = (f32[12,8,128]{2,1,0:T(8,128)}, f32[12,8,128]{2,1,0:T(8,128)S(1)}, u32[]{:S(2)}, u32[]{:S(2)}) collective-permute-start(f32[12,8,128]{2,1,0:T(8,128)} %get-tuple-element.11), channel_id=1, source_target_pairs={{0,2},{1,3},{2,0},{3,1},{4,6},{5,7},{6,4},{7,5},{8,10},{9,11},{10,... | collective-permute-start | bytes 147464 | tf_op jit(solution)/shard_map/ppermute | solution.py:281
  39.7 3.8 %collective-permute-start.8 = (f32[12,8,128]{2,1,0:T(8,128)}, f32[12,8,128]{2,1,0:T(8,128)S(1)}, u32[]{:S(2)}, u32[]{:S(2)}) collective-permute-start(f32[12,8,128]{2,1,0:T(8,128)} %get-tuple-element.11), channel_id=1, source_target_pairs={{0,3},{1,0},{2,1},{3,2},{4,7},{5,4},{6,5},{7,6},{8,11},{9,8},{10,9... | collective-permute-start | bytes 147464 | tf_op jit(solution)/shard_map/ppermute | solution.py:281
  45.1 1.0 %copy-start.6 = (f32[64,8,128]{2,1,0:T(8,128)S(1)}, f32[64,8,128]{2,1,0:T(8,128)}, u32[]{:S(2)}) copy-start(f32[64,8,128]{2,1,0:T(8,128)} %get-tuple-element.10) | copy-start | bytes 786436
  45.1 1.0 %copy-start.7 = (f32[64,8,128]{2,1,0:T(8,128)S(1)}, f32[64,8,128]{2,1,0:T(8,128)}, u32[]{:S(2)}) copy-start(f32[64,8,128]{2,1,0:T(8,128)} %get-tuple-element.14) | copy-start | bytes 786436
  46.1 1.3 %copy-start.4 = (f32[64,8,128]{2,1,0:T(8,128)S(1)}, f32[64,8,128]{2,1,0:T(8,128)}, u32[]{:S(2)}) copy-start(f32[64,8,128]{2,1,0:T(8,128)} %get-tuple-element.15) | copy-start | bytes 786436
  46.1 1.3 %copy-start.5 = (f32[64,8,128]{2,1,0:T(8,128)S(1)}, f32[64,8,128]{2,1,0:T(8,128)}, u32[]{:S(2)}) copy-start(f32[64,8,128]{2,1,0:T(8,128)} %get-tuple-element.16) | copy-start | bytes 786436
  47.3 1.1 %copy-start.1 = (f32[3,64,8,128]{3,2,1,0:T(8,128)S(1)}, f32[3,64,8,128]{3,2,1,0:T(8,128)}, u32[]{:S(2)}) copy-start(f32[3,64,8,128]{3,2,1,0:T(8,128)} %h_ref.1) | copy-start | bytes 2359300
  48.6 14.5 %copy-start.8 = (f32[64,8,128]{2,1,0:T(8,128)S(1)}, f32[64,8,128]{2,1,0:T(8,128)}, u32[]{:S(2)}) copy-start(f32[64,8,128]{2,1,0:T(8,128)} %get-tuple-element.17) | copy-start | bytes 786436
  48.8 15.4 %collective-permute-start.10 = (f32[64,8,1]{2,1,0:T(8,128)S(1)}, f32[64,8,1]{2,1,0:T(8,128)S(1)}, u32[]{:S(2)}, u32[]{:S(2)}) collective-permute-start(f32[64,8,1]{2,1,0:T(8,128)S(1)} %slice.341), channel_id=1, source_target_pairs={{0,4},{4,8},{8,12},{1,5},{5,9},{9,13},{2,6},{6,10},{10,14},{3,7},{... | collective-permute-start | bytes 6152 | tf_op jit(solution)/shard_map/ppermute | solution.py:14
  53.6 10.5 %collective-permute-start.9 = (f32[64,1,128]{2,1,0:T(1,128)S(1)}, f32[64,1,128]{2,1,0:T(1,128)S(1)}, u32[]{:S(2)}, u32[]{:S(2)}) collective-permute-start(f32[64,1,128]{2,1,0:T(1,128)S(1)} %slice.338), channel_id=1, source_target_pairs={{0,16},{16,32},{32,48},{48,64},{64,80},{80,96},{96,112},{112,128},... | collective-permute-start | bytes 98312 | tf_op jit(solution)/shard_map/ppermute | solution.py:14

commit v10 on v9

--- a/solution.py
+++ b/solution.py
@@ -336,22 +336,30 @@
 
     previous_last = incoming + factor[None] * leading + below
     following = following + above
-    electric_x_new = (
-        partial_x + previous_last[0][None] * low_weight + following[0][None] * high_weight
-    )
-    electric_y_new = (
-        partial_y + previous_last[1][None] * low_weight + following[1][None] * high_weight
-    )
-    sum_x = electric_x + electric_x_new
-    sum_y = electric_y + electric_y_new
-    top_x = following[0]
-    top_y = following[1]
-    rise_x = jnp.concatenate([sum_x[1:], top_x[None]], axis=0) - sum_x
-    rise_y = jnp.concatenate([sum_y[1:], top_y[None]], axis=0) - sum_y
-    magnetic_y_new = magnetic_y - 0.5 * z_courant * rise_x + time_step * slope_zx
-    magnetic_x_new = magnetic_x - time_step * slope_zy + 0.5 * z_courant * rise_y
-    before_hy = from_prev(magnetic_y_new[:, -1:, :], "gx")
-    before_hx = from_prev(magnetic_x_new[:, :, -1:], "gy")
+    def updated(sel):
+        row_sel = sel[1:]
+        new_x = (
+            partial_x[sel]
+            + previous_last[0][row_sel][None] * low_weight[sel]
+            + following[0][row_sel][None] * high_weight[sel]
+        )
+        new_y = (
+            partial_y[sel]
+            + previous_last[1][row_sel][None] * low_weight[sel]
+            + following[1][row_sel][None] * high_weight[sel]
+        )
+        sum_x = electric_x[sel] + new_x
+        sum_y = electric_y[sel] + new_y
+        rise_x = jnp.concatenate([sum_x[1:], following[0][row_sel][None]], axis=0) - sum_x
+        rise_y = jnp.concatenate([sum_y[1:], following[1][row_sel][None]], axis=0) - sum_y
+        new_hy = magnetic_y[sel] - 0.5 * z_courant * rise_x + time_step * slope_zx[sel]
+        new_hx = magnetic_x[sel] - time_step * slope_zy[sel] + 0.5 * z_courant * rise_y
+        return new_x, new_y, new_hx, new_hy
+
+    every = slice(None)
+    before_hy = from_prev(updated((every, slice(-1, None), every))[3], "gx")
+    before_hx = from_prev(updated((every, every, slice(-1, None)))[2], "gy")
+    electric_x_new, electric_y_new, magnetic_x_new, magnetic_y_new = updated((every,) * 3)
     change_hy = magnetic_y_new - jnp.concatenate([before_hy, magnetic_y_new[:, :-1]], axis=1)
     change_hx = magnetic_x_new - jnp.concatenate([before_hx, magnetic_x_new[:, :, :-1]], axis=2)
     electric_z_new = keep_rate * electric_z + curl_rate * (change_hy - change_hx)

time: 66.2 us -> 69 us (1.042)
  other arithmetic: 8.45 us -> 10.1 us
  local copies, waits for them, and re-layouts: 8.9 us -> 10.1 us
    unnamed x33 -> x37, local copies, waits for them, and re-layouts: 3.1 us -> 5.02 us
    add x2 -> x6, other arithmetic: 1.35 us -> 2.98 us  [the longest x2 1.47 us: updated(): sum_y = electric_y[sel] + new_y]
    slice x7, local copies, waits for them, and re-layouts: 1.17 us -> 0.25 us  [the longest x1 0.18 us: updated(): previous_last[1][row_sel][None] * low_weight[sel]]
  transfers between devices with their start and end apart: 11 -> 11, of which waited for: 3 -> 2; matrix products, arithmetic and copies ran while one was open for 11% -> 12% of each run, Pallas kernels for 0% -> 0%
where the time goes in v10:
time: 69 us; the launch traced here: 68.3 us
  starting transfers between devices  40.5 us (59%)
  local copies, waits for them, and re-layouts  10.1 us (15%)
  other arithmetic  10.1 us (15%)
  Pallas kernels  4.35 us (6%)
  waiting for transfers between devices  2.03 us (3%)
  between operations  1.18 us (2%)
    ppermute x4, starting transfers between devices, from_prev(): return lax.ppermute(block, axis, [(i, i + 1) for i in range(count - 1)])  22.7 us
    ppermute x2, starting transfers between devices, from_diagonal(): return lax.ppermute(block, axes, pairs)  7.67 us
    ppermute x2, starting transfers between devices, from_next(): return lax.ppermute(block, axis, [(i + 1, i) for i in range(count - 1)])  5.21 us
    unnamed x37, local copies, waits for them, and re-layouts  5.02 us
    ppermute x3, starting transfers between devices, body(): lax.ppermute(own, 'gz', [(i, (i + shift) % slab_count) for i in range(sla...  4.88 us
    pallas_call x1, Pallas kernels, make_sources(): pl.pallas_call(source_kernel, out_shape=(shape,) * 7 + (edges,), in_specs...  4.35 us
    another operation x3, other arithmetic, body(): rate_stack = jnp.stack([keep_rate, curl_rate, z_rate, stiffness])  2.3 us
    ppermute x3, waiting for transfers between devices, body(): lax.ppermute(own, 'gz', [(i, (i + shift) % slab_count) for i in range(sla...  2.01 us
  transfers between devices with their start and end apart: 11, of which 2 were waited for; matrix products, arithmetic and copies ran while one was open for 12% of the time, Pallas kernels for 0%

profile of v10, /device:TPU:97, one launch (start us, length us, event | category | flops | bytes accessed | tf_op | source)
XLA Modules:
  0.0 68.3 jit_solution(13869506603510391522)
XLA Ops:
  0.6 1.2 %slice_bitcast_fusion.2 = (f32[64,8,128]{2,1,0:T(8,128)S(1)}, f32[64,8,128]{2,1,0:T(8,128)S(1)}, f32[64,8,128]{2,1,0:T(8,128)S(1)}) fusion(f32[3,64,8,128]{3,2,1,0:T(8,128)} %e_ref.1), kind=kLoop, calls=%fused_computation.27 | loop fusion | bytes 1572864 | tf_op jit(solution)/shard_map/squeeze | solution.py:256
  2.4 0.7 %copy-done.1 = f32[3,64,8,128]{3,2,1,0:T(8,128)S(1)} copy-done((f32[3,64,8,128]{3,2,1,0:T(8,128)S(1)}, f32[3,64,8,128]{3,2,1,0:T(8,128)}, u32[]{:S(2)}) %copy-start.1) | copy-done | bytes 786456
  3.5 3.8 %collective-permute-start.3 = (f32[3,64,8,1]{1,2,3,0:T(8,128)S(1)}, f32[3,64,8,1]{1,2,3,0:T(8,128)S(1)}, u32[]{:S(2)}, u32[]{:S(2)}) collective-permute-start(f32[3,64,8,1]{1,2,3,0:T(8,128)S(1)} %pad_maximum_fusion.6), channel_id=1, source_target_pairs={{0,4},{4,8},{8,12},{1,5},{5,9},{9,13},{2,6},{6,10},{10,14},{3,7},{... | collective-permute-start | bytes 18440 | tf_op jit(solution)/shard_map/ppermute | solution.py:14
  7.4 4.5 %collective-permute-start.1 = (f32[3,64,1,128]{3,1,2,0:T(8,128)S(1)}, f32[3,64,1,128]{3,1,2,0:T(8,128)S(1)}, u32[]{:S(2)}, u32[]{:S(2)}) collective-permute-start(f32[3,64,1,128]{3,1,2,0:T(8,128)S(1)} %pad_maximum_fusion.4), channel_id=1, source_target_pairs={{0,16},{16,32},{32,48},{48,64},{64,80},{80,96},{96,112},{112,128},... | collective-permute-start | bytes 294920 | tf_op jit(solution)/shard_map/ppermute | solution.py:14
  12.5 2.1 %collective-permute-start.2 = (f32[2,64,8,1]{3,2,1,0:T(8,128)S(1)}, f32[2,64,8,1]{3,2,1,0:T(8,128)S(1)}, u32[]{:S(2)}, u32[]{:S(2)}) collective-permute-start(f32[2,64,8,1]{3,2,1,0:T(8,128)S(1)} %copy.238), channel_id=1, source_target_pairs={{4,0},{8,4},{12,8},{5,1},{9,5},{13,9},{6,2},{10,6},{14,10},{7,3},{... | collective-permute-start | bytes 12296 | tf_op jit(solution)/shard_map/ppermute | solution.py:19
  14.6 3.2 %collective-permute-start = (f32[2,64,1,128]{3,1,2,0:T(8,128)S(1)}, f32[2,64,1,128]{3,1,2,0:T(8,128)S(1)}, u32[]{:S(2)}, u32[]{:S(2)}) collective-permute-start(f32[2,64,1,128]{3,1,2,0:T(8,128)S(1)} %pad_maximum_fusion.5), channel_id=1, source_target_pairs={{16,0},{32,16},{48,32},{64,48},{80,64},{96,80},{112,96},{128,112},... | collective-permute-start | bytes 196616 | tf_op jit(solution)/shard_map/ppermute | solution.py:19
  17.8 2.4 %collective-permute-start.4 = (f32[64,1,1]{2,1,0:T(1,128)S(1)}, f32[64,1,1]{2,1,0:T(1,128)S(1)}, u32[]{:S(2)}, u32[]{:S(2)}) collective-permute-start(f32[64,1,1]{2,1,0:T(1,128)S(1)} %slice.401), channel_id=1, source_target_pairs={{4,16},{8,20},{12,24},{20,32},{24,36},{28,40},{36,48},{40,52},{44,... | collective-permute-start | bytes 776 | tf_op jit(solution)/shard_map/ppermute | solution.py:31
  21.0 1.2 %fusion.11 = (f32[1,64,8,128]{3,2,1,0:T(8,128)S(1)}, f32[64,8,128]{2,1,0:T(8,128)S(1)}, f32[64,8,128]{2,1,0:T(8,128)S(1)}) fusion(pred[64,8,128]{2,1,0:T(8,128)(4,1)S(1)} %get-tuple-element.88, f32[64]{0:T(128)S(1)} %get-tuple-element.123, pred[64,8,128]{2,1,0:T(8,128)(4,1)S(1)} %get-tuple-element.89, f32[64]{0:T(128)S(1)} %get-tuple-element.122, ...), kind=kLoop, calls=%fused_computation.46 | loop fusion | flops 2359296 | bytes 1314816 | tf_op jit(solution)/shard_map/stack | solution.py:271
  22.3 1.0 %pad_maximum_fusion.rate_ref = f32[4,64,8,128]{3,2,1,0:T(8,128)} fusion(f32[1,64,8,128]{3,2,1,0:T(8,128)S(1)} %get-tuple-element.76, f32[1,64,8,128]{3,2,1,0:T(8,128)S(1)} %get-tuple-element.77, f32[1,64,8,128]{3,2,1,0:T(8,128)S(1)} %get-tuple-element.75, f32[1,64,8,128]{3,2,1,0:T(8,128)S(1)} %get-tuple-element.62), kind=kLoop, calls=%fused_computation | loop fusion | flops 786432 | bytes 2097152 | tf_op jit(solution)/shard_map/stack | solution.py:271
  23.5 5.3 %collective-permute-start.5 = (f32[64,1,1]{2,1,0:T(1,128)S(1)}, f32[64,1,1]{2,1,0:T(1,128)S(1)}, u32[]{:S(2)}, u32[]{:S(2)}) collective-permute-start(f32[64,1,1]{2,1,0:T(1,128)S(1)} %slice.402), channel_id=1, source_target_pairs={{16,4},{20,8},{24,12},{32,20},{36,24},{40,28},{48,36},{52,40},{56,... | collective-permute-start | bytes 776 | tf_op jit(solution)/shard_map/ppermute | solution.py:31
  28.8 0.6 add_convert_fusion.flag_ref
  29.4 1.2 %copy.243.yl_ref = f32[3,64,8,1]{3,2,1,0:T(8,128)} copy(f32[3,64,8,1]{1,2,3,0:T(8,128)S(1)} %collective-permute-done.3) | data formatting | bytes 12288 | tf_op jit(solution)/shard_map/ppermute | solution.py:14
  30.7 0.5 copy-done.13
  31.5 4.4 %shard_map.77 = (f32[64,8,128]{2,1,0:T(8,128)}, f32[64,8,128]{2,1,0:T(8,128)}, f32[64,8,128]{2,1,0:T(8,128)}, f32[64,8,128]{2,1,0:T(8,128)}, f32[64,8,128]{2,1,0...) custom-call(s32[3]{0:T(128)} %add_convert_fusion.flag_ref, ...), custom_call_target="tpu_custom_call" | custom-call | tf_op jit(solution)/shard_map/pallas_call | solution.py:227
  35.8 1.3 %collective-permute-start.6 = (f32[12,8,128]{2,1,0:T(8,128)}, f32[12,8,128]{2,1,0:T(8,128)S(1)}, u32[]{:S(2)}, u32[]{:S(2)}) collective-permute-start(f32[12,8,128]{2,1,0:T(8,128)} %get-tuple-element.11), channel_id=1, source_target_pairs={{0,1},{1,2},{2,3},{3,0},{4,5},{5,6},{6,7},{7,4},{8,9},{9,10},{10,1... | collective-permute-start | bytes 147464 | tf_op jit(solution)/shard_map/ppermute | solution.py:281
  37.1 2.5 %collective-permute-start.7 = (f32[12,8,128]{2,1,0:T(8,128)}, f32[12,8,128]{2,1,0:T(8,128)S(1)}, u32[]{:S(2)}, u32[]{:S(2)}) collective-permute-start(f32[12,8,128]{2,1,0:T(8,128)} %get-tuple-element.11), channel_id=1, source_target_pairs={{0,2},{1,3},{2,0},{3,1},{4,6},{5,7},{6,4},{7,5},{8,10},{9,11},{10,... | collective-permute-start | bytes 147464 | tf_op jit(solution)/shard_map/ppermute | solution.py:281
  39.6 1.2 %collective-permute-start.8 = (f32[12,8,128]{2,1,0:T(8,128)}, f32[12,8,128]{2,1,0:T(8,128)S(1)}, u32[]{:S(2)}, u32[]{:S(2)}) collective-permute-start(f32[12,8,128]{2,1,0:T(8,128)} %get-tuple-element.11), channel_id=1, source_target_pairs={{0,3},{1,0},{2,1},{3,2},{4,7},{5,4},{6,5},{7,6},{8,11},{9,8},{10,9... | collective-permute-start | bytes 147464 | tf_op jit(solution)/shard_map/ppermute | solution.py:281
  40.7 0.6 dynamic-slice.23
  41.3 1.0 %collective-permute-done.7 = f32[12,8,128]{2,1,0:T(8,128)S(1)} collective-permute-done((f32[12,8,128]{2,1,0:T(8,128)}, f32[12,8,128]{2,1,0:T(8,128)S(1)}, u32[]{:S(2)}, u32[]{:S(2)}) %collective-permute-start.7) | collective-permute-done | bytes 49184 | tf_op jit(solution)/shard_map/ppermute | solution.py:281
  42.3 1.0 %collective-permute-done.8 = f32[12,8,128]{2,1,0:T(8,128)S(1)} collective-permute-done((f32[12,8,128]{2,1,0:T(8,128)}, f32[12,8,128]{2,1,0:T(8,128)S(1)}, u32[]{:S(2)}, u32[]{:S(2)}) %collective-permute-start.8) | collective-permute-done | bytes 49184 | tf_op jit(solution)/shard_map/ppermute | solution.py:281
  43.3 0.8 %pad_maximum_fusion.3 = f32[4,12,8,128]{3,2,1,0:T(8,128)S(1)} fusion(f32[1,12,8,128]{3,2,1,0:T(8,128)S(1)} %bitcast.240, f32[1,12,8,128]{3,2,1,0:T(8,128)S(1)} %bitcast.239, f32[1,12,8,128]{3,2,1,0:T(8,128)S(1)} %bitcast.238, f32[1,12,8,128]{3,2,1,0:T(8,128)} %bitcast.237), kind=kLoop, calls=%fused_computation.37 | loop fusion | flops 147456 | bytes 393216 | tf_op jit(solution)/shard_map/stack | solution.py:283
  44.3 0.7 fusion.69
  45.6 0.4 copy-done.3
  46.0 1.1 %fusion.91 = (f32[64,8,128]{2,1,0:T(8,128)S(1)}, f32[64,8,128]{2,1,0:T(8,128)S(1)}, f32[64,8,128]{2,1,0:T(8,128)S(1)}, f32[64,8,128]{2,1,0:T(8,128)S(1)}) fusion(f32[3,64,8,128]{3,2,1,0:T(8,128)S(1)} %copy-done, f32[64,8,128]{2,1,0:T(8,128)S(1)} %copy-done.4, f32[8,128]{1,0:T(8,128)S(1)} %get-tuple-element.93, f32[64,8,128]{2,1,0:T(8,128)} %get-tuple-element.14, ...), kind=kLoop, calls=%fused_computation.230 | loop fusion | flops 655360 | bytes 2637824 | tf_op jit(solution)/shard_map/add | solution.py:352
  47.2 0.9 %copy-done.6 = f32[64,8,128]{2,1,0:T(8,128)S(1)} copy-done((f32[64,8,128]{2,1,0:T(8,128)S(1)}, f32[64,8,128]{2,1,0:T(8,128)}, u32[]{:S(2)}) %copy-start.6) | copy-done | bytes 262168
  48.5 0.9 %copy-done.5 = f32[64,8,128]{2,1,0:T(8,128)S(1)} copy-done((f32[64,8,128]{2,1,0:T(8,128)S(1)}, f32[64,8,128]{2,1,0:T(8,128)}, u32[]{:S(2)}) %copy-start.5) | copy-done | bytes 262168
  49.6 5.0 %collective-permute-start.10 = (f32[64,8,1]{2,1,0:T(8,128)S(1)}, f32[64,8,1]{2,1,0:T(8,128)S(1)}, u32[]{:S(2)}, u32[]{:S(2)}) collective-permute-start(f32[64,8,1]{2,1,0:T(8,128)S(1)} %fusion), channel_id=1, source_target_pairs={{0,4},{4,8},{8,12},{1,5},{5,9},{9,13},{2,6},{6,10},{10,14},{3,7},{... | collective-permute-start | bytes 6152 | tf_op jit(solution)/shard_map/ppermute | solution.py:14
  54.6 1.1 %add_add_fusion.1 = f32[64,1,128]{2,1,0:T(1,128)S(1)} fusion(f32[64,8,128]{2,1,0:T(8,128)S(1)} %copy-done.4, f32[64,8,128]{2,1,0:T(8,128)S(1)} %copy-done.3, f32[64,8,128]{2,1,0:T(8,128)} %get-tuple-element.10, f32[128]{0:T(128)S(1)} %get-tuple-element.98, f32[128]{0:T(128)S(1)} %slice_bitcast_fusion.13, f32[64,8,128]{2,1,0:T(8,128)S(1)} %get-tuple-element.72), kind=kLoop, calls=%fused_computation.72 | loop fusion | flops 40960 | bytes 164864 | tf_op jit(solution)/shard_map/add | solution.py:351
  55.8 9.5 %collective-permute-start.9 = (f32[64,1,128]{2,1,0:T(1,128)S(1)}, f32[64,1,128]{2,1,0:T(1,128)S(1)}, u32[]{:S(2)}, u32[]{:S(2)}) collective-permute-start(f32[64,1,128]{2,1,0:T(1,128)S(1)} %fusion.12), channel_id=1, source_target_pairs={{0,16},{16,32},{32,48},{48,64},{64,80},{80,96},{96,112},{112,128},... | collective-permute-start | bytes 98312 | tf_op jit(solution)/shard_map/ppermute | solution.py:14
  65.4 0.8 %copy-done.10 = f32[64,8,128]{2,1,0:T(8,128)S(1)} copy-done((f32[64,8,128]{2,1,0:T(8,128)S(1)}, f32[64,8,128]{2,1,0:T(8,128)}, u32[]{:S(2)}) %copy-start.10) | copy-done | bytes 262168
  66.2 0.9 %pad_maximum_fusion.2 = f32[3,64,8,128]{3,2,1,0:T(8,128)} fusion(f32[1,64,8,128]{3,2,1,0:T(8,128)S(1)} %bitcast.230, f32[1,64,8,128]{3,2,1,0:T(8,128)S(1)} %bitcast.223, f32[1,64,8,128]{3,2,1,0:T(8,128)S(1)} %bitcast.221), kind=kLoop, calls=%fused_computation.2 | loop fusion | flops 393216 | bytes 1572864 | tf_op jit(solution)/shard_map/stack | solution.py:368
  67.4 0.9 %pad_maximum_fusion.1 = f32[3,64,8,128]{3,2,1,0:T(8,128)} fusion(f32[1,64,8,128]{3,2,1,0:T(8,128)S(1)} %fusion.7, f32[1,64,8,128]{3,2,1,0:T(8,128)S(1)} %bitcast.228, f32[1,64,8,128]{3,2,1,0:T(8,128)S(1)} %bitcast.229), kind=kLoop, calls=%fused_computation.1 | loop fusion | flops 393216 | bytes 1572864 | tf_op jit(solution)/shard_map/stack | solution.py:367
  (87 shorter events, 4.8 us)
Async XLA Ops:
  1.9 1.1 %copy-start.1 = (f32[3,64,8,128]{3,2,1,0:T(8,128)S(1)}, f32[3,64,8,128]{3,2,1,0:T(8,128)}, u32[]{:S(2)}) copy-start(f32[3,64,8,128]{3,2,1,0:T(8,128)} %h_ref.1) | copy-start | bytes 2359300
  3.5 20.0 %collective-permute-start.3 = (f32[3,64,8,1]{1,2,3,0:T(8,128)S(1)}, f32[3,64,8,1]{1,2,3,0:T(8,128)S(1)}, u32[]{:S(2)}, u32[]{:S(2)}) collective-permute-start(f32[3,64,8,1]{1,2,3,0:T(8,128)S(1)} %pad_maximum_fusion.6), channel_id=1, source_target_pairs={{0,4},{4,8},{8,12},{1,5},{5,9},{9,13},{2,6},{6,10},{10,14},{3,7},{... | collective-permute-start | bytes 18440 | tf_op jit(solution)/shard_map/ppermute | solution.py:14
  7.4 23.3 %collective-permute-start.1 = (f32[3,64,1,128]{3,1,2,0:T(8,128)S(1)}, f32[3,64,1,128]{3,1,2,0:T(8,128)S(1)}, u32[]{:S(2)}, u32[]{:S(2)}) collective-permute-start(f32[3,64,1,128]{3,1,2,0:T(8,128)S(1)} %pad_maximum_fusion.4), channel_id=1, source_target_pairs={{0,16},{16,32},{32,48},{48,64},{64,80},{80,96},{96,112},{112,128},... | collective-permute-start | bytes 294920 | tf_op jit(solution)/shard_map/ppermute | solution.py:14
  12.5 7.8 %copy-start.9 = (s32[64,8,128]{2,1,0:T(8,128)S(1)}, s32[64,8,128]{2,1,0:T(8,128)}, u32[]{:S(2)}) copy-start(s32[64,8,128]{2,1,0:T(8,128)} %param.8) | copy-start | bytes 786436
  12.5 18.1 %collective-permute-start.2 = (f32[2,64,8,1]{3,2,1,0:T(8,128)S(1)}, f32[2,64,8,1]{3,2,1,0:T(8,128)S(1)}, u32[]{:S(2)}, u32[]{:S(2)}) collective-permute-start(f32[2,64,8,1]{3,2,1,0:T(8,128)S(1)} %copy.238), channel_id=1, source_target_pairs={{4,0},{8,4},{12,8},{5,1},{9,5},{13,9},{6,2},{10,6},{14,10},{7,3},{... | collective-permute-start | bytes 12296 | tf_op jit(solution)/shard_map/ppermute | solution.py:19
  14.6 5.6 %copy-start.17 = (s32[64]{0:T(128)S(1)}, s32[64]{0:T(128)}, u32[]{:S(2)}) copy-start(s32[64]{0:T(128)} %param.9) | copy-start | bytes 772
  14.6 16.0 %collective-permute-start = (f32[2,64,1,128]{3,1,2,0:T(8,128)S(1)}, f32[2,64,1,128]{3,1,2,0:T(8,128)S(1)}, u32[]{:S(2)}, u32[]{:S(2)}) collective-permute-start(f32[2,64,1,128]{3,1,2,0:T(8,128)S(1)} %pad_maximum_fusion.5), channel_id=1, source_target_pairs={{16,0},{32,16},{48,32},{64,48},{80,64},{96,80},{112,96},{128,112},... | collective-permute-start | bytes 196616 | tf_op jit(solution)/shard_map/ppermute | solution.py:19
  17.8 12.8 %collective-permute-start.4 = (f32[64,1,1]{2,1,0:T(1,128)S(1)}, f32[64,1,1]{2,1,0:T(1,128)S(1)}, u32[]{:S(2)}, u32[]{:S(2)}) collective-permute-start(f32[64,1,1]{2,1,0:T(1,128)S(1)} %slice.401), channel_id=1, source_target_pairs={{4,16},{8,20},{12,24},{20,32},{24,36},{28,40},{36,48},{40,52},{44,... | collective-permute-start | bytes 776 | tf_op jit(solution)/shard_map/ppermute | solution.py:31
  20.3 0.7 %copy-start.15 = (f32[4,8]{1,0:T(4,128)S(1)}, f32[4,8]{1,0:T(4,128)}, u32[]{:S(2)}) copy-start(f32[4,8]{1,0:T(4,128)} %param.11) | copy-start | bytes 388
  20.3 0.7 %copy-start.16 = (f32[4,8]{1,0:T(4,128)S(1)}, f32[4,8]{1,0:T(4,128)}, u32[]{:S(2)}) copy-start(f32[4,8]{1,0:T(4,128)} %param.10) | copy-start | bytes 388
  23.5 7.1 %collective-permute-start.5 = (f32[64,1,1]{2,1,0:T(1,128)S(1)}, f32[64,1,1]{2,1,0:T(1,128)S(1)}, u32[]{:S(2)}, u32[]{:S(2)}) collective-permute-start(f32[64,1,1]{2,1,0:T(1,128)S(1)} %slice.402), channel_id=1, source_target_pairs={{16,4},{20,8},{24,12},{32,20},{36,24},{40,28},{48,36},{52,40},{56,... | collective-permute-start | bytes 776 | tf_op jit(solution)/shard_map/ppermute | solution.py:31
  30.6 0.6 copy-start.13
  30.6 0.6 copy-start.14
  30.6 0.8 %copy-start.7 = (f32[2,64,8,1]{3,2,1,0:T(8,128)}, f32[2,64,8,1]{3,2,1,0:T(8,128)S(1)}, u32[]{:S(2)}) copy-start(f32[2,64,8,1]{3,2,1,0:T(8,128)S(1)} %collective-permute-done.2.yh_ref) | copy-start | bytes 12292
  30.7 0.8 %copy-start.12 = (f32[2,64,1,128]{3,1,2,0:T(8,128)}, f32[2,64,1,128]{3,1,2,0:T(8,128)S(1)}, u32[]{:S(2)}) copy-start(f32[2,64,1,128]{3,1,2,0:T(8,128)S(1)} %collective-permute-done) | copy-start | bytes 196612
  30.7 0.8 %copy-start.11 = (f32[3,64,1,128]{3,1,2,0:T(8,128)}, f32[3,64,1,128]{3,1,2,0:T(8,128)S(1)}, u32[]{:S(2)}) copy-start(f32[3,64,1,128]{3,1,2,0:T(8,128)S(1)} %collective-permute-done.1) | copy-start | bytes 294916
  35.8 9.7 %copy-start = (f32[3,64,8,128]{3,2,1,0:T(8,128)S(1)}, f32[3,64,8,128]{3,2,1,0:T(8,128)}, u32[]{:S(2)}) copy-start(f32[3,64,8,128]{3,2,1,0:T(8,128)} %e_ref.1) | copy-start | bytes 2359300
  35.8 5.5 %collective-permute-start.6 = (f32[12,8,128]{2,1,0:T(8,128)}, f32[12,8,128]{2,1,0:T(8,128)S(1)}, u32[]{:S(2)}, u32[]{:S(2)}) collective-permute-start(f32[12,8,128]{2,1,0:T(8,128)} %get-tuple-element.11), channel_id=1, source_target_pairs={{0,1},{1,2},{2,3},{3,0},{4,5},{5,6},{6,7},{7,4},{8,9},{9,10},{10,1... | collective-permute-start | bytes 147464 | tf_op jit(solution)/shard_map/ppermute | solution.py:281
  37.1 5.2 %collective-permute-start.7 = (f32[12,8,128]{2,1,0:T(8,128)}, f32[12,8,128]{2,1,0:T(8,128)S(1)}, u32[]{:S(2)}, u32[]{:S(2)}) collective-permute-start(f32[12,8,128]{2,1,0:T(8,128)} %get-tuple-element.11), channel_id=1, source_target_pairs={{0,2},{1,3},{2,0},{3,1},{4,6},{5,7},{6,4},{7,5},{8,10},{9,11},{10,... | collective-permute-start | bytes 147464 | tf_op jit(solution)/shard_map/ppermute | solution.py:281
  39.6 3.8 %collective-permute-start.8 = (f32[12,8,128]{2,1,0:T(8,128)}, f32[12,8,128]{2,1,0:T(8,128)S(1)}, u32[]{:S(2)}, u32[]{:S(2)}) collective-permute-start(f32[12,8,128]{2,1,0:T(8,128)} %get-tuple-element.11), channel_id=1, source_target_pairs={{0,3},{1,0},{2,1},{3,2},{4,7},{5,4},{6,5},{7,6},{8,11},{9,8},{10,9... | collective-permute-start | bytes 147464 | tf_op jit(solution)/shard_map/ppermute | solution.py:281
  45.0 1.0 %copy-start.3 = (f32[64,8,128]{2,1,0:T(8,128)S(1)}, f32[64,8,128]{2,1,0:T(8,128)}, u32[]{:S(2)}) copy-start(f32[64,8,128]{2,1,0:T(8,128)} %get-tuple-element.12) | copy-start | bytes 786436
  45.0 1.0 %copy-start.4 = (f32[64,8,128]{2,1,0:T(8,128)S(1)}, f32[64,8,128]{2,1,0:T(8,128)}, u32[]{:S(2)}) copy-start(f32[64,8,128]{2,1,0:T(8,128)} %get-tuple-element.13) | copy-start | bytes 786436
  47.2 1.0 %copy-start.6 = (f32[64,8,128]{2,1,0:T(8,128)S(1)}, f32[64,8,128]{2,1,0:T(8,128)}, u32[]{:S(2)}) copy-start(f32[64,8,128]{2,1,0:T(8,128)} %get-tuple-element.14) | copy-start | bytes 786436
  48.4 1.0 %copy-start.5 = (f32[64,8,128]{2,1,0:T(8,128)S(1)}, f32[64,8,128]{2,1,0:T(8,128)}, u32[]{:S(2)}) copy-start(f32[64,8,128]{2,1,0:T(8,128)} %get-tuple-element.16) | copy-start | bytes 786436
  49.4 6.3 %copy-start.8 = (f32[64,8,128]{2,1,0:T(8,128)S(1)}, f32[64,8,128]{2,1,0:T(8,128)}, u32[]{:S(2)}) copy-start(f32[64,8,128]{2,1,0:T(8,128)} %get-tuple-element.15) | copy-start | bytes 786436
  49.4 15.9 %copy-start.2 = (f32[3,64,8,128]{3,2,1,0:T(8,128)S(1)}, f32[3,64,8,128]{3,2,1,0:T(8,128)}, u32[]{:S(2)}) copy-start(f32[3,64,8,128]{3,2,1,0:T(8,128)} %h_ref.1) | copy-start | bytes 2359300
  49.6 17.6 %collective-permute-start.10 = (f32[64,8,1]{2,1,0:T(8,128)S(1)}, f32[64,8,1]{2,1,0:T(8,128)S(1)}, u32[]{:S(2)}, u32[]{:S(2)}) collective-permute-start(f32[64,8,1]{2,1,0:T(8,128)S(1)} %fusion), channel_id=1, source_target_pairs={{0,4},{4,8},{8,12},{1,5},{5,9},{9,13},{2,6},{6,10},{10,14},{3,7},{... | collective-permute-start | bytes 6152 | tf_op jit(solution)/shard_map/ppermute | solution.py:14
  55.8 11.4 %collective-permute-start.9 = (f32[64,1,128]{2,1,0:T(1,128)S(1)}, f32[64,1,128]{2,1,0:T(1,128)S(1)}, u32[]{:S(2)}, u32[]{:S(2)}) collective-permute-start(f32[64,1,128]{2,1,0:T(1,128)S(1)} %fusion.12), channel_id=1, source_target_pairs={{0,16},{16,32},{32,48},{48,64},{64,80},{80,96},{96,112},{112,128},... | collective-permute-start | bytes 98312 | tf_op jit(solution)/shard_map/ppermute | solution.py:14
  65.3 1.0 %copy-start.10 = (f32[64,8,128]{2,1,0:T(8,128)S(1)}, f32[64,8,128]{2,1,0:T(8,128)}, u32[]{:S(2)}) copy-start(f32[64,8,128]{2,1,0:T(8,128)} %get-tuple-element.17) | copy-start | bytes 786436

commit v11 on v9

--- a/solution.py
+++ b/solution.py
@@ -351,7 +351,9 @@
     magnetic_y_new = magnetic_y - 0.5 * z_courant * rise_x + time_step * slope_zx
     magnetic_x_new = magnetic_x - time_step * slope_zy + 0.5 * z_courant * rise_y
     before_hy = from_prev(magnetic_y_new[:, -1:, :], "gx")
-    before_hx = from_prev(magnetic_x_new[:, :, -1:], "gy")
+    before_hx = from_prev(magnetic_x_new[:, :, -1].reshape(-1), "gy").reshape(
+        magnetic_x_new.shape[:2] + (1,)
+    )
     change_hy = magnetic_y_new - jnp.concatenate([before_hy, magnetic_y_new[:, :-1]], axis=1)
     change_hx = magnetic_x_new - jnp.concatenate([before_hx, magnetic_x_new[:, :, :-1]], axis=2)
     electric_z_new = keep_rate * electric_z + curl_rate * (change_hy - change_hx)

time: 66.2 us -> 66.4 us (level)
  transfers between devices with their start and end apart: 11 -> 11, of which waited for: 3 -> 2; matrix products, arithmetic and copies ran while one was open for 11% -> 11% of each run, Pallas kernels for 0% -> 0%
where the time goes in v11:
time: 66.4 us; the launch traced here: 65.7 us
  starting transfers between devices  40.4 us (61%)
  local copies, waits for them, and re-layouts  9.31 us (14%)
  other arithmetic  8.46 us (13%)
  Pallas kernels  4.35 us (7%)
  waiting for transfers between devices  2.03 us (3%)
  between operations  1.15 us (2%)
    ppermute x4, starting transfers between devices, from_prev(): return lax.ppermute(block, axis, [(i, i + 1) for i in range(count - 1)])  22.6 us
    ppermute x2, starting transfers between devices, from_diagonal(): return lax.ppermute(block, axes, pairs)  7.67 us
    ppermute x2, starting transfers between devices, from_next(): return lax.ppermute(block, axis, [(i + 1, i) for i in range(count - 1)])  5.21 us
    ppermute x3, starting transfers between devices, body(): lax.ppermute(own, 'gz', [(i, (i + shift) % slab_count) for i in range(sla...  4.88 us
    pallas_call x1, Pallas kernels, make_sources(): pl.pallas_call(source_kernel, out_shape=(shape,) * 7 + (edges,), in_specs...  4.35 us
    unnamed x33, local copies, waits for them, and re-layouts  3.11 us
    another operation x3, other arithmetic, body(): rate_stack = jnp.stack([keep_rate, curl_rate, z_rate, stiffness])  2.3 us
    ppermute x3, waiting for transfers between devices, body(): lax.ppermute(own, 'gz', [(i, (i + shift) % slab_count) for i in range(sla...  2.01 us
  transfers between devices with their start and end apart: 11, of which 2 were waited for; matrix products, arithmetic and copies ran while one was open for 11% of the time, Pallas kernels for 0%

profile of v11, /device:TPU:97, one launch (start us, length us, event | category | flops | bytes accessed | tf_op | source)
XLA Modules:
  0.0 65.7 jit_solution(16532685736623402332)
XLA Ops:
  0.6 1.2 %slice_bitcast_fusion = (f32[64,8,128]{2,1,0:T(8,128)S(1)}, f32[64,8,128]{2,1,0:T(8,128)S(1)}, f32[64,8,128]{2,1,0:T(8,128)S(1)}) fusion(f32[3,64,8,128]{3,2,1,0:T(8,128)} %e_ref.1), kind=kLoop, calls=%fused_computation.22 | loop fusion | bytes 1572864 | tf_op jit(solution)/shard_map/squeeze | solution.py:256
  2.4 1.0 %slice-done = f32[1,64,8,128]{3,2,1,0:T(8,128)S(1)} async-done(((f32[3,64,8,128]{3,2,1,0:T(8,128)}), f32[1,64,8,128]{3,2,1,0:T(8,128)S(1)}, s32[]{:S(2)}) %slice-start) | async-done | bytes 262168 | tf_op jit(solution)/shard_map/slice | solution.py:257
  3.7 3.8 %collective-permute-start.3 = (f32[3,64,8,1]{1,2,3,0:T(8,128)S(1)}, f32[3,64,8,1]{1,2,3,0:T(8,128)S(1)}, u32[]{:S(2)}, u32[]{:S(2)}) collective-permute-start(f32[3,64,8,1]{1,2,3,0:T(8,128)S(1)} %pad_maximum_fusion.6), channel_id=1, source_target_pairs={{0,4},{4,8},{8,12},{1,5},{5,9},{9,13},{2,6},{6,10},{10,14},{3,7},{... | collective-permute-start | bytes 18440 | tf_op jit(solution)/shard_map/ppermute | solution.py:14
  7.6 4.5 %collective-permute-start.1 = (f32[3,64,1,128]{3,1,2,0:T(8,128)S(1)}, f32[3,64,1,128]{3,1,2,0:T(8,128)S(1)}, u32[]{:S(2)}, u32[]{:S(2)}) collective-permute-start(f32[3,64,1,128]{3,1,2,0:T(8,128)S(1)} %pad_maximum_fusion.4), channel_id=1, source_target_pairs={{0,16},{16,32},{32,48},{48,64},{64,80},{80,96},{96,112},{112,128},... | collective-permute-start | bytes 294920 | tf_op jit(solution)/shard_map/ppermute | solution.py:14
  12.4 0.3 copy.125
  12.7 2.1 %collective-permute-start.2 = (f32[2,64,8,1]{3,2,1,0:T(8,128)S(1)}, f32[2,64,8,1]{3,2,1,0:T(8,128)S(1)}, u32[]{:S(2)}, u32[]{:S(2)}) collective-permute-start(f32[2,64,8,1]{3,2,1,0:T(8,128)S(1)} %copy.125), channel_id=1, source_target_pairs={{4,0},{8,4},{12,8},{5,1},{9,5},{13,9},{6,2},{10,6},{14,10},{7,3},{... | collective-permute-start | bytes 12296 | tf_op jit(solution)/shard_map/ppermute | solution.py:19
  14.8 3.2 %collective-permute-start = (f32[2,64,1,128]{3,1,2,0:T(8,128)S(1)}, f32[2,64,1,128]{3,1,2,0:T(8,128)S(1)}, u32[]{:S(2)}, u32[]{:S(2)}) collective-permute-start(f32[2,64,1,128]{3,1,2,0:T(8,128)S(1)} %pad_maximum_fusion.5), channel_id=1, source_target_pairs={{16,0},{32,16},{48,32},{64,48},{80,64},{96,80},{112,96},{128,112},... | collective-permute-start | bytes 196616 | tf_op jit(solution)/shard_map/ppermute | solution.py:19
  18.0 2.4 %collective-permute-start.4 = (f32[64,1,1]{2,1,0:T(1,128)S(1)}, f32[64,1,1]{2,1,0:T(1,128)S(1)}, u32[]{:S(2)}, u32[]{:S(2)}) collective-permute-start(f32[64,1,1]{2,1,0:T(1,128)S(1)} %slice.331), channel_id=1, source_target_pairs={{4,16},{8,20},{12,24},{20,32},{24,36},{28,40},{36,48},{40,52},{44,... | collective-permute-start | bytes 776 | tf_op jit(solution)/shard_map/ppermute | solution.py:31
  20.5 0.3 broadcast_compare_fusion.7
  20.8 0.3 copy-done.13
  21.3 1.2 %fusion.9 = (f32[1,64,8,128]{3,2,1,0:T(8,128)S(1)}, f32[64,8,128]{2,1,0:T(8,128)S(1)}, f32[64,8,128]{2,1,0:T(8,128)S(1)}) fusion(pred[64,8,128]{2,1,0:T(8,128)(4,1)S(1)} %get-tuple-element.85, f32[64]{0:T(128)S(1)} %get-tuple-element.116, pred[64,8,128]{2,1,0:T(8,128)(4,1)S(1)} %get-tuple-element.86, f32[64]{0:T(128)S(1)} %get-tuple-element.115, ...), kind=kLoop, calls=%fused_computation.41 | loop fusion | flops 2359296 | bytes 1314816 | tf_op jit(solution)/shard_map/stack | solution.py:271
  22.5 1.0 %pad_maximum_fusion.rate_ref = f32[4,64,8,128]{3,2,1,0:T(8,128)} fusion(f32[1,64,8,128]{3,2,1,0:T(8,128)S(1)} %get-tuple-element.73, f32[1,64,8,128]{3,2,1,0:T(8,128)S(1)} %get-tuple-element.74, f32[1,64,8,128]{3,2,1,0:T(8,128)S(1)} %get-tuple-element.72, f32[1,64,8,128]{3,2,1,0:T(8,128)S(1)} %get-tuple-element.62), kind=kLoop, calls=%fused_computation | loop fusion | flops 786432 | bytes 2097152 | tf_op jit(solution)/shard_map/stack | solution.py:271
  23.7 5.3 %collective-permute-start.5 = (f32[64,1,1]{2,1,0:T(1,128)S(1)}, f32[64,1,1]{2,1,0:T(1,128)S(1)}, u32[]{:S(2)}, u32[]{:S(2)}) collective-permute-start(f32[64,1,1]{2,1,0:T(1,128)S(1)} %slice.332), channel_id=1, source_target_pairs={{16,4},{20,8},{24,12},{32,20},{36,24},{40,28},{48,36},{52,40},{56,... | collective-permute-start | bytes 776 | tf_op jit(solution)/shard_map/ppermute | solution.py:31
  29.0 0.6 add_convert_fusion.flag_ref
  29.6 1.2 %copy.130.yl_ref = f32[3,64,8,1]{3,2,1,0:T(8,128)} copy(f32[3,64,8,1]{1,2,3,0:T(8,128)S(1)} %collective-permute-done.3) | data formatting | bytes 12288 | tf_op jit(solution)/shard_map/ppermute | solution.py:14
  30.9 0.5 copy-done.11
  31.7 4.4 %shard_map.77 = (f32[64,8,128]{2,1,0:T(8,128)}, f32[64,8,128]{2,1,0:T(8,128)}, f32[64,8,128]{2,1,0:T(8,128)}, f32[64,8,128]{2,1,0:T(8,128)}, f32[64,8,128]{2,1,0...) custom-call(s32[3]{0:T(128)} %add_convert_fusion.flag_ref, ...), custom_call_target="tpu_custom_call" | custom-call | tf_op jit(solution)/shard_map/pallas_call | solution.py:227
  36.0 1.3 %collective-permute-start.6 = (f32[12,8,128]{2,1,0:T(8,128)}, f32[12,8,128]{2,1,0:T(8,128)S(1)}, u32[]{:S(2)}, u32[]{:S(2)}) collective-permute-start(f32[12,8,128]{2,1,0:T(8,128)} %get-tuple-element.11), channel_id=1, source_target_pairs={{0,1},{1,2},{2,3},{3,0},{4,5},{5,6},{6,7},{7,4},{8,9},{9,10},{10,1... | collective-permute-start | bytes 147464 | tf_op jit(solution)/shard_map/ppermute | solution.py:281
  37.3 2.5 %collective-permute-start.7 = (f32[12,8,128]{2,1,0:T(8,128)}, f32[12,8,128]{2,1,0:T(8,128)S(1)}, u32[]{:S(2)}, u32[]{:S(2)}) collective-permute-start(f32[12,8,128]{2,1,0:T(8,128)} %get-tuple-element.11), channel_id=1, source_target_pairs={{0,2},{1,3},{2,0},{3,1},{4,6},{5,7},{6,4},{7,5},{8,10},{9,11},{10,... | collective-permute-start | bytes 147464 | tf_op jit(solution)/shard_map/ppermute | solution.py:281
  39.8 1.2 %collective-permute-start.8 = (f32[12,8,128]{2,1,0:T(8,128)}, f32[12,8,128]{2,1,0:T(8,128)S(1)}, u32[]{:S(2)}, u32[]{:S(2)}) collective-permute-start(f32[12,8,128]{2,1,0:T(8,128)} %get-tuple-element.11), channel_id=1, source_target_pairs={{0,3},{1,0},{2,1},{3,2},{4,7},{5,4},{6,5},{7,6},{8,11},{9,8},{10,9... | collective-permute-start | bytes 147464 | tf_op jit(solution)/shard_map/ppermute | solution.py:281
  40.9 0.6 dynamic-slice.23
  41.5 1.0 %collective-permute-done.7 = f32[12,8,128]{2,1,0:T(8,128)S(1)} collective-permute-done((f32[12,8,128]{2,1,0:T(8,128)}, f32[12,8,128]{2,1,0:T(8,128)S(1)}, u32[]{:S(2)}, u32[]{:S(2)}) %collective-permute-start.7) | collective-permute-done | bytes 49184 | tf_op jit(solution)/shard_map/ppermute | solution.py:281
  42.5 1.0 %collective-permute-done.8 = f32[12,8,128]{2,1,0:T(8,128)S(1)} collective-permute-done((f32[12,8,128]{2,1,0:T(8,128)}, f32[12,8,128]{2,1,0:T(8,128)S(1)}, u32[]{:S(2)}, u32[]{:S(2)}) %collective-permute-start.8) | collective-permute-done | bytes 49184 | tf_op jit(solution)/shard_map/ppermute | solution.py:281
  43.5 0.8 %pad_maximum_fusion.3 = f32[4,12,8,128]{3,2,1,0:T(8,128)S(1)} fusion(f32[1,12,8,128]{3,2,1,0:T(8,128)S(1)} %bitcast.231, f32[1,12,8,128]{3,2,1,0:T(8,128)S(1)} %bitcast.230, f32[1,12,8,128]{3,2,1,0:T(8,128)S(1)} %bitcast.229, f32[1,12,8,128]{3,2,1,0:T(8,128)} %bitcast.228), kind=kLoop, calls=%fused_computation.32 | loop fusion | flops 147456 | bytes 393216 | tf_op jit(solution)/shard_map/stack | solution.py:283
  44.5 0.7 %fusion.65 = f32[8,128]{1,0:T(8,128)S(1)} fusion(s32[]{:T(128)S(6)} %select_n.124, f32[1,8,128]{2,1,0:T(8,128)S(1)} %get-tuple-element.26, f32[1,8,128]{2,1,0:T(8,128)S(1)} %get-tuple-element.25, f32[1,8,128]{2,1,0:T(8,128)S(1)} %get-tuple-element.24, f32[1]{0:T(128)} %dynamic-slice.23), kind=kLoop, calls=%fused_computation.155 | loop fusion | flops 3072 | bytes 16392 | tf_op jit(solution)/shard_map/mul | solution.py:337
  45.4 0.7 %copy-done.6 = f32[64,8,128]{2,1,0:T(8,128)S(1)} copy-done((f32[64,8,128]{2,1,0:T(8,128)S(1)}, f32[64,8,128]{2,1,0:T(8,128)}, u32[]{:S(2)}) %copy-start.6) | copy-done | bytes 262168
  46.2 1.2 %fusion.87 = (f32[64,8,128]{2,1,0:T(8,128)S(1)}, f32[64,8,128]{2,1,0:T(8,128)S(1)}, f32[64,8,128]{2,1,0:T(8,128)S(1)}, f32[64,8,128]{2,1,0:T(8,128)S(1)}) fusion(f32[3,64,8,128]{3,2,1,0:T(8,128)S(1)} %copy-done, f32[64,8,128]{2,1,0:T(8,128)} %get-tuple-element.13, f32[8,128]{1,0:T(8,128)S(1)} %get-tuple-element.90, f32[64,8,128]{2,1,0:T(8,128)S(1)} %copy-done.7, ...), kind=kLoop, calls=%fused_computation.215 | loop fusion | flops 655360 | bytes 2637824 | tf_op jit(solution)/shard_map/add | solution.py:346
  47.5 1.1 %copy-done.1 = f32[3,64,8,128]{3,2,1,0:T(8,128)S(1)} copy-done((f32[3,64,8,128]{3,2,1,0:T(8,128)S(1)}, f32[3,64,8,128]{3,2,1,0:T(8,128)}, u32[]{:S(2)}) %copy-start.1) | copy-done | bytes 786456
  49.0 4.9 %collective-permute-start.10 = (f32[512]{0:T(512)S(1)}, f32[512]{0:T(512)S(1)}, u32[]{:S(2)}, u32[]{:S(2)}) collective-permute-start(f32[512]{0:T(512)S(1)} %reshape_squeeze.3), channel_id=1, source_target_pairs={{0,4},{4,8},{8,12},{1,5},{5,9},{9,13},{2,6},{6,10},{10,14},{3,7},{... | collective-permute-start | bytes 6152 | tf_op jit(solution)/shard_map/ppermute | solution.py:14
  53.9 9.5 %collective-permute-start.9 = (f32[64,1,128]{2,1,0:T(1,128)S(1)}, f32[64,1,128]{2,1,0:T(1,128)S(1)}, u32[]{:S(2)}, u32[]{:S(2)}) collective-permute-start(f32[64,1,128]{2,1,0:T(1,128)S(1)} %slice.338), channel_id=1, source_target_pairs={{0,16},{16,32},{32,48},{48,64},{64,80},{80,96},{96,112},{112,128},... | collective-permute-start | bytes 98312 | tf_op jit(solution)/shard_map/ppermute | solution.py:14
  63.4 0.9 %pad_maximum_fusion.2 = f32[3,64,8,128]{3,2,1,0:T(8,128)} fusion(f32[1,64,8,128]{3,2,1,0:T(8,128)S(1)} %bitcast.221, f32[1,64,8,128]{3,2,1,0:T(8,128)S(1)} %bitcast.214, f32[1,64,8,128]{3,2,1,0:T(8,128)S(1)} %bitcast.212), kind=kLoop, calls=%fused_computation.2 | loop fusion | flops 393216 | bytes 1572864 | tf_op jit(solution)/shard_map/stack | solution.py:362
  64.7 0.9 %pad_maximum_fusion.1 = f32[3,64,8,128]{3,2,1,0:T(8,128)} fusion(f32[1,64,8,128]{3,2,1,0:T(8,128)S(1)} %fusion.6, f32[1,64,8,128]{3,2,1,0:T(8,128)S(1)} %bitcast.219, f32[1,64,8,128]{3,2,1,0:T(8,128)S(1)} %bitcast.220), kind=kLoop, calls=%fused_computation.1 | loop fusion | flops 393216 | bytes 1572864 | tf_op jit(solution)/shard_map/stack | solution.py:361
  (78 shorter events, 3.3 us)
Async XLA Ops:
  2.4 1.0 %slice-start = ((f32[3,64,8,128]{3,2,1,0:T(8,128)}), f32[1,64,8,128]{3,2,1,0:T(8,128)S(1)}, s32[]{:S(2)}) async-start(f32[3,64,8,128]{3,2,1,0:T(8,128)} %h_ref.1), calls=%async_computation | async-start | bytes 524288 | tf_op jit(solution)/shard_map/slice | solution.py:257
  3.7 20.0 %collective-permute-start.3 = (f32[3,64,8,1]{1,2,3,0:T(8,128)S(1)}, f32[3,64,8,1]{1,2,3,0:T(8,128)S(1)}, u32[]{:S(2)}, u32[]{:S(2)}) collective-permute-start(f32[3,64,8,1]{1,2,3,0:T(8,128)S(1)} %pad_maximum_fusion.6), channel_id=1, source_target_pairs={{0,4},{4,8},{8,12},{1,5},{5,9},{9,13},{2,6},{6,10},{10,14},{3,7},{... | collective-permute-start | bytes 18440 | tf_op jit(solution)/shard_map/ppermute | solution.py:14
  7.6 23.3 %collective-permute-start.1 = (f32[3,64,1,128]{3,1,2,0:T(8,128)S(1)}, f32[3,64,1,128]{3,1,2,0:T(8,128)S(1)}, u32[]{:S(2)}, u32[]{:S(2)}) collective-permute-start(f32[3,64,1,128]{3,1,2,0:T(8,128)S(1)} %pad_maximum_fusion.4), channel_id=1, source_target_pairs={{0,16},{16,32},{32,48},{48,64},{64,80},{80,96},{96,112},{112,128},... | collective-permute-start | bytes 294920 | tf_op jit(solution)/shard_map/ppermute | solution.py:14
  12.7 7.8 %copy-start.3 = (s32[64,8,128]{2,1,0:T(8,128)S(1)}, s32[64,8,128]{2,1,0:T(8,128)}, u32[]{:S(2)}) copy-start(s32[64,8,128]{2,1,0:T(8,128)} %param.8) | copy-start | bytes 786436
  12.7 18.1 %collective-permute-start.2 = (f32[2,64,8,1]{3,2,1,0:T(8,128)S(1)}, f32[2,64,8,1]{3,2,1,0:T(8,128)S(1)}, u32[]{:S(2)}, u32[]{:S(2)}) collective-permute-start(f32[2,64,8,1]{3,2,1,0:T(8,128)S(1)} %copy.125), channel_id=1, source_target_pairs={{4,0},{8,4},{12,8},{5,1},{9,5},{13,9},{6,2},{10,6},{14,10},{7,3},{... | collective-permute-start | bytes 12296 | tf_op jit(solution)/shard_map/ppermute | solution.py:19
  14.8 5.6 %copy-start.15 = (s32[64]{0:T(128)S(1)}, s32[64]{0:T(128)}, u32[]{:S(2)}) copy-start(s32[64]{0:T(128)} %param.9) | copy-start | bytes 772
  14.8 16.0 %collective-permute-start = (f32[2,64,1,128]{3,1,2,0:T(8,128)S(1)}, f32[2,64,1,128]{3,1,2,0:T(8,128)S(1)}, u32[]{:S(2)}, u32[]{:S(2)}) collective-permute-start(f32[2,64,1,128]{3,1,2,0:T(8,128)S(1)} %pad_maximum_fusion.5), channel_id=1, source_target_pairs={{16,0},{32,16},{48,32},{64,48},{80,64},{96,80},{112,96},{128,112},... | collective-permute-start | bytes 196616 | tf_op jit(solution)/shard_map/ppermute | solution.py:19
  18.0 12.8 %collective-permute-start.4 = (f32[64,1,1]{2,1,0:T(1,128)S(1)}, f32[64,1,1]{2,1,0:T(1,128)S(1)}, u32[]{:S(2)}, u32[]{:S(2)}) collective-permute-start(f32[64,1,1]{2,1,0:T(1,128)S(1)} %slice.331), channel_id=1, source_target_pairs={{4,16},{8,20},{12,24},{20,32},{24,36},{28,40},{36,48},{40,52},{44,... | collective-permute-start | bytes 776 | tf_op jit(solution)/shard_map/ppermute | solution.py:31
  20.5 0.7 %copy-start.13 = (f32[4,8]{1,0:T(4,128)S(1)}, f32[4,8]{1,0:T(4,128)}, u32[]{:S(2)}) copy-start(f32[4,8]{1,0:T(4,128)} %param.11) | copy-start | bytes 388
  20.5 0.7 %copy-start.14 = (f32[4,8]{1,0:T(4,128)S(1)}, f32[4,8]{1,0:T(4,128)}, u32[]{:S(2)}) copy-start(f32[4,8]{1,0:T(4,128)} %param.10) | copy-start | bytes 388
  23.7 7.1 %collective-permute-start.5 = (f32[64,1,1]{2,1,0:T(1,128)S(1)}, f32[64,1,1]{2,1,0:T(1,128)S(1)}, u32[]{:S(2)}, u32[]{:S(2)}) collective-permute-start(f32[64,1,1]{2,1,0:T(1,128)S(1)} %slice.332), channel_id=1, source_target_pairs={{16,4},{20,8},{24,12},{32,20},{36,24},{40,28},{48,36},{52,40},{56,... | collective-permute-start | bytes 776 | tf_op jit(solution)/shard_map/ppermute | solution.py:31
  30.8 0.6 copy-start.11
  30.8 0.6 copy-start.12
  30.8 0.8 %copy-start.2 = (f32[2,64,8,1]{3,2,1,0:T(8,128)}, f32[2,64,8,1]{3,2,1,0:T(8,128)S(1)}, u32[]{:S(2)}) copy-start(f32[2,64,8,1]{3,2,1,0:T(8,128)S(1)} %collective-permute-done.2.yh_ref) | copy-start | bytes 12292
  30.9 0.8 %copy-start.10 = (f32[2,64,1,128]{3,1,2,0:T(8,128)}, f32[2,64,1,128]{3,1,2,0:T(8,128)S(1)}, u32[]{:S(2)}) copy-start(f32[2,64,1,128]{3,1,2,0:T(8,128)S(1)} %collective-permute-done) | copy-start | bytes 196612
  30.9 0.8 %copy-start.9 = (f32[3,64,1,128]{3,1,2,0:T(8,128)}, f32[3,64,1,128]{3,1,2,0:T(8,128)S(1)}, u32[]{:S(2)}) copy-start(f32[3,64,1,128]{3,1,2,0:T(8,128)S(1)} %collective-permute-done.1) | copy-start | bytes 294916
  36.0 9.3 %copy-start = (f32[3,64,8,128]{3,2,1,0:T(8,128)S(1)}, f32[3,64,8,128]{3,2,1,0:T(8,128)}, u32[]{:S(2)}) copy-start(f32[3,64,8,128]{3,2,1,0:T(8,128)} %e_ref.1) | copy-start | bytes 2359300
  36.0 5.5 %collective-permute-start.6 = (f32[12,8,128]{2,1,0:T(8,128)}, f32[12,8,128]{2,1,0:T(8,128)S(1)}, u32[]{:S(2)}, u32[]{:S(2)}) collective-permute-start(f32[12,8,128]{2,1,0:T(8,128)} %get-tuple-element.11), channel_id=1, source_target_pairs={{0,1},{1,2},{2,3},{3,0},{4,5},{5,6},{6,7},{7,4},{8,9},{9,10},{10,1... | collective-permute-start | bytes 147464 | tf_op jit(solution)/shard_map/ppermute | solution.py:281
  37.3 5.2 %collective-permute-start.7 = (f32[12,8,128]{2,1,0:T(8,128)}, f32[12,8,128]{2,1,0:T(8,128)S(1)}, u32[]{:S(2)}, u32[]{:S(2)}) collective-permute-start(f32[12,8,128]{2,1,0:T(8,128)} %get-tuple-element.11), channel_id=1, source_target_pairs={{0,2},{1,3},{2,0},{3,1},{4,6},{5,7},{6,4},{7,5},{8,10},{9,11},{10,... | collective-permute-start | bytes 147464 | tf_op jit(solution)/shard_map/ppermute | solution.py:281
  39.8 3.8 %collective-permute-start.8 = (f32[12,8,128]{2,1,0:T(8,128)}, f32[12,8,128]{2,1,0:T(8,128)S(1)}, u32[]{:S(2)}, u32[]{:S(2)}) collective-permute-start(f32[12,8,128]{2,1,0:T(8,128)} %get-tuple-element.11), channel_id=1, source_target_pairs={{0,3},{1,0},{2,1},{3,2},{4,7},{5,4},{6,5},{7,6},{8,11},{9,8},{10,9... | collective-permute-start | bytes 147464 | tf_op jit(solution)/shard_map/ppermute | solution.py:281
  45.2 1.0 %copy-start.6 = (f32[64,8,128]{2,1,0:T(8,128)S(1)}, f32[64,8,128]{2,1,0:T(8,128)}, u32[]{:S(2)}) copy-start(f32[64,8,128]{2,1,0:T(8,128)} %get-tuple-element.10) | copy-start | bytes 786436
  45.2 1.0 %copy-start.7 = (f32[64,8,128]{2,1,0:T(8,128)S(1)}, f32[64,8,128]{2,1,0:T(8,128)}, u32[]{:S(2)}) copy-start(f32[64,8,128]{2,1,0:T(8,128)} %get-tuple-element.14) | copy-start | bytes 786436
  46.2 1.3 %copy-start.4 = (f32[64,8,128]{2,1,0:T(8,128)S(1)}, f32[64,8,128]{2,1,0:T(8,128)}, u32[]{:S(2)}) copy-start(f32[64,8,128]{2,1,0:T(8,128)} %get-tuple-element.15) | copy-start | bytes 786436
  46.2 1.3 %copy-start.5 = (f32[64,8,128]{2,1,0:T(8,128)S(1)}, f32[64,8,128]{2,1,0:T(8,128)}, u32[]{:S(2)}) copy-start(f32[64,8,128]{2,1,0:T(8,128)} %get-tuple-element.16) | copy-start | bytes 786436
  47.4 1.1 %copy-start.1 = (f32[3,64,8,128]{3,2,1,0:T(8,128)S(1)}, f32[3,64,8,128]{3,2,1,0:T(8,128)}, u32[]{:S(2)}) copy-start(f32[3,64,8,128]{3,2,1,0:T(8,128)} %h_ref.1) | copy-start | bytes 2359300
  48.7 14.7 %copy-start.8 = (f32[64,8,128]{2,1,0:T(8,128)S(1)}, f32[64,8,128]{2,1,0:T(8,128)}, u32[]{:S(2)}) copy-start(f32[64,8,128]{2,1,0:T(8,128)} %get-tuple-element.17) | copy-start | bytes 786436
  49.0 15.3 %collective-permute-start.10 = (f32[512]{0:T(512)S(1)}, f32[512]{0:T(512)S(1)}, u32[]{:S(2)}, u32[]{:S(2)}) collective-permute-start(f32[512]{0:T(512)S(1)} %reshape_squeeze.3), channel_id=1, source_target_pairs={{0,4},{4,8},{8,12},{1,5},{5,9},{9,13},{2,6},{6,10},{10,14},{3,7},{... | collective-permute-start | bytes 6152 | tf_op jit(solution)/shard_map/ppermute | solution.py:14
  53.9 10.6 %collective-permute-start.9 = (f32[64,1,128]{2,1,0:T(1,128)S(1)}, f32[64,1,128]{2,1,0:T(1,128)S(1)}, u32[]{:S(2)}, u32[]{:S(2)}) collective-permute-start(f32[64,1,128]{2,1,0:T(1,128)S(1)} %slice.338), channel_id=1, source_target_pairs={{0,16},{16,32},{32,48},{48,64},{64,80},{80,96},{96,112},{112,128},... | collective-permute-start | bytes 98312 | tf_op jit(solution)/shard_map/ppermute | solution.py:14

commit v12 on v9

--- a/solution.py
+++ b/solution.py
@@ -65,7 +65,7 @@
     lw_ref[0] = inv
 
     def forward(z, carry):
-        upper, value_x, value_y, value_low, unused = carry
+        upper, value_x, value_y, value_low, _ = carry
         stiff = stiff_ref[z]
         inv = 1.0 / (diag_ref[z] + stiff * upper)
         upper = -stiff * inv
@@ -108,16 +108,6 @@
     edge_ref[5] = lw_ref[depth - 1]
     edge_ref[6] = hw_ref[0]
     edge_ref[7] = hw_ref[depth - 1]
-
-
-def solve_slab(stiffness, diagonal, source_x, source_y):
-    shape = jax.ShapeDtypeStruct(stiffness.shape, jnp.float32)
-    edges = jax.ShapeDtypeStruct((8,) + stiffness.shape[1:], jnp.float32)
-    return pl.pallas_call(
-        thomas_kernel,
-        out_shape=(shape, shape, shape, shape, edges),
-        scratch_shapes=[pltpu.VMEM(stiffness.shape, jnp.float32)],
-    )(stiffness, diagonal, source_x, source_y)
 
 
 def source_kernel(
@@ -244,11 +234,10 @@
     return (offset, coupling, outgoing, factor_out)
 
 
-def body(electric, magnetic, material, layer_map, permittivity, conductivity):
+def step_body(electric, magnetic, material, layer_map, permittivity, conductivity):
     epsilon_cell = lookup(permittivity, layer_map, material)
     sigma_cell = lookup(conductivity, layer_map, material)
     keep_rate, curl_rate, z_rate, stiffness = rates(epsilon_cell, sigma_cell)
-    depth_rows, span_x, span_y = material.shape
     slab = lax.axis_index("gz")
     bottom = slab == 0
     first_x = lax.axis_index("gx") == 0
@@ -256,16 +245,15 @@
     electric_x, electric_y, electric_z = (electric[0], electric[1], electric[2])
     magnetic_x, magnetic_y, magnetic_z = (magnetic[0], magnetic[1], magnetic[2])
 
+    corner_ex = from_diagonal(electric_x[:, -1:, :1], ("gx", "gy"), 1, -1)
+    corner_ey = from_diagonal(electric_y[:, :1, -1:], ("gx", "gy"), -1, 1)
     x_high = from_next(jnp.stack([electric_y[:, :1], electric_z[:, :1]]), "gx")
-    x_low = from_prev(
-        jnp.stack([electric_x[:, -1:], electric_y[:, -1:], magnetic_z[:, -1:]]), "gx"
-    )
+    x_low = from_prev(jnp.stack([electric_x[:, -1:], electric_y[:, -1:], magnetic_z[:, -1:]]), "gx")
     y_high = from_next(jnp.stack([electric_x[:, :, :1], electric_z[:, :, :1]]), "gy")
     y_low = from_prev(
-        jnp.stack([electric_x[:, :, -1:], electric_y[:, :, -1:], magnetic_z[:, :, -1:]]), "gy"
-    )
-    corner_ex = from_diagonal(electric_x[:, -1:, :1], ("gx", "gy"), 1, -1)
-    corner_ey = from_diagonal(electric_y[:, :1, -1:], ("gx", "gy"), -1, 1)
+        jnp.stack([electric_x[:, :, -1:], electric_y[:, :, -1:], magnetic_z[:, :, -1:]]),
+        "gy",
+    )
 
     flags = jnp.stack([bottom, first_x, first_y]).astype(jnp.int32)
     rate_stack = jnp.stack([keep_rate, curl_rate, z_rate, stiffness])
@@ -363,7 +351,7 @@
 
 def solution(mesh):
     return jax.shard_map(
-        body,
+        step_body,
         mesh=mesh,
         in_specs=(
             P(None, "gz", "gx", "gy"),

time: 66.2 us -> 66.2 us (level)
  no operation moved by 1% of the time
where the time goes in v12:
time: 66.2 us; the launch traced here: 65.3 us
  starting transfers between devices  40.4 us (61%)
  local copies, waits for them, and re-layouts  8.9 us (13%)
  other arithmetic  8.45 us (13%)
  Pallas kernels  4.33 us (7%)
  waiting for transfers between devices  2.09 us (3%)
  between operations  1.13 us (2%)
    ppermute x4, starting transfers between devices, from_prev(): return lax.ppermute(block, axis, [(i, i + 1) for i in range(count - 1)])  22.6 us
    ppermute x2, starting transfers between devices, from_diagonal(): return lax.ppermute(block, axes, pairs)  7.67 us
    ppermute x2, starting transfers between devices, from_next(): return lax.ppermute(block, axis, [(i + 1, i) for i in range(count - 1)])  5.21 us
    ppermute x3, starting transfers between devices, step_body(): lax.ppermute(own, 'gz', [(i, (i + shift) % slab_count) for i in range(sla...  4.89 us
    pallas_call x1, Pallas kernels, make_sources(): pl.pallas_call(source_kernel, out_shape=(shape,) * 7 + (edges,), in_specs...  4.33 us
    unnamed x33, local copies, waits for them, and re-layouts  3.1 us
    another operation x3, other arithmetic, step_body(): rate_stack = jnp.stack([keep_rate, curl_rate, z_rate, stiffness])  2.31 us
    ppermute x3, waiting for transfers between devices, step_body(): lax.ppermute(own, 'gz', [(i, (i + shift) % slab_count) for i in range(sla...  2.01 us
  transfers between devices with their start and end apart: 11, of which 3 were waited for; matrix products, arithmetic and copies ran while one was open for 11% of the time, Pallas kernels for 0%

profile of v12, /device:TPU:97, one launch (start us, length us, event | category | flops | bytes accessed | tf_op | source)
XLA Modules:
  0.0 65.3 jit_solution(15551586982848243821)
XLA Ops:
  0.6 1.2 %slice_bitcast_fusion = (f32[64,8,128]{2,1,0:T(8,128)S(1)}, f32[64,8,128]{2,1,0:T(8,128)S(1)}, f32[64,8,128]{2,1,0:T(8,128)S(1)}) fusion(f32[3,64,8,128]{3,2,1,0:T(8,128)} %e_ref.1), kind=kLoop, calls=%fused_computation.21 | loop fusion | bytes 1572864 | tf_op jit(solution)/shard_map/squeeze | solution.py:245
  2.4 1.0 %slice-done = f32[1,64,8,128]{3,2,1,0:T(8,128)S(1)} async-done(((f32[3,64,8,128]{3,2,1,0:T(8,128)}), f32[1,64,8,128]{3,2,1,0:T(8,128)S(1)}, s32[]{:S(2)}) %slice-start) | async-done | bytes 262168 | tf_op jit(solution)/shard_map/slice | solution.py:246
  3.7 3.8 %collective-permute-start.3 = (f32[3,64,8,1]{1,2,3,0:T(8,128)S(1)}, f32[3,64,8,1]{1,2,3,0:T(8,128)S(1)}, u32[]{:S(2)}, u32[]{:S(2)}) collective-permute-start(f32[3,64,8,1]{1,2,3,0:T(8,128)S(1)} %pad_maximum_fusion.6), channel_id=1, source_target_pairs={{0,4},{4,8},{8,12},{1,5},{5,9},{9,13},{2,6},{6,10},{10,14},{3,7},{... | collective-permute-start | bytes 18440 | tf_op jit(solution)/shard_map/ppermute | solution.py:14
  7.6 4.5 %collective-permute-start.1 = (f32[3,64,1,128]{3,1,2,0:T(8,128)S(1)}, f32[3,64,1,128]{3,1,2,0:T(8,128)S(1)}, u32[]{:S(2)}, u32[]{:S(2)}) collective-permute-start(f32[3,64,1,128]{3,1,2,0:T(8,128)S(1)} %pad_maximum_fusion.4), channel_id=1, source_target_pairs={{0,16},{16,32},{32,48},{48,64},{64,80},{80,96},{96,112},{112,128},... | collective-permute-start | bytes 294920 | tf_op jit(solution)/shard_map/ppermute | solution.py:14
  12.4 0.3 copy.121
  12.7 2.1 %collective-permute-start.2 = (f32[2,64,8,1]{3,2,1,0:T(8,128)S(1)}, f32[2,64,8,1]{3,2,1,0:T(8,128)S(1)}, u32[]{:S(2)}, u32[]{:S(2)}) collective-permute-start(f32[2,64,8,1]{3,2,1,0:T(8,128)S(1)} %copy.121), channel_id=1, source_target_pairs={{4,0},{8,4},{12,8},{5,1},{9,5},{13,9},{6,2},{10,6},{14,10},{7,3},{... | collective-permute-start | bytes 12296 | tf_op jit(solution)/shard_map/ppermute | solution.py:19
  14.8 3.2 %collective-permute-start = (f32[2,64,1,128]{3,1,2,0:T(8,128)S(1)}, f32[2,64,1,128]{3,1,2,0:T(8,128)S(1)}, u32[]{:S(2)}, u32[]{:S(2)}) collective-permute-start(f32[2,64,1,128]{3,1,2,0:T(8,128)S(1)} %pad_maximum_fusion.5), channel_id=1, source_target_pairs={{16,0},{32,16},{48,32},{64,48},{80,64},{96,80},{112,96},{128,112},... | collective-permute-start | bytes 196616 | tf_op jit(solution)/shard_map/ppermute | solution.py:19
  18.0 2.4 %collective-permute-start.4 = (f32[64,1,1]{2,1,0:T(1,128)S(1)}, f32[64,1,1]{2,1,0:T(1,128)S(1)}, u32[]{:S(2)}, u32[]{:S(2)}) collective-permute-start(f32[64,1,1]{2,1,0:T(1,128)S(1)} %slice.331), channel_id=1, source_target_pairs={{4,16},{8,20},{12,24},{20,32},{24,36},{28,40},{36,48},{40,52},{44,... | collective-permute-start | bytes 776 | tf_op jit(solution)/shard_map/ppermute | solution.py:31
  20.5 0.3 broadcast_compare_fusion.7
  20.8 0.3 copy-done.13
  21.3 1.2 %fusion.9 = (f32[1,64,8,128]{3,2,1,0:T(8,128)S(1)}, f32[64,8,128]{2,1,0:T(8,128)S(1)}, f32[64,8,128]{2,1,0:T(8,128)S(1)}) fusion(pred[64,8,128]{2,1,0:T(8,128)(4,1)S(1)} %get-tuple-element.85, f32[64]{0:T(128)S(1)} %get-tuple-element.116, pred[64,8,128]{2,1,0:T(8,128)(4,1)S(1)} %get-tuple-element.86, f32[64]{0:T(128)S(1)} %get-tuple-element.115, ...), kind=kLoop, calls=%fused_computation.40 | loop fusion | flops 2359296 | bytes 1314816 | tf_op jit(solution)/shard_map/stack | solution.py:259
  22.5 1.0 %pad_maximum_fusion.rate_ref = f32[4,64,8,128]{3,2,1,0:T(8,128)} fusion(f32[1,64,8,128]{3,2,1,0:T(8,128)S(1)} %get-tuple-element.73, f32[1,64,8,128]{3,2,1,0:T(8,128)S(1)} %get-tuple-element.74, f32[1,64,8,128]{3,2,1,0:T(8,128)S(1)} %get-tuple-element.72, f32[1,64,8,128]{3,2,1,0:T(8,128)S(1)} %get-tuple-element.62), kind=kLoop, calls=%fused_computation | loop fusion | flops 786432 | bytes 2097152 | tf_op jit(solution)/shard_map/stack | solution.py:259
  23.7 5.3 %collective-permute-start.5 = (f32[64,1,1]{2,1,0:T(1,128)S(1)}, f32[64,1,1]{2,1,0:T(1,128)S(1)}, u32[]{:S(2)}, u32[]{:S(2)}) collective-permute-start(f32[64,1,1]{2,1,0:T(1,128)S(1)} %slice.332), channel_id=1, source_target_pairs={{16,4},{20,8},{24,12},{32,20},{36,24},{40,28},{48,36},{52,40},{56,... | collective-permute-start | bytes 776 | tf_op jit(solution)/shard_map/ppermute | solution.py:31
  29.0 0.6 add_convert_fusion.flag_ref
  29.6 1.2 %copy.126.yl_ref = f32[3,64,8,1]{3,2,1,0:T(8,128)} copy(f32[3,64,8,1]{1,2,3,0:T(8,128)S(1)} %collective-permute-done.3) | data formatting | bytes 12288 | tf_op jit(solution)/shard_map/ppermute | solution.py:14
  30.9 0.5 copy-done.11
  31.6 4.3 %shard_map.77 = (f32[64,8,128]{2,1,0:T(8,128)}, f32[64,8,128]{2,1,0:T(8,128)}, f32[64,8,128]{2,1,0:T(8,128)}, f32[64,8,128]{2,1,0:T(8,128)}, f32[64,8,128]{2,1,0...) custom-call(s32[3]{0:T(128)} %add_convert_fusion.flag_ref, ...), custom_call_target="tpu_custom_call" | custom-call | tf_op jit(solution)/shard_map/pallas_call | solution.py:217
  36.0 1.3 %collective-permute-start.6 = (f32[12,8,128]{2,1,0:T(8,128)}, f32[12,8,128]{2,1,0:T(8,128)S(1)}, u32[]{:S(2)}, u32[]{:S(2)}) collective-permute-start(f32[12,8,128]{2,1,0:T(8,128)} %get-tuple-element.11), channel_id=1, source_target_pairs={{0,1},{1,2},{2,3},{3,0},{4,5},{5,6},{6,7},{7,4},{8,9},{9,10},{10,1... | collective-permute-start | bytes 147464 | tf_op jit(solution)/shard_map/ppermute | solution.py:269
  37.3 2.5 %collective-permute-start.7 = (f32[12,8,128]{2,1,0:T(8,128)}, f32[12,8,128]{2,1,0:T(8,128)S(1)}, u32[]{:S(2)}, u32[]{:S(2)}) collective-permute-start(f32[12,8,128]{2,1,0:T(8,128)} %get-tuple-element.11), channel_id=1, source_target_pairs={{0,2},{1,3},{2,0},{3,1},{4,6},{5,7},{6,4},{7,5},{8,10},{9,11},{10,... | collective-permute-start | bytes 147464 | tf_op jit(solution)/shard_map/ppermute | solution.py:269
  39.7 1.2 %collective-permute-start.8 = (f32[12,8,128]{2,1,0:T(8,128)}, f32[12,8,128]{2,1,0:T(8,128)S(1)}, u32[]{:S(2)}, u32[]{:S(2)}) collective-permute-start(f32[12,8,128]{2,1,0:T(8,128)} %get-tuple-element.11), channel_id=1, source_target_pairs={{0,3},{1,0},{2,1},{3,2},{4,7},{5,4},{6,5},{7,6},{8,11},{9,8},{10,9... | collective-permute-start | bytes 147464 | tf_op jit(solution)/shard_map/ppermute | solution.py:269
  40.9 0.6 dynamic-slice.23
  41.5 1.0 %collective-permute-done.7 = f32[12,8,128]{2,1,0:T(8,128)S(1)} collective-permute-done((f32[12,8,128]{2,1,0:T(8,128)}, f32[12,8,128]{2,1,0:T(8,128)S(1)}, u32[]{:S(2)}, u32[]{:S(2)}) %collective-permute-start.7) | collective-permute-done | bytes 49184 | tf_op jit(solution)/shard_map/ppermute | solution.py:269
  42.4 1.0 %collective-permute-done.8 = f32[12,8,128]{2,1,0:T(8,128)S(1)} collective-permute-done((f32[12,8,128]{2,1,0:T(8,128)}, f32[12,8,128]{2,1,0:T(8,128)S(1)}, u32[]{:S(2)}, u32[]{:S(2)}) %collective-permute-start.8) | collective-permute-done | bytes 49184 | tf_op jit(solution)/shard_map/ppermute | solution.py:269
  43.5 0.8 %pad_maximum_fusion.3 = f32[4,12,8,128]{3,2,1,0:T(8,128)S(1)} fusion(f32[1,12,8,128]{3,2,1,0:T(8,128)S(1)} %bitcast.231, f32[1,12,8,128]{3,2,1,0:T(8,128)S(1)} %bitcast.230, f32[1,12,8,128]{3,2,1,0:T(8,128)S(1)} %bitcast.229, f32[1,12,8,128]{3,2,1,0:T(8,128)} %bitcast.228), kind=kLoop, calls=%fused_computation.31 | loop fusion | flops 147456 | bytes 393216 | tf_op jit(solution)/shard_map/stack | solution.py:271
  44.4 0.7 %fusion.65 = f32[8,128]{1,0:T(8,128)S(1)} fusion(s32[]{:T(128)S(6)} %select_n.124, f32[1,8,128]{2,1,0:T(8,128)S(1)} %get-tuple-element.26, f32[1,8,128]{2,1,0:T(8,128)S(1)} %get-tuple-element.25, f32[1,8,128]{2,1,0:T(8,128)S(1)} %get-tuple-element.24, f32[1]{0:T(128)} %dynamic-slice.23), kind=kLoop, calls=%fused_computation.154 | loop fusion | flops 3072 | bytes 16392 | tf_op jit(solution)/shard_map/mul | solution.py:325
  45.3 0.7 %copy-done.6 = f32[64,8,128]{2,1,0:T(8,128)S(1)} copy-done((f32[64,8,128]{2,1,0:T(8,128)S(1)}, f32[64,8,128]{2,1,0:T(8,128)}, u32[]{:S(2)}) %copy-start.6) | copy-done | bytes 262168
  46.1 1.2 %fusion.87 = (f32[64,8,128]{2,1,0:T(8,128)S(1)}, f32[64,8,128]{2,1,0:T(8,128)S(1)}, f32[64,8,128]{2,1,0:T(8,128)S(1)}, f32[64,8,128]{2,1,0:T(8,128)S(1)}) fusion(f32[3,64,8,128]{3,2,1,0:T(8,128)S(1)} %copy-done, f32[64,8,128]{2,1,0:T(8,128)} %get-tuple-element.13, f32[8,128]{1,0:T(8,128)S(1)} %get-tuple-element.90, f32[64,8,128]{2,1,0:T(8,128)S(1)} %copy-done.7, ...), kind=kLoop, calls=%fused_computation.214 | loop fusion | flops 655360 | bytes 2637824 | tf_op jit(solution)/shard_map/add | solution.py:334
  47.4 1.1 %copy-done.1 = f32[3,64,8,128]{3,2,1,0:T(8,128)S(1)} copy-done((f32[3,64,8,128]{3,2,1,0:T(8,128)S(1)}, f32[3,64,8,128]{3,2,1,0:T(8,128)}, u32[]{:S(2)}) %copy-start.1) | copy-done | bytes 786456
  48.8 4.8 %collective-permute-start.10 = (f32[64,8,1]{2,1,0:T(8,128)S(1)}, f32[64,8,1]{2,1,0:T(8,128)S(1)}, u32[]{:S(2)}, u32[]{:S(2)}) collective-permute-start(f32[64,8,1]{2,1,0:T(8,128)S(1)} %slice.341), channel_id=1, source_target_pairs={{0,4},{4,8},{8,12},{1,5},{5,9},{9,13},{2,6},{6,10},{10,14},{3,7},{... | collective-permute-start | bytes 6152 | tf_op jit(solution)/shard_map/ppermute | solution.py:14
  53.6 9.5 %collective-permute-start.9 = (f32[64,1,128]{2,1,0:T(1,128)S(1)}, f32[64,1,128]{2,1,0:T(1,128)S(1)}, u32[]{:S(2)}, u32[]{:S(2)}) collective-permute-start(f32[64,1,128]{2,1,0:T(1,128)S(1)} %slice.338), channel_id=1, source_target_pairs={{0,16},{16,32},{32,48},{48,64},{64,80},{80,96},{96,112},{112,128},... | collective-permute-start | bytes 98312 | tf_op jit(solution)/shard_map/ppermute | solution.py:14
  63.2 0.9 %pad_maximum_fusion.2 = f32[3,64,8,128]{3,2,1,0:T(8,128)} fusion(f32[1,64,8,128]{3,2,1,0:T(8,128)S(1)} %bitcast.221, f32[1,64,8,128]{3,2,1,0:T(8,128)S(1)} %bitcast.214, f32[1,64,8,128]{3,2,1,0:T(8,128)S(1)} %bitcast.212), kind=kLoop, calls=%fused_computation.2 | loop fusion | flops 393216 | bytes 1572864 | tf_op jit(solution)/shard_map/stack | solution.py:348
  64.4 0.9 %pad_maximum_fusion.1 = f32[3,64,8,128]{3,2,1,0:T(8,128)} fusion(f32[1,64,8,128]{3,2,1,0:T(8,128)S(1)} %fusion.6, f32[1,64,8,128]{3,2,1,0:T(8,128)S(1)} %bitcast.219, f32[1,64,8,128]{3,2,1,0:T(8,128)S(1)} %bitcast.220), kind=kLoop, calls=%fused_computation.1 | loop fusion | flops 393216 | bytes 1572864 | tf_op jit(solution)/shard_map/stack | solution.py:347
  (76 shorter events, 3.0 us)
Async XLA Ops:
  2.4 1.0 %slice-start = ((f32[3,64,8,128]{3,2,1,0:T(8,128)}), f32[1,64,8,128]{3,2,1,0:T(8,128)S(1)}, s32[]{:S(2)}) async-start(f32[3,64,8,128]{3,2,1,0:T(8,128)} %h_ref.1), calls=%async_computation | async-start | bytes 524288 | tf_op jit(solution)/shard_map/slice | solution.py:246
  3.7 20.0 %collective-permute-start.3 = (f32[3,64,8,1]{1,2,3,0:T(8,128)S(1)}, f32[3,64,8,1]{1,2,3,0:T(8,128)S(1)}, u32[]{:S(2)}, u32[]{:S(2)}) collective-permute-start(f32[3,64,8,1]{1,2,3,0:T(8,128)S(1)} %pad_maximum_fusion.6), channel_id=1, source_target_pairs={{0,4},{4,8},{8,12},{1,5},{5,9},{9,13},{2,6},{6,10},{10,14},{3,7},{... | collective-permute-start | bytes 18440 | tf_op jit(solution)/shard_map/ppermute | solution.py:14
  7.6 23.3 %collective-permute-start.1 = (f32[3,64,1,128]{3,1,2,0:T(8,128)S(1)}, f32[3,64,1,128]{3,1,2,0:T(8,128)S(1)}, u32[]{:S(2)}, u32[]{:S(2)}) collective-permute-start(f32[3,64,1,128]{3,1,2,0:T(8,128)S(1)} %pad_maximum_fusion.4), channel_id=1, source_target_pairs={{0,16},{16,32},{32,48},{48,64},{64,80},{80,96},{96,112},{112,128},... | collective-permute-start | bytes 294920 | tf_op jit(solution)/shard_map/ppermute | solution.py:14
  12.7 7.8 %copy-start.3 = (s32[64,8,128]{2,1,0:T(8,128)S(1)}, s32[64,8,128]{2,1,0:T(8,128)}, u32[]{:S(2)}) copy-start(s32[64,8,128]{2,1,0:T(8,128)} %param.8) | copy-start | bytes 786436
  12.7 18.1 %collective-permute-start.2 = (f32[2,64,8,1]{3,2,1,0:T(8,128)S(1)}, f32[2,64,8,1]{3,2,1,0:T(8,128)S(1)}, u32[]{:S(2)}, u32[]{:S(2)}) collective-permute-start(f32[2,64,8,1]{3,2,1,0:T(8,128)S(1)} %copy.121), channel_id=1, source_target_pairs={{4,0},{8,4},{12,8},{5,1},{9,5},{13,9},{6,2},{10,6},{14,10},{7,3},{... | collective-permute-start | bytes 12296 | tf_op jit(solution)/shard_map/ppermute | solution.py:19
  14.8 5.6 %copy-start.15 = (s32[64]{0:T(128)S(1)}, s32[64]{0:T(128)}, u32[]{:S(2)}) copy-start(s32[64]{0:T(128)} %param.9) | copy-start | bytes 772
  14.8 16.0 %collective-permute-start = (f32[2,64,1,128]{3,1,2,0:T(8,128)S(1)}, f32[2,64,1,128]{3,1,2,0:T(8,128)S(1)}, u32[]{:S(2)}, u32[]{:S(2)}) collective-permute-start(f32[2,64,1,128]{3,1,2,0:T(8,128)S(1)} %pad_maximum_fusion.5), channel_id=1, source_target_pairs={{16,0},{32,16},{48,32},{64,48},{80,64},{96,80},{112,96},{128,112},... | collective-permute-start | bytes 196616 | tf_op jit(solution)/shard_map/ppermute | solution.py:19
  18.0 12.8 %collective-permute-start.4 = (f32[64,1,1]{2,1,0:T(1,128)S(1)}, f32[64,1,1]{2,1,0:T(1,128)S(1)}, u32[]{:S(2)}, u32[]{:S(2)}) collective-permute-start(f32[64,1,1]{2,1,0:T(1,128)S(1)} %slice.331), channel_id=1, source_target_pairs={{4,16},{8,20},{12,24},{20,32},{24,36},{28,40},{36,48},{40,52},{44,... | collective-permute-start | bytes 776 | tf_op jit(solution)/shard_map/ppermute | solution.py:31
  20.5 0.7 %copy-start.13 = (f32[4,8]{1,0:T(4,128)S(1)}, f32[4,8]{1,0:T(4,128)}, u32[]{:S(2)}) copy-start(f32[4,8]{1,0:T(4,128)} %param.11) | copy-start | bytes 388
  20.5 0.7 %copy-start.14 = (f32[4,8]{1,0:T(4,128)S(1)}, f32[4,8]{1,0:T(4,128)}, u32[]{:S(2)}) copy-start(f32[4,8]{1,0:T(4,128)} %param.10) | copy-start | bytes 388
  23.7 7.1 %collective-permute-start.5 = (f32[64,1,1]{2,1,0:T(1,128)S(1)}, f32[64,1,1]{2,1,0:T(1,128)S(1)}, u32[]{:S(2)}, u32[]{:S(2)}) collective-permute-start(f32[64,1,1]{2,1,0:T(1,128)S(1)} %slice.332), channel_id=1, source_target_pairs={{16,4},{20,8},{24,12},{32,20},{36,24},{40,28},{48,36},{52,40},{56,... | collective-permute-start | bytes 776 | tf_op jit(solution)/shard_map/ppermute | solution.py:31
  30.8 0.6 copy-start.11
  30.8 0.6 copy-start.12
  30.8 0.8 %copy-start.2 = (f32[2,64,8,1]{3,2,1,0:T(8,128)}, f32[2,64,8,1]{3,2,1,0:T(8,128)S(1)}, u32[]{:S(2)}) copy-start(f32[2,64,8,1]{3,2,1,0:T(8,128)S(1)} %collective-permute-done.2.yh_ref) | copy-start | bytes 12292
  30.8 0.8 %copy-start.10 = (f32[2,64,1,128]{3,1,2,0:T(8,128)}, f32[2,64,1,128]{3,1,2,0:T(8,128)S(1)}, u32[]{:S(2)}) copy-start(f32[2,64,1,128]{3,1,2,0:T(8,128)S(1)} %collective-permute-done) | copy-start | bytes 196612
  30.9 0.8 %copy-start.9 = (f32[3,64,1,128]{3,1,2,0:T(8,128)}, f32[3,64,1,128]{3,1,2,0:T(8,128)S(1)}, u32[]{:S(2)}) copy-start(f32[3,64,1,128]{3,1,2,0:T(8,128)S(1)} %collective-permute-done.1) | copy-start | bytes 294916
  36.0 9.3 %copy-start = (f32[3,64,8,128]{3,2,1,0:T(8,128)S(1)}, f32[3,64,8,128]{3,2,1,0:T(8,128)}, u32[]{:S(2)}) copy-start(f32[3,64,8,128]{3,2,1,0:T(8,128)} %e_ref.1) | copy-start | bytes 2359300
  36.0 5.5 %collective-permute-start.6 = (f32[12,8,128]{2,1,0:T(8,128)}, f32[12,8,128]{2,1,0:T(8,128)S(1)}, u32[]{:S(2)}, u32[]{:S(2)}) collective-permute-start(f32[12,8,128]{2,1,0:T(8,128)} %get-tuple-element.11), channel_id=1, source_target_pairs={{0,1},{1,2},{2,3},{3,0},{4,5},{5,6},{6,7},{7,4},{8,9},{9,10},{10,1... | collective-permute-start | bytes 147464 | tf_op jit(solution)/shard_map/ppermute | solution.py:269
  37.3 5.2 %collective-permute-start.7 = (f32[12,8,128]{2,1,0:T(8,128)}, f32[12,8,128]{2,1,0:T(8,128)S(1)}, u32[]{:S(2)}, u32[]{:S(2)}) collective-permute-start(f32[12,8,128]{2,1,0:T(8,128)} %get-tuple-element.11), channel_id=1, source_target_pairs={{0,2},{1,3},{2,0},{3,1},{4,6},{5,7},{6,4},{7,5},{8,10},{9,11},{10,... | collective-permute-start | bytes 147464 | tf_op jit(solution)/shard_map/ppermute | solution.py:269
  39.7 3.8 %collective-permute-start.8 = (f32[12,8,128]{2,1,0:T(8,128)}, f32[12,8,128]{2,1,0:T(8,128)S(1)}, u32[]{:S(2)}, u32[]{:S(2)}) collective-permute-start(f32[12,8,128]{2,1,0:T(8,128)} %get-tuple-element.11), channel_id=1, source_target_pairs={{0,3},{1,0},{2,1},{3,2},{4,7},{5,4},{6,5},{7,6},{8,11},{9,8},{10,9... | collective-permute-start | bytes 147464 | tf_op jit(solution)/shard_map/ppermute | solution.py:269
  45.1 1.0 %copy-start.6 = (f32[64,8,128]{2,1,0:T(8,128)S(1)}, f32[64,8,128]{2,1,0:T(8,128)}, u32[]{:S(2)}) copy-start(f32[64,8,128]{2,1,0:T(8,128)} %get-tuple-element.10) | copy-start | bytes 786436
  45.1 1.0 %copy-start.7 = (f32[64,8,128]{2,1,0:T(8,128)S(1)}, f32[64,8,128]{2,1,0:T(8,128)}, u32[]{:S(2)}) copy-start(f32[64,8,128]{2,1,0:T(8,128)} %get-tuple-element.14) | copy-start | bytes 786436
  46.1 1.3 %copy-start.4 = (f32[64,8,128]{2,1,0:T(8,128)S(1)}, f32[64,8,128]{2,1,0:T(8,128)}, u32[]{:S(2)}) copy-start(f32[64,8,128]{2,1,0:T(8,128)} %get-tuple-element.15) | copy-start | bytes 786436
  46.1 1.3 %copy-start.5 = (f32[64,8,128]{2,1,0:T(8,128)S(1)}, f32[64,8,128]{2,1,0:T(8,128)}, u32[]{:S(2)}) copy-start(f32[64,8,128]{2,1,0:T(8,128)} %get-tuple-element.16) | copy-start | bytes 786436
  47.3 1.1 %copy-start.1 = (f32[3,64,8,128]{3,2,1,0:T(8,128)S(1)}, f32[3,64,8,128]{3,2,1,0:T(8,128)}, u32[]{:S(2)}) copy-start(f32[3,64,8,128]{3,2,1,0:T(8,128)} %h_ref.1) | copy-start | bytes 2359300
  48.6 14.5 %copy-start.8 = (f32[64,8,128]{2,1,0:T(8,128)S(1)}, f32[64,8,128]{2,1,0:T(8,128)}, u32[]{:S(2)}) copy-start(f32[64,8,128]{2,1,0:T(8,128)} %get-tuple-element.17) | copy-start | bytes 786436
  48.8 15.4 %collective-permute-start.10 = (f32[64,8,1]{2,1,0:T(8,128)S(1)}, f32[64,8,1]{2,1,0:T(8,128)S(1)}, u32[]{:S(2)}, u32[]{:S(2)}) collective-permute-start(f32[64,8,1]{2,1,0:T(8,128)S(1)} %slice.341), channel_id=1, source_target_pairs={{0,4},{4,8},{8,12},{1,5},{5,9},{9,13},{2,6},{6,10},{10,14},{3,7},{... | collective-permute-start | bytes 6152 | tf_op jit(solution)/shard_map/ppermute | solution.py:14
  53.6 10.5 %collective-permute-start.9 = (f32[64,1,128]{2,1,0:T(1,128)S(1)}, f32[64,1,128]{2,1,0:T(1,128)S(1)}, u32[]{:S(2)}, u32[]{:S(2)}) collective-permute-start(f32[64,1,128]{2,1,0:T(1,128)S(1)} %slice.338), channel_id=1, source_target_pairs={{0,16},{16,32},{32,48},{48,64},{64,80},{80,96},{96,112},{112,128},... | collective-permute-start | bytes 98312 | tf_op jit(solution)/shard_map/ppermute | solution.py:14

commit v13 on v9

--- a/solution.py
+++ b/solution.py
@@ -355,8 +355,9 @@
     change_hy = magnetic_y_new - jnp.concatenate([before_hy, magnetic_y_new[:, :-1]], axis=1)
     change_hx = magnetic_x_new - jnp.concatenate([before_hx, magnetic_x_new[:, :, :-1]], axis=2)
     electric_z_new = keep_rate * electric_z + curl_rate * (change_hy - change_hx)
+    electric_next = jnp.stack([electric_x_new, electric_y_new, jnp.zeros_like(electric_z)])
     return (
-        jnp.stack([electric_x_new, electric_y_new, electric_z_new]),
+        electric_next.at[2].set(electric_z_new),
         jnp.stack([magnetic_x_new, magnetic_y_new, magnetic_z_new]),
     )
 

time: 66.2 us -> 66.7 us (level)
  local copies, waits for them, and re-layouts: 8.9 us -> 10.7 us
  other arithmetic: 8.45 us -> 7.71 us
    unnamed x33 -> x35, local copies, waits for them, and re-layouts: 3.1 us -> 4.79 us
    another operation x2 -> x1, other arithmetic: 1.14 us -> 0.12 us  [body(): jnp.stack([electric_x_new, electric_y_new, jnp.zeros_like(electric_z)])]
  transfers between devices with their start and end apart: 11 -> 11, of which waited for: 3 -> 2; matrix products, arithmetic and copies ran while one was open for 11% -> 11% of each run, Pallas kernels for 0% -> 0%
where the time goes in v13:
time: 66.7 us; the launch traced here: 66.2 us
  starting transfers between devices  40.4 us (61%)
  local copies, waits for them, and re-layouts  10.7 us (16%)
  other arithmetic  7.71 us (12%)
  Pallas kernels  4.32 us (6%)
  waiting for transfers between devices  1.96 us (3%)
  between operations  1.14 us (2%)
    ppermute x4, starting transfers between devices, from_prev(): return lax.ppermute(block, axis, [(i, i + 1) for i in range(count - 1)])  22.6 us
    ppermute x2, starting transfers between devices, from_diagonal(): return lax.ppermute(block, axes, pairs)  7.67 us
    ppermute x2, starting transfers between devices, from_next(): return lax.ppermute(block, axis, [(i + 1, i) for i in range(count - 1)])  5.21 us
    ppermute x3, starting transfers between devices, body(): lax.ppermute(own, 'gz', [(i, (i + shift) % slab_count) for i in range(sla...  4.89 us
    unnamed x35, local copies, waits for them, and re-layouts  4.79 us
    pallas_call x1, Pallas kernels, make_sources(): pl.pallas_call(source_kernel, out_shape=(shape,) * 7 + (edges,), in_specs...  4.32 us
    another operation x3, other arithmetic, body(): rate_stack = jnp.stack([keep_rate, curl_rate, z_rate, stiffness])  2.3 us
    ppermute x3, waiting for transfers between devices, body(): lax.ppermute(own, 'gz', [(i, (i + shift) % slab_count) for i in range(sla...  1.94 us
  transfers between devices with their start and end apart: 11, of which 2 were waited for; matrix products, arithmetic and copies ran while one was open for 11% of the time, Pallas kernels for 0%

profile of v13, /device:TPU:97, one launch (start us, length us, event | category | flops | bytes accessed | tf_op | source)
XLA Modules:
  0.0 66.2 jit_solution(1400646748253953285)
XLA Ops:
  0.6 1.2 %slice_bitcast_fusion = (f32[64,8,128]{2,1,0:T(8,128)S(1)}, f32[64,8,128]{2,1,0:T(8,128)S(1)}, f32[64,8,128]{2,1,0:T(8,128)S(1)}) fusion(f32[3,64,8,128]{3,2,1,0:T(8,128)} %e_ref.1), kind=kLoop, calls=%fused_computation.22 | loop fusion | bytes 1572864 | tf_op jit(solution)/shard_map/squeeze | solution.py:256
  2.4 1.0 %slice-done = f32[1,64,8,128]{3,2,1,0:T(8,128)S(1)} async-done(((f32[3,64,8,128]{3,2,1,0:T(8,128)}), f32[1,64,8,128]{3,2,1,0:T(8,128)S(1)}, s32[]{:S(2)}) %slice-start) | async-done | bytes 262168 | tf_op jit(solution)/shard_map/slice | solution.py:257
  3.7 3.8 %collective-permute-start.3 = (f32[3,64,8,1]{1,2,3,0:T(8,128)S(1)}, f32[3,64,8,1]{1,2,3,0:T(8,128)S(1)}, u32[]{:S(2)}, u32[]{:S(2)}) collective-permute-start(f32[3,64,8,1]{1,2,3,0:T(8,128)S(1)} %pad_maximum_fusion.5), channel_id=1, source_target_pairs={{0,4},{4,8},{8,12},{1,5},{5,9},{9,13},{2,6},{6,10},{10,14},{3,7},{... | collective-permute-start | bytes 18440 | tf_op jit(solution)/shard_map/ppermute | solution.py:14
  7.6 4.5 %collective-permute-start.1 = (f32[3,64,1,128]{3,1,2,0:T(8,128)S(1)}, f32[3,64,1,128]{3,1,2,0:T(8,128)S(1)}, u32[]{:S(2)}, u32[]{:S(2)}) collective-permute-start(f32[3,64,1,128]{3,1,2,0:T(8,128)S(1)} %pad_maximum_fusion.3), channel_id=1, source_target_pairs={{0,16},{16,32},{32,48},{48,64},{64,80},{80,96},{96,112},{112,128},... | collective-permute-start | bytes 294920 | tf_op jit(solution)/shard_map/ppermute | solution.py:14
  12.7 2.1 %collective-permute-start.2 = (f32[2,64,8,1]{3,2,1,0:T(8,128)S(1)}, f32[2,64,8,1]{3,2,1,0:T(8,128)S(1)}, u32[]{:S(2)}, u32[]{:S(2)}) collective-permute-start(f32[2,64,8,1]{3,2,1,0:T(8,128)S(1)} %copy.106), channel_id=1, source_target_pairs={{4,0},{8,4},{12,8},{5,1},{9,5},{13,9},{6,2},{10,6},{14,10},{7,3},{... | collective-permute-start | bytes 12296 | tf_op jit(solution)/shard_map/ppermute | solution.py:19
  14.8 3.2 %collective-permute-start = (f32[2,64,1,128]{3,1,2,0:T(8,128)S(1)}, f32[2,64,1,128]{3,1,2,0:T(8,128)S(1)}, u32[]{:S(2)}, u32[]{:S(2)}) collective-permute-start(f32[2,64,1,128]{3,1,2,0:T(8,128)S(1)} %pad_maximum_fusion.4), channel_id=1, source_target_pairs={{16,0},{32,16},{48,32},{64,48},{80,64},{96,80},{112,96},{128,112},... | collective-permute-start | bytes 196616 | tf_op jit(solution)/shard_map/ppermute | solution.py:19
  18.0 2.4 %collective-permute-start.4 = (f32[64,1,1]{2,1,0:T(1,128)S(1)}, f32[64,1,1]{2,1,0:T(1,128)S(1)}, u32[]{:S(2)}, u32[]{:S(2)}) collective-permute-start(f32[64,1,1]{2,1,0:T(1,128)S(1)} %slice.356), channel_id=1, source_target_pairs={{4,16},{8,20},{12,24},{20,32},{24,36},{28,40},{36,48},{40,52},{44,... | collective-permute-start | bytes 776 | tf_op jit(solution)/shard_map/ppermute | solution.py:31
  20.5 0.3 broadcast_compare_fusion.7
  20.8 0.3 copy-done.14
  21.3 1.2 %fusion.10 = (f32[1,64,8,128]{3,2,1,0:T(8,128)S(1)}, f32[64,8,128]{2,1,0:T(8,128)S(1)}, f32[64,8,128]{2,1,0:T(8,128)S(1)}) fusion(pred[64,8,128]{2,1,0:T(8,128)(4,1)S(1)} %get-tuple-element.99, f32[64]{0:T(128)S(1)} %get-tuple-element.130, pred[64,8,128]{2,1,0:T(8,128)(4,1)S(1)} %get-tuple-element.100, f32[64]{0:T(128)S(1)} %get-tuple-element.129, ...), kind=kLoop, calls=%fused_computation.41 | loop fusion | flops 2359296 | bytes 1314816 | tf_op jit(solution)/shard_map/stack | solution.py:271
  22.5 1.0 %pad_maximum_fusion.rate_ref = f32[4,64,8,128]{3,2,1,0:T(8,128)} fusion(f32[1,64,8,128]{3,2,1,0:T(8,128)S(1)} %get-tuple-element.87, f32[1,64,8,128]{3,2,1,0:T(8,128)S(1)} %get-tuple-element.88, f32[1,64,8,128]{3,2,1,0:T(8,128)S(1)} %get-tuple-element.86, f32[1,64,8,128]{3,2,1,0:T(8,128)S(1)} %get-tuple-element.76), kind=kLoop, calls=%fused_computation | loop fusion | flops 786432 | bytes 2097152 | tf_op jit(solution)/shard_map/stack | solution.py:271
  23.7 5.3 %collective-permute-start.5 = (f32[64,1,1]{2,1,0:T(1,128)S(1)}, f32[64,1,1]{2,1,0:T(1,128)S(1)}, u32[]{:S(2)}, u32[]{:S(2)}) collective-permute-start(f32[64,1,1]{2,1,0:T(1,128)S(1)} %slice.357), channel_id=1, source_target_pairs={{16,4},{20,8},{24,12},{32,20},{36,24},{40,28},{48,36},{52,40},{56,... | collective-permute-start | bytes 776 | tf_op jit(solution)/shard_map/ppermute | solution.py:31
  29.0 0.6 add_convert_fusion.flag_ref
  29.6 1.2 %copy.111.yl_ref = f32[3,64,8,1]{3,2,1,0:T(8,128)} copy(f32[3,64,8,1]{1,2,3,0:T(8,128)S(1)} %collective-permute-done.3) | data formatting | bytes 12288 | tf_op jit(solution)/shard_map/ppermute | solution.py:14
  30.9 0.5 copy-done.12
  31.7 4.3 %shard_map.77 = (f32[64,8,128]{2,1,0:T(8,128)}, f32[64,8,128]{2,1,0:T(8,128)}, f32[64,8,128]{2,1,0:T(8,128)}, f32[64,8,128]{2,1,0:T(8,128)}, f32[64,8,128]{2,1,0...) custom-call(s32[3]{0:T(128)} %add_convert_fusion.flag_ref, ...), custom_call_target="tpu_custom_call" | custom-call | tf_op jit(solution)/shard_map/pallas_call | solution.py:227
  36.0 1.3 %collective-permute-start.6 = (f32[12,8,128]{2,1,0:T(8,128)}, f32[12,8,128]{2,1,0:T(8,128)S(1)}, u32[]{:S(2)}, u32[]{:S(2)}) collective-permute-start(f32[12,8,128]{2,1,0:T(8,128)} %get-tuple-element.23), channel_id=1, source_target_pairs={{0,1},{1,2},{2,3},{3,0},{4,5},{5,6},{6,7},{7,4},{8,9},{9,10},{10,1... | collective-permute-start | bytes 147464 | tf_op jit(solution)/shard_map/ppermute | solution.py:281
  37.3 2.5 %collective-permute-start.7 = (f32[12,8,128]{2,1,0:T(8,128)}, f32[12,8,128]{2,1,0:T(8,128)S(1)}, u32[]{:S(2)}, u32[]{:S(2)}) collective-permute-start(f32[12,8,128]{2,1,0:T(8,128)} %get-tuple-element.23), channel_id=1, source_target_pairs={{0,2},{1,3},{2,0},{3,1},{4,6},{5,7},{6,4},{7,5},{8,10},{9,11},{10,... | collective-permute-start | bytes 147464 | tf_op jit(solution)/shard_map/ppermute | solution.py:281
  39.7 1.2 %collective-permute-start.8 = (f32[12,8,128]{2,1,0:T(8,128)}, f32[12,8,128]{2,1,0:T(8,128)S(1)}, u32[]{:S(2)}, u32[]{:S(2)}) collective-permute-start(f32[12,8,128]{2,1,0:T(8,128)} %get-tuple-element.23), channel_id=1, source_target_pairs={{0,3},{1,0},{2,1},{3,2},{4,7},{5,4},{6,5},{7,6},{8,11},{9,8},{10,9... | collective-permute-start | bytes 147464 | tf_op jit(solution)/shard_map/ppermute | solution.py:281
  41.0 0.6 dynamic-slice.31
  41.6 0.9 %collective-permute-done.7 = f32[12,8,128]{2,1,0:T(8,128)S(1)} collective-permute-done((f32[12,8,128]{2,1,0:T(8,128)}, f32[12,8,128]{2,1,0:T(8,128)S(1)}, u32[]{:S(2)}, u32[]{:S(2)}) %collective-permute-start.7) | collective-permute-done | bytes 49184 | tf_op jit(solution)/shard_map/ppermute | solution.py:281
  42.5 1.0 %collective-permute-done.8 = f32[12,8,128]{2,1,0:T(8,128)S(1)} collective-permute-done((f32[12,8,128]{2,1,0:T(8,128)}, f32[12,8,128]{2,1,0:T(8,128)S(1)}, u32[]{:S(2)}, u32[]{:S(2)}) %collective-permute-start.8) | collective-permute-done | bytes 49184 | tf_op jit(solution)/shard_map/ppermute | solution.py:281
  43.5 0.8 %pad_maximum_fusion.2 = f32[4,12,8,128]{3,2,1,0:T(8,128)S(1)} fusion(f32[1,12,8,128]{3,2,1,0:T(8,128)S(1)} %bitcast.236, f32[1,12,8,128]{3,2,1,0:T(8,128)S(1)} %bitcast.235, f32[1,12,8,128]{3,2,1,0:T(8,128)S(1)} %bitcast.234, f32[1,12,8,128]{3,2,1,0:T(8,128)} %bitcast.233), kind=kLoop, calls=%fused_computation.32 | loop fusion | flops 147456 | bytes 393216 | tf_op jit(solution)/shard_map/stack | solution.py:283
  44.5 0.7 %fusion.66 = f32[8,128]{1,0:T(8,128)S(1)} fusion(s32[]{:T(128)S(6)} %select_n.124, f32[1,8,128]{2,1,0:T(8,128)S(1)} %get-tuple-element.40, f32[1,8,128]{2,1,0:T(8,128)S(1)} %get-tuple-element.39, f32[1,8,128]{2,1,0:T(8,128)S(1)} %get-tuple-element.38, f32[1]{0:T(128)} %dynamic-slice.31), kind=kLoop, calls=%fused_computation.155 | loop fusion | flops 3072 | bytes 16392 | tf_op jit(solution)/shard_map/mul | solution.py:337
  45.4 0.7 %copy-done.7 = f32[64,8,128]{2,1,0:T(8,128)S(1)} copy-done((f32[64,8,128]{2,1,0:T(8,128)S(1)}, f32[64,8,128]{2,1,0:T(8,128)}, u32[]{:S(2)}) %copy-start.7) | copy-done | bytes 262168
  46.2 1.2 %fusion.89 = (f32[64,8,128]{2,1,0:T(8,128)S(1)}, f32[64,8,128]{2,1,0:T(8,128)S(1)}, f32[64,8,128]{2,1,0:T(8,128)S(1)}, f32[64,8,128]{2,1,0:T(8,128)S(1)}) fusion(f32[3,64,8,128]{3,2,1,0:T(8,128)S(1)} %copy-done, f32[64,8,128]{2,1,0:T(8,128)} %get-tuple-element.25, f32[8,128]{1,0:T(8,128)S(1)} %get-tuple-element.105, f32[64,8,128]{2,1,0:T(8,128)S(1)} %copy-done.7, ...), kind=kLoop, calls=%fused_computation.216 | loop fusion | flops 655360 | bytes 2637824 | tf_op jit(solution)/shard_map/add | solution.py:345
  47.4 1.1 %copy-done.1 = f32[3,64,8,128]{3,2,1,0:T(8,128)S(1)} copy-done((f32[3,64,8,128]{3,2,1,0:T(8,128)S(1)}, f32[3,64,8,128]{3,2,1,0:T(8,128)}, u32[]{:S(2)}) %copy-start.1) | copy-done | bytes 786456
  48.8 4.9 %collective-permute-start.10 = (f32[64,8,1]{2,1,0:T(8,128)S(1)}, f32[64,8,1]{2,1,0:T(8,128)S(1)}, u32[]{:S(2)}, u32[]{:S(2)}) collective-permute-start(f32[64,8,1]{2,1,0:T(8,128)S(1)} %slice.366), channel_id=1, source_target_pairs={{0,4},{4,8},{8,12},{1,5},{5,9},{9,13},{2,6},{6,10},{10,14},{3,7},{... | collective-permute-start | bytes 6152 | tf_op jit(solution)/shard_map/ppermute | solution.py:14
  53.7 9.5 %collective-permute-start.9 = (f32[64,1,128]{2,1,0:T(1,128)S(1)}, f32[64,1,128]{2,1,0:T(1,128)S(1)}, u32[]{:S(2)}, u32[]{:S(2)}) collective-permute-start(f32[64,1,128]{2,1,0:T(1,128)S(1)} %slice.363), channel_id=1, source_target_pairs={{0,16},{16,32},{32,48},{48,64},{64,80},{80,96},{96,112},{112,128},... | collective-permute-start | bytes 98312 | tf_op jit(solution)/shard_map/ppermute | solution.py:14
  63.3 0.8 %copy-done.9 = f32[64,8,128]{2,1,0:T(8,128)S(1)} copy-done((f32[64,8,128]{2,1,0:T(8,128)S(1)}, f32[64,8,128]{2,1,0:T(8,128)}, u32[]{:S(2)}) %copy-start.9) | copy-done | bytes 262168
  64.1 1.0 %pad_maximum_fusion.1 = f32[3,64,8,128]{3,2,1,0:T(8,128)} fusion(f32[1,64,8,128]{3,2,1,0:T(8,128)S(1)} %bitcast.226, f32[1,64,8,128]{3,2,1,0:T(8,128)S(1)} %bitcast.219, f32[1,64,8,128]{3,2,1,0:T(8,128)S(1)} %bitcast.217), kind=kLoop, calls=%fused_computation.2 | loop fusion | flops 393216 | bytes 1572864 | tf_op jit(solution)/shard_map/stack | solution.py:361
  65.3 0.9 %copy-done.2 = f32[3,64,8,128]{3,2,1,0:T(8,128)} copy-done((f32[3,64,8,128]{3,2,1,0:T(8,128)}, f32[3,64,8,128]{3,2,1,0:T(8,128)S(1)}, u32[]{:S(2)}) %copy-start.2) | copy-done | bytes 786456
  (79 shorter events, 3.4 us)
Async XLA Ops:
  2.4 1.0 %slice-start = ((f32[3,64,8,128]{3,2,1,0:T(8,128)}), f32[1,64,8,128]{3,2,1,0:T(8,128)S(1)}, s32[]{:S(2)}) async-start(f32[3,64,8,128]{3,2,1,0:T(8,128)} %h_ref.1), calls=%async_computation | async-start | bytes 524288 | tf_op jit(solution)/shard_map/slice | solution.py:257
  3.7 20.0 %collective-permute-start.3 = (f32[3,64,8,1]{1,2,3,0:T(8,128)S(1)}, f32[3,64,8,1]{1,2,3,0:T(8,128)S(1)}, u32[]{:S(2)}, u32[]{:S(2)}) collective-permute-start(f32[3,64,8,1]{1,2,3,0:T(8,128)S(1)} %pad_maximum_fusion.5), channel_id=1, source_target_pairs={{0,4},{4,8},{8,12},{1,5},{5,9},{9,13},{2,6},{6,10},{10,14},{3,7},{... | collective-permute-start | bytes 18440 | tf_op jit(solution)/shard_map/ppermute | solution.py:14
  7.6 23.3 %collective-permute-start.1 = (f32[3,64,1,128]{3,1,2,0:T(8,128)S(1)}, f32[3,64,1,128]{3,1,2,0:T(8,128)S(1)}, u32[]{:S(2)}, u32[]{:S(2)}) collective-permute-start(f32[3,64,1,128]{3,1,2,0:T(8,128)S(1)} %pad_maximum_fusion.3), channel_id=1, source_target_pairs={{0,16},{16,32},{32,48},{48,64},{64,80},{80,96},{96,112},{112,128},... | collective-permute-start | bytes 294920 | tf_op jit(solution)/shard_map/ppermute | solution.py:14
  12.7 7.8 %copy-start.4 = (s32[64,8,128]{2,1,0:T(8,128)S(1)}, s32[64,8,128]{2,1,0:T(8,128)}, u32[]{:S(2)}) copy-start(s32[64,8,128]{2,1,0:T(8,128)} %param.10) | copy-start | bytes 786436
  12.7 18.1 %collective-permute-start.2 = (f32[2,64,8,1]{3,2,1,0:T(8,128)S(1)}, f32[2,64,8,1]{3,2,1,0:T(8,128)S(1)}, u32[]{:S(2)}, u32[]{:S(2)}) collective-permute-start(f32[2,64,8,1]{3,2,1,0:T(8,128)S(1)} %copy.106), channel_id=1, source_target_pairs={{4,0},{8,4},{12,8},{5,1},{9,5},{13,9},{6,2},{10,6},{14,10},{7,3},{... | collective-permute-start | bytes 12296 | tf_op jit(solution)/shard_map/ppermute | solution.py:19
  14.8 5.6 %copy-start.16 = (s32[64]{0:T(128)S(1)}, s32[64]{0:T(128)}, u32[]{:S(2)}) copy-start(s32[64]{0:T(128)} %param.11) | copy-start | bytes 772
  14.8 16.0 %collective-permute-start = (f32[2,64,1,128]{3,1,2,0:T(8,128)S(1)}, f32[2,64,1,128]{3,1,2,0:T(8,128)S(1)}, u32[]{:S(2)}, u32[]{:S(2)}) collective-permute-start(f32[2,64,1,128]{3,1,2,0:T(8,128)S(1)} %pad_maximum_fusion.4), channel_id=1, source_target_pairs={{16,0},{32,16},{48,32},{64,48},{80,64},{96,80},{112,96},{128,112},... | collective-permute-start | bytes 196616 | tf_op jit(solution)/shard_map/ppermute | solution.py:19
  18.0 12.8 %collective-permute-start.4 = (f32[64,1,1]{2,1,0:T(1,128)S(1)}, f32[64,1,1]{2,1,0:T(1,128)S(1)}, u32[]{:S(2)}, u32[]{:S(2)}) collective-permute-start(f32[64,1,1]{2,1,0:T(1,128)S(1)} %slice.356), channel_id=1, source_target_pairs={{4,16},{8,20},{12,24},{20,32},{24,36},{28,40},{36,48},{40,52},{44,... | collective-permute-start | bytes 776 | tf_op jit(solution)/shard_map/ppermute | solution.py:31
  20.5 0.7 %copy-start.14 = (f32[4,8]{1,0:T(4,128)S(1)}, f32[4,8]{1,0:T(4,128)}, u32[]{:S(2)}) copy-start(f32[4,8]{1,0:T(4,128)} %param.13) | copy-start | bytes 388
  20.5 0.7 %copy-start.15 = (f32[4,8]{1,0:T(4,128)S(1)}, f32[4,8]{1,0:T(4,128)}, u32[]{:S(2)}) copy-start(f32[4,8]{1,0:T(4,128)} %param.12) | copy-start | bytes 388
  23.7 7.1 %collective-permute-start.5 = (f32[64,1,1]{2,1,0:T(1,128)S(1)}, f32[64,1,1]{2,1,0:T(1,128)S(1)}, u32[]{:S(2)}, u32[]{:S(2)}) collective-permute-start(f32[64,1,1]{2,1,0:T(1,128)S(1)} %slice.357), channel_id=1, source_target_pairs={{16,4},{20,8},{24,12},{32,20},{36,24},{40,28},{48,36},{52,40},{56,... | collective-permute-start | bytes 776 | tf_op jit(solution)/shard_map/ppermute | solution.py:31
  30.8 0.6 copy-start.12
  30.8 0.6 copy-start.13
  30.8 0.8 %copy-start.3 = (f32[2,64,8,1]{3,2,1,0:T(8,128)}, f32[2,64,8,1]{3,2,1,0:T(8,128)S(1)}, u32[]{:S(2)}) copy-start(f32[2,64,8,1]{3,2,1,0:T(8,128)S(1)} %collective-permute-done.2.yh_ref) | copy-start | bytes 12292
  30.9 0.8 %copy-start.11 = (f32[2,64,1,128]{3,1,2,0:T(8,128)}, f32[2,64,1,128]{3,1,2,0:T(8,128)S(1)}, u32[]{:S(2)}) copy-start(f32[2,64,1,128]{3,1,2,0:T(8,128)S(1)} %collective-permute-done) | copy-start | bytes 196612
  30.9 0.8 %copy-start.10 = (f32[3,64,1,128]{3,1,2,0:T(8,128)}, f32[3,64,1,128]{3,1,2,0:T(8,128)S(1)}, u32[]{:S(2)}) copy-start(f32[3,64,1,128]{3,1,2,0:T(8,128)S(1)} %collective-permute-done.1) | copy-start | bytes 294916
  36.0 9.3 %copy-start = (f32[3,64,8,128]{3,2,1,0:T(8,128)S(1)}, f32[3,64,8,128]{3,2,1,0:T(8,128)}, u32[]{:S(2)}) copy-start(f32[3,64,8,128]{3,2,1,0:T(8,128)} %e_ref.1) | copy-start | bytes 2359300
  36.0 5.6 %collective-permute-start.6 = (f32[12,8,128]{2,1,0:T(8,128)}, f32[12,8,128]{2,1,0:T(8,128)S(1)}, u32[]{:S(2)}, u32[]{:S(2)}) collective-permute-start(f32[12,8,128]{2,1,0:T(8,128)} %get-tuple-element.23), channel_id=1, source_target_pairs={{0,1},{1,2},{2,3},{3,0},{4,5},{5,6},{6,7},{7,4},{8,9},{9,10},{10,1... | collective-permute-start | bytes 147464 | tf_op jit(solution)/shard_map/ppermute | solution.py:281
  37.3 5.2 %collective-permute-start.7 = (f32[12,8,128]{2,1,0:T(8,128)}, f32[12,8,128]{2,1,0:T(8,128)S(1)}, u32[]{:S(2)}, u32[]{:S(2)}) collective-permute-start(f32[12,8,128]{2,1,0:T(8,128)} %get-tuple-element.23), channel_id=1, source_target_pairs={{0,2},{1,3},{2,0},{3,1},{4,6},{5,7},{6,4},{7,5},{8,10},{9,11},{10,... | collective-permute-start | bytes 147464 | tf_op jit(solution)/shard_map/ppermute | solution.py:281
  39.7 3.8 %collective-permute-start.8 = (f32[12,8,128]{2,1,0:T(8,128)}, f32[12,8,128]{2,1,0:T(8,128)S(1)}, u32[]{:S(2)}, u32[]{:S(2)}) collective-permute-start(f32[12,8,128]{2,1,0:T(8,128)} %get-tuple-element.23), channel_id=1, source_target_pairs={{0,3},{1,0},{2,1},{3,2},{4,7},{5,4},{6,5},{7,6},{8,11},{9,8},{10,9... | collective-permute-start | bytes 147464 | tf_op jit(solution)/shard_map/ppermute | solution.py:281
  45.1 1.0 %copy-start.7 = (f32[64,8,128]{2,1,0:T(8,128)S(1)}, f32[64,8,128]{2,1,0:T(8,128)}, u32[]{:S(2)}) copy-start(f32[64,8,128]{2,1,0:T(8,128)} %get-tuple-element.22) | copy-start | bytes 786436
  45.1 1.0 %copy-start.8 = (f32[64,8,128]{2,1,0:T(8,128)S(1)}, f32[64,8,128]{2,1,0:T(8,128)}, u32[]{:S(2)}) copy-start(f32[64,8,128]{2,1,0:T(8,128)} %get-tuple-element.26) | copy-start | bytes 786436
  46.2 1.3 %copy-start.5 = (f32[64,8,128]{2,1,0:T(8,128)S(1)}, f32[64,8,128]{2,1,0:T(8,128)}, u32[]{:S(2)}) copy-start(f32[64,8,128]{2,1,0:T(8,128)} %get-tuple-element.27) | copy-start | bytes 786436
  46.2 1.3 %copy-start.6 = (f32[64,8,128]{2,1,0:T(8,128)S(1)}, f32[64,8,128]{2,1,0:T(8,128)}, u32[]{:S(2)}) copy-start(f32[64,8,128]{2,1,0:T(8,128)} %get-tuple-element.28) | copy-start | bytes 786436
  47.4 1.1 %copy-start.1 = (f32[3,64,8,128]{3,2,1,0:T(8,128)S(1)}, f32[3,64,8,128]{3,2,1,0:T(8,128)}, u32[]{:S(2)}) copy-start(f32[3,64,8,128]{3,2,1,0:T(8,128)} %h_ref.1) | copy-start | bytes 2359300
  48.8 16.3 %collective-permute-start.10 = (f32[64,8,1]{2,1,0:T(8,128)S(1)}, f32[64,8,1]{2,1,0:T(8,128)S(1)}, u32[]{:S(2)}, u32[]{:S(2)}) collective-permute-start(f32[64,8,1]{2,1,0:T(8,128)S(1)} %slice.366), channel_id=1, source_target_pairs={{0,4},{4,8},{8,12},{1,5},{5,9},{9,13},{2,6},{6,10},{10,14},{3,7},{... | collective-permute-start | bytes 6152 | tf_op jit(solution)/shard_map/ppermute | solution.py:14
  53.7 11.4 %collective-permute-start.9 = (f32[64,1,128]{2,1,0:T(1,128)S(1)}, f32[64,1,128]{2,1,0:T(1,128)S(1)}, u32[]{:S(2)}, u32[]{:S(2)}) collective-permute-start(f32[64,1,128]{2,1,0:T(1,128)S(1)} %slice.363), channel_id=1, source_target_pairs={{0,16},{16,32},{32,48},{48,64},{64,80},{80,96},{96,112},{112,128},... | collective-permute-start | bytes 98312 | tf_op jit(solution)/shard_map/ppermute | solution.py:14
  63.2 1.0 %copy-start.9 = (f32[64,8,128]{2,1,0:T(8,128)S(1)}, f32[64,8,128]{2,1,0:T(8,128)}, u32[]{:S(2)}) copy-start(f32[64,8,128]{2,1,0:T(8,128)} %get-tuple-element.29) | copy-start | bytes 786436
  65.3 0.9 %copy-start.2 = (f32[3,64,8,128]{3,2,1,0:T(8,128)}, f32[3,64,8,128]{3,2,1,0:T(8,128)S(1)}, u32[]{:S(2)}) copy-start(f32[3,64,8,128]{3,2,1,0:T(8,128)S(1)} %fusion.7) | copy-start | bytes 2359300
